TPU v7x, 512 devices: a whole 4x4x16 slice. The times are simulated.
512 devices in a mesh: row: 32 (over y, x, core), col: 16 (over z).
Axes of the slice: x: 4, y: 4, z: 16, core: 2. Of those that a mesh axis runs over, the one named last changes fastest.
Arguments:
- ancestor_inverse: bfloat16 [8192, 8192], P('row', 'col'), may hold values from -6 to 6
- panel_one: bfloat16 [8192, 512], P(('row', 'col')), may hold values from -0.0625 to 0.0625
- ancestors_one: int32 [2, 28], replicated, may hold values from 0 to 31, as said below
- diag_inverse_one: bfloat16 [2, 256, 256], replicated, may hold values from -6 to 6
- panel_two: bfloat16 [8192, 512], P(('row', 'col')), may hold values from -0.0625 to 0.0625
- link_two: bfloat16 [2, 256, 256], replicated, may hold values from -0.375 to 0.375
- ancestors_two: int32 [2, 24], replicated, may hold values from 0 to 31, as said below
- diag_inverse_two: bfloat16 [2, 256, 256], replicated, may hold values from -6 to 6
- widths: int32 [4], replicated, may hold values from 128 to 256, as said below
Outputs:
- column_one: bfloat16 [8192, 512], P(('row', 'col'))
- block_one: bfloat16 [2, 256, 256], replicated
- column_two: bfloat16 [8192, 512], P(('row', 'col'))
- parent_rows_two: bfloat16 [2, 256, 256], replicated
- block_two: bfloat16 [2, 256, 256], replicated
Inputs may be any that keep to these rules, and one draw needn't show every extreme that they name: `ancestors_one`: each row lists 28 distinct tiles in ascending order; 0 and 31 are always among them. `ancestors_two`: row s lists 24 distinct entries of row s of ancestors_one in ascending order; 0 and 31 are always among them. `widths`: at least one supernode uses all 256 columns.
All inputs are finite; a program needn't handle non-finite values.
Results may differ from a plain program's by a relative error of at most 0.0055.
Values may be sent and summed in bfloat16 or wider, within the bound.
No kernel may reach another device: no remote copies, remote signals or barrier semaphores. Data moves between devices by JAX's collectives and lax.ppermute only.
A program may use at most 64 MiB of HBM per device.

v0:
```python
import jax
import jax.numpy as jnp
from jax import lax
from jax.sharding import PartitionSpec as P


def from_root(value, axis, source):
    kept = jnp.where(lax.axis_index(axis) == source, value, 0).astype(value.dtype)
    return lax.psum(kept, axis)


def tile_members(ancestors, first_row, row_count, tile_width):
    row_ids = first_row + jnp.arange(row_count, dtype=jnp.int32)
    tile_of_row = row_ids // tile_width
    matches = (ancestors[:, None, :] == tile_of_row[None, :, None]).astype(jnp.int32)
    return jnp.sum(matches, axis=2).astype(jnp.bfloat16)


def row_mask(members, keep_pair, tile_width):
    combined = members.T[:, :, None] * keep_pair[None, :, :]
    return combined.reshape(members.shape[1], 2 * tile_width)


def columns_in_order(share_block):
    whole_rows = lax.all_gather(share_block, "col", axis=0, tiled=True)
    per_group = lax.axis_size("row") // lax.axis_size("col")
    first_root = lax.axis_index("col") * per_group
    pieces = []
    for offset in range(per_group):
        pieces.append(from_root(whole_rows, "row", first_root + offset))
    return jnp.concatenate(pieces, axis=0)


def product_in_order(ancestor_inverse, lower_columns):
    return lax.psum_scatter(
        jnp.dot(ancestor_inverse, lower_columns, preferred_element_type=jnp.float32),
        "col",
        scatter_dimension=0,
        tiled=True,
    )


def local(
    ancestor_inverse,
    panel_one,
    ancestors_one,
    diag_inverse_one,
    panel_two,
    link_two,
    ancestors_two,
    diag_inverse_two,
    widths,
):
    tile_width = diag_inverse_one.shape[-1]
    local_rows = ancestor_inverse.shape[0]
    share_rows = panel_one.shape[0]
    share_start = lax.axis_index("row") * local_rows + lax.axis_index("col") * share_rows
    columns = jnp.arange(tile_width, dtype=jnp.int32)
    keep_columns = (columns[None, :] < widths[:, None]).astype(jnp.bfloat16)
    member_one = tile_members(ancestors_one, share_start, share_rows, tile_width)
    member_two = tile_members(ancestors_two, share_start, share_rows, tile_width)
    lower_one = panel_one * row_mask(member_one, keep_columns[0:2], tile_width)
    lower_two = panel_two * row_mask(member_two, keep_columns[2:4], tile_width)
    split_one = lower_one.reshape(share_rows, 2, tile_width)
    split_two = lower_two.reshape(share_rows, 2, tile_width)
    keep_parent = keep_columns[0:2]
    keep_child = keep_columns[2:4]
    pivot_one = diag_inverse_one.astype(jnp.float32) * (
        keep_parent[:, :, None] * keep_parent[:, None, :]
    ).astype(jnp.float32)
    pivot_two = diag_inverse_two.astype(jnp.float32) * (
        keep_child[:, :, None] * keep_child[:, None, :]
    ).astype(jnp.float32)
    link_masked = link_two * keep_parent[:, :, None] * keep_child[:, None, :]
    product_one = product_in_order(ancestor_inverse, columns_in_order(lower_one))
    view_one = product_one.reshape(share_rows, 2, tile_width)
    column_one = (-(view_one * member_one.T[:, :, None].astype(jnp.float32))).astype(jnp.bfloat16)
    diag_part = jnp.einsum(
        "isa,isb->sab", split_one, column_one, preferred_element_type=jnp.float32
    )
    diag_total = lax.psum(diag_part, ("row", "col"))
    block_one = (pivot_one - diag_total).astype(jnp.bfloat16)
    cross_part = jnp.einsum(
        "isa,isb->sab", column_one, split_two, preferred_element_type=jnp.float32
    )
    cross_total = lax.psum(cross_part, ("row", "col"))
    product_rest = product_in_order(ancestor_inverse, columns_in_order(lower_two))
    view_two = product_rest.reshape(share_rows, 2, tile_width)
    second_total = view_two + jnp.einsum(
        "isa,sab->isb", column_one, link_masked, preferred_element_type=jnp.float32
    )
    column_two = (-(second_total * member_two.T[:, :, None].astype(jnp.float32))).astype(
        jnp.bfloat16
    )
    lower_part = jnp.einsum(
        "isa,isb->sab", split_two, column_two, preferred_element_type=jnp.float32
    )
    lower_total = lax.psum(lower_part, ("row", "col"))
    parent_block = (
        -(
            jnp.einsum("sab,sbc->sac", block_one, link_masked, preferred_element_type=jnp.float32)
            + cross_total
        )
    ).astype(jnp.bfloat16)
    block_two = (
        pivot_two
        - jnp.einsum("sba,sbc->sac", link_masked, parent_block, preferred_element_type=jnp.float32)
        - lower_total
    ).astype(jnp.bfloat16)
    return (
        column_one.reshape(share_rows, 2 * tile_width),
        block_one,
        column_two.reshape(share_rows, 2 * tile_width),
        parent_block,
        block_two,
    )


def solution(mesh):
    in_specs = (
        P("row", "col"),
        P(("row", "col"), None),
        P(),
        P(),
        P(("row", "col"), None),
        P(),
        P(),
        P(),
        P(),
    )
    out_specs = (P(("row", "col"), None), P(), P(("row", "col"), None), P(), P())
    return jax.shard_map(local, mesh=mesh, in_specs=in_specs, out_specs=out_specs, check_vma=False)
```

profile of v0, /device:TPU:1, one launch (start us, length us, event | category | flops | bytes accessed | tf_op | source)
XLA Modules:
  0.0 839.4 jit_solution(12976401835930232403)
XLA Ops:
  7.2 0.0 all-reduce.7.cloned.1.call-start
  7.3 0.7 copy-done.10
  8.0 0.2 convert_reduce_fusion.1
  8.1 0.5 copy-done.11
  8.6 0.2 convert_reduce_fusion
  8.8 0.6 copy-done.12
  9.5 0.1 fusion.31
  9.6 0.1 copy.57
  9.7 0.1 copy.61
  9.8 0.1 mul.134
  9.9 0.1 mul.120
  10.0 0.7 copy-done.8
  10.7 30.6 %all_gather.6 = bf16[256,512]{1,0:T(8,128)(2,1)S(1)} all-gather(bf16[16,512]{1,0:T(8,128)(2,1)S(1)} %multiply_multiply_fusion.5), channel_id=1, replica_groups=mesh['row'=32,'col'=16] {'col'}, dimensions={0}, use_global_device_ids=true | all-gather | bytes 278528 | tf_op jit(solution)/shard_map/all_gather | solution.py:25
  41.3 20.6 %all_gather.7 = bf16[256,512]{1,0:T(8,128)(2,1)S(1)} all-gather(bf16[16,512]{1,0:T(8,128)(2,1)S(1)} %multiply_multiply_fusion.4), channel_id=1, replica_groups=mesh['row'=32,'col'=16] {'col'}, dimensions={0}, use_global_device_ids=true | all-gather | bytes 278528 | tf_op jit(solution)/shard_map/all_gather | solution.py:25
  61.9 0.8 broadcast_select_fusion.2
  62.8 0.8 broadcast_select_fusion.3
  63.6 0.0 all-reduce.7.cloned.1.call-update
  63.6 0.0 reduce-scatter.7.cloned.1.call-start
  63.7 147.0 %all-reduce.7.cloned.1.call-done = (bf16[256,512]{1,0:T(8,128)(2,1)}, bf16[256,512]{1,0:T(8,128)(2,1)}, bf16[256,512]{1,0:T(8,128)(2,1)}, bf16[256,512]{1,0:T(8,128)(2,1)}) async-done(((bf16[256,512]{1,0:T(8,128)(2,1)}, bf16[256,512]{1,0:T(8,128)(2,1)}, bf16[256,512]{1,0:T(8,128)(2,1)}, bf16[256,512]{1,0:T(8,128)(2,1)}), (bf16[256,512]{1,0:T(8,128)(2,1)}, bf16[256,512]{1,0:T(8,128)(2,1)}, ...) | async-done | bytes 1048592 | tf_op jit(solution)/shard_map/psum | solution.py:9
  210.7 1.4 convolution_bitcast_fusion.1
  212.1 1.0 copy.72
  213.1 0.0 reduce-scatter.7.cloned.1.call-update
  213.1 0.0 reduce-scatter.9.cloned.1.call-start
  213.2 0.9 copy-done.13
  214.1 0.1 copy-done.14
  214.1 0.4 convolution_bitcast_fusion
  214.5 1.0 copy.74
  215.5 0.0 all-reduce.5.cloned.1.call-start
  215.6 55.9 %reduce-scatter.7.cloned.1.call-done = f32[16,512]{1,0:T(8,128)} async-done(((f32[256,512]{1,0:T(8,128)}), f32[16,512]{1,0:T(8,128)}) %reduce-scatter.7.cloned.1.call-update) | async-done | bytes 32784
  271.4 0.9 copy.73
  272.3 0.1 copy.59
  272.4 68.7 %reduce-scatter.9.cloned.1.call-done = f32[16,512]{1,0:T(8,128)} async-done(((f32[256,512]{1,0:T(8,128)}), f32[16,512]{1,0:T(8,128)}) %reduce-scatter.9.cloned.1.call-update) | async-done | bytes 32784
  341.2 0.9 copy.75
  342.0 0.1 copy.63
  342.1 0.1 negate_convert_fusion
  342.2 1.1 fusion.26
  343.3 1.1 fusion.24
  344.4 0.3 fusion.7
  344.7 1.1 fusion.22
  345.8 0.7 copy.68
  346.5 0.6 copy.79
  347.1 482.2 %all-reduce.5.cloned.1.call-done = (f32[2,256,256]{2,1,0:T(8,128)}, f32[2,256,256]{2,1,0:T(8,128)}, f32[2,256,256]{2,1,0:T(8,128)}) async-done(((f32[2,256,256]{2,1,0:T(8,128)}, f32[2,256,256]{2,1,0:T(8,128)}, f32[2,256,256]{2,1,0:T(8,128)}), (f32[2,256,256]{2,1,0:T(8,128)}, f32[2,256,256]{2,1,0:T(8,128)}, f32[2,256,256]{2,1,0:T(8,128)})) %all-reduce.5.cloned.1.call-update) | async-done | bytes 1572880 | tf_op jit(solution)/shard_map/psum | solution.py:81
  829.3 1.2 subtract_convert_fusion
  830.6 0.3 fusion.3
  830.9 0.3 copy-done.2
  831.2 0.5 copy-done.5
  831.7 0.1 copy-done.7
  831.7 1.1 fusion.2
  (34 shorter events, 0.2 us)
Async XLA Ops:
  7.2 203.6 %copy-start = (bf16[256,512]{1,0:T(8,128)(2,1)S(1)}, bf16[256,512]{1,0:T(8,128)(2,1)}, u32[]{:S(2)}) copy-start(bf16[256,512]{1,0:T(8,128)(2,1)} %param.9) | copy-start | bytes 786436
  7.2 203.5 %all-reduce.7.cloned.1.call-start = ((), (), s32[]{:S(2)}) async-start(), calls=%async_computation.5 | async-start | bytes 2097152 | tf_op jit(solution)/shard_map/psum | solution.py:9
  7.2 0.7 copy-start.10
  7.9 0.7 copy-start.11
  8.8 0.7 copy-start.12
  10.0 0.7 copy-start.8
  10.7 30.6 %copy-start.9 = (bf16[16,512]{1,0:T(8,128)(2,1)S(1)}, bf16[16,512]{1,0:T(8,128)(2,1)}, u32[]{:S(2)}) copy-start(bf16[16,512]{1,0:T(8,128)(2,1)} %param.13) | copy-start | bytes 49156
  63.6 207.8 %reduce-scatter.7.cloned.1.call-start = ((), (), s32[]{:S(2)}) async-start(), calls=%async_computation.2 | async-start | bytes 557056
  213.1 0.9 copy-start.13
  213.1 1.0 copy-start.14
  213.1 128.0 %reduce-scatter.9.cloned.1.call-start = ((), (), s32[]{:S(2)}) async-start(), calls=%async_computation.3 | async-start | bytes 557056
  215.5 613.7 %all-reduce.5.cloned.1.call-start = ((), (), s32[]{:S(2)}) async-start(), calls=%async_computation.4 | async-start | bytes 3145728 | tf_op jit(solution)/shard_map/psum | solution.py:81
  343.3 1.1 copy-start.1
  345.8 483.5 %copy-start.6 = (bf16[2,256,256]{2,1,0:T(8,128)(2,1)S(1)}, bf16[2,256,256]{2,1,0:T(8,128)(2,1)}, u32[]{:S(2)}) copy-start(bf16[2,256,256]{2,1,0:T(8,128)(2,1)} %param.12) | copy-start | bytes 786436
  829.3 1.3 copy-start.4
  830.5 0.7 copy-start.2
  830.5 1.1 copy-start.5
  830.6 1.2 copy-start.7
  831.2 1.6 copy-start.3
Sparse Core Ops, SparseCore 0:
  63.7 146.9 all-reduce.6
  213.7 57.6 reduce-scatter.6
  274.2 66.8 reduce-scatter.8
  347.7 481.5 all-reduce.4
where the time goes:
time: 840 us; the launch traced here: 839 us
  waiting for transfers between devices  754 us (90%)
  blocking collectives  51.2 us (6%)
  between operations  14 us (2%)
  local copies, waits for them, and re-layouts  10 us (1%)
    psum x1, waiting for transfers between devices, local(): diag_total = lax.psum(diag_part, ('row', 'col'))  482 us
    psum x1, waiting for transfers between devices, from_root(): return lax.psum(kept, axis)  147 us
    unnamed x6, waiting for transfers between devices  125 us
    all_gather x2, blocking collectives, columns_in_order(): whole_rows = lax.all_gather(share_block, 'col', axis=0, tiled=True)  51.2 us
  transfers between devices with their start and end apart: 4, of which 4 were waited for; matrix products, arithmetic and copies ran while one was open for 0% of the time, Pallas kernels for 0%

commit v1 on v0

v1 whole, which is shorter than its diff:
```python
import jax
import jax.numpy as jnp
from jax import lax
from jax.sharding import PartitionSpec as P

F32 = jnp.float32
BF16 = jnp.bfloat16


def exchange(blocks, axis):
    return lax.all_to_all(blocks, axis, split_axis=0, concat_axis=0, tiled=True)


def spread(block, axis):
    copies = jnp.broadcast_to(block[None], (lax.axis_size(axis),) + block.shape)
    return exchange(copies, axis)


def tile_members(ancestors, first_row, row_count, tile_width):
    row_ids = first_row + jnp.arange(row_count, dtype=jnp.int32)
    tile_of_row = row_ids // tile_width
    matches = (ancestors[:, None, :] == tile_of_row[None, :, None]).astype(jnp.int32)
    return jnp.sum(matches, axis=2).astype(BF16)


def row_mask(members, keep_pair):
    combined = members.T[:, :, None] * keep_pair[None, :, :]
    return combined.reshape(members.shape[1], -1)


def dot_t(left, right):
    return lax.dot_general(left, right, (((0,), (0,)), ((), ())), preferred_element_type=F32)


def local(
    ancestor_inverse,
    panel_one,
    ancestors_one,
    diag_inverse_one,
    panel_two,
    link_two,
    ancestors_two,
    diag_inverse_two,
    widths,
):
    w = diag_inverse_one.shape[-1]
    rows_n = lax.axis_size("row")
    cols_n = lax.axis_size("col")
    local_rows = ancestor_inverse.shape[0]
    share = panel_one.shape[0]
    start = lax.axis_index("row") * local_rows + lax.axis_index("col") * share
    columns = jnp.arange(w, dtype=jnp.int32)
    keep = (columns[None, :] < widths[:, None]).astype(BF16)
    member_one = tile_members(ancestors_one, start, share, w)
    member_two = tile_members(ancestors_two, start, share, w)
    lower = jnp.concatenate(
        [panel_one * row_mask(member_one, keep[0:2]), panel_two * row_mask(member_two, keep[2:4])],
        axis=1,
    )
    group = rows_n // cols_n
    pairs = []
    for r in range(rows_n):
        for c in range(cols_n):
            pairs.append((r * cols_n + c, ((r % group) * cols_n + c) * cols_n + r // group))
    moved = lax.ppermute(lower, ("row", "col"), pairs)
    lower_rows = spread(lower, "col").reshape(local_rows, 4 * w)
    lower_cols = spread(moved, "row").reshape(rows_n * share, 4 * w)

    part = jnp.dot(ancestor_inverse, lower_cols, preferred_element_type=F32).astype(BF16)
    blocks = []
    for s in range(2):
        first = slice(s * w, (s + 1) * w)
        second = slice((2 + s) * w, (3 + s) * w)
        blocks.append(dot_t(lower_rows[:, first], part[:, first]))
        blocks.append(dot_t(lower_rows[:, second], part[:, first]))
        blocks.append(dot_t(lower_rows[:, second], part[:, second]))
    sums = jnp.stack(blocks).astype(BF16).reshape(rows_n, -1, w)
    sums = jnp.sum(exchange(sums, "row").astype(F32), axis=0).astype(BF16)
    chunk = sums.shape[0]

    part4 = part.reshape(cols_n, share, 4, w).transpose(0, 2, 1, 3).reshape(cols_n, 4 * share, w)
    packed = jnp.concatenate([jnp.broadcast_to(sums[None], (cols_n, chunk, w)), part4], axis=1)
    packed = jnp.sum(exchange(packed, "col").astype(F32), axis=0)
    total = spread(packed[:chunk].astype(BF16), "row").reshape(6, w, w)
    product = packed[chunk:].reshape(4, share, w)

    keep_parent, keep_child = keep[0:2], keep[2:4]
    link = link_two * keep_parent[:, :, None] * keep_child[:, None, :]
    column_one = []
    column_two = []
    block_one = []
    parent_rows = []
    block_two = []
    for s in range(2):
        one = -(product[s] * member_one[s][:, None].astype(F32))
        one = one.astype(BF16)
        two = product[2 + s] + jnp.dot(one, link[s], preferred_element_type=F32)
        two = (-(two * member_two[s][:, None].astype(F32))).astype(BF16)
        column_one.append(one)
        column_two.append(two)
        pivot_one = diag_inverse_one[s] * keep_parent[s][:, None] * keep_parent[s][None, :]
        pivot_two = diag_inverse_two[s] * keep_child[s][:, None] * keep_child[s][None, :]
        corner = total[3 * s].astype(F32)
        cross_t = total[3 * s + 1]
        last = total[3 * s + 2].astype(F32)
        block = (pivot_one.astype(F32) + corner).astype(BF16)
        parent = jnp.dot(block, link[s], preferred_element_type=F32) - cross_t.T.astype(F32)
        parent = (-parent).astype(BF16)
        child = pivot_two.astype(F32) + last
        child = child - jnp.dot(cross_t, link[s], preferred_element_type=F32)
        child = (child - dot_t(link[s], parent)).astype(BF16)
        block_one.append(block)
        parent_rows.append(parent)
        block_two.append(child)
    return (
        jnp.concatenate(column_one, axis=1),
        jnp.stack(block_one),
        jnp.concatenate(column_two, axis=1),
        jnp.stack(parent_rows),
        jnp.stack(block_two),
    )


def solution(mesh):
    shared = P(("row", "col"), None)
    in_specs = (P("row", "col"), shared, P(), P(), shared, P(), P(), P(), P())
    out_specs = (shared, P(), shared, P(), P())
    return jax.shard_map(local, mesh=mesh, in_specs=in_specs, out_specs=out_specs, check_vma=False)
```

time: 840 us -> 191 us (0.23)
  waiting for transfers between devices: 754 us -> 89 us
  starting transfers between devices: 0.16 us -> 46.6 us
  blocking collectives: 51.2 us -> 35 us
  between operations: 14 us -> 0.94 us
    psum x2 -> x0, waiting for transfers between devices: 629 us -> none  [the longest x1 482 us: local(): diag_total = lax.psum(diag_part, ('row', 'col'))]
    unnamed x6 -> x0, waiting for transfers between devices: 125 us -> none
    all_to_all x0 -> x4, waiting for transfers between devices: none -> 88 us  [exchange(): return lax.all_to_all(blocks, axis, split_axis=0, concat_axis=0, tiled=True)]
    all_gather x2 -> x0, blocking collectives: 51.2 us -> none  [columns_in_order(): whole_rows = lax.all_gather(share_block, 'col', axis=0, tiled=True)]
    all_to_all x0 -> x4, starting transfers between devices: none -> 40.4 us  [exchange(): return lax.all_to_all(blocks, axis, split_axis=0, concat_axis=0, tiled=True)]
    all_to_all x0 -> x1, blocking collectives: none -> 35 us  [exchange(): return lax.all_to_all(blocks, axis, split_axis=0, concat_axis=0, tiled=True)]
    unnamed x39 -> x14, local copies, waits for them, and re-layouts: 8.83 us -> 0.25 us
  transfers between devices with their start and end apart: 4 -> 5, of which waited for: 4 -> 5; matrix products, arithmetic and copies ran while one was open for 0% -> 2% of each run, Pallas kernels for 0% -> 0%
where the time goes in v1:
time: 191 us; the launch traced here: 190 us
  waiting for transfers between devices  89 us (47%)
  starting transfers between devices  46.6 us (24%)
  blocking collectives  35 us (18%)
  other arithmetic  8.38 us (4%)
  matrix products  7.23 us (4%)
  local copies, waits for them, and re-layouts  3.26 us (2%)
    all_to_all x4, waiting for transfers between devices, exchange(): return lax.all_to_all(blocks, axis, split_axis=0, concat_axis=0, tiled=True)  88 us
    all_to_all x4, starting transfers between devices, exchange(): return lax.all_to_all(blocks, axis, split_axis=0, concat_axis=0, tiled=True)  40.4 us
    all_to_all x1, blocking collectives, exchange(): return lax.all_to_all(blocks, axis, split_axis=0, concat_axis=0, tiled=True)  35 us
    ppermute x1, starting transfers between devices, local(): moved = lax.ppermute(lower, ('row', 'col'), pairs)  6.21 us
    dot_general x8, matrix products, dot_t(): lax.dot_general(left, right, (((0,), (0,)), ((), ())), preferred_element_...  5.72 us
  transfers between devices with their start and end apart: 5, of which 5 were waited for; matrix products, arithmetic and copies ran while one was open for 2% of the time, Pallas kernels for 0%

profile of v1, /device:TPU:1, one launch (start us, length us, event | category | flops | bytes accessed | tf_op | source)
XLA Modules:
  0.0 190.5 jit_solution(1174360394311973205)
XLA Ops:
  0.7 0.9 convert_reduce_fusion.2
  1.6 0.1 copy.32
  1.8 0.9 convert_reduce_fusion.1
  2.9 0.7 fusion.49
  3.6 0.7 multiply_multiply_fusion.1
  4.4 6.2 %collective-permute-start = (bf16[16,1024]{1,0:T(8,128)(2,1)S(1)}, bf16[16,1024]{1,0:T(8,128)(2,1)S(1)}, u32[]{:S(2)}, u32[]{:S(2)}) collective-permute-start(bf16[16,1024]{1,0:T(8,128)(2,1)S(1)} %pad_maximum_fusion.4), channel_id=1, source_target_pairs={{0,0},{1,16},{2,32},{3,48},{4,64},{5,80},{6,96},{7,112},{8,128},{9... | collective-permute-start | bytes 98312 | tf_op jit(solution)/shard_map/ppermute | solution.py:65
  10.6 1.0 collective-permute-done
  11.6 0.1 broadcast_in_dim.9
  11.7 35.0 %all_to_all.25 = bf16[32,16,1024]{2,1,0:T(8,128)(2,1)S(1)} all-to-all(bf16[32,16,1024]{2,1,0:T(8,128)(2,1)S(1)} %broadcast_in_dim.9), channel_id=1, replica_groups=mesh['row'=32,'col'=16] {'row'}, dimensions={0} | all-to-all | bytes 2097152 | tf_op jit(solution)/shard_map/all_to_all | solution.py:11
  46.8 0.8 broadcast_in_dim.8
  47.6 12.9 %all-to-all-start = ((bf16[16,16,1024]{2,1,0:T(8,128)(2,1)}), bf16[16,16,1024]{2,1,0:T(8,128)(2,1)S(1)}, u32[]{:S(2)}, u32[]{:S(2)}) async-start(bf16[16,16,1024]{2,1,0:T(8,128)(2,1)} %broadcast_in_dim.8), calls=%async_computation | async-start | bytes 1048576 | tf_op jit(solution)/shard_map/all_to_all | solution.py:11
  60.5 0.5 fusion
  61.0 22.3 %all-to-all-done = bf16[16,16,1024]{2,1,0:T(8,128)(2,1)S(1)} async-done(((bf16[16,16,1024]{2,1,0:T(8,128)(2,1)}), bf16[16,16,1024]{2,1,0:T(8,128)(2,1)S(1)}, u32[]{:S(2)}, u32[]{:S(2)}) %all-to-all-start) | async-done | bytes 524320 | tf_op jit(solution)/shard_map/all_to_all | solution.py:11
  83.3 0.9 fusion.10
  84.1 0.9 fusion.12
  85.0 0.9 fusion.14
  85.9 0.9 fusion.16
  86.8 0.9 fusion.18
  87.7 0.9 fusion.20
  88.5 10.7 %all-to-all-start.2 = ((bf16[32,48,256]{2,1,0:T(8,128)(2,1)}), bf16[32,48,256]{2,1,0:T(8,128)(2,1)S(1)}, u32[]{:S(2)}, u32[]{:S(2)}) async-start(bf16[32,48,256]{2,1,0:T(8,128)(2,1)} %bitcast.11), calls=%async_computation.2 | async-start | bytes 1572864 | tf_op jit(solution)/shard_map/all_to_all | solution.py:11
  99.3 0.2 copy.34
  99.5 0.4 reshape.185
  100.0 13.7 %all-to-all-done.2 = bf16[32,48,256]{2,1,0:T(8,128)(2,1)S(1)} async-done(((bf16[32,48,256]{2,1,0:T(8,128)(2,1)}), bf16[32,48,256]{2,1,0:T(8,128)(2,1)S(1)}, u32[]{:S(2)}, u32[]{:S(2)}) %all-to-all-start.2) | async-done | bytes 786464 | tf_op jit(solution)/shard_map/all_to_all | solution.py:11
  113.6 0.1 reduce_sum.41
  113.8 1.0 pad_maximum_fusion
  114.8 6.3 %all-to-all-start.3 = ((bf16[16,112,256]{2,1,0:T(8,128)(2,1)}), bf16[16,112,256]{2,1,0:T(8,128)(2,1)S(1)}, u32[]{:S(2)}, u32[]{:S(2)}) async-start(bf16[16,112,256]{2,1,0:T(8,128)(2,1)} %pad_maximum_fusion), calls=%async_computation.3 | async-start | bytes 1835008 | tf_op jit(solution)/shard_map/all_to_all | solution.py:11
  121.1 0.1 multiply_multiply_fusion
  121.3 39.5 %all-to-all-done.3 = bf16[16,112,256]{2,1,0:T(8,128)(2,1)S(1)} async-done(((bf16[16,112,256]{2,1,0:T(8,128)(2,1)}), bf16[16,112,256]{2,1,0:T(8,128)(2,1)S(1)}, u32[]{:S(2)}, u32[]{:S(2)}) %all-to-all-start.3) | async-done | bytes 917536 | tf_op jit(solution)/shard_map/all_to_all | solution.py:11
  160.7 0.1 convert_reduce_fusion
  160.9 0.9 broadcast_in_dim.11
  161.8 10.5 %all-to-all-start.4 = ((bf16[32,48,256]{2,1,0:T(8,128)(2,1)}), bf16[32,48,256]{2,1,0:T(8,128)(2,1)S(1)}, u32[]{:S(2)}, u32[]{:S(2)}) async-start(bf16[32,48,256]{2,1,0:T(8,128)(2,1)} %broadcast_in_dim.11), calls=%async_computation.4 | async-start | bytes 1572864 | tf_op jit(solution)/shard_map/all_to_all | solution.py:11
  172.4 0.6 pad_maximum_fusion.5
  173.0 0.1 fusion.25
  173.1 0.2 fusion.26
  173.3 0.7 pad_maximum_fusion.6
  173.9 12.6 %all-to-all-done.4 = bf16[32,48,256]{2,1,0:T(8,128)(2,1)S(1)} async-done(((bf16[32,48,256]{2,1,0:T(8,128)(2,1)}), bf16[32,48,256]{2,1,0:T(8,128)(2,1)S(1)}, u32[]{:S(2)}, u32[]{:S(2)}) %all-to-all-start.4) | async-done | bytes 786464 | tf_op jit(solution)/shard_map/all_to_all | solution.py:11
  186.6 0.1 copy.38
  186.7 0.1 copy.39
  186.8 0.2 add_convert_fusion.1
  187.0 0.2 fusion.3
  187.2 0.7 pad_maximum_fusion.1
  187.9 0.2 fusion.4
  188.1 0.2 convolution_subtract_fusion.3
  188.3 0.2 convolution_subtract_fusion.1
  188.5 0.2 fusion.8
  188.8 0.2 fusion.7
  189.0 0.7 pad_maximum_fusion.3
  189.7 0.7 pad_maximum_fusion.2
  (30 shorter events, 0.6 us)
Async XLA Ops:
  0.6 59.9 %copy-start = (bf16[256,512]{1,0:T(8,128)(2,1)S(1)}, bf16[256,512]{1,0:T(8,128)(2,1)}, u32[]{:S(2)}) copy-start(bf16[256,512]{1,0:T(8,128)(2,1)} %param.9) | copy-start | bytes 786436
  4.4 7.2 %collective-permute-start = (bf16[16,1024]{1,0:T(8,128)(2,1)S(1)}, bf16[16,1024]{1,0:T(8,128)(2,1)S(1)}, u32[]{:S(2)}, u32[]{:S(2)}) collective-permute-start(bf16[16,1024]{1,0:T(8,128)(2,1)S(1)} %pad_maximum_fusion.4), channel_id=1, source_target_pairs={{0,0},{1,16},{2,32},{3,48},{4,64},{5,80},{6,96},{7,112},{8,128},{9... | collective-permute-start | bytes 98312 | tf_op jit(solution)/shard_map/ppermute | solution.py:65
  47.6 35.7 %all-to-all-start = ((bf16[16,16,1024]{2,1,0:T(8,128)(2,1)}), bf16[16,16,1024]{2,1,0:T(8,128)(2,1)S(1)}, u32[]{:S(2)}, u32[]{:S(2)}) async-start(bf16[16,16,1024]{2,1,0:T(8,128)(2,1)} %broadcast_in_dim.8), calls=%async_computation | async-start | bytes 1048576 | tf_op jit(solution)/shard_map/all_to_all | solution.py:11
  88.5 25.1 %all-to-all-start.2 = ((bf16[32,48,256]{2,1,0:T(8,128)(2,1)}), bf16[32,48,256]{2,1,0:T(8,128)(2,1)S(1)}, u32[]{:S(2)}, u32[]{:S(2)}) async-start(bf16[32,48,256]{2,1,0:T(8,128)(2,1)} %bitcast.11), calls=%async_computation.2 | async-start | bytes 1572864 | tf_op jit(solution)/shard_map/all_to_all | solution.py:11
  114.8 6.4 %copy-start.2 = (bf16[2,256,256]{2,1,0:T(8,128)(2,1)S(1)}, bf16[2,256,256]{2,1,0:T(8,128)(2,1)}, u32[]{:S(2)}) copy-start(bf16[2,256,256]{2,1,0:T(8,128)(2,1)} %param.14) | copy-start | bytes 786436
  114.8 46.0 %all-to-all-start.3 = ((bf16[16,112,256]{2,1,0:T(8,128)(2,1)}), bf16[16,112,256]{2,1,0:T(8,128)(2,1)S(1)}, u32[]{:S(2)}, u32[]{:S(2)}) async-start(bf16[16,112,256]{2,1,0:T(8,128)(2,1)} %pad_maximum_fusion), calls=%async_computation.3 | async-start | bytes 1835008 | tf_op jit(solution)/shard_map/all_to_all | solution.py:11
  161.8 24.7 %all-to-all-start.4 = ((bf16[32,48,256]{2,1,0:T(8,128)(2,1)}), bf16[32,48,256]{2,1,0:T(8,128)(2,1)S(1)}, u32[]{:S(2)}, u32[]{:S(2)}) async-start(bf16[32,48,256]{2,1,0:T(8,128)(2,1)} %broadcast_in_dim.11), calls=%async_computation.4 | async-start | bytes 1572864 | tf_op jit(solution)/shard_map/all_to_all | solution.py:11
  172.3 14.5 %copy-start.1 = (bf16[2,256,256]{2,1,0:T(8,128)(2,1)S(1)}, bf16[2,256,256]{2,1,0:T(8,128)(2,1)}, u32[]{:S(2)}) copy-start(bf16[2,256,256]{2,1,0:T(8,128)(2,1)} %param.12) | copy-start | bytes 786436
  186.8 1.3 copy-start.3

commit v2 on v1

v2 whole, which is shorter than its diff:
```python
import functools

import jax
import jax.numpy as jnp
from jax import lax
from jax.experimental import pallas as pl
from jax.experimental.pallas import tpu as pltpu
from jax.sharding import PartitionSpec as P

F32 = jnp.float32
BF16 = jnp.bfloat16
VMEM = pl.BlockSpec(memory_space=pltpu.VMEM)
SMEM = pl.BlockSpec(memory_space=pltpu.SMEM)


def kernel_call(body, name, specs, outs, cost=(0, 0)):
    return pl.pallas_call(
        body,
        name=name,
        in_specs=specs,
        out_specs=[VMEM] * len(outs),
        out_shape=[jax.ShapeDtypeStruct(shape, BF16) for shape in outs],
        compiler_params=pltpu.CompilerParams(vmem_limit_bytes=40 * 1024 * 1024),
        cost_estimate=pl.CostEstimate(flops=cost[0], bytes_accessed=cost[1], transcendentals=0),
    )


def exchange(blocks, axis):
    return lax.all_to_all(blocks, axis, split_axis=0, concat_axis=0, tiled=True)


def dot(left, right):
    return jnp.dot(left, right, preferred_element_type=F32)


def dot_t(left, right):
    return lax.dot_general(left, right, (((0,), (0,)), ((), ())), preferred_element_type=F32)


def is_member(table, s, tile):
    found = table[s, 0] == tile
    for i in range(1, table.shape[1]):
        found = found | (table[s, i] == tile)
    return found


def mask_body(w, tile, one, two, anc_one, anc_two, widths, lower):
    column = lax.broadcasted_iota(jnp.int32, (one.shape[0], w), 1)
    for k in range(4):
        source, table, s = (one, anc_one, k) if k < 2 else (two, anc_two, k - 2)
        width = jnp.where(is_member(table, s, tile[0]), widths[k], 0)
        value = source[:, s * w : (s + 1) * w]
        lower[:, k * w : (k + 1) * w] = jnp.where(column < width, value, jnp.zeros_like(value))


def product_body(w, core, same, other, lower, part):
    share = part.shape[1]
    half = same.shape[0] // share
    for source, place in ((same, core[0] * half), (other, (1 - core[0]) * half)):
        for k in range(4):
            span = slice(k * w, (k + 1) * w)
            value = dot(source[...], lower[:, span]).astype(BF16)
            part[pl.ds(place, half), :, span] = value.reshape(half, share, w)


def reduced(received):
    total = received[0].astype(F32)
    for i in range(1, received.shape[0]):
        total = total + received[i].astype(F32)
    return total


def row_sum_body(received, copies):
    value = reduced(received).astype(BF16)
    for i in range(copies.shape[0]):
        copies[i] = value


def col_sum_body(received, pivot, copies):
    value = (reduced(received) + pivot[...].astype(F32)).astype(BF16)
    for i in range(copies.shape[0]):
        copies[i] = value


def masked_link(w, link, widths, s):
    row = lax.broadcasted_iota(jnp.int32, (w, w), 0)
    column = lax.broadcasted_iota(jnp.int32, (w, w), 1)
    value = link[s]
    inside = (row < widths[s]) & (column < widths[2 + s])
    return jnp.where(inside, value, jnp.zeros_like(value))


def column_body(w, tile, received, lower, link, anc_one, anc_two, widths, columns, sums):
    total = reduced(received)
    for s in range(2):
        first = slice(s * w, (s + 1) * w)
        second = slice((2 + s) * w, (3 + s) * w)
        here_one = jnp.where(is_member(anc_one, s, tile[0]), 1.0, 0.0)
        here_two = jnp.where(is_member(anc_two, s, tile[0]), 1.0, 0.0)
        one = (-(total[:, first] * here_one)).astype(BF16)
        two = total[:, second] + dot(one, masked_link(w, link, widths, s))
        two = (-(two * here_two)).astype(BF16)
        columns[:, first] = one
        columns[:, second] = two
        sums[3 * s] = (-dot_t(lower[:, first], one)).astype(BF16)
        sums[3 * s + 1] = dot_t(one, lower[:, second]).astype(BF16)
        sums[3 * s + 2] = (-dot_t(lower[:, second], two)).astype(BF16)


def final_body(w, total, link, widths, block_one, parent_rows, block_two):
    for s in range(2):
        tie = masked_link(w, link, widths, s)
        block = total[3 * s]
        block_one[s] = block
        parent = (-(dot(block, tie) + total[3 * s + 1].astype(F32))).astype(BF16)
        parent_rows[s] = parent
        block_two[s] = (total[3 * s + 2].astype(F32) - dot_t(tie, parent)).astype(BF16)


def local(
    ancestor_inverse,
    panel_one,
    ancestors_one,
    diag_inverse_one,
    panel_two,
    link_two,
    ancestors_two,
    diag_inverse_two,
    widths,
):
    w = diag_inverse_one.shape[-1]
    rows_n = lax.axis_size("row")
    cols_n = lax.axis_size("col")
    local_rows = ancestor_inverse.shape[0]
    share = panel_one.shape[0]
    group = rows_n // cols_n
    row, col = lax.axis_index("row"), lax.axis_index("col")
    core = (row % group).astype(jnp.int32)
    home_tile = row.astype(jnp.int32).reshape(1)
    away_tile = (col * group + row // cols_n).astype(jnp.int32).reshape(1)

    same_pairs, other_pairs, out_pairs, back_pairs = [], [], [], []
    for r in range(rows_n):
        for c in range(cols_n):
            here, core_r = r * cols_n + c, r % group
            same_pairs.append((here, (c * group + core_r) * cols_n + r // group))
            other_pairs.append((here, (c * group + 1 - core_r) * cols_n + r // group))
            away = (core_r * cols_n + c) * cols_n + r // group
            out_pairs.append((here, away))
            back_pairs.append((away, here))
    both = ("row", "col")
    same = lax.dynamic_slice_in_dim(ancestor_inverse, core * w, w, axis=1)
    other = lax.dynamic_slice_in_dim(ancestor_inverse, (1 - core) * w, w, axis=1)
    same = lax.ppermute(same, both, same_pairs)
    other = lax.ppermute(other, both, other_pairs)

    (lower,) = kernel_call(
        functools.partial(mask_body, w),
        "mask",
        [SMEM, VMEM, VMEM, SMEM, SMEM, SMEM],
        [(share, 4 * w)],
    )(home_tile, panel_one, panel_two, ancestors_one, ancestors_two, widths)
    moved = lax.ppermute(lower, both, out_pairs)
    lower_tile = lax.all_gather(lower, "col", axis=0, tiled=True)

    (part,) = kernel_call(
        functools.partial(product_body, w),
        "product",
        [SMEM] + [VMEM] * 3,
        [(rows_n, share, 4 * w)],
    )(core.reshape(1), same, other, lower_tile)
    part = exchange(part, "row")
    columns, sums = kernel_call(
        functools.partial(column_body, w),
        "columns",
        [SMEM, VMEM, VMEM, VMEM, SMEM, SMEM, SMEM],
        [(share, 4 * w), (6, w, w)],
    )(away_tile, part, moved, link_two, ancestors_one, ancestors_two, widths)
    columns = lax.ppermute(columns, both, back_pairs)

    chunk = 6 * w // rows_n
    sums = exchange(sums.reshape(rows_n, chunk, w), "row")
    (sum_copies,) = kernel_call(row_sum_body, "row_sum", [VMEM], [(cols_n, chunk, w)])(sums)
    sums = exchange(sum_copies, "col")

    keep = (jnp.arange(w, dtype=jnp.int32)[None, :] < widths[:, None]).astype(BF16)
    pivot_one = diag_inverse_one * keep[0:2, :, None] * keep[0:2, None, :]
    pivot_two = diag_inverse_two * keep[2:4, :, None] * keep[2:4, None, :]
    pivots = jnp.stack([pivot_one, jnp.zeros_like(pivot_one), pivot_two], axis=1)
    pivot = lax.dynamic_slice_in_dim(
        pivots.reshape(6 * w, w), lax.axis_index("row") * chunk, chunk, axis=0
    )
    (total_copies,) = kernel_call(col_sum_body, "col_sum", [VMEM] * 2, [(rows_n, chunk, w)])(
        sums, pivot
    )
    total = exchange(total_copies, "row").reshape(6, w, w)

    block_one, parent_rows, block_two = kernel_call(
        functools.partial(final_body, w), "final", [VMEM, VMEM, SMEM], [(2, w, w)] * 3
    )(total, link_two, widths)
    return columns[:, : 2 * w], block_one, columns[:, 2 * w :], parent_rows, block_two


def solution(mesh):
    shared = P(("row", "col"), None)
    in_specs = (P("row", "col"), shared, P(), P(), shared, P(), P(), P(), P())
    out_specs = (shared, P(), shared, P(), P())
    return jax.shard_map(local, mesh=mesh, in_specs=in_specs, out_specs=out_specs, check_vma=False)
```

time: 191 us -> 199 us (1.042); the launches traced: 190 us -> 196 us
  blocking collectives: 35 us -> 88.7 us
  waiting for transfers between devices: 89 us -> 41.1 us
  starting transfers between devices: 46.6 us -> 56 us
  other arithmetic: 8.38 us -> 0.41 us
  matrix products: 7.23 us -> 0 us
  Pallas kernels: 0 us -> 6.81 us
    all_gather x0 -> x1, blocking collectives: none -> 67.3 us  [local(): lower_tile = lax.all_gather(lower, 'col', axis=0, tiled=True)]
    all_to_all x4 -> x3, waiting for transfers between devices: 88 us -> 29.6 us  [exchange(): return lax.all_to_all(blocks, axis, split_axis=0, concat_axis=0, tiled=True)]
    all_to_all x1, blocking collectives: 35 us -> 21.4 us  [exchange(): return lax.all_to_all(blocks, axis, split_axis=0, concat_axis=0, tiled=True)]
    ppermute x1 -> x4, waiting for transfers between devices: 1 us -> 11.5 us  [the longest x1 6.88 us: local(): columns = lax.ppermute(columns, both, back_pairs)]
    ppermute x1 -> x4, starting transfers between devices: 6.21 us -> 16.6 us  [the longest x1 8.92 us: local(): other = lax.ppermute(other, both, other_pairs)]
    dot_general x15 -> x0, matrix products: 7.23 us -> none  [the longest x8 5.72 us: dot_t(): lax.dot_general(left, right, (((0,), (0,)), ((), ())), preferred_element_...]
    pallas_call x0 -> x6, Pallas kernels: none -> 6.81 us  [the longest x1 1.74 us: local(): kernel_call(functools.partial(final_body, w), 'final', [VMEM, VMEM, SMEM]...]
    concatenate x4 -> x0, other arithmetic: 2.27 us -> none  [the longest x1 0.99 us: local(): jnp.concatenate([jnp.broadcast_to(sums[None], (cols_n, chunk, w)), part4]...]
  transfers between devices with their start and end apart: 5 -> 7, of which waited for: 5 -> 5; matrix products, arithmetic and copies ran while one was open for 2% -> 1% of each run, Pallas kernels for 0% -> 0%
where the time goes in v2:
time: 199 us; the launch traced here: 196 us
  blocking collectives  88.7 us (45%)
  starting transfers between devices  56 us (28%)
  waiting for transfers between devices  41.1 us (21%)
  Pallas kernels  6.81 us (3%)
    all_gather x1, blocking collectives, local(): lower_tile = lax.all_gather(lower, 'col', axis=0, tiled=True)  67.3 us
    all_to_all x3, starting transfers between devices, exchange(): return lax.all_to_all(blocks, axis, split_axis=0, concat_axis=0, tiled=True)  39.4 us
    all_to_all x3, waiting for transfers between devices, exchange(): return lax.all_to_all(blocks, axis, split_axis=0, concat_axis=0, tiled=True)  29.6 us
    all_to_all x1, blocking collectives, exchange(): return lax.all_to_all(blocks, axis, split_axis=0, concat_axis=0, tiled=True)  21.4 us
    ppermute x1, starting transfers between devices, local(): other = lax.ppermute(other, both, other_pairs)  8.92 us
    ppermute x1, waiting for transfers between devices, local(): columns = lax.ppermute(columns, both, back_pairs)  6.88 us
    ppermute x1, starting transfers between devices, local(): moved = lax.ppermute(lower, both, out_pairs)  5.05 us
    ppermute x1, waiting for transfers between devices, local(): moved = lax.ppermute(lower, both, out_pairs)  4.64 us
  transfers between devices with their start and end apart: 7, of which 5 were waited for; matrix products, arithmetic and copies ran while one was open for 1% of the time, Pallas kernels for 0%

profile of v2, /device:TPU:1, one launch (start us, length us, event | category | flops | bytes accessed | tf_op | source)
XLA Modules:
  0.0 195.6 jit_solution(431152164049464440)
XLA Ops:
  0.7 0.0 copy-start.1
  0.7 0.0 copy-start.2
  0.7 1.0 constant_dynamic-slice_fusion.1
  1.7 0.7 collective-permute-start
  2.4 0.0 copy-start.5
  2.4 0.0 copy-start.3
  2.4 0.0 copy-start.4
  2.4 8.9 %collective-permute-start.1 = (bf16[256,256]{1,0:T(8,128)(2,1)S(1)}, bf16[256,256]{1,0:T(8,128)(2,1)S(1)}, u32[]{:S(2)}, u32[]{:S(2)}) collective-permute-start(bf16[256,256]{1,0:T(8,128)(2,1)S(1)} %get-tuple-element.15), channel_id=1, source_target_pairs={{0,16},{1,48},{2,80},{3,112},{4,144},{5,176},{6,208},{7,240},{8,27... | collective-permute-start | bytes 393224 | tf_op jit(solution)/shard_map/ppermute | solution.py:155
  11.3 0.0 copy-done.1
  11.3 0.0 copy-done.2
  11.3 0.0 copy-done.5
  11.3 0.0 copy-done.3
  11.4 0.0 copy-done.4
  11.4 0.7 mask.1
  12.0 67.3 %all_gather.3.lower = bf16[256,1024]{1,0:T(8,128)(2,1)S(1)} all-gather(bf16[16,1024]{1,0:T(8,128)(2,1)S(1)} %mask.1), channel_id=1, replica_groups=mesh['row'=32,'col'=16] {'col'}, dimensions={0}, use_global_device_ids=true | all-gather | bytes 557056 | tf_op jit(solution)/shard_map/all_gather | solution.py:164
  79.3 0.0 collective-permute-done.same
  79.3 0.0 collective-permute-done.1.other
  79.3 1.4 product.1
  80.8 0.0 copy-start
  80.8 23.1 %all-to-all-start = ((bf16[32,16,1024]{2,1,0:T(8,128)(2,1)}), bf16[32,16,1024]{2,1,0:T(8,128)(2,1)S(1)}, u32[]{:S(2)}, u32[]{:S(2)}) async-start(bf16[32,16,1024]{2,1,0:T(8,128)(2,1)} %product.1), calls=%async_computation | async-start | bytes 2097152 | tf_op jit(solution)/shard_map/all_to_all | solution.py:29
  103.9 5.1 %collective-permute-start.2 = (bf16[16,1024]{1,0:T(8,128)(2,1)S(1)}, bf16[16,1024]{1,0:T(8,128)(2,1)S(1)}, u32[]{:S(2)}, u32[]{:S(2)}) collective-permute-start(bf16[16,1024]{1,0:T(8,128)(2,1)S(1)} %mask.1), channel_id=1, source_target_pairs={{0,0},{1,16},{2,32},{3,48},{4,64},{5,80},{6,96},{7,112},{8,128},{9... | collective-permute-start | bytes 98312 | tf_op jit(solution)/shard_map/ppermute | solution.py:163
  109.0 4.6 %collective-permute-done.2.lower = bf16[16,1024]{1,0:T(8,128)(2,1)S(1)} collective-permute-done((bf16[16,1024]{1,0:T(8,128)(2,1)S(1)}, bf16[16,1024]{1,0:T(8,128)(2,1)S(1)}, u32[]{:S(2)}, u32[]{:S(2)}) %collective-permute-start.2) | collective-permute-done | bytes 32800 | tf_op jit(solution)/shard_map/ppermute | solution.py:163
  113.6 7.6 %all-to-all-done.received = bf16[32,16,1024]{2,1,0:T(8,128)(2,1)S(1)} async-done(((bf16[32,16,1024]{2,1,0:T(8,128)(2,1)}), bf16[32,16,1024]{2,1,0:T(8,128)(2,1)S(1)}, u32[]{:S(2)}, u32[]{:S(2)}) %all-to-all-start) | async-done | bytes 1048608 | tf_op jit(solution)/shard_map/all_to_all | solution.py:29
  121.2 0.0 copy-done
  121.2 1.1 columns.1
  122.3 21.4 %all_to_all.20.received = bf16[32,48,256]{2,1,0:T(8,128)(2,1)S(1)} all-to-all(bf16[32,48,256]{2,1,0:T(8,128)(2,1)S(1)} %bitcast.12), channel_id=1, replica_groups=mesh['row'=32,'col'=16] {'row'}, dimensions={0} | all-to-all | bytes 1572864 | tf_op jit(solution)/shard_map/all_to_all | solution.py:29
  143.8 0.9 row_sum.1
  144.6 0.0 copy-start.6
  144.6 0.0 copy-start.7
  144.6 4.5 %all-to-all-start.2 = ((bf16[16,48,256]{2,1,0:T(8,128)(2,1)}), bf16[16,48,256]{2,1,0:T(8,128)(2,1)S(1)}, u32[]{:S(2)}, u32[]{:S(2)}) async-start(bf16[16,48,256]{2,1,0:T(8,128)(2,1)} %row_sum.1), calls=%async_computation.2 | async-start | bytes 786432 | tf_op jit(solution)/shard_map/all_to_all | solution.py:29
  149.2 0.1 pad.1.clone
  149.2 0.1 fusion
  149.3 0.0 copy-done.6
  149.3 0.0 copy-done.7
  149.3 0.2 multiply_bitcast_fusion
  149.5 0.1 pad_maximum_fusion
  149.7 0.1 copy.14
  149.7 17.2 %all-to-all-done.2.received = bf16[16,48,256]{2,1,0:T(8,128)(2,1)S(1)} async-done(((bf16[16,48,256]{2,1,0:T(8,128)(2,1)}), bf16[16,48,256]{2,1,0:T(8,128)(2,1)S(1)}, u32[]{:S(2)}, u32[]{:S(2)}) %all-to-all-start.2) | async-done | bytes 393248 | tf_op jit(solution)/shard_map/all_to_all | solution.py:29
  167.0 1.0 col_sum.1
  167.9 11.7 %all-to-all-start.3 = ((bf16[32,48,256]{2,1,0:T(8,128)(2,1)}), bf16[32,48,256]{2,1,0:T(8,128)(2,1)S(1)}, u32[]{:S(2)}, u32[]{:S(2)}) async-start(bf16[32,48,256]{2,1,0:T(8,128)(2,1)} %col_sum.1), calls=%async_computation.3 | async-start | bytes 1572864 | tf_op jit(solution)/shard_map/all_to_all | solution.py:29
  179.7 1.9 collective-permute-start.3
  181.6 6.9 %collective-permute-done.3 = bf16[16,1024]{1,0:T(8,128)(2,1)S(1)} collective-permute-done((bf16[16,1024]{1,0:T(8,128)(2,1)S(1)}, bf16[16,1024]{1,0:T(8,128)(2,1)S(1)}, u32[]{:S(2)}, u32[]{:S(2)}) %collective-permute-start.3) | collective-permute-done | bytes 32800 | tf_op jit(solution)/shard_map/ppermute | solution.py:179
  188.5 0.6 fusion.1
  189.1 4.8 %all-to-all-done.3 = bf16[32,48,256]{2,1,0:T(8,128)(2,1)S(1)} async-done(((bf16[32,48,256]{2,1,0:T(8,128)(2,1)}), bf16[32,48,256]{2,1,0:T(8,128)(2,1)S(1)}, u32[]{:S(2)}, u32[]{:S(2)}) %all-to-all-start.3) | async-done | bytes 786464 | tf_op jit(solution)/shard_map/all_to_all | solution.py:29
  193.9 1.7 final.1
  (2 shorter events, 0.0 us)
Async XLA Ops:
  0.7 10.7 %copy-start.1 = (bf16[16,512]{1,0:T(8,128)(2,1)S(1)}, bf16[16,512]{1,0:T(8,128)(2,1)}, u32[]{:S(2)}) copy-start(bf16[16,512]{1,0:T(8,128)(2,1)} %one.1) | copy-start | bytes 49156
  0.7 10.7 %copy-start.2 = (bf16[16,512]{1,0:T(8,128)(2,1)S(1)}, bf16[16,512]{1,0:T(8,128)(2,1)}, u32[]{:S(2)}) copy-start(bf16[16,512]{1,0:T(8,128)(2,1)} %two.1) | copy-start | bytes 49156
  1.7 77.6 %collective-permute-start = (bf16[256,256]{1,0:T(8,128)(2,1)S(1)}, bf16[256,256]{1,0:T(8,128)(2,1)S(1)}, u32[]{:S(2)}, u32[]{:S(2)}) collective-permute-start(bf16[256,256]{1,0:T(8,128)(2,1)S(1)} %get-tuple-element.16), channel_id=1, source_target_pairs={{0,0},{1,32},{2,64},{3,96},{4,128},{5,160},{6,192},{7,224},{8,256}... | collective-permute-start | bytes 393224 | tf_op jit(solution)/shard_map/ppermute | solution.py:154
  2.4 9.0 %copy-start.5 = (s32[2,24]{1,0:T(2,128)S(1)}, s32[2,24]{1,0:T(2,128)}, u32[]{:S(2)}) copy-start(s32[2,24]{1,0:T(2,128)} %anc_two.3) | copy-start | bytes 580
  2.4 9.0 %copy-start.3 = (s32[4]{0:T(128)S(1)}, s32[4]{0:T(128)}, u32[]{:S(2)}) copy-start(s32[4]{0:T(128)} %widths.5) | copy-start | bytes 52
  2.4 9.0 %copy-start.4 = (s32[2,28]{1,0:T(2,128)S(1)}, s32[2,28]{1,0:T(2,128)}, u32[]{:S(2)}) copy-start(s32[2,28]{1,0:T(2,128)} %anc_one.3) | copy-start | bytes 676
  2.4 76.9 %collective-permute-start.1 = (bf16[256,256]{1,0:T(8,128)(2,1)S(1)}, bf16[256,256]{1,0:T(8,128)(2,1)S(1)}, u32[]{:S(2)}, u32[]{:S(2)}) collective-permute-start(bf16[256,256]{1,0:T(8,128)(2,1)S(1)} %get-tuple-element.15), channel_id=1, source_target_pairs={{0,16},{1,48},{2,80},{3,112},{4,144},{5,176},{6,208},{7,240},{8,27... | collective-permute-start | bytes 393224 | tf_op jit(solution)/shard_map/ppermute | solution.py:155
  80.8 40.4 %copy-start = (bf16[2,256,256]{2,1,0:T(8,128)(2,1)S(1)}, bf16[2,256,256]{2,1,0:T(8,128)(2,1)}, u32[]{:S(2)}) copy-start(bf16[2,256,256]{2,1,0:T(8,128)(2,1)} %link.3) | copy-start | bytes 786436
  80.8 40.4 %all-to-all-start = ((bf16[32,16,1024]{2,1,0:T(8,128)(2,1)}), bf16[32,16,1024]{2,1,0:T(8,128)(2,1)S(1)}, u32[]{:S(2)}, u32[]{:S(2)}) async-start(bf16[32,16,1024]{2,1,0:T(8,128)(2,1)} %product.1), calls=%async_computation | async-start | bytes 2097152 | tf_op jit(solution)/shard_map/all_to_all | solution.py:29
  103.9 9.7 %collective-permute-start.2 = (bf16[16,1024]{1,0:T(8,128)(2,1)S(1)}, bf16[16,1024]{1,0:T(8,128)(2,1)S(1)}, u32[]{:S(2)}, u32[]{:S(2)}) collective-permute-start(bf16[16,1024]{1,0:T(8,128)(2,1)S(1)} %mask.1), channel_id=1, source_target_pairs={{0,0},{1,16},{2,32},{3,48},{4,64},{5,80},{6,96},{7,112},{8,128},{9... | collective-permute-start | bytes 98312 | tf_op jit(solution)/shard_map/ppermute | solution.py:163
  144.6 4.7 %copy-start.6 = (bf16[2,256,256]{2,1,0:T(8,128)(2,1)S(1)}, bf16[2,256,256]{2,1,0:T(8,128)(2,1)}, u32[]{:S(2)}) copy-start(bf16[2,256,256]{2,1,0:T(8,128)(2,1)} %param.16) | copy-start | bytes 786436
  144.6 4.7 %copy-start.7 = (bf16[2,256,256]{2,1,0:T(8,128)(2,1)S(1)}, bf16[2,256,256]{2,1,0:T(8,128)(2,1)}, u32[]{:S(2)}) copy-start(bf16[2,256,256]{2,1,0:T(8,128)(2,1)} %param.12) | copy-start | bytes 786436
  144.6 22.3 %all-to-all-start.2 = ((bf16[16,48,256]{2,1,0:T(8,128)(2,1)}), bf16[16,48,256]{2,1,0:T(8,128)(2,1)S(1)}, u32[]{:S(2)}, u32[]{:S(2)}) async-start(bf16[16,48,256]{2,1,0:T(8,128)(2,1)} %row_sum.1), calls=%async_computation.2 | async-start | bytes 786432 | tf_op jit(solution)/shard_map/all_to_all | solution.py:29
  167.9 26.0 %all-to-all-start.3 = ((bf16[32,48,256]{2,1,0:T(8,128)(2,1)}), bf16[32,48,256]{2,1,0:T(8,128)(2,1)S(1)}, u32[]{:S(2)}, u32[]{:S(2)}) async-start(bf16[32,48,256]{2,1,0:T(8,128)(2,1)} %col_sum.1), calls=%async_computation.3 | async-start | bytes 1572864 | tf_op jit(solution)/shard_map/all_to_all | solution.py:29
  179.7 8.8 %collective-permute-start.3 = (bf16[16,1024]{1,0:T(8,128)(2,1)S(1)}, bf16[16,1024]{1,0:T(8,128)(2,1)S(1)}, u32[]{:S(2)}, u32[]{:S(2)}) collective-permute-start(bf16[16,1024]{1,0:T(8,128)(2,1)S(1)} %get-tuple-element.10), channel_id=1, source_target_pairs={{0,0},{16,1},{32,2},{48,3},{64,4},{80,5},{96,6},{112,7},{128,8},{1... | collective-permute-start | bytes 98312 | tf_op jit(solution)/shard_map/ppermute | solution.py:179

commit v3 on v2

v3 whole, which is shorter than its diff:
```python
import functools

import jax
import jax.numpy as jnp
from jax import lax
from jax.experimental import pallas as pl
from jax.experimental.pallas import tpu as pltpu
from jax.sharding import Mesh
from jax.sharding import PartitionSpec as P

F32 = jnp.float32
BF16 = jnp.bfloat16
VMEM = pl.BlockSpec(memory_space=pltpu.VMEM)
SMEM = pl.BlockSpec(memory_space=pltpu.SMEM)
NEAR = 4
CORES = 2
GRID = ("chip", "core", "far", "near")


def kernel_call(body, name, specs, outs):
    return pl.pallas_call(
        body,
        name=name,
        in_specs=specs,
        out_specs=[VMEM] * len(outs),
        out_shape=[jax.ShapeDtypeStruct(shape, kind) for shape, kind in outs],
        compiler_params=pltpu.CompilerParams(vmem_limit_bytes=40 * 1024 * 1024),
    )


def exchange(blocks, axis):
    return lax.all_to_all(blocks, axis, split_axis=0, concat_axis=0, tiled=True)


def swap_cores(block):
    return lax.ppermute(block, "core", [(0, 1), (1, 0)])


def dot(left, right):
    return jnp.dot(left, right, preferred_element_type=F32)


def dot_t(left, right):
    return lax.dot_general(left, right, (((0,), (0,)), ((), ())), preferred_element_type=F32)


def reduced(received):
    total = received[0].astype(F32)
    for i in range(1, received.shape[0]):
        total = total + received[i].astype(F32)
    return total


def is_member(table, s, tile):
    found = table[s, 0] == tile
    for i in range(1, table.shape[1]):
        found = found | (table[s, i] == tile)
    return found


def masked_link(w, link, widths, s):
    row = lax.broadcasted_iota(jnp.int32, (w, w), 0)
    column = lax.broadcasted_iota(jnp.int32, (w, w), 1)
    value = link[s]
    inside = (row < widths[s]) & (column < widths[2 + s])
    return jnp.where(inside, value, jnp.zeros_like(value))


def mask_body(w, tile, one, two, anc_one, anc_two, widths, lower):
    column = lax.broadcasted_iota(jnp.int32, (one.shape[0], w), 1)
    for k in range(4):
        source, table, s = (one, anc_one, k) if k < 2 else (two, anc_two, k - 2)
        width = jnp.where(is_member(table, s, tile[0]), widths[k], 0)
        value = source[:, s * w : (s + 1) * w]
        lower[:, k * w : (k + 1) * w] = jnp.where(column < width, value, jnp.zeros_like(value))


def copy_body(source, copies):
    value = source[...]
    for i in range(copies.shape[0]):
        copies[i] = value


def product_body(w, core, inverse, mine, other, part):
    near, far, share, _ = part.shape
    half = mine.shape[0]
    left = inverse[:, pl.ds(pl.multiple_of(core[0] * half, half), half)]
    right = inverse[:, pl.ds(pl.multiple_of((1 - core[0]) * half, half), half)]
    for k in range(4):
        span = slice(k * w, (k + 1) * w)
        value = (dot(left, mine[:, span]) + dot(right, other[:, span])).astype(BF16)
        for i in range(near * far):
            part[i % near, i // near, :, span] = value[i * share : (i + 1) * share]


def quad_body(w, core, received, rows, block, mine, other, held):
    far, _, share = block.shape[0], block.shape[1], received.shape[2]
    for f in range(far):
        total = received[0, f].astype(F32)
        for i in range(1, received.shape[0]):
            total = total + received[i, f].astype(F32)
        total = total.astype(BF16)
        held[f * share : (f + 1) * share, :] = total
        for k in range(4):
            block[f, k * share : (k + 1) * share, :] = total[:, k * w : (k + 1) * w]
    for out, sibling in ((mine, core[0]), (other, 1 - core[0])):
        first = pl.ds(pl.multiple_of(sibling * w, w), w)
        second = pl.ds(pl.multiple_of((2 + sibling) * w, w), w)
        out[0] = dot_t(rows[:, first], held[:, first])
        out[1] = dot_t(held[:, first], rows[:, second])
        out[2] = dot_t(rows[:, second], held[:, second])


def core_sum_body(mine, other, sums):
    sums[...] = (mine[...] + other[...]).astype(BF16)


def chip_sum_body(received, copies):
    value = reduced(received)
    for i in range(copies.shape[0]):
        copies[i] = value


def near_sum_body(received, block, packed):
    chunk = received.shape[1]
    value = reduced(received).astype(BF16)
    for i in range(packed.shape[0]):
        packed[i, :chunk, :] = value
        packed[i, chunk:, :] = block[i]


def far_sum_body(received, pivot, copies):
    total = pivot[...].astype(F32)
    for i in range(received.shape[0]):
        total = total + received[i, : pivot.shape[0], :].astype(F32)
    total = total.astype(BF16)
    for i in range(copies.shape[0]):
        copies[i] = total


def column_body(w, chunk, tile, received, link, anc_one, anc_two, widths, column_one, column_two):
    total = received[0, chunk:, :].astype(F32)
    for i in range(1, received.shape[0]):
        total = total + received[i, chunk:, :].astype(F32)
    share = column_one.shape[0]
    for s in range(2):
        span = slice(s * w, (s + 1) * w)
        here_one = jnp.where(is_member(anc_one, s, tile[0]), 1.0, 0.0)
        here_two = jnp.where(is_member(anc_two, s, tile[0]), 1.0, 0.0)
        one = (-(total[s * share : (s + 1) * share] * here_one)).astype(BF16)
        column_one[:, span] = one
        two = total[(2 + s) * share : (3 + s) * share] + dot(one, masked_link(w, link, widths, s))
        column_two[:, span] = (-(two * here_two)).astype(BF16)


def final_body(w, core, mine, other, link, widths, block_one, parent_rows, block_two):
    for total, sibling in ((mine, core[0]), (other, 1 - core[0])):
        tie = masked_link(w, link, widths, sibling)
        block = total[0]
        cross = total[1]
        block_one[sibling] = block
        parent = (cross.astype(F32) - dot(block, tie)).astype(BF16)
        parent_rows[sibling] = parent
        rest = total[2].astype(F32) - dot_t(cross, tie) - dot_t(tie, parent)
        block_two[sibling] = rest.astype(BF16)


def local(
    ancestor_inverse,
    panel_one,
    ancestors_one,
    diag_inverse_one,
    panel_two,
    link_two,
    ancestors_two,
    diag_inverse_two,
    widths,
):
    w = diag_inverse_one.shape[-1]
    chips, far_n = lax.axis_size("chip"), lax.axis_size("far")
    planes = far_n * NEAR
    local_rows = ancestor_inverse.shape[0]
    share = panel_one.shape[0]
    chip = lax.axis_index("chip").astype(jnp.int32)
    core = lax.axis_index("core").astype(jnp.int32)
    tile = (chip * CORES + core).reshape(1)
    core_ref = core.reshape(1)
    whole = (share, 4 * w)

    (lower,) = kernel_call(
        functools.partial(mask_body, w),
        "mask",
        [SMEM, VMEM, VMEM, SMEM, SMEM, SMEM],
        [(whole, BF16)],
    )(tile, panel_one, panel_two, ancestors_one, ancestors_two, widths)

    pairs = []
    for q in range(chips):
        for k in range(CORES):
            for z in range(planes):
                pairs.append(((q * CORES + k) * planes + z, (z * CORES + k) * planes + q))
    moved = lax.ppermute(lower, GRID, pairs)
    rows = lax.all_gather(lower, "far", axis=0, tiled=True)
    (moved,) = kernel_call(copy_body, "copies", [VMEM], [((chips,) + whole, BF16)])(moved)
    mine = exchange(moved, "chip").reshape(chips * share, 4 * w)
    other = swap_cores(mine)

    (part,) = kernel_call(
        functools.partial(product_body, w),
        "product",
        [SMEM] + [VMEM] * 3,
        [((NEAR, far_n) + whole, BF16)],
    )(core_ref, ancestor_inverse, mine, other)
    part = exchange(part, "near")

    block, mine, other = pl.pallas_call(
        functools.partial(quad_body, w),
        name="quad",
        in_specs=[SMEM, VMEM, VMEM],
        out_specs=[VMEM] * 3,
        out_shape=[
            jax.ShapeDtypeStruct((far_n, 4 * share, w), BF16),
            jax.ShapeDtypeStruct((3, w, w), F32),
            jax.ShapeDtypeStruct((3, w, w), F32),
        ],
        scratch_shapes=[pltpu.VMEM((far_n * share, 4 * w), BF16)],
        compiler_params=pltpu.CompilerParams(vmem_limit_bytes=40 * 1024 * 1024),
    )(core_ref, part, rows)
    other = swap_cores(other)
    chunk = 3 * w // chips
    (sums,) = kernel_call(core_sum_body, "core_sum", [VMEM] * 2, [((3, w, w), BF16)])(mine, other)
    sums = exchange(sums.reshape(chips, chunk, w), "chip")
    (sums,) = kernel_call(chip_sum_body, "chip_sum", [VMEM], [((NEAR, chunk, w), F32)])(sums)
    sums = exchange(sums, "near")
    (packed,) = kernel_call(
        near_sum_body, "near_sum", [VMEM] * 2, [((far_n, chunk + 4 * share, w), BF16)]
    )(sums, block)
    packed = exchange(packed, "far")

    keep = (jnp.arange(w, dtype=jnp.int32)[None, :] < widths[:, None]).astype(BF16)
    pivot_one = diag_inverse_one * keep[0:2, :, None] * keep[0:2, None, :]
    pivot_two = diag_inverse_two * keep[2:4, :, None] * keep[2:4, None, :]
    pivots = jnp.stack([pivot_one, jnp.zeros_like(pivot_one), pivot_two], axis=1)
    pivot = lax.dynamic_slice_in_dim(
        pivots.reshape(6 * w, w), core * (3 * w) + chip * chunk, chunk, axis=0
    )
    (total,) = kernel_call(far_sum_body, "far_sum", [VMEM] * 2, [((chips, chunk, w), BF16)])(
        packed, pivot
    )
    mine = exchange(total, "chip").reshape(3, w, w)
    other = swap_cores(mine)
    column_one, column_two = kernel_call(
        functools.partial(column_body, w, chunk),
        "columns",
        [SMEM, VMEM, VMEM, SMEM, SMEM, SMEM],
        [((share, 2 * w), BF16)] * 2,
    )(tile, packed, link_two, ancestors_one, ancestors_two, widths)
    block_one, parent_rows, block_two = kernel_call(
        functools.partial(final_body, w),
        "final",
        [SMEM, VMEM, VMEM, VMEM, SMEM],
        [((2, w, w), BF16)] * 3,
    )(core_ref, mine, other, link_two, widths)
    return column_one, block_one, column_two, parent_rows, block_two


def solution(mesh):
    rows_n, cols_n = mesh.devices.shape
    fine = Mesh(mesh.devices.reshape(rows_n // CORES, CORES, cols_n // NEAR, NEAR), GRID)
    row, col = ("chip", "core"), ("far", "near")
    shared = P(GRID, None)
    in_specs = (P(row, col), shared, P(), P(), shared, P(), P(), P(), P())
    out_specs = (shared, P(), shared, P(), P())
    return jax.shard_map(local, mesh=fine, in_specs=in_specs, out_specs=out_specs, check_vma=False)
```

time: 199 us -> 153 us (0.77); the launches traced: 196 us -> 152 us
  starting transfers between devices: 56 us -> 34.7 us
  waiting for transfers between devices: 41.1 us -> 24.4 us
  blocking collectives: 88.7 us -> 83.3 us
    all_gather x1, blocking collectives: 67.3 us -> 24.9 us  [local(): rows = lax.all_gather(lower, 'far', axis=0, tiled=True)]
    all_to_all x1 -> x3, blocking collectives: 21.4 us -> 58.4 us  [exchange(): return lax.all_to_all(blocks, axis, split_axis=0, concat_axis=0, tiled=True)]
    all_to_all x3, starting transfers between devices: 39.4 us -> 17.6 us  [exchange(): return lax.all_to_all(blocks, axis, split_axis=0, concat_axis=0, tiled=True)]
    all_to_all x3, waiting for transfers between devices: 29.6 us -> 21 us  [exchange(): return lax.all_to_all(blocks, axis, split_axis=0, concat_axis=0, tiled=True)]
    ppermute x4, waiting for transfers between devices: 11.5 us -> 3.41 us  [the longest x3 3.41 us: swap_cores(): return lax.ppermute(block, 'core', [(0, 1), (1, 0)])]
    pallas_call x4 -> x8, Pallas kernels: 4.71 us -> 5.23 us  [the longest x1 1.77 us: local(): kernel_call(functools.partial(final_body, w), 'final', [SMEM, VMEM, VMEM,...]
  transfers between devices with their start and end apart: 7 -> 7, of which waited for: 5 -> 4; matrix products, arithmetic and copies ran while one was open for 1% -> 0% of each run, Pallas kernels for 0% -> 1%
where the time goes in v3:
time: 153 us; the launch traced here: 152 us
  blocking collectives  83.3 us (54%)
  starting transfers between devices  34.7 us (23%)
  waiting for transfers between devices  24.4 us (16%)
  Pallas kernels  7.13 us (5%)
  local copies, waits for them, and re-layouts  1.57 us (1%)
    all_to_all x3, blocking collectives, exchange(): return lax.all_to_all(blocks, axis, split_axis=0, concat_axis=0, tiled=True)  58.4 us
    all_gather x1, blocking collectives, local(): rows = lax.all_gather(lower, 'far', axis=0, tiled=True)  24.9 us
    all_to_all x3, waiting for transfers between devices, exchange(): return lax.all_to_all(blocks, axis, split_axis=0, concat_axis=0, tiled=True)  21 us
    all_to_all x3, starting transfers between devices, exchange(): return lax.all_to_all(blocks, axis, split_axis=0, concat_axis=0, tiled=True)  17.6 us
    ppermute x3, starting transfers between devices, swap_cores(): return lax.ppermute(block, 'core', [(0, 1), (1, 0)])  16.4 us
    ppermute x3, waiting for transfers between devices, swap_cores(): return lax.ppermute(block, 'core', [(0, 1), (1, 0)])  3.41 us
  transfers between devices with their start and end apart: 7, of which 4 were waited for; matrix products, arithmetic and copies ran while one was open for 0% of the time, Pallas kernels for 1%

profile of v3, /device:TPU:1, one launch (start us, length us, event | category | flops | bytes accessed | tf_op | source)
XLA Modules:
  0.0 152.3 jit_solution(10642813732328371457)
XLA Ops:
  0.6 0.0 copy-start.2
  0.7 0.0 copy-start.6
  0.7 0.0 copy-start.4
  0.7 0.0 copy-start.5
  0.7 0.7 copy-done.2
  1.4 0.0 copy-done.6
  1.4 0.0 copy-done.4
  1.4 0.0 copy-done.5
  1.4 0.0 copy-start.3
  1.4 0.7 copy-done.3
  2.1 0.7 mask.1
  2.7 0.7 collective-permute-start
  3.4 0.0 collective-permute-done.source
  3.5 0.0 copy-start.1
  3.5 35.2 %all_to_all.30 = bf16[16,16,1024]{2,1,0:T(8,128)(2,1)S(1)} all-to-all(bf16[16,16,1024]{2,1,0:T(8,128)(2,1)S(1)} %copies.1), channel_id=1, replica_groups=mesh['chip'=16,'core'=2,'far'=4,'near'=4] {'chip'}, dimensions={0} | all-to-all | bytes 1048576 | tf_op jit(solution)/shard_map/all_to_all | solution.py:32
  38.7 3.9 %collective-permute-start.1 = (bf16[256,1024]{1,0:T(8,128)(2,1)S(1)}, bf16[256,1024]{1,0:T(8,128)(2,1)S(1)}, u32[]{:S(2)}, u32[]{:S(2)}) collective-permute-start(bf16[256,1024]{1,0:T(8,128)(2,1)S(1)} %bitcast.11), channel_id=1, source_target_pairs={{0,16},{16,0},{1,17},{17,1},{2,18},{18,2},{3,19},{19,3},{4,20},{20... | collective-permute-start | bytes 1572872 | tf_op jit(solution)/shard_map/ppermute | solution.py:36
  42.6 1.5 collective-permute-done.1.other
  44.1 0.0 copy-done.1
  44.1 1.2 product.1
  45.4 3.9 %all-to-all-start.1 = ((bf16[4,4,16,1024]{3,2,1,0:T(8,128)(2,1)}), bf16[4,4,16,1024]{3,2,1,0:T(8,128)(2,1)S(1)}, u32[]{:S(2)}, u32[]{:S(2)}) async-start(bf16[4,4,16,1024]{3,2,1,0:T(8,128)(2,1)} %product.1), calls=%async_computation.1 | async-start | bytes 1048576 | tf_op jit(solution)/shard_map/all_to_all | solution.py:32
  49.3 24.9 %all_gather.3.rows = bf16[64,1024]{1,0:T(8,128)(2,1)S(1)} all-gather(bf16[16,1024]{1,0:T(8,128)(2,1)S(1)} %mask.1), channel_id=1, replica_groups=mesh['chip'=16,'core'=2,'far'=4,'near'=4] {'far'}, dimensions={0}, use_global_device_ids=true | all-gather | bytes 163840 | tf_op jit(solution)/shard_map/all_gather | solution.py:203
  74.2 0.0 all-to-all-done.1.received
  74.2 0.5 quad.1
  74.6 4.8 %collective-permute-start.2 = (f32[3,256,256]{2,1,0:T(8,128)S(1)}, f32[3,256,256]{2,1,0:T(8,128)S(1)}, u32[]{:S(2)}, u32[]{:S(2)}) collective-permute-start(f32[3,256,256]{2,1,0:T(8,128)S(1)} %get-tuple-element.14), channel_id=1, source_target_pairs={{0,16},{16,0},{1,17},{17,1},{2,18},{18,2},{3,19},{19,3},{4,20},{20... | collective-permute-start | bytes 2359304 | tf_op jit(solution)/shard_map/ppermute | solution.py:36
  79.5 1.9 %collective-permute-done.2.other = f32[3,256,256]{2,1,0:T(8,128)S(1)} collective-permute-done((f32[3,256,256]{2,1,0:T(8,128)S(1)}, f32[3,256,256]{2,1,0:T(8,128)S(1)}, u32[]{:S(2)}, u32[]{:S(2)}) %collective-permute-start.2) | collective-permute-done | bytes 786464 | tf_op jit(solution)/shard_map/ppermute | solution.py:36
  81.3 0.1 core_sum.1
  81.4 12.1 %all_to_all.31.received = bf16[16,48,256]{2,1,0:T(8,128)(2,1)S(1)} all-to-all(bf16[16,48,256]{2,1,0:T(8,128)(2,1)S(1)} %bitcast.15), channel_id=1, replica_groups=mesh['chip'=16,'core'=2,'far'=4,'near'=4] {'chip'}, dimensions={0} | all-to-all | bytes 786432 | tf_op jit(solution)/shard_map/all_to_all | solution.py:32
  93.5 0.7 chip_sum.1
  94.3 7.2 %all-to-all-start.3 = ((f32[4,48,256]{2,1,0:T(8,128)}), f32[4,48,256]{2,1,0:T(8,128)S(1)}, u32[]{:S(2)}, u32[]{:S(2)}) async-start(f32[4,48,256]{2,1,0:T(8,128)} %chip_sum.1), calls=%async_computation.3 | async-start | bytes 393216 | tf_op jit(solution)/shard_map/all_to_all | solution.py:32
  101.5 0.1 fusion
  101.6 5.0 %all-to-all-done.3.received = f32[4,48,256]{2,1,0:T(8,128)S(1)} async-done(((f32[4,48,256]{2,1,0:T(8,128)}), f32[4,48,256]{2,1,0:T(8,128)S(1)}, u32[]{:S(2)}, u32[]{:S(2)}) %all-to-all-start.3) | async-done | bytes 196640 | tf_op jit(solution)/shard_map/all_to_all | solution.py:32
  106.6 0.7 near_sum.1
  107.4 0.0 copy-start.7
  107.4 6.5 %all-to-all-start.4 = ((bf16[4,112,256]{2,1,0:T(8,128)(2,1)}), bf16[4,112,256]{2,1,0:T(8,128)(2,1)S(1)}, u32[]{:S(2)}, u32[]{:S(2)}) async-start(bf16[4,112,256]{2,1,0:T(8,128)(2,1)} %near_sum.1), calls=%async_computation.4 | async-start | bytes 458752 | tf_op jit(solution)/shard_map/all_to_all | solution.py:32
  113.8 0.1 pad.1.clone
  113.9 0.0 copy-done.8
  113.9 0.0 copy-done.7
  113.9 0.2 multiply_bitcast_fusion
  114.1 0.1 pad_maximum_fusion
  114.3 0.1 copy.14
  114.4 16.0 %all-to-all-done.4.received = bf16[4,112,256]{2,1,0:T(8,128)(2,1)S(1)} async-done(((bf16[4,112,256]{2,1,0:T(8,128)(2,1)}), bf16[4,112,256]{2,1,0:T(8,128)(2,1)S(1)}, u32[]{:S(2)}, u32[]{:S(2)}) %all-to-all-start.4) | async-done | bytes 229408 | tf_op jit(solution)/shard_map/all_to_all | solution.py:32
  130.4 0.0 copy-start
  130.4 11.0 %all_to_all.32 = bf16[16,48,256]{2,1,0:T(8,128)(2,1)S(1)} all-to-all(bf16[16,48,256]{2,1,0:T(8,128)(2,1)S(1)} %far_sum.1), channel_id=1, replica_groups=mesh['chip'=16,'core'=2,'far'=4,'near'=4] {'chip'}, dimensions={0} | all-to-all | bytes 786432 | tf_op jit(solution)/shard_map/all_to_all | solution.py:32
  141.4 7.7 %collective-permute-start.3 = (bf16[3,256,256]{2,1,0:T(8,128)(2,1)S(1)}, bf16[3,256,256]{2,1,0:T(8,128)(2,1)S(1)}, u32[]{:S(2)}, u32[]{:S(2)}) collective-permute-start(bf16[3,256,256]{2,1,0:T(8,128)(2,1)S(1)} %bitcast.13), channel_id=1, source_target_pairs={{0,16},{16,0},{1,17},{17,1},{2,18},{18,2},{3,19},{19,3},{4,20},{20... | collective-permute-start | bytes 1179656 | tf_op jit(solution)/shard_map/ppermute | solution.py:36
  149.1 0.0 copy-done
  149.1 1.4 columns.1
  150.5 0.0 collective-permute-done.3.other
  150.5 1.8 %final.1 = (bf16[2,256,256]{2,1,0:T(8,128)(2,1)}, bf16[2,256,256]{2,1,0:T(8,128)(2,1)}, bf16[2,256,256]{2,1,0:T(8,128)(2,1)}) custom-call(s32[1]{0:T(128)} %bitcast.1.core, bf16[3,256,256]{2,1,0:T(8,128)(2,1)S(1)} %bitcast.14, bf16[3,256,256]{2,1,0:T(8,128)(2,1)S(1)} %collective-permute-done.3.other, bf16[2,256,256]{2,1,0:T(8,128)(2,1)S(1)} %copy-done, ...), custom_call_target="tpu_custom_call" | custom-call | tf_op jit(solution)/shard_map/final/pallas_call | solution.py:258
  (5 shorter events, 0.1 us)
Async XLA Ops:
  0.6 0.7 copy-start.2
  0.7 0.7 copy-start.6
  0.7 0.7 copy-start.4
  0.7 0.7 copy-start.5
  1.4 0.7 copy-start.3
  2.7 0.7 collective-permute-start
  3.5 40.7 %copy-start.1 = (bf16[256,512]{1,0:T(8,128)(2,1)S(1)}, bf16[256,512]{1,0:T(8,128)(2,1)}, u32[]{:S(2)}) copy-start(bf16[256,512]{1,0:T(8,128)(2,1)} %inverse.1) | copy-start | bytes 786436
  38.7 5.4 %collective-permute-start.1 = (bf16[256,1024]{1,0:T(8,128)(2,1)S(1)}, bf16[256,1024]{1,0:T(8,128)(2,1)S(1)}, u32[]{:S(2)}, u32[]{:S(2)}) collective-permute-start(bf16[256,1024]{1,0:T(8,128)(2,1)S(1)} %bitcast.11), channel_id=1, source_target_pairs={{0,16},{16,0},{1,17},{17,1},{2,18},{18,2},{3,19},{19,3},{4,20},{20... | collective-permute-start | bytes 1572872 | tf_op jit(solution)/shard_map/ppermute | solution.py:36
  45.4 28.8 %all-to-all-start.1 = ((bf16[4,4,16,1024]{3,2,1,0:T(8,128)(2,1)}), bf16[4,4,16,1024]{3,2,1,0:T(8,128)(2,1)S(1)}, u32[]{:S(2)}, u32[]{:S(2)}) async-start(bf16[4,4,16,1024]{3,2,1,0:T(8,128)(2,1)} %product.1), calls=%async_computation.1 | async-start | bytes 1048576 | tf_op jit(solution)/shard_map/all_to_all | solution.py:32
  74.6 6.7 %collective-permute-start.2 = (f32[3,256,256]{2,1,0:T(8,128)S(1)}, f32[3,256,256]{2,1,0:T(8,128)S(1)}, u32[]{:S(2)}, u32[]{:S(2)}) collective-permute-start(f32[3,256,256]{2,1,0:T(8,128)S(1)} %get-tuple-element.14), channel_id=1, source_target_pairs={{0,16},{16,0},{1,17},{17,1},{2,18},{18,2},{3,19},{19,3},{4,20},{20... | collective-permute-start | bytes 2359304 | tf_op jit(solution)/shard_map/ppermute | solution.py:36
  94.3 12.4 %all-to-all-start.3 = ((f32[4,48,256]{2,1,0:T(8,128)}), f32[4,48,256]{2,1,0:T(8,128)S(1)}, u32[]{:S(2)}, u32[]{:S(2)}) async-start(f32[4,48,256]{2,1,0:T(8,128)} %chip_sum.1), calls=%async_computation.3 | async-start | bytes 393216 | tf_op jit(solution)/shard_map/all_to_all | solution.py:32
  106.6 7.3 %copy-start.8 = (bf16[2,256,256]{2,1,0:T(8,128)(2,1)S(1)}, bf16[2,256,256]{2,1,0:T(8,128)(2,1)}, u32[]{:S(2)}) copy-start(bf16[2,256,256]{2,1,0:T(8,128)(2,1)} %param.12) | copy-start | bytes 786436
  107.4 6.6 %copy-start.7 = (bf16[2,256,256]{2,1,0:T(8,128)(2,1)S(1)}, bf16[2,256,256]{2,1,0:T(8,128)(2,1)}, u32[]{:S(2)}) copy-start(bf16[2,256,256]{2,1,0:T(8,128)(2,1)} %param.16) | copy-start | bytes 786436
  107.4 23.0 %all-to-all-start.4 = ((bf16[4,112,256]{2,1,0:T(8,128)(2,1)}), bf16[4,112,256]{2,1,0:T(8,128)(2,1)S(1)}, u32[]{:S(2)}, u32[]{:S(2)}) async-start(bf16[4,112,256]{2,1,0:T(8,128)(2,1)} %near_sum.1), calls=%async_computation.4 | async-start | bytes 458752 | tf_op jit(solution)/shard_map/all_to_all | solution.py:32
  130.4 18.7 %copy-start = (bf16[2,256,256]{2,1,0:T(8,128)(2,1)S(1)}, bf16[2,256,256]{2,1,0:T(8,128)(2,1)}, u32[]{:S(2)}) copy-start(bf16[2,256,256]{2,1,0:T(8,128)(2,1)} %link.3) | copy-start | bytes 786436
  141.4 9.1 %collective-permute-start.3 = (bf16[3,256,256]{2,1,0:T(8,128)(2,1)S(1)}, bf16[3,256,256]{2,1,0:T(8,128)(2,1)S(1)}, u32[]{:S(2)}, u32[]{:S(2)}) collective-permute-start(bf16[3,256,256]{2,1,0:T(8,128)(2,1)S(1)} %bitcast.13), channel_id=1, source_target_pairs={{0,16},{16,0},{1,17},{17,1},{2,18},{18,2},{3,19},{19,3},{4,20},{20... | collective-permute-start | bytes 1179656 | tf_op jit(solution)/shard_map/ppermute | solution.py:36

commit v4 on v3

--- a/solution.py
+++ b/solution.py
@@ -66,13 +66,16 @@
     return jnp.where(inside, value, jnp.zeros_like(value))
 
 
-def mask_body(w, tile, one, two, anc_one, anc_two, widths, lower):
+def mask_body(w, tile, one, two, anc_one, anc_two, widths, lower, copies):
     column = lax.broadcasted_iota(jnp.int32, (one.shape[0], w), 1)
     for k in range(4):
         source, table, s = (one, anc_one, k) if k < 2 else (two, anc_two, k - 2)
         width = jnp.where(is_member(table, s, tile[0]), widths[k], 0)
         value = source[:, s * w : (s + 1) * w]
-        lower[:, k * w : (k + 1) * w] = jnp.where(column < width, value, jnp.zeros_like(value))
+        value = jnp.where(column < width, value, jnp.zeros_like(value))
+        lower[:, k * w : (k + 1) * w] = value
+        for i in range(copies.shape[0]):
+            copies[i, :, k * w : (k + 1) * w] = value
 
 
 def copy_body(source, copies):
@@ -187,11 +190,11 @@
     core_ref = core.reshape(1)
     whole = (share, 4 * w)
 
-    (lower,) = kernel_call(
+    lower, lower_copies = kernel_call(
         functools.partial(mask_body, w),
         "mask",
         [SMEM, VMEM, VMEM, SMEM, SMEM, SMEM],
-        [(whole, BF16)],
+        [(whole, BF16), ((far_n,) + whole, BF16)],
     )(tile, panel_one, panel_two, ancestors_one, ancestors_two, widths)
 
     pairs = []
@@ -200,7 +203,8 @@
             for z in range(planes):
                 pairs.append(((q * CORES + k) * planes + z, (z * CORES + k) * planes + q))
     moved = lax.ppermute(lower, GRID, pairs)
-    rows = lax.all_gather(lower, "far", axis=0, tiled=True)
+    rows = exchange(lower_copies, "far").reshape(far_n * share, 4 * w)
+    moved, rows = lax.optimization_barrier((moved, rows))
     (moved,) = kernel_call(copy_body, "copies", [VMEM], [((chips,) + whole, BF16)])(moved)
     mine = exchange(moved, "chip").reshape(chips * share, 4 * w)
     other = swap_cores(mine)

time: 153 us -> 152 us (level)
  blocking collectives: 83.3 us -> 62.6 us
  waiting for transfers between devices: 24.4 us -> 36.6 us
  starting transfers between devices: 34.7 us -> 42 us
    all_gather x1 -> x0, blocking collectives: 24.9 us -> none  [local(): rows = lax.all_gather(lower, 'far', axis=0, tiled=True)]
    all_to_all x3, waiting for transfers between devices: 21 us -> 33.2 us  [exchange(): return lax.all_to_all(blocks, axis, split_axis=0, concat_axis=0, tiled=True)]
    all_to_all x3, starting transfers between devices: 17.6 us -> 26.7 us  [exchange(): return lax.all_to_all(blocks, axis, split_axis=0, concat_axis=0, tiled=True)]
    all_to_all x3 -> x4, blocking collectives: 58.4 us -> 62.6 us  [exchange(): return lax.all_to_all(blocks, axis, split_axis=0, concat_axis=0, tiled=True)]
    ppermute x3, starting transfers between devices: 16.4 us -> 14.7 us  [swap_cores(): return lax.ppermute(block, 'core', [(0, 1), (1, 0)])]
  transfers between devices with their start and end apart: 7 -> 7, of which waited for: 4 -> 5; matrix products, arithmetic and copies ran while one was open for 0% -> 0% of each run, Pallas kernels for 1% -> 1%
where the time goes in v4:
time: 152 us; the launch traced here: 151 us
  blocking collectives  62.6 us (41%)
  starting transfers between devices  42 us (28%)
  waiting for transfers between devices  36.6 us (24%)
  Pallas kernels  6.98 us (5%)
  local copies, waits for them, and re-layouts  1.57 us (1%)
    all_to_all x4, blocking collectives, exchange(): return lax.all_to_all(blocks, axis, split_axis=0, concat_axis=0, tiled=True)  62.6 us
    all_to_all x3, waiting for transfers between devices, exchange(): return lax.all_to_all(blocks, axis, split_axis=0, concat_axis=0, tiled=True)  33.2 us
    all_to_all x3, starting transfers between devices, exchange(): return lax.all_to_all(blocks, axis, split_axis=0, concat_axis=0, tiled=True)  26.7 us
    ppermute x3, starting transfers between devices, swap_cores(): return lax.ppermute(block, 'core', [(0, 1), (1, 0)])  14.7 us
    ppermute x3, waiting for transfers between devices, swap_cores(): return lax.ppermute(block, 'core', [(0, 1), (1, 0)])  3.41 us
  transfers between devices with their start and end apart: 7, of which 5 were waited for; matrix products, arithmetic and copies ran while one was open for 0% of the time, Pallas kernels for 1%

profile of v4, /device:TPU:1, one launch (start us, length us, event | category | flops | bytes accessed | tf_op | source)
XLA Modules:
  0.0 151.0 jit_solution(2146111666888994412)
XLA Ops:
  0.6 0.0 copy-start.2
  0.7 0.0 copy-start.6
  0.7 0.0 copy-start.4
  0.7 0.0 copy-start.5
  0.7 0.7 copy-done.2
  1.4 0.0 copy-done.6
  1.4 0.0 copy-done.4
  1.4 0.0 copy-done.5
  1.4 0.0 copy-start.3
  1.4 0.7 copy-done.3
  2.1 1.3 mask.1
  3.4 15.6 %all-to-all-start = ((bf16[4,16,1024]{2,1,0:T(8,128)(2,1)}), bf16[4,16,1024]{2,1,0:T(8,128)(2,1)S(1)}, u32[]{:S(2)}, u32[]{:S(2)}) async-start(bf16[4,16,1024]{2,1,0:T(8,128)(2,1)} %get-tuple-element.18), calls=%async_computation | async-start | bytes 262144 | tf_op jit(solution)/shard_map/all_to_all | solution.py:32
  19.0 0.7 collective-permute-start
  19.7 0.0 collective-permute-done.source
  19.7 12.0 %all-to-all-done = bf16[4,16,1024]{2,1,0:T(8,128)(2,1)S(1)} async-done(((bf16[4,16,1024]{2,1,0:T(8,128)(2,1)}), bf16[4,16,1024]{2,1,0:T(8,128)(2,1)S(1)}, u32[]{:S(2)}, u32[]{:S(2)}) %all-to-all-start) | async-done | bytes 131104 | tf_op jit(solution)/shard_map/all_to_all | solution.py:32
  31.8 0.0 copy-start.1
  31.8 22.8 %all_to_all.35 = bf16[16,16,1024]{2,1,0:T(8,128)(2,1)S(1)} all-to-all(bf16[16,16,1024]{2,1,0:T(8,128)(2,1)S(1)} %copies.1), channel_id=1, replica_groups=mesh['chip'=16,'core'=2,'far'=4,'near'=4] {'chip'}, dimensions={0} | all-to-all | bytes 1048576 | tf_op jit(solution)/shard_map/all_to_all | solution.py:32
  54.6 3.8 %collective-permute-start.1 = (bf16[256,1024]{1,0:T(8,128)(2,1)S(1)}, bf16[256,1024]{1,0:T(8,128)(2,1)S(1)}, u32[]{:S(2)}, u32[]{:S(2)}) collective-permute-start(bf16[256,1024]{1,0:T(8,128)(2,1)S(1)} %bitcast.12), channel_id=1, source_target_pairs={{0,16},{16,0},{1,17},{17,1},{2,18},{18,2},{3,19},{19,3},{4,20},{20... | collective-permute-start | bytes 1572872 | tf_op jit(solution)/shard_map/ppermute | solution.py:36
  58.4 1.5 %collective-permute-done.1.other = bf16[256,1024]{1,0:T(8,128)(2,1)S(1)} collective-permute-done((bf16[256,1024]{1,0:T(8,128)(2,1)S(1)}, bf16[256,1024]{1,0:T(8,128)(2,1)S(1)}, u32[]{:S(2)}, u32[]{:S(2)}) %collective-permute-start.1) | collective-permute-done | bytes 524320 | tf_op jit(solution)/shard_map/ppermute | solution.py:36
  59.9 0.0 copy-done.1
  59.9 0.4 product.1
  60.3 16.6 %all_to_all.36.received = bf16[4,4,16,1024]{3,2,1,0:T(8,128)(2,1)S(1)} all-to-all(bf16[4,4,16,1024]{3,2,1,0:T(8,128)(2,1)S(1)} %product.1), channel_id=1, replica_groups=mesh['chip'=16,'core'=2,'far'=4,'near'=4] {'near'}, dimensions={0} | all-to-all | bytes 1048576 | tf_op jit(solution)/shard_map/all_to_all | solution.py:32
  76.9 0.5 quad.1
  77.4 3.3 %collective-permute-start.2 = (f32[3,256,256]{2,1,0:T(8,128)S(1)}, f32[3,256,256]{2,1,0:T(8,128)S(1)}, u32[]{:S(2)}, u32[]{:S(2)}) collective-permute-start(f32[3,256,256]{2,1,0:T(8,128)S(1)} %get-tuple-element.22), channel_id=1, source_target_pairs={{0,16},{16,0},{1,17},{17,1},{2,18},{18,2},{3,19},{19,3},{4,20},{20... | collective-permute-start | bytes 2359304 | tf_op jit(solution)/shard_map/ppermute | solution.py:36
  80.7 1.9 %collective-permute-done.2.other = f32[3,256,256]{2,1,0:T(8,128)S(1)} collective-permute-done((f32[3,256,256]{2,1,0:T(8,128)S(1)}, f32[3,256,256]{2,1,0:T(8,128)S(1)}, u32[]{:S(2)}, u32[]{:S(2)}) %collective-permute-start.2) | collective-permute-done | bytes 786464 | tf_op jit(solution)/shard_map/ppermute | solution.py:36
  82.6 0.1 core_sum.1
  82.7 12.2 %all_to_all.37.received = bf16[16,48,256]{2,1,0:T(8,128)(2,1)S(1)} all-to-all(bf16[16,48,256]{2,1,0:T(8,128)(2,1)S(1)} %bitcast.16), channel_id=1, replica_groups=mesh['chip'=16,'core'=2,'far'=4,'near'=4] {'chip'}, dimensions={0} | all-to-all | bytes 786432 | tf_op jit(solution)/shard_map/all_to_all | solution.py:32
  94.9 0.7 chip_sum.1
  95.6 3.4 %all-to-all-start.4 = ((f32[4,48,256]{2,1,0:T(8,128)}), f32[4,48,256]{2,1,0:T(8,128)S(1)}, u32[]{:S(2)}, u32[]{:S(2)}) async-start(f32[4,48,256]{2,1,0:T(8,128)} %chip_sum.1), calls=%async_computation.4 | async-start | bytes 393216 | tf_op jit(solution)/shard_map/all_to_all | solution.py:32
  99.0 0.1 fusion
  99.1 5.0 %all-to-all-done.4.received = f32[4,48,256]{2,1,0:T(8,128)S(1)} async-done(((f32[4,48,256]{2,1,0:T(8,128)}), f32[4,48,256]{2,1,0:T(8,128)S(1)}, u32[]{:S(2)}, u32[]{:S(2)}) %all-to-all-start.4) | async-done | bytes 196640 | tf_op jit(solution)/shard_map/all_to_all | solution.py:32
  104.1 0.0 copy-start.8
  104.1 0.7 near_sum.1
  104.8 7.7 %all-to-all-start.5 = ((bf16[4,112,256]{2,1,0:T(8,128)(2,1)}), bf16[4,112,256]{2,1,0:T(8,128)(2,1)S(1)}, u32[]{:S(2)}, u32[]{:S(2)}) async-start(bf16[4,112,256]{2,1,0:T(8,128)(2,1)} %near_sum.1), calls=%async_computation.5 | async-start | bytes 458752 | tf_op jit(solution)/shard_map/all_to_all | solution.py:32
  112.5 0.1 pad.1.clone
  112.6 0.0 copy-done.8
  112.6 0.0 copy-done.7
  112.6 0.2 multiply_bitcast_fusion
  112.8 0.1 pad_maximum_fusion
  112.9 0.1 copy.14
  113.0 16.1 %all-to-all-done.5.received = bf16[4,112,256]{2,1,0:T(8,128)(2,1)S(1)} async-done(((bf16[4,112,256]{2,1,0:T(8,128)(2,1)}), bf16[4,112,256]{2,1,0:T(8,128)(2,1)S(1)}, u32[]{:S(2)}, u32[]{:S(2)}) %all-to-all-start.5) | async-done | bytes 229408 | tf_op jit(solution)/shard_map/all_to_all | solution.py:32
  129.2 0.0 copy-start
  129.2 11.0 %all_to_all.38 = bf16[16,48,256]{2,1,0:T(8,128)(2,1)S(1)} all-to-all(bf16[16,48,256]{2,1,0:T(8,128)(2,1)S(1)} %far_sum.1), channel_id=1, replica_groups=mesh['chip'=16,'core'=2,'far'=4,'near'=4] {'chip'}, dimensions={0} | all-to-all | bytes 786432 | tf_op jit(solution)/shard_map/all_to_all | solution.py:32
  140.2 7.7 %collective-permute-start.3 = (bf16[3,256,256]{2,1,0:T(8,128)(2,1)S(1)}, bf16[3,256,256]{2,1,0:T(8,128)(2,1)S(1)}, u32[]{:S(2)}, u32[]{:S(2)}) collective-permute-start(bf16[3,256,256]{2,1,0:T(8,128)(2,1)S(1)} %bitcast.14), channel_id=1, source_target_pairs={{0,16},{16,0},{1,17},{17,1},{2,18},{18,2},{3,19},{19,3},{4,20},{20... | collective-permute-start | bytes 1179656 | tf_op jit(solution)/shard_map/ppermute | solution.py:36
  147.8 0.0 copy-done
  147.8 1.4 columns.1
  149.2 0.0 collective-permute-done.3.other
  149.2 1.8 %final.1 = (bf16[2,256,256]{2,1,0:T(8,128)(2,1)}, bf16[2,256,256]{2,1,0:T(8,128)(2,1)}, bf16[2,256,256]{2,1,0:T(8,128)(2,1)}) custom-call(s32[1]{0:T(128)} %bitcast.1.core, bf16[3,256,256]{2,1,0:T(8,128)(2,1)S(1)} %bitcast.15, bf16[3,256,256]{2,1,0:T(8,128)(2,1)S(1)} %collective-permute-done.3.other, bf16[2,256,256]{2,1,0:T(8,128)(2,1)S(1)} %copy-done, ...), custom_call_target="tpu_custom_call" | custom-call | tf_op jit(solution)/shard_map/final/pallas_call | solution.py:262
  (5 shorter events, 0.1 us)
Async XLA Ops:
  0.6 0.7 copy-start.2
  0.7 0.7 copy-start.6
  0.7 0.7 copy-start.4
  0.7 0.7 copy-start.5
  1.4 0.7 copy-start.3
  3.4 28.3 %all-to-all-start = ((bf16[4,16,1024]{2,1,0:T(8,128)(2,1)}), bf16[4,16,1024]{2,1,0:T(8,128)(2,1)S(1)}, u32[]{:S(2)}, u32[]{:S(2)}) async-start(bf16[4,16,1024]{2,1,0:T(8,128)(2,1)} %get-tuple-element.18), calls=%async_computation | async-start | bytes 262144 | tf_op jit(solution)/shard_map/all_to_all | solution.py:32
  19.0 0.7 collective-permute-start
  31.8 28.1 %copy-start.1 = (bf16[256,512]{1,0:T(8,128)(2,1)S(1)}, bf16[256,512]{1,0:T(8,128)(2,1)}, u32[]{:S(2)}) copy-start(bf16[256,512]{1,0:T(8,128)(2,1)} %inverse.1) | copy-start | bytes 786436
  54.6 5.3 %collective-permute-start.1 = (bf16[256,1024]{1,0:T(8,128)(2,1)S(1)}, bf16[256,1024]{1,0:T(8,128)(2,1)S(1)}, u32[]{:S(2)}, u32[]{:S(2)}) collective-permute-start(bf16[256,1024]{1,0:T(8,128)(2,1)S(1)} %bitcast.12), channel_id=1, source_target_pairs={{0,16},{16,0},{1,17},{17,1},{2,18},{18,2},{3,19},{19,3},{4,20},{20... | collective-permute-start | bytes 1572872 | tf_op jit(solution)/shard_map/ppermute | solution.py:36
  77.4 5.2 %collective-permute-start.2 = (f32[3,256,256]{2,1,0:T(8,128)S(1)}, f32[3,256,256]{2,1,0:T(8,128)S(1)}, u32[]{:S(2)}, u32[]{:S(2)}) collective-permute-start(f32[3,256,256]{2,1,0:T(8,128)S(1)} %get-tuple-element.22), channel_id=1, source_target_pairs={{0,16},{16,0},{1,17},{17,1},{2,18},{18,2},{3,19},{19,3},{4,20},{20... | collective-permute-start | bytes 2359304 | tf_op jit(solution)/shard_map/ppermute | solution.py:36
  95.6 8.5 %all-to-all-start.4 = ((f32[4,48,256]{2,1,0:T(8,128)}), f32[4,48,256]{2,1,0:T(8,128)S(1)}, u32[]{:S(2)}, u32[]{:S(2)}) async-start(f32[4,48,256]{2,1,0:T(8,128)} %chip_sum.1), calls=%async_computation.4 | async-start | bytes 393216 | tf_op jit(solution)/shard_map/all_to_all | solution.py:32
  104.1 8.5 %copy-start.8 = (bf16[2,256,256]{2,1,0:T(8,128)(2,1)S(1)}, bf16[2,256,256]{2,1,0:T(8,128)(2,1)}, u32[]{:S(2)}) copy-start(bf16[2,256,256]{2,1,0:T(8,128)(2,1)} %param.12) | copy-start | bytes 786436
  104.8 7.7 %copy-start.7 = (bf16[2,256,256]{2,1,0:T(8,128)(2,1)S(1)}, bf16[2,256,256]{2,1,0:T(8,128)(2,1)}, u32[]{:S(2)}) copy-start(bf16[2,256,256]{2,1,0:T(8,128)(2,1)} %param.16) | copy-start | bytes 786436
  104.8 24.3 %all-to-all-start.5 = ((bf16[4,112,256]{2,1,0:T(8,128)(2,1)}), bf16[4,112,256]{2,1,0:T(8,128)(2,1)S(1)}, u32[]{:S(2)}, u32[]{:S(2)}) async-start(bf16[4,112,256]{2,1,0:T(8,128)(2,1)} %near_sum.1), calls=%async_computation.5 | async-start | bytes 458752 | tf_op jit(solution)/shard_map/all_to_all | solution.py:32
  129.2 18.7 %copy-start = (bf16[2,256,256]{2,1,0:T(8,128)(2,1)S(1)}, bf16[2,256,256]{2,1,0:T(8,128)(2,1)}, u32[]{:S(2)}) copy-start(bf16[2,256,256]{2,1,0:T(8,128)(2,1)} %link.3) | copy-start | bytes 786436
  140.2 9.1 %collective-permute-start.3 = (bf16[3,256,256]{2,1,0:T(8,128)(2,1)S(1)}, bf16[3,256,256]{2,1,0:T(8,128)(2,1)S(1)}, u32[]{:S(2)}, u32[]{:S(2)}) collective-permute-start(bf16[3,256,256]{2,1,0:T(8,128)(2,1)S(1)} %bitcast.14), channel_id=1, source_target_pairs={{0,16},{16,0},{1,17},{17,1},{2,18},{18,2},{3,19},{19,3},{4,20},{20... | collective-permute-start | bytes 1179656 | tf_op jit(solution)/shard_map/ppermute | solution.py:36

commit v5 on v3

--- a/solution.py
+++ b/solution.py
@@ -14,6 +14,7 @@
 SMEM = pl.BlockSpec(memory_space=pltpu.SMEM)
 NEAR = 4
 CORES = 2
+LANES = 128
 GRID = ("chip", "core", "far", "near")
 
 
@@ -34,6 +35,10 @@
 
 def swap_cores(block):
     return lax.ppermute(block, "core", [(0, 1), (1, 0)])
+
+
+def swap_far(block, m):
+    return lax.ppermute(block, "far", [(i, i ^ m) for i in range(lax.axis_size("far"))])
 
 
 def dot(left, right):
@@ -93,17 +98,19 @@
             part[i % near, i // near, :, span] = value[i * share : (i + 1) * share]
 
 
-def quad_body(w, core, received, rows, block, mine, other, held):
-    far, _, share = block.shape[0], block.shape[1], received.shape[2]
-    for f in range(far):
-        total = received[0, f].astype(F32)
+def quad_body(w, place, received, *refs):
+    far, share = received.shape[1], received.shape[2]
+    lowers, parts, (mine, other, rows, held) = refs[:far], refs[far : 2 * far], refs[2 * far :]
+    for m in range(far):
+        block = place[1] ^ m
+        total = received[0, block].astype(F32)
         for i in range(1, received.shape[0]):
-            total = total + received[i, f].astype(F32)
+            total = total + received[i, block].astype(F32)
         total = total.astype(BF16)
-        held[f * share : (f + 1) * share, :] = total
-        for k in range(4):
-            block[f, k * share : (k + 1) * share, :] = total[:, k * w : (k + 1) * w]
-    for out, sibling in ((mine, core[0]), (other, 1 - core[0])):
+        parts[m][...] = total
+        held[m * share : (m + 1) * share, :] = total
+        rows[m * share : (m + 1) * share, :] = lowers[m][...]
+    for out, sibling in ((mine, place[0]), (other, 1 - place[0])):
         first = pl.ds(pl.multiple_of(sibling * w, w), w)
         second = pl.ds(pl.multiple_of((2 + sibling) * w, w), w)
         out[0] = dot_t(rows[:, first], held[:, first])
@@ -111,57 +118,79 @@
         out[2] = dot_t(rows[:, second], held[:, second])
 
 
-def core_sum_body(mine, other, sums):
-    sums[...] = (mine[...] + other[...]).astype(BF16)
-
-
-def chip_sum_body(received, copies):
+def core_sum_body(w, mine, other, sums):
+    lanes = sums.shape[2]
+    for b in range(3):
+        value = (mine[b] + other[b]).astype(BF16)
+        for h in range(w // lanes):
+            sums[h, b * w : (b + 1) * w, :] = value[:, h * lanes : (h + 1) * lanes]
+
+
+def chunk_sum_body(received, copies):
     value = reduced(received)
     for i in range(copies.shape[0]):
         copies[i] = value
 
 
-def near_sum_body(received, block, packed):
-    chunk = received.shape[1]
-    value = reduced(received).astype(BF16)
-    for i in range(packed.shape[0]):
-        packed[i, :chunk, :] = value
-        packed[i, chunk:, :] = block[i]
-
-
-def far_sum_body(received, pivot, copies):
-    total = pivot[...].astype(F32)
-    for i in range(received.shape[0]):
-        total = total + received[i, : pivot.shape[0], :].astype(F32)
-    total = total.astype(BF16)
-    for i in range(copies.shape[0]):
-        copies[i] = total
-
-
-def column_body(w, chunk, tile, received, link, anc_one, anc_two, widths, column_one, column_two):
-    total = received[0, chunk:, :].astype(F32)
-    for i in range(1, received.shape[0]):
-        total = total + received[i, chunk:, :].astype(F32)
-    share = column_one.shape[0]
+def pivot_body(w, place, one, two, widths, pivot, stack):
+    row = lax.broadcasted_iota(jnp.int32, (w, w), 0)
+    column = lax.broadcasted_iota(jnp.int32, (w, w), 1)
+    lanes = stack.shape[1]
+    for b, source, width in (
+        (0, one, widths[place[0]]),
+        (1, None, 0),
+        (2, two, widths[2 + place[0]]),
+    ):
+        value = jnp.zeros((w, w), F32)
+        if source is not None:
+            value = jnp.where((row < width) & (column < width), source[place[0]].astype(F32), value)
+        for h in range(w // lanes):
+            start = (3 * h + b) * w
+            stack[start : start + w, :] = value[:, h * lanes : (h + 1) * lanes]
+    size = pivot.shape[0]
+    pivot[...] = stack[pl.ds(pl.multiple_of(place[2] * size, size), size), :]
+
+
+def all_sum_body(received, pivot, copies):
+    near, chunk = NEAR, received.shape[1]
+    for n in range(near):
+        total = pivot[n * chunk : (n + 1) * chunk, :]
+        for i in range(n, received.shape[0], near):
+            total = total + received[i]
+        total = total.astype(BF16)
+        for i in range(copies.shape[0]):
+            copies[i, n * chunk : (n + 1) * chunk, :] = total
+
+
+def column_body(w, tile, *refs):
+    parts, (link, anc_one, anc_two, widths, column_one, column_two) = refs[:-6], refs[-6:]
+    total = parts[0][...].astype(F32)
+    for part in parts[1:]:
+        total = total + part[...].astype(F32)
     for s in range(2):
         span = slice(s * w, (s + 1) * w)
         here_one = jnp.where(is_member(anc_one, s, tile[0]), 1.0, 0.0)
         here_two = jnp.where(is_member(anc_two, s, tile[0]), 1.0, 0.0)
-        one = (-(total[s * share : (s + 1) * share] * here_one)).astype(BF16)
+        one = (-(total[:, span] * here_one)).astype(BF16)
         column_one[:, span] = one
-        two = total[(2 + s) * share : (3 + s) * share] + dot(one, masked_link(w, link, widths, s))
+        two = total[:, (2 + s) * w : (3 + s) * w] + dot(one, masked_link(w, link, widths, s))
         column_two[:, span] = (-(two * here_two)).astype(BF16)
+
+
+def side_by_side(total, b, w):
+    span = slice(b * w, (b + 1) * w)
+    return jnp.concatenate([total[h, span, :] for h in range(total.shape[0])], axis=1)
 
 
 def final_body(w, core, mine, other, link, widths, block_one, parent_rows, block_two):
     for total, sibling in ((mine, core[0]), (other, 1 - core[0])):
         tie = masked_link(w, link, widths, sibling)
-        block = total[0]
-        cross = total[1]
+        block = side_by_side(total, 0, w)
+        cross = side_by_side(total, 1, w)
         block_one[sibling] = block
         parent = (cross.astype(F32) - dot(block, tie)).astype(BF16)
         parent_rows[sibling] = parent
-        rest = total[2].astype(F32) - dot_t(cross, tie) - dot_t(tie, parent)
+        rest = side_by_side(total, 2, w).astype(F32) - dot_t(cross, tie) - dot_t(tie, parent)
         block_two[sibling] = rest.astype(BF16)
 
 
@@ -200,9 +229,10 @@
             for z in range(planes):
                 pairs.append(((q * CORES + k) * planes + z, (z * CORES + k) * planes + q))
     moved = lax.ppermute(lower, GRID, pairs)
-    rows = lax.all_gather(lower, "far", axis=0, tiled=True)
+    lowers = [lower] + [swap_far(lower, m) for m in range(1, far_n)]
     (moved,) = kernel_call(copy_body, "copies", [VMEM], [((chips,) + whole, BF16)])(moved)
-    mine = exchange(moved, "chip").reshape(chips * share, 4 * w)
+    mine, *lowers[:-1] = lax.optimization_barrier((exchange(moved, "chip"), *lowers[:-1]))
+    mine = mine.reshape(chips * share, 4 * w)
     other = swap_cores(mine)
 
     (part,) = kernel_call(
@@ -213,48 +243,49 @@
     )(core_ref, ancestor_inverse, mine, other)
     part = exchange(part, "near")
 
-    block, mine, other = pl.pallas_call(
+    place = jnp.stack([core, lax.axis_index("far").astype(jnp.int32), chip])
+    *parts, mine, other = pl.pallas_call(
         functools.partial(quad_body, w),
         name="quad",
-        in_specs=[SMEM, VMEM, VMEM],
-        out_specs=[VMEM] * 3,
-        out_shape=[
-            jax.ShapeDtypeStruct((far_n, 4 * share, w), BF16),
-            jax.ShapeDtypeStruct((3, w, w), F32),
-            jax.ShapeDtypeStruct((3, w, w), F32),
-        ],
-        scratch_shapes=[pltpu.VMEM((far_n * share, 4 * w), BF16)],
+        in_specs=[SMEM] + [VMEM] * (1 + far_n),
+        out_specs=[VMEM] * (far_n + 2),
+        out_shape=[jax.ShapeDtypeStruct(whole, BF16)] * far_n
+        + [jax.ShapeDtypeStruct((3, w, w), F32)] * 2,
+        scratch_shapes=[pltpu.VMEM((far_n * share, 4 * w), BF16)] * 2,
         compiler_params=pltpu.CompilerParams(vmem_limit_bytes=40 * 1024 * 1024),
-    )(core_ref, part, rows)
+    )(place, part, *lowers)
+    parts = parts[:1] + [swap_far(parts[m], m) for m in range(1, far_n)]
     other = swap_cores(other)
-    chunk = 3 * w // chips
-    (sums,) = kernel_call(core_sum_body, "core_sum", [VMEM] * 2, [((3, w, w), BF16)])(mine, other)
-    sums = exchange(sums.reshape(chips, chunk, w), "chip")
-    (sums,) = kernel_call(chip_sum_body, "chip_sum", [VMEM], [((NEAR, chunk, w), F32)])(sums)
-    sums = exchange(sums, "near")
-    (packed,) = kernel_call(
-        near_sum_body, "near_sum", [VMEM] * 2, [((far_n, chunk + 4 * share, w), BF16)]
-    )(sums, block)
-    packed = exchange(packed, "far")
-
-    keep = (jnp.arange(w, dtype=jnp.int32)[None, :] < widths[:, None]).astype(BF16)
-    pivot_one = diag_inverse_one * keep[0:2, :, None] * keep[0:2, None, :]
-    pivot_two = diag_inverse_two * keep[2:4, :, None] * keep[2:4, None, :]
-    pivots = jnp.stack([pivot_one, jnp.zeros_like(pivot_one), pivot_two], axis=1)
-    pivot = lax.dynamic_slice_in_dim(
-        pivots.reshape(6 * w, w), core * (3 * w) + chip * chunk, chunk, axis=0
+    flat = (w // LANES, 3 * w, LANES)
+    chunk = 3 * w * w // LANES // (chips * NEAR)
+    (sums,) = kernel_call(
+        functools.partial(core_sum_body, w), "core_sum", [VMEM] * 2, [(flat, BF16)]
+    )(mine, other)
+    sums = exchange(sums.reshape(chips * NEAR, chunk, LANES), ("chip", "near"))
+    sums, *parts[:-1] = lax.optimization_barrier((sums, *parts[:-1]))
+    (sums,) = kernel_call(chunk_sum_body, "chunk_sum", [VMEM], [((planes, chunk, LANES), F32)])(
+        sums
     )
-    (total,) = kernel_call(far_sum_body, "far_sum", [VMEM] * 2, [((chips, chunk, w), BF16)])(
-        packed, pivot
-    )
-    mine = exchange(total, "chip").reshape(3, w, w)
+    sums, parts[-1] = lax.optimization_barrier((exchange(sums, ("far", "near")), parts[-1]))
+    pivot = pl.pallas_call(
+        functools.partial(pivot_body, w),
+        name="pivot",
+        in_specs=[SMEM, VMEM, VMEM, SMEM],
+        out_specs=VMEM,
+        out_shape=jax.ShapeDtypeStruct((NEAR * chunk, LANES), F32),
+        scratch_shapes=[pltpu.VMEM((3 * w * w // LANES, LANES), F32)],
+    )(place, diag_inverse_one, diag_inverse_two, widths)
+    (total,) = kernel_call(
+        all_sum_body, "all_sum", [VMEM] * 2, [((chips, NEAR * chunk, LANES), BF16)]
+    )(sums, pivot)
+    mine = exchange(total, "chip").reshape(flat)
     other = swap_cores(mine)
     column_one, column_two = kernel_call(
-        functools.partial(column_body, w, chunk),
+        functools.partial(column_body, w),
         "columns",
-        [SMEM, VMEM, VMEM, SMEM, SMEM, SMEM],
+        [SMEM] + [VMEM] * (far_n + 1) + [SMEM] * 3,
         [((share, 2 * w), BF16)] * 2,
-    )(tile, packed, link_two, ancestors_one, ancestors_two, widths)
+    )(tile, *parts, link_two, ancestors_one, ancestors_two, widths)
     block_one, parent_rows, block_two = kernel_call(
         functools.partial(final_body, w),
         "final",

time: 153 us -> 163 us (1.065)
  starting transfers between devices: 34.7 us -> 106 us
  blocking collectives: 83.3 us -> 14.8 us
  Pallas kernels: 7.13 us -> 10.4 us
  waiting for transfers between devices: 24.4 us -> 27.3 us
    all_to_all x3 -> x1, blocking collectives: 58.4 us -> 14.8 us  [exchange(): return lax.all_to_all(blocks, axis, split_axis=0, concat_axis=0, tiled=True)]
    ppermute x0 -> x6, starting transfers between devices: none -> 41.1 us  [swap_far(): lax.ppermute(block, 'far', [(i, i ^ m) for i in range(lax.axis_size('far'...]
    all_to_all x3 -> x4, starting transfers between devices: 17.6 us -> 45.8 us  [exchange(): return lax.all_to_all(blocks, axis, split_axis=0, concat_axis=0, tiled=True)]
    all_gather x1 -> x0, blocking collectives: 24.9 us -> none  [local(): rows = lax.all_gather(lower, 'far', axis=0, tiled=True)]
    ppermute x0 -> x6, waiting for transfers between devices: none -> 19.4 us  [swap_far(): lax.ppermute(block, 'far', [(i, i ^ m) for i in range(lax.axis_size('far'...]
    all_to_all x3 -> x4, waiting for transfers between devices: 21 us -> 4.57 us  [exchange(): return lax.all_to_all(blocks, axis, split_axis=0, concat_axis=0, tiled=True)]
    ppermute x3, starting transfers between devices: 16.4 us -> 18.6 us  [swap_cores(): return lax.ppermute(block, 'core', [(0, 1), (1, 0)])]
    pallas_call x5, Pallas kernels: 2.96 us -> 4.83 us  [the longest x1 1.75 us: local(): pl.pallas_call(functools.partial(pivot_body, w), name='pivot', in_specs=[...]
  transfers between devices with their start and end apart: 7 -> 14, of which waited for: 4 -> 7; matrix products, arithmetic and copies ran while one was open for 0% -> 0% of each run, Pallas kernels for 1% -> 2%
where the time goes in v5:
time: 163 us; the launch traced here: 162 us
  starting transfers between devices  106 us (65%)
  waiting for transfers between devices  27.3 us (17%)
  blocking collectives  14.8 us (9%)
  Pallas kernels  10.4 us (6%)
  local copies, waits for them, and re-layouts  2.22 us (1%)
    all_to_all x4, starting transfers between devices, exchange(): return lax.all_to_all(blocks, axis, split_axis=0, concat_axis=0, tiled=True)  45.8 us
    ppermute x6, starting transfers between devices, swap_far(): lax.ppermute(block, 'far', [(i, i ^ m) for i in range(lax.axis_size('far'...  41.1 us
    ppermute x6, waiting for transfers between devices, swap_far(): lax.ppermute(block, 'far', [(i, i ^ m) for i in range(lax.axis_size('far'...  19.4 us
    ppermute x3, starting transfers between devices, swap_cores(): return lax.ppermute(block, 'core', [(0, 1), (1, 0)])  18.6 us
    all_to_all x1, blocking collectives, exchange(): return lax.all_to_all(blocks, axis, split_axis=0, concat_axis=0, tiled=True)  14.8 us
    all_to_all x4, waiting for transfers between devices, exchange(): return lax.all_to_all(blocks, axis, split_axis=0, concat_axis=0, tiled=True)  4.57 us
    ppermute x3, waiting for transfers between devices, swap_cores(): return lax.ppermute(block, 'core', [(0, 1), (1, 0)])  3.41 us
  transfers between devices with their start and end apart: 14, of which 7 were waited for; matrix products, arithmetic and copies ran while one was open for 0% of the time, Pallas kernels for 2%

profile of v5, /device:TPU:1, one launch (start us, length us, event | category | flops | bytes accessed | tf_op | source)
XLA Modules:
  0.0 162.0 jit_solution(15417323686706890671)
XLA Ops:
  0.6 0.0 copy-start.3
  0.7 0.0 copy-start.9
  0.7 0.0 copy-start.5
  0.7 0.7 copy-done.3
  1.4 0.0 copy-done.9
  1.4 0.0 copy-done.8
  1.4 0.7 copy-done.4
  2.1 0.7 mask.1.refs_0_
  2.7 0.7 collective-permute-start
  3.4 0.0 collective-permute-done.source
  3.4 0.9 copies.1
  4.3 24.9 %all-to-all-start = ((bf16[16,16,1024]{2,1,0:T(8,128)(2,1)}), bf16[16,16,1024]{2,1,0:T(8,128)(2,1)S(1)}, u32[]{:S(2)}, u32[]{:S(2)}) async-start(bf16[16,16,1024]{2,1,0:T(8,128)(2,1)} %copies.1), calls=%async_computation | async-start | bytes 1048576 | tf_op jit(solution)/shard_map/all_to_all | solution.py:33
  29.2 7.2 %collective-permute-start.1 = (bf16[16,1024]{1,0:T(8,128)(2,1)S(1)}, bf16[16,1024]{1,0:T(8,128)(2,1)S(1)}, u32[]{:S(2)}, u32[]{:S(2)}) collective-permute-start(bf16[16,1024]{1,0:T(8,128)(2,1)S(1)} %mask.1.refs_0_), channel_id=1, source_target_pairs={{0,4},{4,0},{8,12},{12,8},{1,5},{5,1},{9,13},{13,9},{2,6},{6,2},{1... | collective-permute-start | bytes 98312 | tf_op jit(solution)/shard_map/ppermute | solution.py:41
  36.5 9.2 %collective-permute-start.2 = (bf16[16,1024]{1,0:T(8,128)(2,1)S(1)}, bf16[16,1024]{1,0:T(8,128)(2,1)S(1)}, u32[]{:S(2)}, u32[]{:S(2)}) collective-permute-start(bf16[16,1024]{1,0:T(8,128)(2,1)S(1)} %mask.1.refs_0_), channel_id=1, source_target_pairs={{0,8},{4,12},{8,0},{12,4},{1,9},{5,13},{9,1},{13,5},{2,10},{6,14},... | collective-permute-start | bytes 98312 | tf_op jit(solution)/shard_map/ppermute | solution.py:41
  45.7 0.0 collective-permute-done.1.refs_1_
  45.7 4.2 %collective-permute-done.2.refs_2_ = bf16[16,1024]{1,0:T(8,128)(2,1)S(1)} collective-permute-done((bf16[16,1024]{1,0:T(8,128)(2,1)S(1)}, bf16[16,1024]{1,0:T(8,128)(2,1)S(1)}, u32[]{:S(2)}, u32[]{:S(2)}) %collective-permute-start.2) | collective-permute-done | bytes 32800 | tf_op jit(solution)/shard_map/ppermute | solution.py:41
  49.8 0.0 all-to-all-done
  49.8 5.8 %collective-permute-start.3 = (bf16[256,1024]{1,0:T(8,128)(2,1)S(1)}, bf16[256,1024]{1,0:T(8,128)(2,1)S(1)}, u32[]{:S(2)}, u32[]{:S(2)}) collective-permute-start(bf16[256,1024]{1,0:T(8,128)(2,1)S(1)} %bitcast.7), channel_id=1, source_target_pairs={{0,16},{16,0},{1,17},{17,1},{2,18},{18,2},{3,19},{19,3},{4,20},{20... | collective-permute-start | bytes 1572872 | tf_op jit(solution)/shard_map/ppermute | solution.py:37
  55.6 1.5 collective-permute-done.3.other
  57.2 1.3 product.1
  58.4 4.6 %all-to-all-start.1 = ((bf16[4,4,16,1024]{3,2,1,0:T(8,128)(2,1)}), bf16[4,4,16,1024]{3,2,1,0:T(8,128)(2,1)S(1)}, u32[]{:S(2)}, u32[]{:S(2)}) async-start(bf16[4,4,16,1024]{3,2,1,0:T(8,128)(2,1)} %product.1), calls=%async_computation.1 | async-start | bytes 1048576 | tf_op jit(solution)/shard_map/all_to_all | solution.py:33
  63.0 5.6 %collective-permute-start.4 = (bf16[16,1024]{1,0:T(8,128)(2,1)S(1)}, bf16[16,1024]{1,0:T(8,128)(2,1)S(1)}, u32[]{:S(2)}, u32[]{:S(2)}) collective-permute-start(bf16[16,1024]{1,0:T(8,128)(2,1)S(1)} %mask.1.refs_0_), channel_id=1, source_target_pairs={{0,12},{4,8},{8,4},{12,0},{1,13},{5,9},{9,5},{13,1},{2,14},{6,10},... | collective-permute-start | bytes 98312 | tf_op jit(solution)/shard_map/ppermute | solution.py:41
  68.6 0.1 pad_add_fusion.place
  68.7 7.9 %collective-permute-done.4.refs_3_ = bf16[16,1024]{1,0:T(8,128)(2,1)S(1)} collective-permute-done((bf16[16,1024]{1,0:T(8,128)(2,1)S(1)}, bf16[16,1024]{1,0:T(8,128)(2,1)S(1)}, u32[]{:S(2)}, u32[]{:S(2)}) %collective-permute-start.4) | collective-permute-done | bytes 32800 | tf_op jit(solution)/shard_map/ppermute | solution.py:41
  76.6 1.1 all-to-all-done.1.received
  77.7 1.0 quad.1
  78.8 3.7 %collective-permute-start.5 = (f32[3,256,256]{2,1,0:T(8,128)S(1)}, f32[3,256,256]{2,1,0:T(8,128)S(1)}, u32[]{:S(2)}, u32[]{:S(2)}) collective-permute-start(f32[3,256,256]{2,1,0:T(8,128)S(1)} %get-tuple-element.31), channel_id=1, source_target_pairs={{0,16},{16,0},{1,17},{17,1},{2,18},{18,2},{3,19},{19,3},{4,20},{20... | collective-permute-start | bytes 2359304 | tf_op jit(solution)/shard_map/ppermute | solution.py:37
  82.4 1.9 %collective-permute-done.5.other = f32[3,256,256]{2,1,0:T(8,128)S(1)} collective-permute-done((f32[3,256,256]{2,1,0:T(8,128)S(1)}, f32[3,256,256]{2,1,0:T(8,128)S(1)}, u32[]{:S(2)}, u32[]{:S(2)}) %collective-permute-start.5) | collective-permute-done | bytes 786464 | tf_op jit(solution)/shard_map/ppermute | solution.py:37
  84.3 0.9 core_sum.1
  85.2 10.3 %all-to-all-start.2 = ((bf16[64,24,128]{2,1,0:T(8,128)(2,1)}), bf16[64,24,128]{2,1,0:T(8,128)(2,1)S(1)}, u32[]{:S(2)}, u32[]{:S(2)}) async-start(bf16[64,24,128]{2,1,0:T(8,128)(2,1)} %bitcast.5), calls=%async_computation.2 | async-start | bytes 786432 | tf_op jit(solution)/shard_map/all_to_all | solution.py:33
  95.5 5.8 %collective-permute-start.6 = (bf16[16,1024]{1,0:T(8,128)(2,1)S(1)}, bf16[16,1024]{1,0:T(8,128)(2,1)S(1)}, u32[]{:S(2)}, u32[]{:S(2)}) collective-permute-start(bf16[16,1024]{1,0:T(8,128)(2,1)S(1)} %get-tuple-element.33), channel_id=1, source_target_pairs={{0,4},{4,0},{8,12},{12,8},{1,5},{5,1},{9,13},{13,9},{2,6},{6,2},{1... | collective-permute-start | bytes 98312 | tf_op jit(solution)/shard_map/ppermute | solution.py:41
  101.3 6.1 %collective-permute-start.7 = (bf16[16,1024]{1,0:T(8,128)(2,1)S(1)}, bf16[16,1024]{1,0:T(8,128)(2,1)S(1)}, u32[]{:S(2)}, u32[]{:S(2)}) collective-permute-start(bf16[16,1024]{1,0:T(8,128)(2,1)S(1)} %get-tuple-element.34), channel_id=1, source_target_pairs={{0,8},{4,12},{8,0},{12,4},{1,9},{5,13},{9,1},{13,5},{2,10},{6,14},... | collective-permute-start | bytes 98312 | tf_op jit(solution)/shard_map/ppermute | solution.py:41
  107.4 0.0 collective-permute-done.6.refs_1_
  107.4 7.3 %collective-permute-done.7.refs_2_ = bf16[16,1024]{1,0:T(8,128)(2,1)S(1)} collective-permute-done((bf16[16,1024]{1,0:T(8,128)(2,1)S(1)}, bf16[16,1024]{1,0:T(8,128)(2,1)S(1)}, u32[]{:S(2)}, u32[]{:S(2)}) %collective-permute-start.7) | collective-permute-done | bytes 32800 | tf_op jit(solution)/shard_map/ppermute | solution.py:41
  114.8 0.0 all-to-all-done.2.received
  114.8 0.8 chunk_sum.1
  115.5 6.0 %all-to-all-start.3 = ((f32[16,24,128]{2,1,0:T(8,128)}), f32[16,24,128]{2,1,0:T(8,128)S(1)}, u32[]{:S(2)}, u32[]{:S(2)}) async-start(f32[16,24,128]{2,1,0:T(8,128)} %chunk_sum.1), calls=%async_computation.3 | async-start | bytes 393216 | tf_op jit(solution)/shard_map/all_to_all | solution.py:33
  121.5 7.2 %collective-permute-start.8 = (bf16[16,1024]{1,0:T(8,128)(2,1)S(1)}, bf16[16,1024]{1,0:T(8,128)(2,1)S(1)}, u32[]{:S(2)}, u32[]{:S(2)}) collective-permute-start(bf16[16,1024]{1,0:T(8,128)(2,1)S(1)} %get-tuple-element.39), channel_id=1, source_target_pairs={{0,12},{4,8},{8,4},{12,0},{1,13},{5,9},{9,5},{13,1},{2,14},{6,10},... | collective-permute-start | bytes 98312 | tf_op jit(solution)/shard_map/ppermute | solution.py:41
  128.7 1.7 %pivot.1 = f32[96,128]{1,0:T(8,128)} custom-call(s32[3]{0:T(128)} %copy-done.7, bf16[2,256,256]{2,1,0:T(8,128)(2,1)} %one.3, bf16[2,256,256]{2,1,0:T(8,128)(2,1)} %two.3, s32[4]{0:T(128)} %widths.5), custom_call_target="tpu_custom_call" | custom-call | tf_op jit(solution)/shard_map/pivot/pallas_call | solution.py:270
  130.5 0.0 collective-permute-done.8.refs_3_
  130.5 3.4 %all-to-all-done.3.received = f32[16,24,128]{2,1,0:T(8,128)S(1)} async-done(((f32[16,24,128]{2,1,0:T(8,128)}), f32[16,24,128]{2,1,0:T(8,128)S(1)}, u32[]{:S(2)}, u32[]{:S(2)}) %all-to-all-start.3) | async-done | bytes 196640 | tf_op jit(solution)/shard_map/all_to_all | solution.py:33
  133.9 0.8 copy-done.2
  134.7 0.0 copy-start
  134.8 14.8 %all_to_all.25 = bf16[16,96,128]{2,1,0:T(8,128)(2,1)S(1)} all-to-all(bf16[16,96,128]{2,1,0:T(8,128)(2,1)S(1)} %all_sum.1), channel_id=1, replica_groups=mesh['chip'=16,'core'=2,'far'=4,'near'=4] {'chip'}, dimensions={0} | all-to-all | bytes 786432 | tf_op jit(solution)/shard_map/all_to_all | solution.py:33
  149.6 9.1 %collective-permute-start.9 = (bf16[2,768,128]{2,1,0:T(8,128)(2,1)S(1)}, bf16[2,768,128]{2,1,0:T(8,128)(2,1)S(1)}, u32[]{:S(2)}, u32[]{:S(2)}) collective-permute-start(bf16[2,768,128]{2,1,0:T(8,128)(2,1)S(1)} %bitcast.9), channel_id=1, source_target_pairs={{0,16},{16,0},{1,17},{17,1},{2,18},{18,2},{3,19},{19,3},{4,20},{20... | collective-permute-start | bytes 1179656 | tf_op jit(solution)/shard_map/ppermute | solution.py:37
  158.8 1.4 columns.1
  160.2 0.0 collective-permute-done.9.other
  160.2 1.8 %final.1 = (bf16[2,256,256]{2,1,0:T(8,128)(2,1)}, bf16[2,256,256]{2,1,0:T(8,128)(2,1)}, bf16[2,256,256]{2,1,0:T(8,128)(2,1)}) custom-call(s32[1]{0:T(128)} %bitcast.1.core, bf16[2,768,128]{2,1,0:T(8,128)(2,1)S(1)} %bitcast.10, bf16[2,768,128]{2,1,0:T(8,128)(2,1)S(1)} %collective-permute-done.9.other, bf16[2,256,256]{2,1,0:T(8,128)(2,1)S(1)} %copy-done, ...), custom_call_target="tpu_custom_call" | custom-call | tf_op jit(solution)/shard_map/final/pallas_call | solution.py:289
  (12 shorter events, 0.1 us)
Async XLA Ops:
  0.6 0.7 copy-start.3
  0.7 0.7 copy-start.9
  0.7 0.7 copy-start.5
  0.7 0.7 copy-start.8
  1.4 0.7 copy-start.4
  2.7 0.7 collective-permute-start
  4.3 52.9 %copy-start.1 = (bf16[256,512]{1,0:T(8,128)(2,1)S(1)}, bf16[256,512]{1,0:T(8,128)(2,1)}, u32[]{:S(2)}) copy-start(bf16[256,512]{1,0:T(8,128)(2,1)} %inverse.1) | copy-start | bytes 786436
  4.3 45.5 %all-to-all-start = ((bf16[16,16,1024]{2,1,0:T(8,128)(2,1)}), bf16[16,16,1024]{2,1,0:T(8,128)(2,1)S(1)}, u32[]{:S(2)}, u32[]{:S(2)}) async-start(bf16[16,16,1024]{2,1,0:T(8,128)(2,1)} %copies.1), calls=%async_computation | async-start | bytes 1048576 | tf_op jit(solution)/shard_map/all_to_all | solution.py:33
  29.2 16.4 %collective-permute-start.1 = (bf16[16,1024]{1,0:T(8,128)(2,1)S(1)}, bf16[16,1024]{1,0:T(8,128)(2,1)S(1)}, u32[]{:S(2)}, u32[]{:S(2)}) collective-permute-start(bf16[16,1024]{1,0:T(8,128)(2,1)S(1)} %mask.1.refs_0_), channel_id=1, source_target_pairs={{0,4},{4,0},{8,12},{12,8},{1,5},{5,1},{9,13},{13,9},{2,6},{6,2},{1... | collective-permute-start | bytes 98312 | tf_op jit(solution)/shard_map/ppermute | solution.py:41
  36.5 13.4 %collective-permute-start.2 = (bf16[16,1024]{1,0:T(8,128)(2,1)S(1)}, bf16[16,1024]{1,0:T(8,128)(2,1)S(1)}, u32[]{:S(2)}, u32[]{:S(2)}) collective-permute-start(bf16[16,1024]{1,0:T(8,128)(2,1)S(1)} %mask.1.refs_0_), channel_id=1, source_target_pairs={{0,8},{4,12},{8,0},{12,4},{1,9},{5,13},{9,1},{13,5},{2,10},{6,14},... | collective-permute-start | bytes 98312 | tf_op jit(solution)/shard_map/ppermute | solution.py:41
  49.8 7.3 %collective-permute-start.3 = (bf16[256,1024]{1,0:T(8,128)(2,1)S(1)}, bf16[256,1024]{1,0:T(8,128)(2,1)S(1)}, u32[]{:S(2)}, u32[]{:S(2)}) collective-permute-start(bf16[256,1024]{1,0:T(8,128)(2,1)S(1)} %bitcast.7), channel_id=1, source_target_pairs={{0,16},{16,0},{1,17},{17,1},{2,18},{18,2},{3,19},{19,3},{4,20},{20... | collective-permute-start | bytes 1572872 | tf_op jit(solution)/shard_map/ppermute | solution.py:37
  58.4 19.3 %all-to-all-start.1 = ((bf16[4,4,16,1024]{3,2,1,0:T(8,128)(2,1)}), bf16[4,4,16,1024]{3,2,1,0:T(8,128)(2,1)S(1)}, u32[]{:S(2)}, u32[]{:S(2)}) async-start(bf16[4,4,16,1024]{3,2,1,0:T(8,128)(2,1)} %product.1), calls=%async_computation.1 | async-start | bytes 1048576 | tf_op jit(solution)/shard_map/all_to_all | solution.py:33
  63.0 13.6 %collective-permute-start.4 = (bf16[16,1024]{1,0:T(8,128)(2,1)S(1)}, bf16[16,1024]{1,0:T(8,128)(2,1)S(1)}, u32[]{:S(2)}, u32[]{:S(2)}) collective-permute-start(bf16[16,1024]{1,0:T(8,128)(2,1)S(1)} %mask.1.refs_0_), channel_id=1, source_target_pairs={{0,12},{4,8},{8,4},{12,0},{1,13},{5,9},{9,5},{13,1},{2,14},{6,10},... | collective-permute-start | bytes 98312 | tf_op jit(solution)/shard_map/ppermute | solution.py:41
  68.7 10.0 %copy-start.7 = (s32[3]{0:T(128)}, s32[3]{0:T(128)S(1)}, u32[]{:S(2)}) copy-start(s32[3]{0:T(128)S(1)} %pad_add_fusion.place) | copy-start | bytes 40
  78.8 5.6 %collective-permute-start.5 = (f32[3,256,256]{2,1,0:T(8,128)S(1)}, f32[3,256,256]{2,1,0:T(8,128)S(1)}, u32[]{:S(2)}, u32[]{:S(2)}) collective-permute-start(f32[3,256,256]{2,1,0:T(8,128)S(1)} %get-tuple-element.31), channel_id=1, source_target_pairs={{0,16},{16,0},{1,17},{17,1},{2,18},{18,2},{3,19},{19,3},{4,20},{20... | collective-permute-start | bytes 2359304 | tf_op jit(solution)/shard_map/ppermute | solution.py:37
  85.2 29.6 %all-to-all-start.2 = ((bf16[64,24,128]{2,1,0:T(8,128)(2,1)}), bf16[64,24,128]{2,1,0:T(8,128)(2,1)S(1)}, u32[]{:S(2)}, u32[]{:S(2)}) async-start(bf16[64,24,128]{2,1,0:T(8,128)(2,1)} %bitcast.5), calls=%async_computation.2 | async-start | bytes 786432 | tf_op jit(solution)/shard_map/all_to_all | solution.py:33
  95.5 11.9 %collective-permute-start.6 = (bf16[16,1024]{1,0:T(8,128)(2,1)S(1)}, bf16[16,1024]{1,0:T(8,128)(2,1)S(1)}, u32[]{:S(2)}, u32[]{:S(2)}) collective-permute-start(bf16[16,1024]{1,0:T(8,128)(2,1)S(1)} %get-tuple-element.33), channel_id=1, source_target_pairs={{0,4},{4,0},{8,12},{12,8},{1,5},{5,1},{9,13},{13,9},{2,6},{6,2},{1... | collective-permute-start | bytes 98312 | tf_op jit(solution)/shard_map/ppermute | solution.py:41
  101.3 13.5 %collective-permute-start.7 = (bf16[16,1024]{1,0:T(8,128)(2,1)S(1)}, bf16[16,1024]{1,0:T(8,128)(2,1)S(1)}, u32[]{:S(2)}, u32[]{:S(2)}) collective-permute-start(bf16[16,1024]{1,0:T(8,128)(2,1)S(1)} %get-tuple-element.34), channel_id=1, source_target_pairs={{0,8},{4,12},{8,0},{12,4},{1,9},{5,13},{9,1},{13,5},{2,10},{6,14},... | collective-permute-start | bytes 98312 | tf_op jit(solution)/shard_map/ppermute | solution.py:41
  115.5 18.4 %all-to-all-start.3 = ((f32[16,24,128]{2,1,0:T(8,128)}), f32[16,24,128]{2,1,0:T(8,128)S(1)}, u32[]{:S(2)}, u32[]{:S(2)}) async-start(f32[16,24,128]{2,1,0:T(8,128)} %chunk_sum.1), calls=%async_computation.3 | async-start | bytes 393216 | tf_op jit(solution)/shard_map/all_to_all | solution.py:33
  121.5 8.9 %collective-permute-start.8 = (bf16[16,1024]{1,0:T(8,128)(2,1)S(1)}, bf16[16,1024]{1,0:T(8,128)(2,1)S(1)}, u32[]{:S(2)}, u32[]{:S(2)}) collective-permute-start(bf16[16,1024]{1,0:T(8,128)(2,1)S(1)} %get-tuple-element.39), channel_id=1, source_target_pairs={{0,12},{4,8},{8,4},{12,0},{1,13},{5,9},{9,5},{13,1},{2,14},{6,10},... | collective-permute-start | bytes 98312 | tf_op jit(solution)/shard_map/ppermute | solution.py:41
  133.9 0.8 copy-start.2
  134.7 24.0 %copy-start = (bf16[2,256,256]{2,1,0:T(8,128)(2,1)S(1)}, bf16[2,256,256]{2,1,0:T(8,128)(2,1)}, u32[]{:S(2)}) copy-start(bf16[2,256,256]{2,1,0:T(8,128)(2,1)} %link.1) | copy-start | bytes 786436
  149.6 9.2 %copy-start.6 = (s32[4]{0:T(128)S(1)}, s32[4]{0:T(128)}, u32[]{:S(2)}) copy-start(s32[4]{0:T(128)} %widths.5) | copy-start | bytes 52
  149.6 10.6 %collective-permute-start.9 = (bf16[2,768,128]{2,1,0:T(8,128)(2,1)S(1)}, bf16[2,768,128]{2,1,0:T(8,128)(2,1)S(1)}, u32[]{:S(2)}, u32[]{:S(2)}) collective-permute-start(bf16[2,768,128]{2,1,0:T(8,128)(2,1)S(1)} %bitcast.9), channel_id=1, source_target_pairs={{0,16},{16,0},{1,17},{17,1},{2,18},{18,2},{3,19},{19,3},{4,20},{20... | collective-permute-start | bytes 1179656 | tf_op jit(solution)/shard_map/ppermute | solution.py:37

commit v6 on v5

--- a/solution.py
+++ b/solution.py
@@ -35,10 +35,6 @@
 
 def swap_cores(block):
     return lax.ppermute(block, "core", [(0, 1), (1, 0)])
-
-
-def swap_far(block, m):
-    return lax.ppermute(block, "far", [(i, i ^ m) for i in range(lax.axis_size("far"))])
 
 
 def dot(left, right):
@@ -98,24 +94,32 @@
             part[i % near, i // near, :, span] = value[i * share : (i + 1) * share]
 
 
-def quad_body(w, place, received, *refs):
-    far, share = received.shape[1], received.shape[2]
-    lowers, parts, (mine, other, rows, held) = refs[:far], refs[far : 2 * far], refs[2 * far :]
-    for m in range(far):
-        block = place[1] ^ m
-        total = received[0, block].astype(F32)
+def near_sum_body(received, sums):
+    for f in range(sums.shape[0]):
+        total = received[0, f].astype(F32)
         for i in range(1, received.shape[0]):
-            total = total + received[i, block].astype(F32)
-        total = total.astype(BF16)
-        parts[m][...] = total
-        held[m * share : (m + 1) * share, :] = total
-        rows[m * share : (m + 1) * share, :] = lowers[m][...]
+            total = total + received[i, f].astype(F32)
+        sums[f] = total.astype(BF16)
+
+
+def column_body(
+    w, tile, place, received, lower, link, anc_one, anc_two, widths, column_one, column_two, mine, other
+):
+    total = reduced(received)
+    for s in range(2):
+        span = slice(s * w, (s + 1) * w)
+        here_one = jnp.where(is_member(anc_one, s, tile[0]), 1.0, 0.0)
+        here_two = jnp.where(is_member(anc_two, s, tile[0]), 1.0, 0.0)
+        one = (-(total[:, span] * here_one)).astype(BF16)
+        column_one[:, span] = one
+        two = total[:, (2 + s) * w : (3 + s) * w] + dot(one, masked_link(w, link, widths, s))
+        column_two[:, span] = (-(two * here_two)).astype(BF16)
     for out, sibling in ((mine, place[0]), (other, 1 - place[0])):
         first = pl.ds(pl.multiple_of(sibling * w, w), w)
         second = pl.ds(pl.multiple_of((2 + sibling) * w, w), w)
-        out[0] = dot_t(rows[:, first], held[:, first])
-        out[1] = dot_t(held[:, first], rows[:, second])
-        out[2] = dot_t(rows[:, second], held[:, second])
+        out[0] = -dot_t(lower[:, first], column_one[:, first])
+        out[1] = dot_t(column_one[:, first], lower[:, second])
+        out[2] = -dot_t(lower[:, second], column_two[:, first])
 
 
 def core_sum_body(w, mine, other, sums):
@@ -148,7 +152,7 @@
             start = (3 * h + b) * w
             stack[start : start + w, :] = value[:, h * lanes : (h + 1) * lanes]
     size = pivot.shape[0]
-    pivot[...] = stack[pl.ds(pl.multiple_of(place[2] * size, size), size), :]
+    pivot[...] = stack[pl.ds(pl.multiple_of(place[1] * size, size), size), :]
 
 
 def all_sum_body(received, pivot, copies):
@@ -162,21 +166,6 @@
             copies[i, n * chunk : (n + 1) * chunk, :] = total
 
 
-def column_body(w, tile, *refs):
-    parts, (link, anc_one, anc_two, widths, column_one, column_two) = refs[:-6], refs[-6:]
-    total = parts[0][...].astype(F32)
-    for part in parts[1:]:
-        total = total + part[...].astype(F32)
-    for s in range(2):
-        span = slice(s * w, (s + 1) * w)
-        here_one = jnp.where(is_member(anc_one, s, tile[0]), 1.0, 0.0)
-        here_two = jnp.where(is_member(anc_two, s, tile[0]), 1.0, 0.0)
-        one = (-(total[:, span] * here_one)).astype(BF16)
-        column_one[:, span] = one
-        two = total[:, (2 + s) * w : (3 + s) * w] + dot(one, masked_link(w, link, widths, s))
-        column_two[:, span] = (-(two * here_two)).astype(BF16)
-
-
 def side_by_side(total, b, w):
     span = slice(b * w, (b + 1) * w)
     return jnp.concatenate([total[h, span, :] for h in range(total.shape[0])], axis=1)
@@ -186,11 +175,11 @@
     for total, sibling in ((mine, core[0]), (other, 1 - core[0])):
         tie = masked_link(w, link, widths, sibling)
         block = side_by_side(total, 0, w)
-        cross = side_by_side(total, 1, w)
+        cross = side_by_side(total, 1, w).astype(F32)
         block_one[sibling] = block
-        parent = (cross.astype(F32) - dot(block, tie)).astype(BF16)
+        parent = (-(dot(block, tie) + cross)).astype(BF16)
         parent_rows[sibling] = parent
-        rest = side_by_side(total, 2, w).astype(F32) - dot_t(cross, tie) - dot_t(tie, parent)
+        rest = side_by_side(total, 2, w).astype(F32) - dot_t(tie, parent)
         block_two[sibling] = rest.astype(BF16)
 
 
@@ -229,10 +218,8 @@
             for z in range(planes):
                 pairs.append(((q * CORES + k) * planes + z, (z * CORES + k) * planes + q))
     moved = lax.ppermute(lower, GRID, pairs)
-    lowers = [lower] + [swap_far(lower, m) for m in range(1, far_n)]
     (moved,) = kernel_call(copy_body, "copies", [VMEM], [((chips,) + whole, BF16)])(moved)
-    mine, *lowers[:-1] = lax.optimization_barrier((exchange(moved, "chip"), *lowers[:-1]))
-    mine = mine.reshape(chips * share, 4 * w)
+    mine = exchange(moved, "chip").reshape(chips * share, 4 * w)
     other = swap_cores(mine)
 
     (part,) = kernel_call(
@@ -243,18 +230,15 @@
     )(core_ref, ancestor_inverse, mine, other)
     part = exchange(part, "near")
 
-    place = jnp.stack([core, lax.axis_index("far").astype(jnp.int32), chip])
-    *parts, mine, other = pl.pallas_call(
-        functools.partial(quad_body, w),
-        name="quad",
-        in_specs=[SMEM] + [VMEM] * (1 + far_n),
-        out_specs=[VMEM] * (far_n + 2),
-        out_shape=[jax.ShapeDtypeStruct(whole, BF16)] * far_n
-        + [jax.ShapeDtypeStruct((3, w, w), F32)] * 2,
-        scratch_shapes=[pltpu.VMEM((far_n * share, 4 * w), BF16)] * 2,
-        compiler_params=pltpu.CompilerParams(vmem_limit_bytes=40 * 1024 * 1024),
-    )(place, part, *lowers)
-    parts = parts[:1] + [swap_far(parts[m], m) for m in range(1, far_n)]
+    (part,) = kernel_call(near_sum_body, "near_sum", [VMEM], [((far_n,) + whole, BF16)])(part)
+    part = exchange(part, "far")
+    place = jnp.stack([core, chip])
+    column_one, column_two, mine, other = kernel_call(
+        functools.partial(column_body, w),
+        "columns",
+        [SMEM, SMEM, VMEM, VMEM, VMEM, SMEM, SMEM, SMEM],
+        [((share, 2 * w), BF16)] * 2 + [((3, w, w), F32)] * 2,
+    )(tile, place, part, lower, link_two, ancestors_one, ancestors_two, widths)
     other = swap_cores(other)
     flat = (w // LANES, 3 * w, LANES)
     chunk = 3 * w * w // LANES // (chips * NEAR)
@@ -262,11 +246,9 @@
         functools.partial(core_sum_body, w), "core_sum", [VMEM] * 2, [(flat, BF16)]
     )(mine, other)
     sums = exchange(sums.reshape(chips * NEAR, chunk, LANES), ("chip", "near"))
-    sums, *parts[:-1] = lax.optimization_barrier((sums, *parts[:-1]))
     (sums,) = kernel_call(chunk_sum_body, "chunk_sum", [VMEM], [((planes, chunk, LANES), F32)])(
         sums
     )
-    sums, parts[-1] = lax.optimization_barrier((exchange(sums, ("far", "near")), parts[-1]))
     pivot = pl.pallas_call(
         functools.partial(pivot_body, w),
         name="pivot",
@@ -275,17 +257,13 @@
         out_shape=jax.ShapeDtypeStruct((NEAR * chunk, LANES), F32),
         scratch_shapes=[pltpu.VMEM((3 * w * w // LANES, LANES), F32)],
     )(place, diag_inverse_one, diag_inverse_two, widths)
+    sums, pivot = lax.optimization_barrier((sums, pivot))
+    sums = exchange(sums, ("far", "near"))
     (total,) = kernel_call(
         all_sum_body, "all_sum", [VMEM] * 2, [((chips, NEAR * chunk, LANES), BF16)]
     )(sums, pivot)
     mine = exchange(total, "chip").reshape(flat)
     other = swap_cores(mine)
-    column_one, column_two = kernel_call(
-        functools.partial(column_body, w),
-        "columns",
-        [SMEM] + [VMEM] * (far_n + 1) + [SMEM] * 3,
-        [((share, 2 * w), BF16)] * 2,
-    )(tile, *parts, link_two, ancestors_one, ancestors_two, widths)
     block_one, parent_rows, block_two = kernel_call(
         functools.partial(final_body, w),
         "final",

time: 163 us -> 154 us (0.945)
  starting transfers between devices: 106 us -> 34 us
  blocking collectives: 14.8 us -> 79.4 us
  Pallas kernels: 10.4 us -> 7.77 us
  waiting for transfers between devices: 27.3 us -> 29.7 us
    all_to_all x1 -> x4, blocking collectives: 14.8 us -> 79.4 us  [exchange(): return lax.all_to_all(blocks, axis, split_axis=0, concat_axis=0, tiled=True)]
    ppermute x6 -> x0, starting transfers between devices: 41.1 us -> none  [swap_far(): lax.ppermute(block, 'far', [(i, i ^ m) for i in range(lax.axis_size('far'...]
    all_to_all x4 -> x2, starting transfers between devices: 45.8 us -> 15.4 us  [exchange(): return lax.all_to_all(blocks, axis, split_axis=0, concat_axis=0, tiled=True)]
    all_to_all x4 -> x2, waiting for transfers between devices: 4.57 us -> 24.9 us  [exchange(): return lax.all_to_all(blocks, axis, split_axis=0, concat_axis=0, tiled=True)]
    ppermute x6 -> x0, waiting for transfers between devices: 19.4 us -> none  [swap_far(): lax.ppermute(block, 'far', [(i, i ^ m) for i in range(lax.axis_size('far'...]
  transfers between devices with their start and end apart: 14 -> 6, of which waited for: 7 -> 5; matrix products, arithmetic and copies ran while one was open for 0% -> 0% of each run, Pallas kernels for 2% -> 1%
where the time goes in v6:
time: 154 us; the launch traced here: 153 us
  blocking collectives  79.4 us (52%)
  starting transfers between devices  34 us (22%)
  waiting for transfers between devices  29.7 us (19%)
  Pallas kernels  7.77 us (5%)
    all_to_all x4, blocking collectives, exchange(): return lax.all_to_all(blocks, axis, split_axis=0, concat_axis=0, tiled=True)  79.4 us
    all_to_all x2, waiting for transfers between devices, exchange(): return lax.all_to_all(blocks, axis, split_axis=0, concat_axis=0, tiled=True)  24.9 us
    ppermute x3, starting transfers between devices, swap_cores(): return lax.ppermute(block, 'core', [(0, 1), (1, 0)])  17.9 us
    all_to_all x2, starting transfers between devices, exchange(): return lax.all_to_all(blocks, axis, split_axis=0, concat_axis=0, tiled=True)  15.4 us
    ppermute x3, waiting for transfers between devices, swap_cores(): return lax.ppermute(block, 'core', [(0, 1), (1, 0)])  4.73 us
  transfers between devices with their start and end apart: 6, of which 5 were waited for; matrix products, arithmetic and copies ran while one was open for 0% of the time, Pallas kernels for 1%

profile of v6, /device:TPU:1, one launch (start us, length us, event | category | flops | bytes accessed | tf_op | source)
XLA Modules:
  0.0 153.1 jit_solution(2173228502475352102)
XLA Ops:
  0.6 0.0 copy-start.3
  0.6 0.0 copy-start.8
  0.7 0.0 copy-start.5
  0.7 0.0 copy-start.7
  0.7 0.7 copy-done.3
  1.4 0.0 copy-done.8
  1.4 0.0 copy-done.5
  1.4 0.0 copy-done.7
  1.4 0.0 copy-start.4
  1.4 0.7 copy-done.4
  2.1 0.7 mask.1.lower
  2.7 0.7 collective-permute-start
  3.4 0.0 collective-permute-done.source
  3.5 0.0 copy-start.1
  3.5 35.2 %all_to_all.30 = bf16[16,16,1024]{2,1,0:T(8,128)(2,1)S(1)} all-to-all(bf16[16,16,1024]{2,1,0:T(8,128)(2,1)S(1)} %copies.1), channel_id=1, replica_groups=mesh['chip'=16,'core'=2,'far'=4,'near'=4] {'chip'}, dimensions={0} | all-to-all | bytes 1048576 | tf_op jit(solution)/shard_map/all_to_all | solution.py:33
  38.7 3.9 %collective-permute-start.1 = (bf16[256,1024]{1,0:T(8,128)(2,1)S(1)}, bf16[256,1024]{1,0:T(8,128)(2,1)S(1)}, u32[]{:S(2)}, u32[]{:S(2)}) collective-permute-start(bf16[256,1024]{1,0:T(8,128)(2,1)S(1)} %bitcast.6), channel_id=1, source_target_pairs={{0,16},{16,0},{1,17},{17,1},{2,18},{18,2},{3,19},{19,3},{4,20},{20... | collective-permute-start | bytes 1572872 | tf_op jit(solution)/shard_map/ppermute | solution.py:37
  42.6 1.5 collective-permute-done.1.other
  44.1 0.0 copy-done.1
  44.1 0.4 product.1
  44.6 17.7 %all_to_all.31.received = bf16[4,4,16,1024]{3,2,1,0:T(8,128)(2,1)S(1)} all-to-all(bf16[4,4,16,1024]{3,2,1,0:T(8,128)(2,1)S(1)} %product.1), channel_id=1, replica_groups=mesh['chip'=16,'core'=2,'far'=4,'near'=4] {'near'}, dimensions={0} | all-to-all | bytes 1048576 | tf_op jit(solution)/shard_map/all_to_all | solution.py:33
  62.3 0.7 near_sum.1
  63.0 0.0 copy-start
  63.0 10.1 %all-to-all-start.2 = ((bf16[4,16,1024]{2,1,0:T(8,128)(2,1)}), bf16[4,16,1024]{2,1,0:T(8,128)(2,1)S(1)}, u32[]{:S(2)}, u32[]{:S(2)}) async-start(bf16[4,16,1024]{2,1,0:T(8,128)(2,1)} %near_sum.1), calls=%async_computation.2 | async-start | bytes 262144 | tf_op jit(solution)/shard_map/all_to_all | solution.py:33
  73.2 0.1 pad_add_fusion.place
  73.2 0.0 copy-start.9
  73.2 12.1 %all-to-all-done.2.received = bf16[4,16,1024]{2,1,0:T(8,128)(2,1)S(1)} async-done(((bf16[4,16,1024]{2,1,0:T(8,128)(2,1)}), bf16[4,16,1024]{2,1,0:T(8,128)(2,1)S(1)}, u32[]{:S(2)}, u32[]{:S(2)}) %all-to-all-start.2) | async-done | bytes 131104 | tf_op jit(solution)/shard_map/all_to_all | solution.py:33
  85.3 0.0 copy-done
  85.3 1.4 columns.1
  86.7 0.0 copy-done.9
  86.7 5.4 %collective-permute-start.2 = (f32[3,256,256]{2,1,0:T(8,128)S(1)}, f32[3,256,256]{2,1,0:T(8,128)S(1)}, u32[]{:S(2)}, u32[]{:S(2)}) collective-permute-start(f32[3,256,256]{2,1,0:T(8,128)S(1)} %get-tuple-element.16), channel_id=1, source_target_pairs={{0,16},{16,0},{1,17},{17,1},{2,18},{18,2},{3,19},{19,3},{4,20},{20... | collective-permute-start | bytes 2359304 | tf_op jit(solution)/shard_map/ppermute | solution.py:37
  92.2 1.9 %collective-permute-done.2.other = f32[3,256,256]{2,1,0:T(8,128)S(1)} collective-permute-done((f32[3,256,256]{2,1,0:T(8,128)S(1)}, f32[3,256,256]{2,1,0:T(8,128)S(1)}, u32[]{:S(2)}, u32[]{:S(2)}) %collective-permute-start.2) | collective-permute-done | bytes 786464 | tf_op jit(solution)/shard_map/ppermute | solution.py:37
  94.1 0.9 core_sum.1
  94.9 5.3 %all-to-all-start.3 = ((bf16[64,24,128]{2,1,0:T(8,128)(2,1)}), bf16[64,24,128]{2,1,0:T(8,128)(2,1)S(1)}, u32[]{:S(2)}, u32[]{:S(2)}) async-start(bf16[64,24,128]{2,1,0:T(8,128)(2,1)} %bitcast.4), calls=%async_computation.3 | async-start | bytes 786432 | tf_op jit(solution)/shard_map/all_to_all | solution.py:33
  100.2 1.7 %pivot.1 = f32[96,128]{1,0:T(8,128)} custom-call(s32[2]{0:T(128)} %copy-done.9, bf16[2,256,256]{2,1,0:T(8,128)(2,1)} %one.3, bf16[2,256,256]{2,1,0:T(8,128)(2,1)} %two.3, s32[4]{0:T(128)} %widths.7), custom_call_target="tpu_custom_call" | custom-call | tf_op jit(solution)/shard_map/pivot/pallas_call | solution.py:252
  102.0 12.9 %all-to-all-done.3.received = bf16[64,24,128]{2,1,0:T(8,128)(2,1)S(1)} async-done(((bf16[64,24,128]{2,1,0:T(8,128)(2,1)}), bf16[64,24,128]{2,1,0:T(8,128)(2,1)S(1)}, u32[]{:S(2)}, u32[]{:S(2)}) %all-to-all-start.3) | async-done | bytes 393248 | tf_op jit(solution)/shard_map/all_to_all | solution.py:33
  114.8 0.1 chunk_sum.1
  114.9 0.0 copy-start.2
  114.9 15.6 %all_to_all.32.received = f32[16,24,128]{2,1,0:T(8,128)S(1)} all-to-all(f32[16,24,128]{2,1,0:T(8,128)S(1)} %chunk_sum.1), channel_id=1, replica_groups=mesh['chip'=16,'core'=2,'far'=4,'near'=4] {'far','near'}, dimensions={0} | all-to-all | bytes 393216 | tf_op jit(solution)/shard_map/all_to_all | solution.py:33
  130.5 0.0 copy-done.2
  130.6 10.9 %all_to_all.33 = bf16[16,96,128]{2,1,0:T(8,128)(2,1)S(1)} all-to-all(bf16[16,96,128]{2,1,0:T(8,128)(2,1)S(1)} %all_sum.1), channel_id=1, replica_groups=mesh['chip'=16,'core'=2,'far'=4,'near'=4] {'chip'}, dimensions={0} | all-to-all | bytes 786432 | tf_op jit(solution)/shard_map/all_to_all | solution.py:33
  141.4 0.0 copy-start.6
  141.4 8.6 %collective-permute-start.3 = (bf16[2,768,128]{2,1,0:T(8,128)(2,1)S(1)}, bf16[2,768,128]{2,1,0:T(8,128)(2,1)S(1)}, u32[]{:S(2)}, u32[]{:S(2)}) collective-permute-start(bf16[2,768,128]{2,1,0:T(8,128)(2,1)S(1)} %bitcast.8), channel_id=1, source_target_pairs={{0,16},{16,0},{1,17},{17,1},{2,18},{18,2},{3,19},{19,3},{4,20},{20... | collective-permute-start | bytes 1179656 | tf_op jit(solution)/shard_map/ppermute | solution.py:37
  150.0 1.3 collective-permute-done.3.other
  151.4 0.0 copy-done.6
  151.4 1.7 %final.1 = (bf16[2,256,256]{2,1,0:T(8,128)(2,1)}, bf16[2,256,256]{2,1,0:T(8,128)(2,1)}, bf16[2,256,256]{2,1,0:T(8,128)(2,1)}) custom-call(s32[1]{0:T(128)} %bitcast.1.core, bf16[2,768,128]{2,1,0:T(8,128)(2,1)S(1)} %bitcast.9, bf16[2,768,128]{2,1,0:T(8,128)(2,1)S(1)} %collective-permute-done.3.other, bf16[2,256,256]{2,1,0:T(8,128)(2,1)S(1)} %copy-done, ...), custom_call_target="tpu_custom_call" | custom-call | tf_op jit(solution)/shard_map/final/pallas_call | solution.py:267
  (2 shorter events, 0.1 us)
Async XLA Ops:
  0.6 0.7 copy-start.3
  0.6 0.7 copy-start.8
  0.7 0.7 copy-start.5
  0.7 0.7 copy-start.7
  1.4 0.7 copy-start.4
  2.7 0.7 collective-permute-start
  3.5 40.7 %copy-start.1 = (bf16[256,512]{1,0:T(8,128)(2,1)S(1)}, bf16[256,512]{1,0:T(8,128)(2,1)}, u32[]{:S(2)}) copy-start(bf16[256,512]{1,0:T(8,128)(2,1)} %inverse.1) | copy-start | bytes 786436
  38.7 5.4 %collective-permute-start.1 = (bf16[256,1024]{1,0:T(8,128)(2,1)S(1)}, bf16[256,1024]{1,0:T(8,128)(2,1)S(1)}, u32[]{:S(2)}, u32[]{:S(2)}) collective-permute-start(bf16[256,1024]{1,0:T(8,128)(2,1)S(1)} %bitcast.6), channel_id=1, source_target_pairs={{0,16},{16,0},{1,17},{17,1},{2,18},{18,2},{3,19},{19,3},{4,20},{20... | collective-permute-start | bytes 1572872 | tf_op jit(solution)/shard_map/ppermute | solution.py:37
  63.0 22.3 %copy-start = (bf16[2,256,256]{2,1,0:T(8,128)(2,1)S(1)}, bf16[2,256,256]{2,1,0:T(8,128)(2,1)}, u32[]{:S(2)}) copy-start(bf16[2,256,256]{2,1,0:T(8,128)(2,1)} %link.3) | copy-start | bytes 786436
  63.0 22.3 %all-to-all-start.2 = ((bf16[4,16,1024]{2,1,0:T(8,128)(2,1)}), bf16[4,16,1024]{2,1,0:T(8,128)(2,1)S(1)}, u32[]{:S(2)}, u32[]{:S(2)}) async-start(bf16[4,16,1024]{2,1,0:T(8,128)(2,1)} %near_sum.1), calls=%async_computation.2 | async-start | bytes 262144 | tf_op jit(solution)/shard_map/all_to_all | solution.py:33
  73.2 13.5 %copy-start.9 = (s32[2]{0:T(128)}, s32[2]{0:T(128)S(1)}, u32[]{:S(2)}) copy-start(s32[2]{0:T(128)S(1)} %pad_add_fusion.place) | copy-start | bytes 28
  86.7 7.3 %collective-permute-start.2 = (f32[3,256,256]{2,1,0:T(8,128)S(1)}, f32[3,256,256]{2,1,0:T(8,128)S(1)}, u32[]{:S(2)}, u32[]{:S(2)}) collective-permute-start(f32[3,256,256]{2,1,0:T(8,128)S(1)} %get-tuple-element.16), channel_id=1, source_target_pairs={{0,16},{16,0},{1,17},{17,1},{2,18},{18,2},{3,19},{19,3},{4,20},{20... | collective-permute-start | bytes 2359304 | tf_op jit(solution)/shard_map/ppermute | solution.py:37
  94.9 19.9 %all-to-all-start.3 = ((bf16[64,24,128]{2,1,0:T(8,128)(2,1)}), bf16[64,24,128]{2,1,0:T(8,128)(2,1)S(1)}, u32[]{:S(2)}, u32[]{:S(2)}) async-start(bf16[64,24,128]{2,1,0:T(8,128)(2,1)} %bitcast.4), calls=%async_computation.3 | async-start | bytes 786432 | tf_op jit(solution)/shard_map/all_to_all | solution.py:33
  114.9 15.6 %copy-start.2 = (f32[96,128]{1,0:T(8,128)S(1)}, f32[96,128]{1,0:T(8,128)}, u32[]{:S(2)}) copy-start(f32[96,128]{1,0:T(8,128)} %pivot.1) | copy-start | bytes 147460
  141.4 9.9 %copy-start.6 = (s32[4]{0:T(128)S(1)}, s32[4]{0:T(128)}, u32[]{:S(2)}) copy-start(s32[4]{0:T(128)} %widths.7) | copy-start | bytes 52
  141.4 9.9 %collective-permute-start.3 = (bf16[2,768,128]{2,1,0:T(8,128)(2,1)S(1)}, bf16[2,768,128]{2,1,0:T(8,128)(2,1)S(1)}, u32[]{:S(2)}, u32[]{:S(2)}) collective-permute-start(bf16[2,768,128]{2,1,0:T(8,128)(2,1)S(1)} %bitcast.8), channel_id=1, source_target_pairs={{0,16},{16,0},{1,17},{17,1},{2,18},{18,2},{3,19},{19,3},{4,20},{20... | collective-permute-start | bytes 1179656 | tf_op jit(solution)/shard_map/ppermute | solution.py:37

commit v7 on v6

--- a/solution.py
+++ b/solution.py
@@ -11,6 +11,7 @@
 F32 = jnp.float32
 BF16 = jnp.bfloat16
 VMEM = pl.BlockSpec(memory_space=pltpu.VMEM)
+ANY = pl.BlockSpec(memory_space=pl.ANY)
 SMEM = pl.BlockSpec(memory_space=pltpu.SMEM)
 NEAR = 4
 CORES = 2
@@ -33,6 +34,21 @@
     return lax.all_to_all(blocks, axis, split_axis=0, concat_axis=0, tiled=True)
 
 
+def landing_places(chips, planes):
+    side = int(chips**0.5)
+
+    def steps(a, b):
+        return abs(a // side - b // side) + abs(a % side - b % side)
+
+    places = []
+    for q in range(chips):
+        far_first = sorted(range(planes), key=lambda z: (-abs(z - q), z))
+        close_first = sorted(range(chips), key=lambda p: (steps(p, q), p))
+        spots = dict(zip(far_first, close_first))
+        places.append([spots[z] for z in range(planes)])
+    return places
+
+
 def swap_cores(block):
     return lax.ppermute(block, "core", [(0, 1), (1, 0)])
 
@@ -67,13 +83,24 @@
     return jnp.where(inside, value, jnp.zeros_like(value))
 
 
-def mask_body(w, tile, one, two, anc_one, anc_two, widths, lower):
+def mask_body(w, tile, one, two, anc_one, anc_two, widths, lower, held_one, held_two, sems):
+    copies = [
+        pltpu.make_async_copy(one, held_one, sems.at[0]),
+        pltpu.make_async_copy(two, held_two, sems.at[1]),
+    ]
+    for copy in copies:
+        copy.start()
     column = lax.broadcasted_iota(jnp.int32, (one.shape[0], w), 1)
+    limits = [
+        jnp.where(is_member(anc_one if k < 2 else anc_two, k % 2, tile[0]), widths[k], 0)
+        for k in range(4)
+    ]
+    for copy in copies:
+        copy.wait()
     for k in range(4):
-        source, table, s = (one, anc_one, k) if k < 2 else (two, anc_two, k - 2)
-        width = jnp.where(is_member(table, s, tile[0]), widths[k], 0)
-        value = source[:, s * w : (s + 1) * w]
-        lower[:, k * w : (k + 1) * w] = jnp.where(column < width, value, jnp.zeros_like(value))
+        value = (held_one if k < 2 else held_two)[:, (k % 2) * w : (k % 2 + 1) * w]
+        value = jnp.where(column < limits[k], value, jnp.zeros_like(value))
+        lower[:, k * w : (k + 1) * w] = value
 
 
 def copy_body(source, copies):
@@ -82,24 +109,19 @@
         copies[i] = value
 
 
-def product_body(w, core, inverse, mine, other, part):
-    near, far, share, _ = part.shape
-    half = mine.shape[0]
+def product_body(w, core, order, inverse, mine, other, part, held):
+    blocks, share, _ = mine.shape
+    half = blocks * share
+    for i in range(blocks):
+        held[i * share : (i + 1) * share, :] = mine[order[i]]
+        held[half + i * share : half + (i + 1) * share, :] = other[order[i]]
     left = inverse[:, pl.ds(pl.multiple_of(core[0] * half, half), half)]
     right = inverse[:, pl.ds(pl.multiple_of((1 - core[0]) * half, half), half)]
     for k in range(4):
         span = slice(k * w, (k + 1) * w)
-        value = (dot(left, mine[:, span]) + dot(right, other[:, span])).astype(BF16)
-        for i in range(near * far):
-            part[i % near, i // near, :, span] = value[i * share : (i + 1) * share]
-
-
-def near_sum_body(received, sums):
-    for f in range(sums.shape[0]):
-        total = received[0, f].astype(F32)
-        for i in range(1, received.shape[0]):
-            total = total + received[i, f].astype(F32)
-        sums[f] = total.astype(BF16)
+        value = (dot(left, held[:half, span]) + dot(right, held[half:, span])).astype(BF16)
+        for i in range(part.shape[0]):
+            part[i, :, span] = value[i * share : (i + 1) * share]
 
 
 def column_body(
@@ -131,7 +153,7 @@
 
 
 def chunk_sum_body(received, copies):
-    value = reduced(received)
+    value = reduced(received).astype(BF16)
     for i in range(copies.shape[0]):
         copies[i] = value
 
@@ -160,7 +182,7 @@
     for n in range(near):
         total = pivot[n * chunk : (n + 1) * chunk, :]
         for i in range(n, received.shape[0], near):
-            total = total + received[i]
+            total = total + received[i].astype(F32)
         total = total.astype(BF16)
         for i in range(copies.shape[0]):
             copies[i, n * chunk : (n + 1) * chunk, :] = total
@@ -205,33 +227,38 @@
     core_ref = core.reshape(1)
     whole = (share, 4 * w)
 
-    (lower,) = kernel_call(
+    lower = pl.pallas_call(
         functools.partial(mask_body, w),
-        "mask",
-        [SMEM, VMEM, VMEM, SMEM, SMEM, SMEM],
-        [(whole, BF16)],
+        name="mask",
+        in_specs=[SMEM, ANY, ANY, SMEM, SMEM, SMEM],
+        out_specs=VMEM,
+        out_shape=jax.ShapeDtypeStruct(whole, BF16),
+        scratch_shapes=[pltpu.VMEM(panel_one.shape, BF16)] * 2 + [pltpu.SemaphoreType.DMA((2,))],
     )(tile, panel_one, panel_two, ancestors_one, ancestors_two, widths)
 
+    places = landing_places(chips, planes)
     pairs = []
     for q in range(chips):
         for k in range(CORES):
             for z in range(planes):
-                pairs.append(((q * CORES + k) * planes + z, (z * CORES + k) * planes + q))
+                pairs.append(((q * CORES + k) * planes + z, (places[q][z] * CORES + k) * planes + q))
     moved = lax.ppermute(lower, GRID, pairs)
+    plane = lax.axis_index("far") * NEAR + lax.axis_index("near")
+    order = lax.dynamic_index_in_dim(jnp.array(places, jnp.int32), plane, 0, keepdims=False)
     (moved,) = kernel_call(copy_body, "copies", [VMEM], [((chips,) + whole, BF16)])(moved)
-    mine = exchange(moved, "chip").reshape(chips * share, 4 * w)
+    mine = exchange(moved, "chip")
     other = swap_cores(mine)
 
-    (part,) = kernel_call(
+    part = pl.pallas_call(
         functools.partial(product_body, w),
-        "product",
-        [SMEM] + [VMEM] * 3,
-        [((NEAR, far_n) + whole, BF16)],
-    )(core_ref, ancestor_inverse, mine, other)
-    part = exchange(part, "near")
-
-    (part,) = kernel_call(near_sum_body, "near_sum", [VMEM], [((far_n,) + whole, BF16)])(part)
-    part = exchange(part, "far")
+        name="product",
+        in_specs=[SMEM, SMEM] + [VMEM] * 3,
+        out_specs=VMEM,
+        out_shape=jax.ShapeDtypeStruct((planes,) + whole, BF16),
+        scratch_shapes=[pltpu.VMEM((CORES * chips * share, 4 * w), BF16)],
+        compiler_params=pltpu.CompilerParams(vmem_limit_bytes=40 * 1024 * 1024),
+    )(core_ref, order, ancestor_inverse, mine, other)
+    part = exchange(part, ("far", "near"))
     place = jnp.stack([core, chip])
     column_one, column_two, mine, other = kernel_call(
         functools.partial(column_body, w),
@@ -246,7 +273,7 @@
         functools.partial(core_sum_body, w), "core_sum", [VMEM] * 2, [(flat, BF16)]
     )(mine, other)
     sums = exchange(sums.reshape(chips * NEAR, chunk, LANES), ("chip", "near"))
-    (sums,) = kernel_call(chunk_sum_body, "chunk_sum", [VMEM], [((planes, chunk, LANES), F32)])(
+    (sums,) = kernel_call(chunk_sum_body, "chunk_sum", [VMEM], [((planes, chunk, LANES), BF16)])(
         sums
     )
     pivot = pl.pallas_call(

time: 154 us -> 153 us (level)
  blocking collectives: 79.4 us -> 48.9 us
  waiting for transfers between devices: 29.7 us -> 45.3 us
  starting transfers between devices: 34 us -> 46.3 us
  Pallas kernels: 7.77 us -> 9.81 us
    all_to_all x4 -> x3, blocking collectives: 79.4 us -> 48.9 us  [exchange(): return lax.all_to_all(blocks, axis, split_axis=0, concat_axis=0, tiled=True)]
    all_to_all x2, waiting for transfers between devices: 24.9 us -> 35.5 us  [exchange(): return lax.all_to_all(blocks, axis, split_axis=0, concat_axis=0, tiled=True)]
    ppermute x1, starting transfers between devices: 0.66 us -> 7.67 us  [local(): moved = lax.ppermute(lower, GRID, pairs)]
    ppermute x1, waiting for transfers between devices: 0.01 us -> 5.78 us  [local(): moved = lax.ppermute(lower, GRID, pairs)]
    all_to_all x2, starting transfers between devices: 15.4 us -> 18.4 us  [exchange(): return lax.all_to_all(blocks, axis, split_axis=0, concat_axis=0, tiled=True)]
    ppermute x3, starting transfers between devices: 17.9 us -> 20.3 us  [swap_cores(): return lax.ppermute(block, 'core', [(0, 1), (1, 0)])]
    pallas_call x3 -> x2, Pallas kernels: 1.82 us -> 3.87 us  [the longest x1 2.08 us: local(): pl.pallas_call(functools.partial(mask_body, w), name='mask', in_specs=[SM...]
  transfers between devices with their start and end apart: 6 -> 6, of which waited for: 5 -> 6; matrix products, arithmetic and copies ran while one was open for 0% -> 1% of each run, Pallas kernels for 1% -> 1%
where the time goes in v7:
time: 153 us; the launch traced here: 152 us
  blocking collectives  48.9 us (32%)
  starting transfers between devices  46.3 us (30%)
  waiting for transfers between devices  45.3 us (30%)
  Pallas kernels  9.81 us (6%)
    all_to_all x3, blocking collectives, exchange(): return lax.all_to_all(blocks, axis, split_axis=0, concat_axis=0, tiled=True)  48.9 us
    all_to_all x2, waiting for transfers between devices, exchange(): return lax.all_to_all(blocks, axis, split_axis=0, concat_axis=0, tiled=True)  35.5 us
    ppermute x3, starting transfers between devices, swap_cores(): return lax.ppermute(block, 'core', [(0, 1), (1, 0)])  20.3 us
    all_to_all x2, starting transfers between devices, exchange(): return lax.all_to_all(blocks, axis, split_axis=0, concat_axis=0, tiled=True)  18.4 us
    ppermute x1, starting transfers between devices, local(): moved = lax.ppermute(lower, GRID, pairs)  7.67 us
    ppermute x1, waiting for transfers between devices, local(): moved = lax.ppermute(lower, GRID, pairs)  5.78 us
    ppermute x3, waiting for transfers between devices, swap_cores(): return lax.ppermute(block, 'core', [(0, 1), (1, 0)])  4.03 us
  transfers between devices with their start and end apart: 6, of which 6 were waited for; matrix products, arithmetic and copies ran while one was open for 1% of the time, Pallas kernels for 1%

profile of v7, /device:TPU:1, one launch (start us, length us, event | category | flops | bytes accessed | tf_op | source)
XLA Modules:
  0.0 151.9 jit_solution(8769518599693287506)
XLA Ops:
  0.6 2.1 %mask.1.lower = bf16[16,1024]{1,0:T(8,128)(2,1)} custom-call(s32[1]{0:T(128)} %bitcast.tile, bf16[16,512]{1,0:T(8,128)(2,1)} %one.2, bf16[16,512]{1,0:T(8,128)(2,1)} %two.2, s32[2,28]{1,0:T(2,128)} %anc_one.3, s32[2,24]{1,0:T(2,128)} %anc_two.3, s32[4]{0:T(128)} %widths.7), custom_call_target="tpu_custom_call" | custom-call | tf_op jit(solution)/shard_map/mask/pallas_call | solution.py:230
  2.7 7.7 %collective-permute-start = (bf16[16,1024]{1,0:T(8,128)(2,1)}, bf16[16,1024]{1,0:T(8,128)(2,1)S(1)}, u32[]{:S(2)}, u32[]{:S(2)}) collective-permute-start(bf16[16,1024]{1,0:T(8,128)(2,1)} %mask.1.lower), channel_id=1, source_target_pairs={{0,480},{1,448},{2,352},{3,416},{4,320},{5,224},{6,384},{7,288},{8... | collective-permute-start | bytes 98312 | tf_op jit(solution)/shard_map/ppermute | solution.py:245
  10.4 5.8 %collective-permute-done.source = bf16[16,1024]{1,0:T(8,128)(2,1)S(1)} collective-permute-done((bf16[16,1024]{1,0:T(8,128)(2,1)}, bf16[16,1024]{1,0:T(8,128)(2,1)S(1)}, u32[]{:S(2)}, u32[]{:S(2)}) %collective-permute-start) | collective-permute-done | bytes 32800 | tf_op jit(solution)/shard_map/ppermute | solution.py:245
  16.2 0.0 copy-start.1
  16.3 19.9 %all_to_all.25.mine = bf16[16,16,1024]{2,1,0:T(8,128)(2,1)S(1)} all-to-all(bf16[16,16,1024]{2,1,0:T(8,128)(2,1)S(1)} %copies.1), channel_id=1, replica_groups=mesh['chip'=16,'core'=2,'far'=4,'near'=4] {'chip'}, dimensions={0} | all-to-all | bytes 1048576 | tf_op jit(solution)/shard_map/all_to_all | solution.py:34
  36.1 4.5 %collective-permute-start.1 = (bf16[16,16,1024]{2,1,0:T(8,128)(2,1)S(1)}, bf16[16,16,1024]{2,1,0:T(8,128)(2,1)S(1)}, u32[]{:S(2)}, u32[]{:S(2)}) collective-permute-start(bf16[16,16,1024]{2,1,0:T(8,128)(2,1)S(1)} %all_to_all.25.mine), channel_id=1, source_target_pairs={{0,16},{16,0},{1,17},{17,1},{2,18},{18,2},{3,19},{19,3},{4,20},{20... | collective-permute-start | bytes 1572872 | tf_op jit(solution)/shard_map/ppermute | solution.py:53
  40.6 0.7 dynamic-slice_bitcast_fusion.order
  41.3 0.8 collective-permute-done.1.other
  42.1 0.0 copy-done.1
  42.1 1.8 %product.1 = bf16[16,16,1024]{2,1,0:T(8,128)(2,1)} custom-call(s32[1]{0:T(128)} %bitcast.1.core, s32[16]{0:T(128)S(1)} %dynamic-slice_bitcast_fusion.order, bf16[256,512]{1,0:T(8,128)(2,1)S(1)} %copy-done.1, bf16[16,16,1024]{2,1,0:T(8,128)(2,1)S(1)} %all_to_all.25.mine, bf16[16,16,1024]{2,1,0:T(8,128)(2,1)S(1)} %collective-permute-done.1.other), custom_call_target="tpu_custom_call" | custom-call | tf_op jit(solution)/shard_map/product/pallas_call | solution.py:252
  43.9 0.0 copy-start
  43.9 0.0 copy-start.3
  43.9 0.0 copy-start.7
  43.9 12.5 %all-to-all-start.1 = ((bf16[16,16,1024]{2,1,0:T(8,128)(2,1)}), bf16[16,16,1024]{2,1,0:T(8,128)(2,1)S(1)}, u32[]{:S(2)}, u32[]{:S(2)}) async-start(bf16[16,16,1024]{2,1,0:T(8,128)(2,1)} %product.1), calls=%async_computation.1 | async-start | bytes 1048576 | tf_op jit(solution)/shard_map/all_to_all | solution.py:34
  56.4 0.0 copy-start.4
  56.5 0.0 copy-start.6
  56.5 0.1 pad_add_fusion.place
  56.5 0.0 copy-start.8
  56.5 22.6 %all-to-all-done.1.received = bf16[16,16,1024]{2,1,0:T(8,128)(2,1)S(1)} async-done(((bf16[16,16,1024]{2,1,0:T(8,128)(2,1)}), bf16[16,16,1024]{2,1,0:T(8,128)(2,1)S(1)}, u32[]{:S(2)}, u32[]{:S(2)}) %all-to-all-start.1) | async-done | bytes 524320 | tf_op jit(solution)/shard_map/all_to_all | solution.py:34
  79.2 0.0 copy-done
  79.2 0.0 copy-done.3
  79.2 0.0 copy-done.7
  79.2 0.0 copy-done.4
  79.2 0.0 copy-done.6
  79.2 1.4 columns.1
  80.6 0.0 copy-done.8
  80.6 9.1 %collective-permute-start.2 = (f32[3,256,256]{2,1,0:T(8,128)S(1)}, f32[3,256,256]{2,1,0:T(8,128)S(1)}, u32[]{:S(2)}, u32[]{:S(2)}) collective-permute-start(f32[3,256,256]{2,1,0:T(8,128)S(1)} %get-tuple-element.16), channel_id=1, source_target_pairs={{0,16},{16,0},{1,17},{17,1},{2,18},{18,2},{3,19},{19,3},{4,20},{20... | collective-permute-start | bytes 2359304 | tf_op jit(solution)/shard_map/ppermute | solution.py:53
  89.7 1.9 %collective-permute-done.2.other = f32[3,256,256]{2,1,0:T(8,128)S(1)} collective-permute-done((f32[3,256,256]{2,1,0:T(8,128)S(1)}, f32[3,256,256]{2,1,0:T(8,128)S(1)}, u32[]{:S(2)}, u32[]{:S(2)}) %collective-permute-start.2) | collective-permute-done | bytes 786464 | tf_op jit(solution)/shard_map/ppermute | solution.py:53
  91.6 0.8 core_sum.1
  92.5 5.9 %all-to-all-start.2 = ((bf16[64,24,128]{2,1,0:T(8,128)(2,1)}), bf16[64,24,128]{2,1,0:T(8,128)(2,1)S(1)}, u32[]{:S(2)}, u32[]{:S(2)}) async-start(bf16[64,24,128]{2,1,0:T(8,128)(2,1)} %bitcast.4), calls=%async_computation.2 | async-start | bytes 786432 | tf_op jit(solution)/shard_map/all_to_all | solution.py:34
  98.4 1.7 %pivot.1 = f32[96,128]{1,0:T(8,128)} custom-call(s32[2]{0:T(128)} %copy-done.8, bf16[2,256,256]{2,1,0:T(8,128)(2,1)} %one.3, bf16[2,256,256]{2,1,0:T(8,128)(2,1)} %two.3, s32[4]{0:T(128)} %widths.7), custom_call_target="tpu_custom_call" | custom-call | tf_op jit(solution)/shard_map/pivot/pallas_call | solution.py:279
  100.1 12.9 %all-to-all-done.2.received = bf16[64,24,128]{2,1,0:T(8,128)(2,1)S(1)} async-done(((bf16[64,24,128]{2,1,0:T(8,128)(2,1)}), bf16[64,24,128]{2,1,0:T(8,128)(2,1)S(1)}, u32[]{:S(2)}, u32[]{:S(2)}) %all-to-all-start.2) | async-done | bytes 393248 | tf_op jit(solution)/shard_map/all_to_all | solution.py:34
  113.0 0.1 chunk_sum.1
  113.1 0.0 copy-start.2
  113.1 18.0 %all_to_all.26.received = bf16[16,24,128]{2,1,0:T(8,128)(2,1)S(1)} all-to-all(bf16[16,24,128]{2,1,0:T(8,128)(2,1)S(1)} %chunk_sum.1), channel_id=1, replica_groups=mesh['chip'=16,'core'=2,'far'=4,'near'=4] {'far','near'}, dimensions={0} | all-to-all | bytes 196608 | tf_op jit(solution)/shard_map/all_to_all | solution.py:34
  131.1 0.0 copy-done.2
  131.2 11.0 %all_to_all.27 = bf16[16,96,128]{2,1,0:T(8,128)(2,1)S(1)} all-to-all(bf16[16,96,128]{2,1,0:T(8,128)(2,1)S(1)} %all_sum.1), channel_id=1, replica_groups=mesh['chip'=16,'core'=2,'far'=4,'near'=4] {'chip'}, dimensions={0} | all-to-all | bytes 786432 | tf_op jit(solution)/shard_map/all_to_all | solution.py:34
  142.1 0.0 copy-start.5
  142.1 6.7 %collective-permute-start.3 = (bf16[2,768,128]{2,1,0:T(8,128)(2,1)S(1)}, bf16[2,768,128]{2,1,0:T(8,128)(2,1)S(1)}, u32[]{:S(2)}, u32[]{:S(2)}) collective-permute-start(bf16[2,768,128]{2,1,0:T(8,128)(2,1)S(1)} %bitcast.7), channel_id=1, source_target_pairs={{0,16},{16,0},{1,17},{17,1},{2,18},{18,2},{3,19},{19,3},{4,20},{20... | collective-permute-start | bytes 1179656 | tf_op jit(solution)/shard_map/ppermute | solution.py:53
  148.8 1.3 collective-permute-done.3.other
  150.2 0.0 copy-done.5
  150.2 1.7 %final.1 = (bf16[2,256,256]{2,1,0:T(8,128)(2,1)}, bf16[2,256,256]{2,1,0:T(8,128)(2,1)}, bf16[2,256,256]{2,1,0:T(8,128)(2,1)}) custom-call(s32[1]{0:T(128)} %bitcast.1.core, bf16[2,768,128]{2,1,0:T(8,128)(2,1)S(1)} %bitcast.8, bf16[2,768,128]{2,1,0:T(8,128)(2,1)S(1)} %collective-permute-done.3.other, bf16[2,256,256]{2,1,0:T(8,128)(2,1)S(1)} %copy-done, ...), custom_call_target="tpu_custom_call" | custom-call | tf_op jit(solution)/shard_map/final/pallas_call | solution.py:294
  (2 shorter events, 0.1 us)
Async XLA Ops:
  2.7 13.5 %collective-permute-start = (bf16[16,1024]{1,0:T(8,128)(2,1)}, bf16[16,1024]{1,0:T(8,128)(2,1)S(1)}, u32[]{:S(2)}, u32[]{:S(2)}) collective-permute-start(bf16[16,1024]{1,0:T(8,128)(2,1)} %mask.1.lower), channel_id=1, source_target_pairs={{0,480},{1,448},{2,352},{3,416},{4,320},{5,224},{6,384},{7,288},{8... | collective-permute-start | bytes 98312 | tf_op jit(solution)/shard_map/ppermute | solution.py:245
  16.2 25.9 %copy-start.1 = (bf16[256,512]{1,0:T(8,128)(2,1)S(1)}, bf16[256,512]{1,0:T(8,128)(2,1)}, u32[]{:S(2)}) copy-start(bf16[256,512]{1,0:T(8,128)(2,1)} %inverse.1) | copy-start | bytes 786436
  36.1 6.0 %collective-permute-start.1 = (bf16[16,16,1024]{2,1,0:T(8,128)(2,1)S(1)}, bf16[16,16,1024]{2,1,0:T(8,128)(2,1)S(1)}, u32[]{:S(2)}, u32[]{:S(2)}) collective-permute-start(bf16[16,16,1024]{2,1,0:T(8,128)(2,1)S(1)} %all_to_all.25.mine), channel_id=1, source_target_pairs={{0,16},{16,0},{1,17},{17,1},{2,18},{18,2},{3,19},{19,3},{4,20},{20... | collective-permute-start | bytes 1572872 | tf_op jit(solution)/shard_map/ppermute | solution.py:53
  43.9 35.2 %copy-start = (bf16[2,256,256]{2,1,0:T(8,128)(2,1)S(1)}, bf16[2,256,256]{2,1,0:T(8,128)(2,1)}, u32[]{:S(2)}) copy-start(bf16[2,256,256]{2,1,0:T(8,128)(2,1)} %link.3) | copy-start | bytes 786436
  43.9 35.2 %copy-start.3 = (bf16[16,1024]{1,0:T(8,128)(2,1)S(1)}, bf16[16,1024]{1,0:T(8,128)(2,1)}, u32[]{:S(2)}) copy-start(bf16[16,1024]{1,0:T(8,128)(2,1)} %mask.1.lower) | copy-start | bytes 98308
  43.9 35.2 %copy-start.7 = (s32[2,24]{1,0:T(2,128)S(1)}, s32[2,24]{1,0:T(2,128)}, u32[]{:S(2)}) copy-start(s32[2,24]{1,0:T(2,128)} %anc_two.3) | copy-start | bytes 580
  43.9 35.2 %all-to-all-start.1 = ((bf16[16,16,1024]{2,1,0:T(8,128)(2,1)}), bf16[16,16,1024]{2,1,0:T(8,128)(2,1)S(1)}, u32[]{:S(2)}, u32[]{:S(2)}) async-start(bf16[16,16,1024]{2,1,0:T(8,128)(2,1)} %product.1), calls=%async_computation.1 | async-start | bytes 1048576 | tf_op jit(solution)/shard_map/all_to_all | solution.py:34
  56.4 22.7 %copy-start.4 = (s32[4]{0:T(128)S(1)}, s32[4]{0:T(128)}, u32[]{:S(2)}) copy-start(s32[4]{0:T(128)} %widths.7) | copy-start | bytes 52
  56.5 22.7 %copy-start.6 = (s32[2,28]{1,0:T(2,128)S(1)}, s32[2,28]{1,0:T(2,128)}, u32[]{:S(2)}) copy-start(s32[2,28]{1,0:T(2,128)} %anc_one.3) | copy-start | bytes 676
  56.5 24.1 %copy-start.8 = (s32[2]{0:T(128)}, s32[2]{0:T(128)S(1)}, u32[]{:S(2)}) copy-start(s32[2]{0:T(128)S(1)} %pad_add_fusion.place) | copy-start | bytes 28
  80.6 11.0 %collective-permute-start.2 = (f32[3,256,256]{2,1,0:T(8,128)S(1)}, f32[3,256,256]{2,1,0:T(8,128)S(1)}, u32[]{:S(2)}, u32[]{:S(2)}) collective-permute-start(f32[3,256,256]{2,1,0:T(8,128)S(1)} %get-tuple-element.16), channel_id=1, source_target_pairs={{0,16},{16,0},{1,17},{17,1},{2,18},{18,2},{3,19},{19,3},{4,20},{20... | collective-permute-start | bytes 2359304 | tf_op jit(solution)/shard_map/ppermute | solution.py:53
  92.5 20.5 %all-to-all-start.2 = ((bf16[64,24,128]{2,1,0:T(8,128)(2,1)}), bf16[64,24,128]{2,1,0:T(8,128)(2,1)S(1)}, u32[]{:S(2)}, u32[]{:S(2)}) async-start(bf16[64,24,128]{2,1,0:T(8,128)(2,1)} %bitcast.4), calls=%async_computation.2 | async-start | bytes 786432 | tf_op jit(solution)/shard_map/all_to_all | solution.py:34
  113.1 18.1 %copy-start.2 = (f32[96,128]{1,0:T(8,128)S(1)}, f32[96,128]{1,0:T(8,128)}, u32[]{:S(2)}) copy-start(f32[96,128]{1,0:T(8,128)} %pivot.1) | copy-start | bytes 147460
  142.1 8.0 %copy-start.5 = (s32[4]{0:T(128)S(1)}, s32[4]{0:T(128)}, u32[]{:S(2)}) copy-start(s32[4]{0:T(128)} %widths.7) | copy-start | bytes 52
  142.1 8.0 %collective-permute-start.3 = (bf16[2,768,128]{2,1,0:T(8,128)(2,1)S(1)}, bf16[2,768,128]{2,1,0:T(8,128)(2,1)S(1)}, u32[]{:S(2)}, u32[]{:S(2)}) collective-permute-start(bf16[2,768,128]{2,1,0:T(8,128)(2,1)S(1)} %bitcast.7), channel_id=1, source_target_pairs={{0,16},{16,0},{1,17},{17,1},{2,18},{18,2},{3,19},{19,3},{4,20},{20... | collective-permute-start | bytes 1179656 | tf_op jit(solution)/shard_map/ppermute | solution.py:53

commit v8 on v7

--- a/solution.py
+++ b/solution.py
@@ -245,6 +245,18 @@
     moved = lax.ppermute(lower, GRID, pairs)
     plane = lax.axis_index("far") * NEAR + lax.axis_index("near")
     order = lax.dynamic_index_in_dim(jnp.array(places, jnp.int32), plane, 0, keepdims=False)
+    place = jnp.stack([core, chip])
+    flat = (w // LANES, 3 * w, LANES)
+    chunk = 3 * w * w // LANES // (chips * NEAR)
+    pivot = pl.pallas_call(
+        functools.partial(pivot_body, w),
+        name="pivot",
+        in_specs=[SMEM, VMEM, VMEM, SMEM],
+        out_specs=VMEM,
+        out_shape=jax.ShapeDtypeStruct((NEAR * chunk, LANES), F32),
+        scratch_shapes=[pltpu.VMEM((3 * w * w // LANES, LANES), F32)],
+    )(place, diag_inverse_one, diag_inverse_two, widths)
+    moved, order, place, pivot = lax.optimization_barrier((moved, order, place, pivot))
     (moved,) = kernel_call(copy_body, "copies", [VMEM], [((chips,) + whole, BF16)])(moved)
     mine = exchange(moved, "chip")
     other = swap_cores(mine)
@@ -259,7 +271,6 @@
         compiler_params=pltpu.CompilerParams(vmem_limit_bytes=40 * 1024 * 1024),
     )(core_ref, order, ancestor_inverse, mine, other)
     part = exchange(part, ("far", "near"))
-    place = jnp.stack([core, chip])
     column_one, column_two, mine, other = kernel_call(
         functools.partial(column_body, w),
         "columns",
@@ -267,8 +278,6 @@
         [((share, 2 * w), BF16)] * 2 + [((3, w, w), F32)] * 2,
     )(tile, place, part, lower, link_two, ancestors_one, ancestors_two, widths)
     other = swap_cores(other)
-    flat = (w // LANES, 3 * w, LANES)
-    chunk = 3 * w * w // LANES // (chips * NEAR)
     (sums,) = kernel_call(
         functools.partial(core_sum_body, w), "core_sum", [VMEM] * 2, [(flat, BF16)]
     )(mine, other)
@@ -276,15 +285,6 @@
     (sums,) = kernel_call(chunk_sum_body, "chunk_sum", [VMEM], [((planes, chunk, LANES), BF16)])(
         sums
     )
-    pivot = pl.pallas_call(
-        functools.partial(pivot_body, w),
-        name="pivot",
-        in_specs=[SMEM, VMEM, VMEM, SMEM],
-        out_specs=VMEM,
-        out_shape=jax.ShapeDtypeStruct((NEAR * chunk, LANES), F32),
-        scratch_shapes=[pltpu.VMEM((3 * w * w // LANES, LANES), F32)],
-    )(place, diag_inverse_one, diag_inverse_two, widths)
-    sums, pivot = lax.optimization_barrier((sums, pivot))
     sums = exchange(sums, ("far", "near"))
     (total,) = kernel_call(
         all_sum_body, "all_sum", [VMEM] * 2, [((chips, NEAR * chunk, LANES), BF16)]

time: 153 us -> 151 us (0.987)
  blocking collectives: 48.9 us -> 105 us
  waiting for transfers between devices: 45.3 us -> 7.48 us
  starting transfers between devices: 46.3 us -> 27.3 us
  Pallas kernels: 9.81 us -> 8.24 us
    all_to_all x3 -> x5, blocking collectives: 48.9 us -> 105 us  [exchange(): return lax.all_to_all(blocks, axis, split_axis=0, concat_axis=0, tiled=True)]
    all_to_all x2 -> x0, waiting for transfers between devices: 35.5 us -> none  [exchange(): return lax.all_to_all(blocks, axis, split_axis=0, concat_axis=0, tiled=True)]
    all_to_all x2 -> x0, starting transfers between devices: 18.4 us -> none  [exchange(): return lax.all_to_all(blocks, axis, split_axis=0, concat_axis=0, tiled=True)]
    ppermute x1, waiting for transfers between devices: 5.78 us -> 2.75 us  [local(): moved = lax.ppermute(lower, GRID, pairs)]
  transfers between devices with their start and end apart: 6 -> 4, of which waited for: 6 -> 4; matrix products, arithmetic and copies ran while one was open for 1% -> 1% of each run, Pallas kernels for 1% -> 1%
where the time goes in v8:
time: 151 us; the launch traced here: 150 us
  blocking collectives  105 us (70%)
  starting transfers between devices  27.3 us (18%)
  Pallas kernels  8.24 us (5%)
  waiting for transfers between devices  7.48 us (5%)
    all_to_all x5, blocking collectives, exchange(): return lax.all_to_all(blocks, axis, split_axis=0, concat_axis=0, tiled=True)  105 us
    ppermute x3, starting transfers between devices, swap_cores(): return lax.ppermute(block, 'core', [(0, 1), (1, 0)])  19.7 us
    ppermute x1, starting transfers between devices, local(): moved = lax.ppermute(lower, GRID, pairs)  7.67 us
    ppermute x3, waiting for transfers between devices, swap_cores(): return lax.ppermute(block, 'core', [(0, 1), (1, 0)])  4.73 us
  transfers between devices with their start and end apart: 4, of which 4 were waited for; matrix products, arithmetic and copies ran while one was open for 1% of the time, Pallas kernels for 1%

profile of v8, /device:TPU:1, one launch (start us, length us, event | category | flops | bytes accessed | tf_op | source)
XLA Modules:
  0.0 149.9 jit_solution(17364795226700649351)
XLA Ops:
  0.6 2.1 %mask.1.lower = bf16[16,1024]{1,0:T(8,128)(2,1)} custom-call(s32[1]{0:T(128)} %bitcast.tile, bf16[16,512]{1,0:T(8,128)(2,1)} %one.2, bf16[16,512]{1,0:T(8,128)(2,1)} %two.2, s32[2,28]{1,0:T(2,128)} %anc_one.3, s32[2,24]{1,0:T(2,128)} %anc_two.3, s32[4]{0:T(128)} %widths.7), custom_call_target="tpu_custom_call" | custom-call | tf_op jit(solution)/shard_map/mask/pallas_call | solution.py:230
  2.7 7.7 %collective-permute-start = (bf16[16,1024]{1,0:T(8,128)(2,1)}, bf16[16,1024]{1,0:T(8,128)(2,1)S(1)}, u32[]{:S(2)}, u32[]{:S(2)}) collective-permute-start(bf16[16,1024]{1,0:T(8,128)(2,1)} %mask.1.lower), channel_id=1, source_target_pairs={{0,480},{1,448},{2,352},{3,416},{4,320},{5,224},{6,384},{7,288},{8... | collective-permute-start | bytes 98312 | tf_op jit(solution)/shard_map/ppermute | solution.py:245
  10.4 0.7 dynamic-slice_bitcast_fusion.order
  11.1 0.6 pad_add_fusion.place
  11.7 1.7 %pivot.1 = f32[96,128]{1,0:T(8,128)} custom-call(s32[2]{0:T(128)} %pad_add_fusion.place, bf16[2,256,256]{2,1,0:T(8,128)(2,1)} %one.3, bf16[2,256,256]{2,1,0:T(8,128)(2,1)} %two.3, s32[4]{0:T(128)} %widths.7), custom_call_target="tpu_custom_call" | custom-call | tf_op jit(solution)/shard_map/pivot/pallas_call | solution.py:251
  13.4 2.8 %collective-permute-done.source = bf16[16,1024]{1,0:T(8,128)(2,1)S(1)} collective-permute-done((bf16[16,1024]{1,0:T(8,128)(2,1)}, bf16[16,1024]{1,0:T(8,128)(2,1)S(1)}, u32[]{:S(2)}, u32[]{:S(2)}) %collective-permute-start) | collective-permute-done | bytes 32800 | tf_op jit(solution)/shard_map/ppermute | solution.py:245
  16.2 0.0 copy-start.1
  16.2 22.0 %all_to_all.25.mine = bf16[16,16,1024]{2,1,0:T(8,128)(2,1)S(1)} all-to-all(bf16[16,16,1024]{2,1,0:T(8,128)(2,1)S(1)} %copies.1), channel_id=1, replica_groups=mesh['chip'=16,'core'=2,'far'=4,'near'=4] {'chip'}, dimensions={0} | all-to-all | bytes 1048576 | tf_op jit(solution)/shard_map/all_to_all | solution.py:34
  38.3 4.0 %collective-permute-start.1 = (bf16[16,16,1024]{2,1,0:T(8,128)(2,1)S(1)}, bf16[16,16,1024]{2,1,0:T(8,128)(2,1)S(1)}, u32[]{:S(2)}, u32[]{:S(2)}) collective-permute-start(bf16[16,16,1024]{2,1,0:T(8,128)(2,1)S(1)} %all_to_all.25.mine), channel_id=1, source_target_pairs={{0,16},{16,0},{1,17},{17,1},{2,18},{18,2},{3,19},{19,3},{4,20},{20... | collective-permute-start | bytes 1572872 | tf_op jit(solution)/shard_map/ppermute | solution.py:53
  42.3 1.5 %collective-permute-done.1.other = bf16[16,16,1024]{2,1,0:T(8,128)(2,1)S(1)} collective-permute-done((bf16[16,16,1024]{2,1,0:T(8,128)(2,1)S(1)}, bf16[16,16,1024]{2,1,0:T(8,128)(2,1)S(1)}, u32[]{:S(2)}, u32[]{:S(2)}) %collective-permute-start.1) | collective-permute-done | bytes 524320 | tf_op jit(solution)/shard_map/ppermute | solution.py:53
  43.8 0.0 copy-done.1
  43.8 1.0 product.1
  44.8 0.0 copy-start
  44.8 0.0 copy-start.3
  44.8 0.0 copy-start.4
  44.8 0.0 copy-start.5
  44.9 0.0 copy-start.6
  44.9 0.0 copy-start.7
  44.9 33.3 %all_to_all.26.received = bf16[16,16,1024]{2,1,0:T(8,128)(2,1)S(1)} all-to-all(bf16[16,16,1024]{2,1,0:T(8,128)(2,1)S(1)} %product.1), channel_id=1, replica_groups=mesh['chip'=16,'core'=2,'far'=4,'near'=4] {'far','near'}, dimensions={0} | all-to-all | bytes 1048576 | tf_op jit(solution)/shard_map/all_to_all | solution.py:34
  78.2 0.0 copy-done
  78.2 0.0 copy-done.3
  78.2 0.0 copy-done.4
  78.2 0.0 copy-done.5
  78.2 0.0 copy-done.6
  78.3 0.0 copy-done.7
  78.3 1.4 columns.1
  79.7 9.1 %collective-permute-start.2 = (f32[3,256,256]{2,1,0:T(8,128)S(1)}, f32[3,256,256]{2,1,0:T(8,128)S(1)}, u32[]{:S(2)}, u32[]{:S(2)}) collective-permute-start(f32[3,256,256]{2,1,0:T(8,128)S(1)} %get-tuple-element.21), channel_id=1, source_target_pairs={{0,16},{16,0},{1,17},{17,1},{2,18},{18,2},{3,19},{19,3},{4,20},{20... | collective-permute-start | bytes 2359304 | tf_op jit(solution)/shard_map/ppermute | solution.py:53
  88.8 1.9 %collective-permute-done.2.other = f32[3,256,256]{2,1,0:T(8,128)S(1)} collective-permute-done((f32[3,256,256]{2,1,0:T(8,128)S(1)}, f32[3,256,256]{2,1,0:T(8,128)S(1)}, u32[]{:S(2)}, u32[]{:S(2)}) %collective-permute-start.2) | collective-permute-done | bytes 786464 | tf_op jit(solution)/shard_map/ppermute | solution.py:53
  90.7 0.1 core_sum.1
  90.8 20.3 %all_to_all.27.received = bf16[64,24,128]{2,1,0:T(8,128)(2,1)S(1)} all-to-all(bf16[64,24,128]{2,1,0:T(8,128)(2,1)S(1)} %bitcast.9), channel_id=1, replica_groups=mesh['chip'=16,'core'=2,'far'=4,'near'=4] {'chip','near'}, dimensions={0} | all-to-all | bytes 786432 | tf_op jit(solution)/shard_map/all_to_all | solution.py:34
  111.1 0.1 chunk_sum.1
  111.2 0.0 copy-start.2
  111.2 18.0 %all_to_all.28.received = bf16[16,24,128]{2,1,0:T(8,128)(2,1)S(1)} all-to-all(bf16[16,24,128]{2,1,0:T(8,128)(2,1)S(1)} %chunk_sum.1), channel_id=1, replica_groups=mesh['chip'=16,'core'=2,'far'=4,'near'=4] {'far','near'}, dimensions={0} | all-to-all | bytes 196608 | tf_op jit(solution)/shard_map/all_to_all | solution.py:34
  129.2 0.0 copy-done.2
  129.3 11.0 %all_to_all.29 = bf16[16,96,128]{2,1,0:T(8,128)(2,1)S(1)} all-to-all(bf16[16,96,128]{2,1,0:T(8,128)(2,1)S(1)} %all_sum.1), channel_id=1, replica_groups=mesh['chip'=16,'core'=2,'far'=4,'near'=4] {'chip'}, dimensions={0} | all-to-all | bytes 786432 | tf_op jit(solution)/shard_map/all_to_all | solution.py:34
  140.2 6.6 %collective-permute-start.3 = (bf16[2,768,128]{2,1,0:T(8,128)(2,1)S(1)}, bf16[2,768,128]{2,1,0:T(8,128)(2,1)S(1)}, u32[]{:S(2)}, u32[]{:S(2)}) collective-permute-start(bf16[2,768,128]{2,1,0:T(8,128)(2,1)S(1)} %bitcast.7), channel_id=1, source_target_pairs={{0,16},{16,0},{1,17},{17,1},{2,18},{18,2},{3,19},{19,3},{4,20},{20... | collective-permute-start | bytes 1179656 | tf_op jit(solution)/shard_map/ppermute | solution.py:53
  146.8 1.3 collective-permute-done.3.other
  148.1 1.7 %final.1 = (bf16[2,256,256]{2,1,0:T(8,128)(2,1)}, bf16[2,256,256]{2,1,0:T(8,128)(2,1)}, bf16[2,256,256]{2,1,0:T(8,128)(2,1)}) custom-call(s32[1]{0:T(128)} %bitcast.2.core, bf16[2,768,128]{2,1,0:T(8,128)(2,1)S(1)} %bitcast.8, bf16[2,768,128]{2,1,0:T(8,128)(2,1)S(1)} %collective-permute-done.3.other, bf16[2,256,256]{2,1,0:T(8,128)(2,1)S(1)} %copy-done, ...), custom_call_target="tpu_custom_call" | custom-call | tf_op jit(solution)/shard_map/final/pallas_call | solution.py:294
  (2 shorter events, 0.1 us)
Async XLA Ops:
  2.7 13.5 %collective-permute-start = (bf16[16,1024]{1,0:T(8,128)(2,1)}, bf16[16,1024]{1,0:T(8,128)(2,1)S(1)}, u32[]{:S(2)}, u32[]{:S(2)}) collective-permute-start(bf16[16,1024]{1,0:T(8,128)(2,1)} %mask.1.lower), channel_id=1, source_target_pairs={{0,480},{1,448},{2,352},{3,416},{4,320},{5,224},{6,384},{7,288},{8... | collective-permute-start | bytes 98312 | tf_op jit(solution)/shard_map/ppermute | solution.py:245
  16.2 27.6 %copy-start.1 = (bf16[256,512]{1,0:T(8,128)(2,1)S(1)}, bf16[256,512]{1,0:T(8,128)(2,1)}, u32[]{:S(2)}) copy-start(bf16[256,512]{1,0:T(8,128)(2,1)} %inverse.1) | copy-start | bytes 786436
  38.3 5.5 %collective-permute-start.1 = (bf16[16,16,1024]{2,1,0:T(8,128)(2,1)S(1)}, bf16[16,16,1024]{2,1,0:T(8,128)(2,1)S(1)}, u32[]{:S(2)}, u32[]{:S(2)}) collective-permute-start(bf16[16,16,1024]{2,1,0:T(8,128)(2,1)S(1)} %all_to_all.25.mine), channel_id=1, source_target_pairs={{0,16},{16,0},{1,17},{17,1},{2,18},{18,2},{3,19},{19,3},{4,20},{20... | collective-permute-start | bytes 1572872 | tf_op jit(solution)/shard_map/ppermute | solution.py:53
  44.8 33.4 %copy-start = (bf16[2,256,256]{2,1,0:T(8,128)(2,1)S(1)}, bf16[2,256,256]{2,1,0:T(8,128)(2,1)}, u32[]{:S(2)}) copy-start(bf16[2,256,256]{2,1,0:T(8,128)(2,1)} %link.3) | copy-start | bytes 786436
  44.8 33.4 %copy-start.3 = (bf16[16,1024]{1,0:T(8,128)(2,1)S(1)}, bf16[16,1024]{1,0:T(8,128)(2,1)}, u32[]{:S(2)}) copy-start(bf16[16,1024]{1,0:T(8,128)(2,1)} %mask.1.lower) | copy-start | bytes 98308
  44.8 33.4 %copy-start.4 = (s32[4]{0:T(128)S(1)}, s32[4]{0:T(128)}, u32[]{:S(2)}) copy-start(s32[4]{0:T(128)} %widths.7) | copy-start | bytes 52
  44.8 33.4 %copy-start.5 = (s32[2,28]{1,0:T(2,128)S(1)}, s32[2,28]{1,0:T(2,128)}, u32[]{:S(2)}) copy-start(s32[2,28]{1,0:T(2,128)} %anc_one.3) | copy-start | bytes 676
  44.9 33.4 %copy-start.6 = (s32[2,24]{1,0:T(2,128)S(1)}, s32[2,24]{1,0:T(2,128)}, u32[]{:S(2)}) copy-start(s32[2,24]{1,0:T(2,128)} %anc_two.3) | copy-start | bytes 580
  44.9 33.4 %copy-start.7 = (s32[2]{0:T(128)S(1)}, s32[2]{0:T(128)}, u32[]{:S(2)}) copy-start(s32[2]{0:T(128)} %pad_add_fusion.place) | copy-start | bytes 28
  79.7 11.0 %collective-permute-start.2 = (f32[3,256,256]{2,1,0:T(8,128)S(1)}, f32[3,256,256]{2,1,0:T(8,128)S(1)}, u32[]{:S(2)}, u32[]{:S(2)}) collective-permute-start(f32[3,256,256]{2,1,0:T(8,128)S(1)} %get-tuple-element.21), channel_id=1, source_target_pairs={{0,16},{16,0},{1,17},{17,1},{2,18},{18,2},{3,19},{19,3},{4,20},{20... | collective-permute-start | bytes 2359304 | tf_op jit(solution)/shard_map/ppermute | solution.py:53
  111.2 18.0 %copy-start.2 = (f32[96,128]{1,0:T(8,128)S(1)}, f32[96,128]{1,0:T(8,128)}, u32[]{:S(2)}) copy-start(f32[96,128]{1,0:T(8,128)} %pivot.1) | copy-start | bytes 147460
  140.2 7.9 %collective-permute-start.3 = (bf16[2,768,128]{2,1,0:T(8,128)(2,1)S(1)}, bf16[2,768,128]{2,1,0:T(8,128)(2,1)S(1)}, u32[]{:S(2)}, u32[]{:S(2)}) collective-permute-start(bf16[2,768,128]{2,1,0:T(8,128)(2,1)S(1)} %bitcast.7), channel_id=1, source_target_pairs={{0,16},{16,0},{1,17},{17,1},{2,18},{18,2},{3,19},{19,3},{4,20},{20... | collective-permute-start | bytes 1179656 | tf_op jit(solution)/shard_map/ppermute | solution.py:53

commit v9 on v8

--- a/solution.py
+++ b/solution.py
@@ -109,7 +109,7 @@
         copies[i] = value
 
 
-def product_body(w, core, order, inverse, mine, other, part, held):
+def product_body(w, core, order, inverse, mine, other, rows, part, keep, give, held, dense):
     blocks, share, _ = mine.shape
     half = blocks * share
     for i in range(blocks):
@@ -120,28 +120,38 @@
     for k in range(4):
         span = slice(k * w, (k + 1) * w)
         value = (dot(left, held[:half, span]) + dot(right, held[half:, span])).astype(BF16)
+        dense[:, span] = value
         for i in range(part.shape[0]):
-            part[i, :, span] = value[i * share : (i + 1) * share]
-
-
-def column_body(
-    w, tile, place, received, lower, link, anc_one, anc_two, widths, column_one, column_two, mine, other
-):
-    total = reduced(received)
+            for h in range(w // LANES):
+                place = (k * (w // LANES) + h) * share
+                piece = value[i * share : (i + 1) * share, h * LANES : (h + 1) * LANES]
+                part[i, place : place + share, :] = piece
+    for out, sibling in ((keep, core[0]), (give, 1 - core[0])):
+        first = pl.ds(pl.multiple_of(sibling * w, w), w)
+        second = pl.ds(pl.multiple_of((2 + sibling) * w, w), w)
+        out[0] = dot_t(rows[:, first], dense[:, first])
+        out[1] = dot_t(dense[:, first], rows[:, second])
+        out[2] = dot_t(rows[:, second], dense[:, second])
+
+
+def column_body(w, chunk, tile, received, link, anc_one, anc_two, widths, column_one, column_two):
+    total = received[0, chunk:, :].astype(F32)
+    for i in range(1, received.shape[0]):
+        total = total + received[i, chunk:, :].astype(F32)
+    share, pieces = column_one.shape[0], w // LANES
+
+    def group(k):
+        starts = [(k * pieces + h) * share for h in range(pieces)]
+        return jnp.concatenate([total[a : a + share] for a in starts], axis=1)
+
     for s in range(2):
         span = slice(s * w, (s + 1) * w)
         here_one = jnp.where(is_member(anc_one, s, tile[0]), 1.0, 0.0)
         here_two = jnp.where(is_member(anc_two, s, tile[0]), 1.0, 0.0)
-        one = (-(total[:, span] * here_one)).astype(BF16)
+        one = (-(group(s) * here_one)).astype(BF16)
         column_one[:, span] = one
-        two = total[:, (2 + s) * w : (3 + s) * w] + dot(one, masked_link(w, link, widths, s))
+        two = group(2 + s) + dot(one, masked_link(w, link, widths, s))
         column_two[:, span] = (-(two * here_two)).astype(BF16)
-    for out, sibling in ((mine, place[0]), (other, 1 - place[0])):
-        first = pl.ds(pl.multiple_of(sibling * w, w), w)
-        second = pl.ds(pl.multiple_of((2 + sibling) * w, w), w)
-        out[0] = -dot_t(lower[:, first], column_one[:, first])
-        out[1] = dot_t(column_one[:, first], lower[:, second])
-        out[2] = -dot_t(lower[:, second], column_two[:, first])
 
 
 def core_sum_body(w, mine, other, sums):
@@ -152,10 +162,12 @@
             sums[h, b * w : (b + 1) * w, :] = value[:, h * lanes : (h + 1) * lanes]
 
 
-def chunk_sum_body(received, copies):
+def chunk_sum_body(received, part, packed):
+    chunk = received.shape[1]
     value = reduced(received).astype(BF16)
-    for i in range(copies.shape[0]):
-        copies[i] = value
+    for i in range(packed.shape[0]):
+        packed[i, :chunk, :] = value
+        packed[i, chunk:, :] = part[i]
 
 
 def pivot_body(w, place, one, two, widths, pivot, stack):
@@ -178,11 +190,11 @@
 
 
 def all_sum_body(received, pivot, copies):
-    near, chunk = NEAR, received.shape[1]
+    near, chunk = NEAR, pivot.shape[0] // NEAR
     for n in range(near):
         total = pivot[n * chunk : (n + 1) * chunk, :]
         for i in range(n, received.shape[0], near):
-            total = total + received[i].astype(F32)
+            total = total + received[i, :chunk, :].astype(F32)
         total = total.astype(BF16)
         for i in range(copies.shape[0]):
             copies[i, n * chunk : (n + 1) * chunk, :] = total
@@ -197,11 +209,11 @@
     for total, sibling in ((mine, core[0]), (other, 1 - core[0])):
         tie = masked_link(w, link, widths, sibling)
         block = side_by_side(total, 0, w)
-        cross = side_by_side(total, 1, w).astype(F32)
+        cross = side_by_side(total, 1, w)
         block_one[sibling] = block
-        parent = (-(dot(block, tie) + cross)).astype(BF16)
+        parent = (cross.astype(F32) - dot(block, tie)).astype(BF16)
         parent_rows[sibling] = parent
-        rest = side_by_side(total, 2, w).astype(F32) - dot_t(tie, parent)
+        rest = side_by_side(total, 2, w).astype(F32) - dot_t(cross, tie) - dot_t(tie, parent)
         block_two[sibling] = rest.astype(BF16)
 
 
@@ -256,41 +268,47 @@
         out_shape=jax.ShapeDtypeStruct((NEAR * chunk, LANES), F32),
         scratch_shapes=[pltpu.VMEM((3 * w * w // LANES, LANES), F32)],
     )(place, diag_inverse_one, diag_inverse_two, widths)
-    moved, order, place, pivot = lax.optimization_barrier((moved, order, place, pivot))
+    rows = lax.all_gather(lower, ("far", "near"), axis=0, tiled=True)
+    moved, rows = lax.optimization_barrier((moved, rows))
     (moved,) = kernel_call(copy_body, "copies", [VMEM], [((chips,) + whole, BF16)])(moved)
     mine = exchange(moved, "chip")
     other = swap_cores(mine)
 
-    part = pl.pallas_call(
+    part, mine, other = pl.pallas_call(
         functools.partial(product_body, w),
         name="product",
-        in_specs=[SMEM, SMEM] + [VMEM] * 3,
-        out_specs=VMEM,
-        out_shape=jax.ShapeDtypeStruct((planes,) + whole, BF16),
-        scratch_shapes=[pltpu.VMEM((CORES * chips * share, 4 * w), BF16)],
+        in_specs=[SMEM, SMEM] + [VMEM] * 4,
+        out_specs=[VMEM] * 3,
+        out_shape=[jax.ShapeDtypeStruct((planes, share * 4 * w // LANES, LANES), BF16)]
+        + [jax.ShapeDtypeStruct((3, w, w), F32)] * 2,
+        scratch_shapes=[
+            pltpu.VMEM((CORES * chips * share, 4 * w), BF16),
+            pltpu.VMEM((local_rows, 4 * w), BF16),
+        ],
         compiler_params=pltpu.CompilerParams(vmem_limit_bytes=40 * 1024 * 1024),
-    )(core_ref, order, ancestor_inverse, mine, other)
-    part = exchange(part, ("far", "near"))
-    column_one, column_two, mine, other = kernel_call(
-        functools.partial(column_body, w),
-        "columns",
-        [SMEM, SMEM, VMEM, VMEM, VMEM, SMEM, SMEM, SMEM],
-        [((share, 2 * w), BF16)] * 2 + [((3, w, w), F32)] * 2,
-    )(tile, place, part, lower, link_two, ancestors_one, ancestors_two, widths)
-    other = swap_cores(other)
+    )(core_ref, order, ancestor_inverse, mine, other, rows)
+    other, pivot = lax.optimization_barrier((swap_cores(other), pivot))
     (sums,) = kernel_call(
         functools.partial(core_sum_body, w), "core_sum", [VMEM] * 2, [(flat, BF16)]
     )(mine, other)
     sums = exchange(sums.reshape(chips * NEAR, chunk, LANES), ("chip", "near"))
-    (sums,) = kernel_call(chunk_sum_body, "chunk_sum", [VMEM], [((planes, chunk, LANES), BF16)])(
-        sums
-    )
-    sums = exchange(sums, ("far", "near"))
+    (packed,) = kernel_call(
+        chunk_sum_body, "chunk_sum", [VMEM] * 2, [((planes, chunk + part.shape[1], LANES), BF16)]
+    )(sums, part)
+    packed = exchange(packed, ("far", "near"))
     (total,) = kernel_call(
         all_sum_body, "all_sum", [VMEM] * 2, [((chips, NEAR * chunk, LANES), BF16)]
-    )(sums, pivot)
+    )(
+        packed, pivot
+    )
     mine = exchange(total, "chip").reshape(flat)
     other = swap_cores(mine)
+    column_one, column_two = kernel_call(
+        functools.partial(column_body, w, chunk),
+        "columns",
+        [SMEM, VMEM, VMEM, SMEM, SMEM, SMEM],
+        [((share, 2 * w), BF16)] * 2,
+    )(tile, packed, link_two, ancestors_one, ancestors_two, widths)
     block_one, parent_rows, block_two = kernel_call(
         functools.partial(final_body, w),
         "final",

time: 151 us -> 158 us (1.046)
  blocking collectives: 105 us -> 117 us
  waiting for transfers between devices: 7.48 us -> 0.82 us
    all_gather x0 -> x1, blocking collectives: none -> 28.9 us  [local(): rows = lax.all_gather(lower, ('far', 'near'), axis=0, tiled=True)]
    all_to_all x5 -> x4, blocking collectives: 105 us -> 88.2 us  [exchange(): return lax.all_to_all(blocks, axis, split_axis=0, concat_axis=0, tiled=True)]
    ppermute x3, waiting for transfers between devices: 4.73 us -> 0.81 us  [swap_cores(): return lax.ppermute(block, 'core', [(0, 1), (1, 0)])]
    ppermute x1, waiting for transfers between devices: 2.75 us -> 0.01 us  [local(): moved = lax.ppermute(lower, GRID, pairs)]
  transfers between devices with their start and end apart: 4 -> 4, of which waited for: 4 -> 1; matrix products, arithmetic and copies ran while one was open for 1% -> 1% of each run, Pallas kernels for 1% -> 2%
where the time goes in v9:
time: 158 us
  blocking collectives  117 us (74%)
  starting transfers between devices  28.2 us (18%)
  Pallas kernels  9.59 us (6%)
    all_to_all x4, blocking collectives, exchange(): return lax.all_to_all(blocks, axis, split_axis=0, concat_axis=0, tiled=True)  88.2 us
    all_gather x1, blocking collectives, local(): rows = lax.all_gather(lower, ('far', 'near'), axis=0, tiled=True)  28.9 us
    ppermute x3, starting transfers between devices, swap_cores(): return lax.ppermute(block, 'core', [(0, 1), (1, 0)])  20.6 us
    ppermute x1, starting transfers between devices, local(): moved = lax.ppermute(lower, GRID, pairs)  7.67 us
  transfers between devices with their start and end apart: 4, of which 1 were waited for; matrix products, arithmetic and copies ran while one was open for 1% of the time, Pallas kernels for 2%

profile of v9, /device:TPU:1, one launch (start us, length us, event | category | flops | bytes accessed | tf_op | source)
XLA Modules:
  0.0 157.8 jit_solution(13228591361107361313)
XLA Ops:
  0.6 2.1 %mask.1 = bf16[16,1024]{1,0:T(8,128)(2,1)} custom-call(s32[1]{0:T(128)} %bitcast.tile, bf16[16,512]{1,0:T(8,128)(2,1)} %one.2, bf16[16,512]{1,0:T(8,128)(2,1)} %two.2, s32[2,28]{1,0:T(2,128)} %anc_one.3, s32[2,24]{1,0:T(2,128)} %anc_two.3, s32[4]{0:T(128)} %widths.7), custom_call_target="tpu_custom_call" | custom-call | tf_op jit(solution)/shard_map/mask/pallas_call | solution.py:242
  2.7 7.7 %collective-permute-start = (bf16[16,1024]{1,0:T(8,128)(2,1)}, bf16[16,1024]{1,0:T(8,128)(2,1)S(1)}, u32[]{:S(2)}, u32[]{:S(2)}) collective-permute-start(bf16[16,1024]{1,0:T(8,128)(2,1)} %mask.1), channel_id=1, source_target_pairs={{0,480},{1,448},{2,352},{3,416},{4,320},{5,224},{6,384},{7,288},{8... | collective-permute-start | bytes 98312 | tf_op jit(solution)/shard_map/ppermute | solution.py:257
  10.4 28.9 %all_gather.3.rows = bf16[256,1024]{1,0:T(8,128)(2,1)S(1)} all-gather(bf16[16,1024]{1,0:T(8,128)(2,1)} %mask.1), channel_id=1, replica_groups=mesh['chip'=16,'core'=2,'far'=4,'near'=4] {'far','near'}, dimensions={0}, use_global_device_ids=true | all-gather | bytes 557056 | tf_op jit(solution)/shard_map/all_gather | solution.py:271
  39.3 0.0 collective-permute-done.source
  39.3 0.0 copy-start.1
  39.3 18.8 %all_to_all.20.mine = bf16[16,16,1024]{2,1,0:T(8,128)(2,1)S(1)} all-to-all(bf16[16,16,1024]{2,1,0:T(8,128)(2,1)S(1)} %copies.1), channel_id=1, replica_groups=mesh['chip'=16,'core'=2,'far'=4,'near'=4] {'chip'}, dimensions={0} | all-to-all | bytes 1048576 | tf_op jit(solution)/shard_map/all_to_all | solution.py:34
  58.1 10.8 %collective-permute-start.1 = (bf16[16,16,1024]{2,1,0:T(8,128)(2,1)S(1)}, bf16[16,16,1024]{2,1,0:T(8,128)(2,1)S(1)}, u32[]{:S(2)}, u32[]{:S(2)}) collective-permute-start(bf16[16,16,1024]{2,1,0:T(8,128)(2,1)S(1)} %all_to_all.20.mine), channel_id=1, source_target_pairs={{0,16},{16,0},{1,17},{17,1},{2,18},{18,2},{3,19},{19,3},{4,20},{20... | collective-permute-start | bytes 1572872 | tf_op jit(solution)/shard_map/ppermute | solution.py:53
  68.9 0.7 dynamic-slice_bitcast_fusion.order
  69.6 0.8 collective-permute-done.1.other
  70.4 0.0 copy-done.1
  70.4 2.3 %product.1 = (bf16[16,128,128]{2,1,0:T(8,128)(2,1)S(1)}, f32[3,256,256]{2,1,0:T(8,128)S(1)}, f32[3,256,256]{2,1,0:T(8,128)}) custom-call(s32[1]{0:T(128)} %bitcast.1.core, s32[16]{0:T(128)S(1)} %dynamic-slice_bitcast_fusion.order, bf16[256,512]{1,0:T(8,128)(2,1)S(1)} %copy-done.1, bf16[16,16,1024]{2,1,0:T(8,128)(2,1)S(1)} %all_to_all.20.mine, ...), custom_call_target="tpu_custom_call" | custom-call | tf_op jit(solution)/shard_map/product/pallas_call | solution.py:277
  72.7 2.3 %collective-permute-start.2 = (f32[3,256,256]{2,1,0:T(8,128)}, f32[3,256,256]{2,1,0:T(8,128)S(1)}, u32[]{:S(2)}, u32[]{:S(2)}) collective-permute-start(f32[3,256,256]{2,1,0:T(8,128)} %get-tuple-element.20), channel_id=1, source_target_pairs={{0,16},{16,0},{1,17},{17,1},{2,18},{18,2},{3,19},{19,3},{4,20},{20... | collective-permute-start | bytes 2359304 | tf_op jit(solution)/shard_map/ppermute | solution.py:53
  75.0 0.6 pad_add_fusion.place
  75.6 1.7 %pivot.1 = f32[96,128]{1,0:T(8,128)} custom-call(s32[2]{0:T(128)} %pad_add_fusion.place, bf16[2,256,256]{2,1,0:T(8,128)(2,1)} %one.3, bf16[2,256,256]{2,1,0:T(8,128)(2,1)} %two.3, s32[4]{0:T(128)} %widths.7), custom_call_target="tpu_custom_call" | custom-call | tf_op jit(solution)/shard_map/pivot/pallas_call | solution.py:263
  77.3 0.0 collective-permute-done.2.other
  77.3 0.1 core_sum.1
  77.4 19.4 %all_to_all.21.received = bf16[64,24,128]{2,1,0:T(8,128)(2,1)S(1)} all-to-all(bf16[64,24,128]{2,1,0:T(8,128)(2,1)S(1)} %bitcast.9), channel_id=1, replica_groups=mesh['chip'=16,'core'=2,'far'=4,'near'=4] {'chip','near'}, dimensions={0} | all-to-all | bytes 786432 | tf_op jit(solution)/shard_map/all_to_all | solution.py:34
  96.8 0.1 chunk_sum.1
  96.9 0.0 copy-start.2
  96.9 39.0 %all_to_all.22.received = bf16[16,152,128]{2,1,0:T(8,128)(2,1)S(1)} all-to-all(bf16[16,152,128]{2,1,0:T(8,128)(2,1)S(1)} %chunk_sum.1), channel_id=1, replica_groups=mesh['chip'=16,'core'=2,'far'=4,'near'=4] {'far','near'}, dimensions={0} | all-to-all | bytes 1245184 | tf_op jit(solution)/shard_map/all_to_all | solution.py:34
  135.9 0.0 copy-done.2
  136.0 0.0 copy-start
  136.0 0.0 copy-start.5
  136.0 11.0 %all_to_all.23 = bf16[16,96,128]{2,1,0:T(8,128)(2,1)S(1)} all-to-all(bf16[16,96,128]{2,1,0:T(8,128)(2,1)S(1)} %all_sum.1), channel_id=1, replica_groups=mesh['chip'=16,'core'=2,'far'=4,'near'=4] {'chip'}, dimensions={0} | all-to-all | bytes 786432 | tf_op jit(solution)/shard_map/all_to_all | solution.py:34
  147.0 0.0 copy-start.3
  147.0 0.0 copy-start.4
  147.0 7.5 %collective-permute-start.3 = (bf16[2,768,128]{2,1,0:T(8,128)(2,1)S(1)}, bf16[2,768,128]{2,1,0:T(8,128)(2,1)S(1)}, u32[]{:S(2)}, u32[]{:S(2)}) collective-permute-start(bf16[2,768,128]{2,1,0:T(8,128)(2,1)S(1)} %bitcast.7), channel_id=1, source_target_pairs={{0,16},{16,0},{1,17},{17,1},{2,18},{18,2},{3,19},{19,3},{4,20},{20... | collective-permute-start | bytes 1179656 | tf_op jit(solution)/shard_map/ppermute | solution.py:53
  154.5 0.0 copy-done
  154.6 0.0 copy-done.5
  154.6 0.0 copy-done.3
  154.6 0.0 copy-done.4
  154.6 1.4 columns.1
  156.0 0.0 collective-permute-done.3.other
  156.0 1.8 %final.1 = (bf16[2,256,256]{2,1,0:T(8,128)(2,1)}, bf16[2,256,256]{2,1,0:T(8,128)(2,1)}, bf16[2,256,256]{2,1,0:T(8,128)(2,1)}) custom-call(s32[1]{0:T(128)} %bitcast.1.core, bf16[2,768,128]{2,1,0:T(8,128)(2,1)S(1)} %bitcast.8, bf16[2,768,128]{2,1,0:T(8,128)(2,1)S(1)} %collective-permute-done.3.other, bf16[2,256,256]{2,1,0:T(8,128)(2,1)S(1)} %copy-done, ...), custom_call_target="tpu_custom_call" | custom-call | tf_op jit(solution)/shard_map/final/pallas_call | solution.py:312
  (2 shorter events, 0.1 us)
Async XLA Ops:
  2.7 36.5 %collective-permute-start = (bf16[16,1024]{1,0:T(8,128)(2,1)}, bf16[16,1024]{1,0:T(8,128)(2,1)S(1)}, u32[]{:S(2)}, u32[]{:S(2)}) collective-permute-start(bf16[16,1024]{1,0:T(8,128)(2,1)} %mask.1), channel_id=1, source_target_pairs={{0,480},{1,448},{2,352},{3,416},{4,320},{5,224},{6,384},{7,288},{8... | collective-permute-start | bytes 98312 | tf_op jit(solution)/shard_map/ppermute | solution.py:257
  39.3 31.1 %copy-start.1 = (bf16[256,512]{1,0:T(8,128)(2,1)S(1)}, bf16[256,512]{1,0:T(8,128)(2,1)}, u32[]{:S(2)}) copy-start(bf16[256,512]{1,0:T(8,128)(2,1)} %inverse.1) | copy-start | bytes 786436
  58.1 12.3 %collective-permute-start.1 = (bf16[16,16,1024]{2,1,0:T(8,128)(2,1)S(1)}, bf16[16,16,1024]{2,1,0:T(8,128)(2,1)S(1)}, u32[]{:S(2)}, u32[]{:S(2)}) collective-permute-start(bf16[16,16,1024]{2,1,0:T(8,128)(2,1)S(1)} %all_to_all.20.mine), channel_id=1, source_target_pairs={{0,16},{16,0},{1,17},{17,1},{2,18},{18,2},{3,19},{19,3},{4,20},{20... | collective-permute-start | bytes 1572872 | tf_op jit(solution)/shard_map/ppermute | solution.py:53
  72.7 4.6 %collective-permute-start.2 = (f32[3,256,256]{2,1,0:T(8,128)}, f32[3,256,256]{2,1,0:T(8,128)S(1)}, u32[]{:S(2)}, u32[]{:S(2)}) collective-permute-start(f32[3,256,256]{2,1,0:T(8,128)} %get-tuple-element.20), channel_id=1, source_target_pairs={{0,16},{16,0},{1,17},{17,1},{2,18},{18,2},{3,19},{19,3},{4,20},{20... | collective-permute-start | bytes 2359304 | tf_op jit(solution)/shard_map/ppermute | solution.py:53
  96.9 39.0 %copy-start.2 = (f32[96,128]{1,0:T(8,128)S(1)}, f32[96,128]{1,0:T(8,128)}, u32[]{:S(2)}) copy-start(f32[96,128]{1,0:T(8,128)} %pivot.1) | copy-start | bytes 147460
  136.0 18.6 %copy-start = (bf16[2,256,256]{2,1,0:T(8,128)(2,1)S(1)}, bf16[2,256,256]{2,1,0:T(8,128)(2,1)}, u32[]{:S(2)}) copy-start(bf16[2,256,256]{2,1,0:T(8,128)(2,1)} %link.3) | copy-start | bytes 786436
  136.0 18.6 %copy-start.5 = (s32[2,24]{1,0:T(2,128)S(1)}, s32[2,24]{1,0:T(2,128)}, u32[]{:S(2)}) copy-start(s32[2,24]{1,0:T(2,128)} %anc_two.3) | copy-start | bytes 580
  147.0 7.6 %copy-start.3 = (s32[4]{0:T(128)S(1)}, s32[4]{0:T(128)}, u32[]{:S(2)}) copy-start(s32[4]{0:T(128)} %widths.7) | copy-start | bytes 52
  147.0 7.6 %copy-start.4 = (s32[2,28]{1,0:T(2,128)S(1)}, s32[2,28]{1,0:T(2,128)}, u32[]{:S(2)}) copy-start(s32[2,28]{1,0:T(2,128)} %anc_one.3) | copy-start | bytes 676
  147.0 9.0 %collective-permute-start.3 = (bf16[2,768,128]{2,1,0:T(8,128)(2,1)S(1)}, bf16[2,768,128]{2,1,0:T(8,128)(2,1)S(1)}, u32[]{:S(2)}, u32[]{:S(2)}) collective-permute-start(bf16[2,768,128]{2,1,0:T(8,128)(2,1)S(1)} %bitcast.7), channel_id=1, source_target_pairs={{0,16},{16,0},{1,17},{17,1},{2,18},{18,2},{3,19},{19,3},{4,20},{20... | collective-permute-start | bytes 1179656 | tf_op jit(solution)/shard_map/ppermute | solution.py:53

commit v10 on v8

--- a/solution.py
+++ b/solution.py
@@ -14,9 +14,10 @@
 ANY = pl.BlockSpec(memory_space=pl.ANY)
 SMEM = pl.BlockSpec(memory_space=pltpu.SMEM)
 NEAR = 4
+PAIR = 2
 CORES = 2
 LANES = 128
-GRID = ("chip", "core", "far", "near")
+GRID = ("chip", "core", "far", "mid", "pair")
 
 
 def kernel_call(body, name, specs, outs):
@@ -109,7 +110,7 @@
         copies[i] = value
 
 
-def product_body(w, core, order, inverse, mine, other, part, held):
+def product_body(w, core, parity, order, inverse, mine, other, keep, give, held, part):
     blocks, share, _ = mine.shape
     half = blocks * share
     for i in range(blocks):
@@ -122,6 +123,14 @@
         value = (dot(left, held[:half, span]) + dot(right, held[half:, span])).astype(BF16)
         for i in range(part.shape[0]):
             part[i, :, span] = value[i * share : (i + 1) * share]
+    for i in range(keep.shape[0]):
+        keep[i] = part[PAIR * i + parity[0]]
+        give[i] = part[PAIR * i + 1 - parity[0]]
+
+
+def pair_sum_body(keep, got, sums):
+    for i in range(sums.shape[0]):
+        sums[i] = (keep[i].astype(F32) + got[i].astype(F32)).astype(BF16)
 
 
 def column_body(
@@ -243,7 +252,8 @@
             for z in range(planes):
                 pairs.append(((q * CORES + k) * planes + z, (places[q][z] * CORES + k) * planes + q))
     moved = lax.ppermute(lower, GRID, pairs)
-    plane = lax.axis_index("far") * NEAR + lax.axis_index("near")
+    parity = lax.axis_index("pair").astype(jnp.int32)
+    plane = lax.axis_index("far") * NEAR + lax.axis_index("mid") * PAIR + parity
     order = lax.dynamic_index_in_dim(jnp.array(places, jnp.int32), plane, 0, keepdims=False)
     place = jnp.stack([core, chip])
     flat = (w // LANES, 3 * w, LANES)
@@ -261,16 +271,22 @@
     mine = exchange(moved, "chip")
     other = swap_cores(mine)
 
-    part = pl.pallas_call(
+    half = (planes // PAIR,) + whole
+    keep, give = pl.pallas_call(
         functools.partial(product_body, w),
         name="product",
-        in_specs=[SMEM, SMEM] + [VMEM] * 3,
-        out_specs=VMEM,
-        out_shape=jax.ShapeDtypeStruct((planes,) + whole, BF16),
-        scratch_shapes=[pltpu.VMEM((CORES * chips * share, 4 * w), BF16)],
+        in_specs=[SMEM] * 3 + [VMEM] * 3,
+        out_specs=[VMEM] * 2,
+        out_shape=[jax.ShapeDtypeStruct(half, BF16)] * 2,
+        scratch_shapes=[
+            pltpu.VMEM((CORES * chips * share, 4 * w), BF16),
+            pltpu.VMEM((planes,) + whole, BF16),
+        ],
         compiler_params=pltpu.CompilerParams(vmem_limit_bytes=40 * 1024 * 1024),
-    )(core_ref, order, ancestor_inverse, mine, other)
-    part = exchange(part, ("far", "near"))
+    )(core_ref, parity.reshape(1), order, ancestor_inverse, mine, other)
+    got = lax.ppermute(give, "pair", [(0, 1), (1, 0)])
+    (part,) = kernel_call(pair_sum_body, "pair_sum", [VMEM] * 2, [(half, BF16)])(keep, got)
+    part = exchange(part, ("far", "mid"))
     column_one, column_two, mine, other = kernel_call(
         functools.partial(column_body, w),
         "columns",
@@ -281,11 +297,11 @@
     (sums,) = kernel_call(
         functools.partial(core_sum_body, w), "core_sum", [VMEM] * 2, [(flat, BF16)]
     )(mine, other)
-    sums = exchange(sums.reshape(chips * NEAR, chunk, LANES), ("chip", "near"))
+    sums = exchange(sums.reshape(chips * NEAR, chunk, LANES), ("chip", "mid", "pair"))
     (sums,) = kernel_call(chunk_sum_body, "chunk_sum", [VMEM], [((planes, chunk, LANES), BF16)])(
         sums
     )
-    sums = exchange(sums, ("far", "near"))
+    sums = exchange(sums, ("far", "mid", "pair"))
     (total,) = kernel_call(
         all_sum_body, "all_sum", [VMEM] * 2, [((chips, NEAR * chunk, LANES), BF16)]
     )(sums, pivot)
@@ -302,8 +318,9 @@
 
 def solution(mesh):
     rows_n, cols_n = mesh.devices.shape
-    fine = Mesh(mesh.devices.reshape(rows_n // CORES, CORES, cols_n // NEAR, NEAR), GRID)
-    row, col = ("chip", "core"), ("far", "near")
+    sizes = (rows_n // CORES, CORES, cols_n // NEAR, NEAR // PAIR, PAIR)
+    fine = Mesh(mesh.devices.reshape(sizes), GRID)
+    row, col = GRID[:2], GRID[2:]
     shared = P(GRID, None)
     in_specs = (P(row, col), shared, P(), P(), shared, P(), P(), P(), P())
     out_specs = (shared, P(), shared, P(), P())

time: 151 us -> 149 us (0.987)
  blocking collectives: 105 us -> 93.9 us
  waiting for transfers between devices: 7.48 us -> 13.9 us
  starting transfers between devices: 27.3 us -> 29.8 us
    all_to_all x5, blocking collectives: 105 us -> 93.9 us  [exchange(): return lax.all_to_all(blocks, axis, split_axis=0, concat_axis=0, tiled=True)]
    ppermute x0 -> x1, waiting for transfers between devices: none -> 6.42 us  [local(): got = lax.ppermute(give, 'pair', [(0, 1), (1, 0)])]
    ppermute x0 -> x1, starting transfers between devices: none -> 2.98 us  [local(): got = lax.ppermute(give, 'pair', [(0, 1), (1, 0)])]
  transfers between devices with their start and end apart: 4 -> 5, of which waited for: 4 -> 5; matrix products, arithmetic and copies ran while one was open for 1% -> 1% of each run, Pallas kernels for 1% -> 1%
where the time goes in v10:
time: 149 us; the launch traced here: 148 us
  blocking collectives  93.9 us (63%)
  starting transfers between devices  29.8 us (20%)
  waiting for transfers between devices  13.9 us (9%)
  Pallas kernels  8.35 us (6%)
    all_to_all x5, blocking collectives, exchange(): return lax.all_to_all(blocks, axis, split_axis=0, concat_axis=0, tiled=True)  93.9 us
    ppermute x3, starting transfers between devices, swap_cores(): return lax.ppermute(block, 'core', [(0, 1), (1, 0)])  19.2 us
    ppermute x1, starting transfers between devices, local(): moved = lax.ppermute(lower, GRID, pairs)  7.67 us
    ppermute x1, waiting for transfers between devices, local(): got = lax.ppermute(give, 'pair', [(0, 1), (1, 0)])  6.42 us
    ppermute x3, waiting for transfers between devices, swap_cores(): return lax.ppermute(block, 'core', [(0, 1), (1, 0)])  4.73 us
  transfers between devices with their start and end apart: 5, of which 5 were waited for; matrix products, arithmetic and copies ran while one was open for 1% of the time, Pallas kernels for 1%

profile of v10, /device:TPU:1, one launch (start us, length us, event | category | flops | bytes accessed | tf_op | source)
XLA Modules:
  0.0 148.1 jit_solution(3683201747966717836)
XLA Ops:
  0.6 2.1 %mask.1.lower = bf16[16,1024]{1,0:T(8,128)(2,1)} custom-call(s32[1]{0:T(128)} %bitcast.tile, bf16[16,512]{1,0:T(8,128)(2,1)} %one.2, bf16[16,512]{1,0:T(8,128)(2,1)} %two.2, s32[2,28]{1,0:T(2,128)} %anc_one.3, s32[2,24]{1,0:T(2,128)} %anc_two.3, s32[4]{0:T(128)} %widths.7), custom_call_target="tpu_custom_call" | custom-call | tf_op jit(solution)/shard_map/mask/pallas_call | solution.py:239
  2.7 7.7 %collective-permute-start = (bf16[16,1024]{1,0:T(8,128)(2,1)}, bf16[16,1024]{1,0:T(8,128)(2,1)S(1)}, u32[]{:S(2)}, u32[]{:S(2)}) collective-permute-start(bf16[16,1024]{1,0:T(8,128)(2,1)} %mask.1.lower), channel_id=1, source_target_pairs={{0,480},{1,448},{2,352},{3,416},{4,320},{5,224},{6,384},{7,288},{8... | collective-permute-start | bytes 98312 | tf_op jit(solution)/shard_map/ppermute | solution.py:254
  10.4 0.7 dynamic-slice_bitcast_fusion.order
  11.1 0.6 pad_add_fusion.place
  11.7 1.7 %pivot.1 = f32[96,128]{1,0:T(8,128)} custom-call(s32[2]{0:T(128)} %pad_add_fusion.place, bf16[2,256,256]{2,1,0:T(8,128)(2,1)} %one.3, bf16[2,256,256]{2,1,0:T(8,128)(2,1)} %two.3, s32[4]{0:T(128)} %widths.7), custom_call_target="tpu_custom_call" | custom-call | tf_op jit(solution)/shard_map/pivot/pallas_call | solution.py:261
  13.4 2.7 %collective-permute-done.source = bf16[16,1024]{1,0:T(8,128)(2,1)S(1)} collective-permute-done((bf16[16,1024]{1,0:T(8,128)(2,1)}, bf16[16,1024]{1,0:T(8,128)(2,1)S(1)}, u32[]{:S(2)}, u32[]{:S(2)}) %collective-permute-start) | collective-permute-done | bytes 32800 | tf_op jit(solution)/shard_map/ppermute | solution.py:254
  16.2 0.0 copy-start.1
  16.2 22.0 %all_to_all.25.mine = bf16[16,16,1024]{2,1,0:T(8,128)(2,1)S(1)} all-to-all(bf16[16,16,1024]{2,1,0:T(8,128)(2,1)S(1)} %copies.1), channel_id=1, replica_groups=mesh['chip'=16,'core'=2,'far'=4,'mid'=2,'pair'=2] {'chip'}, dimensions={0} | all-to-all | bytes 1048576 | tf_op jit(solution)/shard_map/all_to_all | solution.py:35
  38.3 4.0 %collective-permute-start.1 = (bf16[16,16,1024]{2,1,0:T(8,128)(2,1)S(1)}, bf16[16,16,1024]{2,1,0:T(8,128)(2,1)S(1)}, u32[]{:S(2)}, u32[]{:S(2)}) collective-permute-start(bf16[16,16,1024]{2,1,0:T(8,128)(2,1)S(1)} %all_to_all.25.mine), channel_id=1, source_target_pairs={{0,16},{16,0},{1,17},{17,1},{2,18},{18,2},{3,19},{19,3},{4,20},{20... | collective-permute-start | bytes 1572872 | tf_op jit(solution)/shard_map/ppermute | solution.py:54
  42.3 1.5 %collective-permute-done.1.other = bf16[16,16,1024]{2,1,0:T(8,128)(2,1)S(1)} collective-permute-done((bf16[16,16,1024]{2,1,0:T(8,128)(2,1)S(1)}, bf16[16,16,1024]{2,1,0:T(8,128)(2,1)S(1)}, u32[]{:S(2)}, u32[]{:S(2)}) %collective-permute-start.1) | collective-permute-done | bytes 524320 | tf_op jit(solution)/shard_map/ppermute | solution.py:54
  43.8 0.0 copy-done.1
  43.8 1.0 product.1
  44.8 3.0 %collective-permute-start.2 = (bf16[8,16,1024]{2,1,0:T(8,128)(2,1)S(1)}, bf16[8,16,1024]{2,1,0:T(8,128)(2,1)S(1)}, u32[]{:S(2)}, u32[]{:S(2)}) collective-permute-start(bf16[8,16,1024]{2,1,0:T(8,128)(2,1)S(1)} %get-tuple-element.22), channel_id=1, source_target_pairs={{0,1},{1,0},{2,3},{3,2},{4,5},{5,4},{6,7},{7,6},{8,9},{9,8},{10,11... | collective-permute-start | bytes 786440 | tf_op jit(solution)/shard_map/ppermute | solution.py:287
  47.8 6.4 %collective-permute-done.2.got = bf16[8,16,1024]{2,1,0:T(8,128)(2,1)S(1)} collective-permute-done((bf16[8,16,1024]{2,1,0:T(8,128)(2,1)S(1)}, bf16[8,16,1024]{2,1,0:T(8,128)(2,1)S(1)}, u32[]{:S(2)}, u32[]{:S(2)}) %collective-permute-start.2) | collective-permute-done | bytes 262176 | tf_op jit(solution)/shard_map/ppermute | solution.py:287
  54.3 0.1 pair_sum.1
  54.3 0.0 copy-start
  54.3 0.0 copy-start.3
  54.3 0.0 copy-start.4
  54.4 0.0 copy-start.5
  54.4 0.0 copy-start.6
  54.4 0.0 copy-start.7
  54.4 26.1 %all_to_all.26.received = bf16[8,16,1024]{2,1,0:T(8,128)(2,1)S(1)} all-to-all(bf16[8,16,1024]{2,1,0:T(8,128)(2,1)S(1)} %pair_sum.1), channel_id=1, replica_groups=mesh['chip'=16,'core'=2,'far'=4,'mid'=2,'pair'=2] {'far','mid'}, dimensions={0} | all-to-all | bytes 524288 | tf_op jit(solution)/shard_map/all_to_all | solution.py:35
  80.5 0.0 copy-done
  80.5 0.0 copy-done.3
  80.5 0.0 copy-done.4
  80.5 0.0 copy-done.5
  80.5 0.0 copy-done.6
  80.5 0.0 copy-done.7
  80.5 1.5 columns.1
  82.0 8.6 %collective-permute-start.3 = (f32[3,256,256]{2,1,0:T(8,128)S(1)}, f32[3,256,256]{2,1,0:T(8,128)S(1)}, u32[]{:S(2)}, u32[]{:S(2)}) collective-permute-start(f32[3,256,256]{2,1,0:T(8,128)S(1)} %get-tuple-element.25), channel_id=1, source_target_pairs={{0,16},{16,0},{1,17},{17,1},{2,18},{18,2},{3,19},{19,3},{4,20},{20... | collective-permute-start | bytes 2359304 | tf_op jit(solution)/shard_map/ppermute | solution.py:54
  90.5 1.9 %collective-permute-done.3.other = f32[3,256,256]{2,1,0:T(8,128)S(1)} collective-permute-done((f32[3,256,256]{2,1,0:T(8,128)S(1)}, f32[3,256,256]{2,1,0:T(8,128)S(1)}, u32[]{:S(2)}, u32[]{:S(2)}) %collective-permute-start.3) | collective-permute-done | bytes 786464 | tf_op jit(solution)/shard_map/ppermute | solution.py:54
  92.4 0.1 core_sum.1
  92.5 18.9 %all_to_all.27.received = bf16[64,24,128]{2,1,0:T(8,128)(2,1)S(1)} all-to-all(bf16[64,24,128]{2,1,0:T(8,128)(2,1)S(1)} %bitcast.10), channel_id=1, replica_groups=mesh['chip'=16,'core'=2,'far'=4,'mid'=2,'pair'=2] {'chip','mid','pair'}, dimensions={0} | all-to-all | bytes 786432 | tf_op jit(solution)/shard_map/all_to_all | solution.py:35
  111.4 0.1 chunk_sum.1
  111.5 0.0 copy-start.2
  111.5 15.9 %all_to_all.28.received = bf16[16,24,128]{2,1,0:T(8,128)(2,1)S(1)} all-to-all(bf16[16,24,128]{2,1,0:T(8,128)(2,1)S(1)} %chunk_sum.1), channel_id=1, replica_groups=mesh['chip'=16,'core'=2,'far'=4,'mid'=2,'pair'=2] {'far','mid','pair'}, dimensions={0} | all-to-all | bytes 196608 | tf_op jit(solution)/shard_map/all_to_all | solution.py:35
  127.4 0.0 copy-done.2
  127.5 11.0 %all_to_all.29 = bf16[16,96,128]{2,1,0:T(8,128)(2,1)S(1)} all-to-all(bf16[16,96,128]{2,1,0:T(8,128)(2,1)S(1)} %all_sum.1), channel_id=1, replica_groups=mesh['chip'=16,'core'=2,'far'=4,'mid'=2,'pair'=2] {'chip'}, dimensions={0} | all-to-all | bytes 786432 | tf_op jit(solution)/shard_map/all_to_all | solution.py:35
  138.4 6.6 %collective-permute-start.4 = (bf16[2,768,128]{2,1,0:T(8,128)(2,1)S(1)}, bf16[2,768,128]{2,1,0:T(8,128)(2,1)S(1)}, u32[]{:S(2)}, u32[]{:S(2)}) collective-permute-start(bf16[2,768,128]{2,1,0:T(8,128)(2,1)S(1)} %bitcast.8), channel_id=1, source_target_pairs={{0,16},{16,0},{1,17},{17,1},{2,18},{18,2},{3,19},{19,3},{4,20},{20... | collective-permute-start | bytes 1179656 | tf_op jit(solution)/shard_map/ppermute | solution.py:54
  145.0 1.3 collective-permute-done.4.other
  146.3 1.7 %final.1 = (bf16[2,256,256]{2,1,0:T(8,128)(2,1)}, bf16[2,256,256]{2,1,0:T(8,128)(2,1)}, bf16[2,256,256]{2,1,0:T(8,128)(2,1)}) custom-call(s32[1]{0:T(128)} %bitcast.2.core, bf16[2,768,128]{2,1,0:T(8,128)(2,1)S(1)} %bitcast.9, bf16[2,768,128]{2,1,0:T(8,128)(2,1)S(1)} %collective-permute-done.4.other, bf16[2,256,256]{2,1,0:T(8,128)(2,1)S(1)} %copy-done, ...), custom_call_target="tpu_custom_call" | custom-call | tf_op jit(solution)/shard_map/final/pallas_call | solution.py:310
  (2 shorter events, 0.1 us)
Async XLA Ops:
  2.7 13.5 %collective-permute-start = (bf16[16,1024]{1,0:T(8,128)(2,1)}, bf16[16,1024]{1,0:T(8,128)(2,1)S(1)}, u32[]{:S(2)}, u32[]{:S(2)}) collective-permute-start(bf16[16,1024]{1,0:T(8,128)(2,1)} %mask.1.lower), channel_id=1, source_target_pairs={{0,480},{1,448},{2,352},{3,416},{4,320},{5,224},{6,384},{7,288},{8... | collective-permute-start | bytes 98312 | tf_op jit(solution)/shard_map/ppermute | solution.py:254
  16.2 27.6 %copy-start.1 = (bf16[256,512]{1,0:T(8,128)(2,1)S(1)}, bf16[256,512]{1,0:T(8,128)(2,1)}, u32[]{:S(2)}) copy-start(bf16[256,512]{1,0:T(8,128)(2,1)} %inverse.1) | copy-start | bytes 786436
  38.3 5.5 %collective-permute-start.1 = (bf16[16,16,1024]{2,1,0:T(8,128)(2,1)S(1)}, bf16[16,16,1024]{2,1,0:T(8,128)(2,1)S(1)}, u32[]{:S(2)}, u32[]{:S(2)}) collective-permute-start(bf16[16,16,1024]{2,1,0:T(8,128)(2,1)S(1)} %all_to_all.25.mine), channel_id=1, source_target_pairs={{0,16},{16,0},{1,17},{17,1},{2,18},{18,2},{3,19},{19,3},{4,20},{20... | collective-permute-start | bytes 1572872 | tf_op jit(solution)/shard_map/ppermute | solution.py:54
  44.8 9.4 %collective-permute-start.2 = (bf16[8,16,1024]{2,1,0:T(8,128)(2,1)S(1)}, bf16[8,16,1024]{2,1,0:T(8,128)(2,1)S(1)}, u32[]{:S(2)}, u32[]{:S(2)}) collective-permute-start(bf16[8,16,1024]{2,1,0:T(8,128)(2,1)S(1)} %get-tuple-element.22), channel_id=1, source_target_pairs={{0,1},{1,0},{2,3},{3,2},{4,5},{5,4},{6,7},{7,6},{8,9},{9,8},{10,11... | collective-permute-start | bytes 786440 | tf_op jit(solution)/shard_map/ppermute | solution.py:287
  54.3 26.1 %copy-start = (bf16[2,256,256]{2,1,0:T(8,128)(2,1)S(1)}, bf16[2,256,256]{2,1,0:T(8,128)(2,1)}, u32[]{:S(2)}) copy-start(bf16[2,256,256]{2,1,0:T(8,128)(2,1)} %link.3) | copy-start | bytes 786436
  54.3 26.1 %copy-start.3 = (bf16[16,1024]{1,0:T(8,128)(2,1)S(1)}, bf16[16,1024]{1,0:T(8,128)(2,1)}, u32[]{:S(2)}) copy-start(bf16[16,1024]{1,0:T(8,128)(2,1)} %mask.1.lower) | copy-start | bytes 98308
  54.3 26.1 %copy-start.4 = (s32[4]{0:T(128)S(1)}, s32[4]{0:T(128)}, u32[]{:S(2)}) copy-start(s32[4]{0:T(128)} %widths.7) | copy-start | bytes 52
  54.4 26.1 %copy-start.5 = (s32[2,28]{1,0:T(2,128)S(1)}, s32[2,28]{1,0:T(2,128)}, u32[]{:S(2)}) copy-start(s32[2,28]{1,0:T(2,128)} %anc_one.3) | copy-start | bytes 676
  54.4 26.1 %copy-start.6 = (s32[2,24]{1,0:T(2,128)S(1)}, s32[2,24]{1,0:T(2,128)}, u32[]{:S(2)}) copy-start(s32[2,24]{1,0:T(2,128)} %anc_two.3) | copy-start | bytes 580
  54.4 26.1 %copy-start.7 = (s32[2]{0:T(128)S(1)}, s32[2]{0:T(128)}, u32[]{:S(2)}) copy-start(s32[2]{0:T(128)} %pad_add_fusion.place) | copy-start | bytes 28
  82.0 10.5 %collective-permute-start.3 = (f32[3,256,256]{2,1,0:T(8,128)S(1)}, f32[3,256,256]{2,1,0:T(8,128)S(1)}, u32[]{:S(2)}, u32[]{:S(2)}) collective-permute-start(f32[3,256,256]{2,1,0:T(8,128)S(1)} %get-tuple-element.25), channel_id=1, source_target_pairs={{0,16},{16,0},{1,17},{17,1},{2,18},{18,2},{3,19},{19,3},{4,20},{20... | collective-permute-start | bytes 2359304 | tf_op jit(solution)/shard_map/ppermute | solution.py:54
  111.5 15.9 %copy-start.2 = (f32[96,128]{1,0:T(8,128)S(1)}, f32[96,128]{1,0:T(8,128)}, u32[]{:S(2)}) copy-start(f32[96,128]{1,0:T(8,128)} %pivot.1) | copy-start | bytes 147460
  138.4 7.9 %collective-permute-start.4 = (bf16[2,768,128]{2,1,0:T(8,128)(2,1)S(1)}, bf16[2,768,128]{2,1,0:T(8,128)(2,1)S(1)}, u32[]{:S(2)}, u32[]{:S(2)}) collective-permute-start(bf16[2,768,128]{2,1,0:T(8,128)(2,1)S(1)} %bitcast.8), channel_id=1, source_target_pairs={{0,16},{16,0},{1,17},{17,1},{2,18},{18,2},{3,19},{19,3},{4,20},{20... | collective-permute-start | bytes 1179656 | tf_op jit(solution)/shard_map/ppermute | solution.py:54

commit v11 on v10

--- a/solution.py
+++ b/solution.py
@@ -69,11 +69,17 @@
     return total
 
 
-def is_member(table, s, tile):
-    found = table[s, 0] == tile
-    for i in range(1, table.shape[1]):
-        found = found | (table[s, i] == tile)
-    return found
+def column_limits(ancestors, widths, tile):
+    here = [jnp.any(table == tile, axis=1) for table in ancestors]
+    return jnp.where(jnp.concatenate(here), widths, 0)
+
+
+def inside_limits(limits, first, shape, w):
+    column = lax.broadcasted_iota(jnp.int32, shape, 1)
+    limit = jnp.zeros(shape, jnp.int32)
+    for k in range(shape[1] // w):
+        limit = jnp.where(column >= k * w, limits[first + k] + k * w, limit)
+    return column < limit
 
 
 def masked_link(w, link, widths, s):
@@ -84,38 +90,23 @@
     return jnp.where(inside, value, jnp.zeros_like(value))
 
 
-def mask_body(w, tile, one, two, anc_one, anc_two, widths, lower, held_one, held_two, sems):
-    copies = [
-        pltpu.make_async_copy(one, held_one, sems.at[0]),
-        pltpu.make_async_copy(two, held_two, sems.at[1]),
-    ]
-    for copy in copies:
-        copy.start()
-    column = lax.broadcasted_iota(jnp.int32, (one.shape[0], w), 1)
-    limits = [
-        jnp.where(is_member(anc_one if k < 2 else anc_two, k % 2, tile[0]), widths[k], 0)
-        for k in range(4)
-    ]
-    for copy in copies:
-        copy.wait()
-    for k in range(4):
-        value = (held_one if k < 2 else held_two)[:, (k % 2) * w : (k % 2 + 1) * w]
-        value = jnp.where(column < limits[k], value, jnp.zeros_like(value))
-        lower[:, k * w : (k + 1) * w] = value
-
-
 def copy_body(source, copies):
     value = source[...]
     for i in range(copies.shape[0]):
         copies[i] = value
 
 
-def product_body(w, core, parity, order, inverse, mine, other, keep, give, held, part):
+def product_body(
+    w, core, parity, order, limits, inverse, mine, other, keep, give, held, part
+):
     blocks, share, _ = mine.shape
     half = blocks * share
-    for i in range(blocks):
-        held[i * share : (i + 1) * share, :] = mine[order[i]]
-        held[half + i * share : half + (i + 1) * share, :] = other[order[i]]
+    for source, first, start in ((mine, 0, 0), (other, 4, half)):
+        inside = inside_limits(limits, first, (share, 4 * w), w)
+        for i in range(blocks):
+            value = source[order[i]]
+            value = jnp.where(inside, value, jnp.zeros_like(value))
+            held[start + i * share : start + (i + 1) * share, :] = value
     left = inverse[:, pl.ds(pl.multiple_of(core[0] * half, half), half)]
     right = inverse[:, pl.ds(pl.multiple_of((1 - core[0]) * half, half), half)]
     for k in range(4):
@@ -134,17 +125,20 @@
 
 
 def column_body(
-    w, tile, place, received, lower, link, anc_one, anc_two, widths, column_one, column_two, mine, other
+    w, place, limits, received, one, two, link, widths, column_one, column_two, mine, other, lower
 ):
     total = reduced(received)
+    inside = inside_limits(limits, 0, lower.shape, w)
+    value = jnp.concatenate([one[...], two[...]], axis=1)
+    lower[...] = jnp.where(inside, value, jnp.zeros_like(value))
     for s in range(2):
         span = slice(s * w, (s + 1) * w)
-        here_one = jnp.where(is_member(anc_one, s, tile[0]), 1.0, 0.0)
-        here_two = jnp.where(is_member(anc_two, s, tile[0]), 1.0, 0.0)
-        one = (-(total[:, span] * here_one)).astype(BF16)
-        column_one[:, span] = one
-        two = total[:, (2 + s) * w : (3 + s) * w] + dot(one, masked_link(w, link, widths, s))
-        column_two[:, span] = (-(two * here_two)).astype(BF16)
+        here_one = jnp.where(limits[s] > 0, 1.0, 0.0)
+        here_two = jnp.where(limits[2 + s] > 0, 1.0, 0.0)
+        column = (-(total[:, span] * here_one)).astype(BF16)
+        column_one[:, span] = column
+        second = total[:, (2 + s) * w : (3 + s) * w] + dot(column, masked_link(w, link, widths, s))
+        column_two[:, span] = (-(second * here_two)).astype(BF16)
     for out, sibling in ((mine, place[0]), (other, 1 - place[0])):
         first = pl.ds(pl.multiple_of(sibling * w, w), w)
         second = pl.ds(pl.multiple_of((2 + sibling) * w, w), w)
@@ -187,7 +181,7 @@
 
 
 def all_sum_body(received, pivot, copies):
-    near, chunk = NEAR, received.shape[1]
+    near, chunk = PAIR, received.shape[1]
     for n in range(near):
         total = pivot[n * chunk : (n + 1) * chunk, :]
         for i in range(n, received.shape[0], near):
@@ -232,19 +226,10 @@
     share = panel_one.shape[0]
     chip = lax.axis_index("chip").astype(jnp.int32)
     core = lax.axis_index("core").astype(jnp.int32)
-    tile = (chip * CORES + core).reshape(1)
     core_ref = core.reshape(1)
     whole = (share, 4 * w)
 
-    lower = pl.pallas_call(
-        functools.partial(mask_body, w),
-        name="mask",
-        in_specs=[SMEM, ANY, ANY, SMEM, SMEM, SMEM],
-        out_specs=VMEM,
-        out_shape=jax.ShapeDtypeStruct(whole, BF16),
-        scratch_shapes=[pltpu.VMEM(panel_one.shape, BF16)] * 2 + [pltpu.SemaphoreType.DMA((2,))],
-    )(tile, panel_one, panel_two, ancestors_one, ancestors_two, widths)
-
+    lower = jnp.concatenate([panel_one, panel_two], axis=1)
     places = landing_places(chips, planes)
     pairs = []
     for q in range(chips):
@@ -257,16 +242,26 @@
     order = lax.dynamic_index_in_dim(jnp.array(places, jnp.int32), plane, 0, keepdims=False)
     place = jnp.stack([core, chip])
     flat = (w // LANES, 3 * w, LANES)
-    chunk = 3 * w * w // LANES // (chips * NEAR)
+    chunk = 3 * w * w // LANES // (chips * PAIR)
     pivot = pl.pallas_call(
         functools.partial(pivot_body, w),
         name="pivot",
         in_specs=[SMEM, VMEM, VMEM, SMEM],
         out_specs=VMEM,
-        out_shape=jax.ShapeDtypeStruct((NEAR * chunk, LANES), F32),
+        out_shape=jax.ShapeDtypeStruct((PAIR * chunk, LANES), F32),
         scratch_shapes=[pltpu.VMEM((3 * w * w // LANES, LANES), F32)],
     )(place, diag_inverse_one, diag_inverse_two, widths)
-    moved, order, place, pivot = lax.optimization_barrier((moved, order, place, pivot))
+    ancestors = (ancestors_one, ancestors_two)
+    limits = column_limits(ancestors, widths, chip * CORES + core)
+    away_limits = jnp.concatenate(
+        [
+            column_limits(ancestors, widths, plane * CORES + core),
+            column_limits(ancestors, widths, plane * CORES + 1 - core),
+        ]
+    )
+    moved, order, place, pivot, limits, away_limits = lax.optimization_barrier(
+        (moved, order, place, pivot, limits, away_limits)
+    )
     (moved,) = kernel_call(copy_body, "copies", [VMEM], [((chips,) + whole, BF16)])(moved)
     mine = exchange(moved, "chip")
     other = swap_cores(mine)
@@ -275,7 +270,7 @@
     keep, give = pl.pallas_call(
         functools.partial(product_body, w),
         name="product",
-        in_specs=[SMEM] * 3 + [VMEM] * 3,
+        in_specs=[SMEM] * 4 + [VMEM] * 3,
         out_specs=[VMEM] * 2,
         out_shape=[jax.ShapeDtypeStruct(half, BF16)] * 2,
         scratch_shapes=[
@@ -283,27 +278,31 @@
             pltpu.VMEM((planes,) + whole, BF16),
         ],
         compiler_params=pltpu.CompilerParams(vmem_limit_bytes=40 * 1024 * 1024),
-    )(core_ref, parity.reshape(1), order, ancestor_inverse, mine, other)
+    )(core_ref, parity.reshape(1), order, away_limits, ancestor_inverse, mine, other)
     got = lax.ppermute(give, "pair", [(0, 1), (1, 0)])
     (part,) = kernel_call(pair_sum_body, "pair_sum", [VMEM] * 2, [(half, BF16)])(keep, got)
     part = exchange(part, ("far", "mid"))
-    column_one, column_two, mine, other = kernel_call(
+    column_one, column_two, mine, other = pl.pallas_call(
         functools.partial(column_body, w),
-        "columns",
-        [SMEM, SMEM, VMEM, VMEM, VMEM, SMEM, SMEM, SMEM],
-        [((share, 2 * w), BF16)] * 2 + [((3, w, w), F32)] * 2,
-    )(tile, place, part, lower, link_two, ancestors_one, ancestors_two, widths)
+        name="columns",
+        in_specs=[SMEM] * 2 + [VMEM] * 4 + [SMEM],
+        out_specs=[VMEM] * 4,
+        out_shape=[jax.ShapeDtypeStruct((share, 2 * w), BF16)] * 2
+        + [jax.ShapeDtypeStruct((3, w, w), F32)] * 2,
+        scratch_shapes=[pltpu.VMEM(whole, BF16)],
+        compiler_params=pltpu.CompilerParams(vmem_limit_bytes=40 * 1024 * 1024),
+    )(place, limits, part, panel_one, panel_two, link_two, widths)
     other = swap_cores(other)
     (sums,) = kernel_call(
         functools.partial(core_sum_body, w), "core_sum", [VMEM] * 2, [(flat, BF16)]
     )(mine, other)
-    sums = exchange(sums.reshape(chips * NEAR, chunk, LANES), ("chip", "mid", "pair"))
+    sums = exchange(sums.reshape(chips * PAIR, chunk, LANES), ("chip", "pair"))
     (sums,) = kernel_call(chunk_sum_body, "chunk_sum", [VMEM], [((planes, chunk, LANES), BF16)])(
         sums
     )
     sums = exchange(sums, ("far", "mid", "pair"))
     (total,) = kernel_call(
-        all_sum_body, "all_sum", [VMEM] * 2, [((chips, NEAR * chunk, LANES), BF16)]
+        all_sum_body, "all_sum", [VMEM] * 2, [((chips, PAIR * chunk, LANES), BF16)]
     )(sums, pivot)
     mine = exchange(total, "chip").reshape(flat)
     other = swap_cores(mine)

time: 149 us -> 143 us (0.960)
  blocking collectives: 93.9 us -> 87.6 us
  waiting for transfers between devices: 13.9 us -> 11.4 us
  Pallas kernels: 8.35 us -> 6.24 us
  starting transfers between devices: 29.8 us -> 31.7 us
  local copies, waits for them, and re-layouts: 0.75 us -> 2.6 us
    all_to_all x5, blocking collectives: 93.9 us -> 87.6 us  [exchange(): return lax.all_to_all(blocks, axis, split_axis=0, concat_axis=0, tiled=True)]
    ppermute x1, waiting for transfers between devices: 2.75 us -> 0.2 us  [local(): moved = lax.ppermute(lower, GRID, pairs)]
    pallas_call x3 -> x2, Pallas kernels: 3.57 us -> 1.45 us  [the longest x1 1.41 us: local(): pl.pallas_call(functools.partial(column_body, w), name='columns', in_spec...]
    ppermute x3, starting transfers between devices: 19.2 us -> 21.1 us  [swap_cores(): return lax.ppermute(block, 'core', [(0, 1), (1, 0)])]
    unnamed x16 -> x20, local copies, waits for them, and re-layouts: 0.05 us -> 1.91 us
where the time goes in v11:
time: 143 us; the launch traced here: 142 us
  blocking collectives  87.6 us (61%)
  starting transfers between devices  31.7 us (22%)
  waiting for transfers between devices  11.4 us (8%)
  Pallas kernels  6.24 us (4%)
  local copies, waits for them, and re-layouts  2.6 us (2%)
  other arithmetic  1.78 us (1%)
    all_to_all x5, blocking collectives, exchange(): return lax.all_to_all(blocks, axis, split_axis=0, concat_axis=0, tiled=True)  87.6 us
    ppermute x3, starting transfers between devices, swap_cores(): return lax.ppermute(block, 'core', [(0, 1), (1, 0)])  21.1 us
    ppermute x1, starting transfers between devices, local(): moved = lax.ppermute(lower, GRID, pairs)  7.65 us
    ppermute x1, waiting for transfers between devices, local(): got = lax.ppermute(give, 'pair', [(0, 1), (1, 0)])  6.43 us
    ppermute x3, waiting for transfers between devices, swap_cores(): return lax.ppermute(block, 'core', [(0, 1), (1, 0)])  4.73 us
    ppermute x1, starting transfers between devices, local(): got = lax.ppermute(give, 'pair', [(0, 1), (1, 0)])  2.98 us
  transfers between devices with their start and end apart: 5, of which 5 were waited for; matrix products, arithmetic and copies ran while one was open for 1% of the time, Pallas kernels for 1%

profile of v11, /device:TPU:1, one launch (start us, length us, event | category | flops | bytes accessed | tf_op | source)
XLA Modules:
  0.0 142.1 jit_solution(242105427532473060)
XLA Ops:
  0.6 0.7 pad_maximum_fusion
  1.4 7.7 %collective-permute-start = (bf16[16,1024]{1,0:T(8,128)(2,1)S(1)}, bf16[16,1024]{1,0:T(8,128)(2,1)S(1)}, u32[]{:S(2)}, u32[]{:S(2)}) collective-permute-start(bf16[16,1024]{1,0:T(8,128)(2,1)S(1)} %pad_maximum_fusion), channel_id=1, source_target_pairs={{0,480},{1,448},{2,352},{3,416},{4,320},{5,224},{6,384},{7,288},{8... | collective-permute-start | bytes 98312 | tf_op jit(solution)/shard_map/ppermute | solution.py:239
  9.1 0.0 copy-start.8
  9.1 0.7 copy-done.8
  9.7 0.0 copy-start.9
  9.7 0.1 compare_reduce_fusion.3
  9.9 0.5 copy-done.9
  10.4 0.1 compare_reduce_fusion.2
  10.6 0.6 pad_add_fusion.place
  11.2 0.7 dynamic-slice_bitcast_fusion.order
  11.9 0.7 copy-done.5
  12.5 0.1 add_select_fusion.1
  12.6 0.1 pad_add_fusion.1.limits
  12.7 1.7 %pivot.1 = f32[96,128]{1,0:T(8,128)} custom-call(s32[2]{0:T(128)} %pad_add_fusion.place, bf16[2,256,256]{2,1,0:T(8,128)(2,1)} %one.2, bf16[2,256,256]{2,1,0:T(8,128)(2,1)} %two.2, s32[4]{0:T(128)} %widths.5), custom_call_target="tpu_custom_call" | custom-call | tf_op jit(solution)/shard_map/pivot/pallas_call | solution.py:246
  14.4 0.2 collective-permute-done.source
  14.7 0.0 copy-start.1
  14.7 24.6 %all_to_all.25.mine = bf16[16,16,1024]{2,1,0:T(8,128)(2,1)S(1)} all-to-all(bf16[16,16,1024]{2,1,0:T(8,128)(2,1)S(1)} %copies.1), channel_id=1, replica_groups=mesh['chip'=16,'core'=2,'far'=4,'mid'=2,'pair'=2] {'chip'}, dimensions={0} | all-to-all | bytes 1048576 | tf_op jit(solution)/shard_map/all_to_all | solution.py:35
  39.3 4.0 %collective-permute-start.1 = (bf16[16,16,1024]{2,1,0:T(8,128)(2,1)S(1)}, bf16[16,16,1024]{2,1,0:T(8,128)(2,1)S(1)}, u32[]{:S(2)}, u32[]{:S(2)}) collective-permute-start(bf16[16,16,1024]{2,1,0:T(8,128)(2,1)S(1)} %all_to_all.25.mine), channel_id=1, source_target_pairs={{0,16},{16,0},{1,17},{17,1},{2,18},{18,2},{3,19},{19,3},{4,20},{20... | collective-permute-start | bytes 1572872 | tf_op jit(solution)/shard_map/ppermute | solution.py:54
  43.3 1.5 %collective-permute-done.1.other = bf16[16,16,1024]{2,1,0:T(8,128)(2,1)S(1)} collective-permute-done((bf16[16,16,1024]{2,1,0:T(8,128)(2,1)S(1)}, bf16[16,16,1024]{2,1,0:T(8,128)(2,1)S(1)}, u32[]{:S(2)}, u32[]{:S(2)}) %collective-permute-start.1) | collective-permute-done | bytes 524320 | tf_op jit(solution)/shard_map/ppermute | solution.py:54
  44.8 0.0 copy-done.1
  44.8 1.0 product.1
  45.8 3.0 %collective-permute-start.2 = (bf16[8,16,1024]{2,1,0:T(8,128)(2,1)S(1)}, bf16[8,16,1024]{2,1,0:T(8,128)(2,1)S(1)}, u32[]{:S(2)}, u32[]{:S(2)}) collective-permute-start(bf16[8,16,1024]{2,1,0:T(8,128)(2,1)S(1)} %get-tuple-element.26), channel_id=1, source_target_pairs={{0,1},{1,0},{2,3},{3,2},{4,5},{5,4},{6,7},{7,6},{8,9},{9,8},{10,11... | collective-permute-start | bytes 786440 | tf_op jit(solution)/shard_map/ppermute | solution.py:282
  48.8 6.4 %collective-permute-done.2.got = bf16[8,16,1024]{2,1,0:T(8,128)(2,1)S(1)} collective-permute-done((bf16[8,16,1024]{2,1,0:T(8,128)(2,1)S(1)}, bf16[8,16,1024]{2,1,0:T(8,128)(2,1)S(1)}, u32[]{:S(2)}, u32[]{:S(2)}) %collective-permute-start.2) | collective-permute-done | bytes 262176 | tf_op jit(solution)/shard_map/ppermute | solution.py:282
  55.2 0.1 pair_sum.1
  55.3 0.0 copy-start
  55.3 0.0 copy-start.3
  55.3 0.0 copy-start.4
  55.3 0.0 copy-start.6
  55.4 0.0 copy-start.7
  55.4 23.6 %all_to_all.26.received = bf16[8,16,1024]{2,1,0:T(8,128)(2,1)S(1)} all-to-all(bf16[8,16,1024]{2,1,0:T(8,128)(2,1)S(1)} %pair_sum.1), channel_id=1, replica_groups=mesh['chip'=16,'core'=2,'far'=4,'mid'=2,'pair'=2] {'far','mid'}, dimensions={0} | all-to-all | bytes 524288 | tf_op jit(solution)/shard_map/all_to_all | solution.py:35
  79.0 0.0 copy-done
  79.0 0.0 copy-done.3
  79.0 0.0 copy-done.4
  79.0 0.0 copy-done.6
  79.0 0.0 copy-done.7
  79.0 1.4 columns.1
  80.4 8.5 %collective-permute-start.3 = (f32[3,256,256]{2,1,0:T(8,128)S(1)}, f32[3,256,256]{2,1,0:T(8,128)S(1)}, u32[]{:S(2)}, u32[]{:S(2)}) collective-permute-start(f32[3,256,256]{2,1,0:T(8,128)S(1)} %get-tuple-element.29), channel_id=1, source_target_pairs={{0,16},{16,0},{1,17},{17,1},{2,18},{18,2},{3,19},{19,3},{4,20},{20... | collective-permute-start | bytes 2359304 | tf_op jit(solution)/shard_map/ppermute | solution.py:54
  88.9 1.9 %collective-permute-done.3.other = f32[3,256,256]{2,1,0:T(8,128)S(1)} collective-permute-done((f32[3,256,256]{2,1,0:T(8,128)S(1)}, f32[3,256,256]{2,1,0:T(8,128)S(1)}, u32[]{:S(2)}, u32[]{:S(2)}) %collective-permute-start.3) | collective-permute-done | bytes 786464 | tf_op jit(solution)/shard_map/ppermute | solution.py:54
  90.8 0.1 core_sum.1
  90.9 13.0 %all_to_all.27.received = bf16[32,48,128]{2,1,0:T(8,128)(2,1)S(1)} all-to-all(bf16[32,48,128]{2,1,0:T(8,128)(2,1)S(1)} %bitcast.9), channel_id=1, replica_groups=mesh['chip'=16,'core'=2,'far'=4,'mid'=2,'pair'=2] {'chip','pair'}, dimensions={0} | all-to-all | bytes 786432 | tf_op jit(solution)/shard_map/all_to_all | solution.py:35
  103.9 0.1 chunk_sum.1
  104.0 0.0 copy-start.2
  104.0 15.1 %all_to_all.28.received = bf16[16,48,128]{2,1,0:T(8,128)(2,1)S(1)} all-to-all(bf16[16,48,128]{2,1,0:T(8,128)(2,1)S(1)} %chunk_sum.1), channel_id=1, replica_groups=mesh['chip'=16,'core'=2,'far'=4,'mid'=2,'pair'=2] {'far','mid','pair'}, dimensions={0} | all-to-all | bytes 393216 | tf_op jit(solution)/shard_map/all_to_all | solution.py:35
  119.2 0.0 copy-done.2
  119.2 11.3 %all_to_all.29 = bf16[16,96,128]{2,1,0:T(8,128)(2,1)S(1)} all-to-all(bf16[16,96,128]{2,1,0:T(8,128)(2,1)S(1)} %all_sum.1), channel_id=1, replica_groups=mesh['chip'=16,'core'=2,'far'=4,'mid'=2,'pair'=2] {'chip'}, dimensions={0} | all-to-all | bytes 786432 | tf_op jit(solution)/shard_map/all_to_all | solution.py:35
  130.5 8.6 %collective-permute-start.4 = (bf16[2,768,128]{2,1,0:T(8,128)(2,1)S(1)}, bf16[2,768,128]{2,1,0:T(8,128)(2,1)S(1)}, u32[]{:S(2)}, u32[]{:S(2)}) collective-permute-start(bf16[2,768,128]{2,1,0:T(8,128)(2,1)S(1)} %bitcast.7), channel_id=1, source_target_pairs={{0,16},{16,0},{1,17},{17,1},{2,18},{18,2},{3,19},{19,3},{4,20},{20... | collective-permute-start | bytes 1179656 | tf_op jit(solution)/shard_map/ppermute | solution.py:54
  139.1 1.3 collective-permute-done.4.other
  140.4 1.7 %final.1 = (bf16[2,256,256]{2,1,0:T(8,128)(2,1)}, bf16[2,256,256]{2,1,0:T(8,128)(2,1)}, bf16[2,256,256]{2,1,0:T(8,128)(2,1)}) custom-call(s32[1]{0:T(128)} %bitcast.1.core, bf16[2,768,128]{2,1,0:T(8,128)(2,1)S(1)} %bitcast.8, bf16[2,768,128]{2,1,0:T(8,128)(2,1)S(1)} %collective-permute-done.4.other, bf16[2,256,256]{2,1,0:T(8,128)(2,1)S(1)} %copy-done, ...), custom_call_target="tpu_custom_call" | custom-call | tf_op jit(solution)/shard_map/final/pallas_call | solution.py:309
  (3 shorter events, 0.1 us)
Async XLA Ops:
  1.4 13.2 %collective-permute-start = (bf16[16,1024]{1,0:T(8,128)(2,1)S(1)}, bf16[16,1024]{1,0:T(8,128)(2,1)S(1)}, u32[]{:S(2)}, u32[]{:S(2)}) collective-permute-start(bf16[16,1024]{1,0:T(8,128)(2,1)S(1)} %pad_maximum_fusion), channel_id=1, source_target_pairs={{0,480},{1,448},{2,352},{3,416},{4,320},{5,224},{6,384},{7,288},{8... | collective-permute-start | bytes 98312 | tf_op jit(solution)/shard_map/ppermute | solution.py:239
  9.1 0.7 copy-start.8
  9.7 0.7 copy-start.9
  11.9 0.7 copy-start.5
  14.7 30.1 %copy-start.1 = (bf16[256,512]{1,0:T(8,128)(2,1)S(1)}, bf16[256,512]{1,0:T(8,128)(2,1)}, u32[]{:S(2)}) copy-start(bf16[256,512]{1,0:T(8,128)(2,1)} %inverse.1) | copy-start | bytes 786436
  39.3 5.5 %collective-permute-start.1 = (bf16[16,16,1024]{2,1,0:T(8,128)(2,1)S(1)}, bf16[16,16,1024]{2,1,0:T(8,128)(2,1)S(1)}, u32[]{:S(2)}, u32[]{:S(2)}) collective-permute-start(bf16[16,16,1024]{2,1,0:T(8,128)(2,1)S(1)} %all_to_all.25.mine), channel_id=1, source_target_pairs={{0,16},{16,0},{1,17},{17,1},{2,18},{18,2},{3,19},{19,3},{4,20},{20... | collective-permute-start | bytes 1572872 | tf_op jit(solution)/shard_map/ppermute | solution.py:54
  45.8 9.4 %collective-permute-start.2 = (bf16[8,16,1024]{2,1,0:T(8,128)(2,1)S(1)}, bf16[8,16,1024]{2,1,0:T(8,128)(2,1)S(1)}, u32[]{:S(2)}, u32[]{:S(2)}) collective-permute-start(bf16[8,16,1024]{2,1,0:T(8,128)(2,1)S(1)} %get-tuple-element.26), channel_id=1, source_target_pairs={{0,1},{1,0},{2,3},{3,2},{4,5},{5,4},{6,7},{7,6},{8,9},{9,8},{10,11... | collective-permute-start | bytes 786440 | tf_op jit(solution)/shard_map/ppermute | solution.py:282
  55.3 23.7 %copy-start = (bf16[2,256,256]{2,1,0:T(8,128)(2,1)S(1)}, bf16[2,256,256]{2,1,0:T(8,128)(2,1)}, u32[]{:S(2)}) copy-start(bf16[2,256,256]{2,1,0:T(8,128)(2,1)} %link.3) | copy-start | bytes 786436
  55.3 23.7 %copy-start.3 = (bf16[16,512]{1,0:T(8,128)(2,1)S(1)}, bf16[16,512]{1,0:T(8,128)(2,1)}, u32[]{:S(2)}) copy-start(bf16[16,512]{1,0:T(8,128)(2,1)} %two.3) | copy-start | bytes 49156
  55.3 23.6 %copy-start.4 = (bf16[16,512]{1,0:T(8,128)(2,1)S(1)}, bf16[16,512]{1,0:T(8,128)(2,1)}, u32[]{:S(2)}) copy-start(bf16[16,512]{1,0:T(8,128)(2,1)} %one.3) | copy-start | bytes 49156
  55.3 23.6 %copy-start.6 = (s32[4]{0:T(128)S(1)}, s32[4]{0:T(128)}, u32[]{:S(2)}) copy-start(s32[4]{0:T(128)} %widths.5) | copy-start | bytes 52
  55.4 23.6 %copy-start.7 = (s32[2]{0:T(128)S(1)}, s32[2]{0:T(128)}, u32[]{:S(2)}) copy-start(s32[2]{0:T(128)} %pad_add_fusion.place) | copy-start | bytes 28
  80.4 10.4 %collective-permute-start.3 = (f32[3,256,256]{2,1,0:T(8,128)S(1)}, f32[3,256,256]{2,1,0:T(8,128)S(1)}, u32[]{:S(2)}, u32[]{:S(2)}) collective-permute-start(f32[3,256,256]{2,1,0:T(8,128)S(1)} %get-tuple-element.29), channel_id=1, source_target_pairs={{0,16},{16,0},{1,17},{17,1},{2,18},{18,2},{3,19},{19,3},{4,20},{20... | collective-permute-start | bytes 2359304 | tf_op jit(solution)/shard_map/ppermute | solution.py:54
  104.0 15.1 %copy-start.2 = (f32[96,128]{1,0:T(8,128)S(1)}, f32[96,128]{1,0:T(8,128)}, u32[]{:S(2)}) copy-start(f32[96,128]{1,0:T(8,128)} %pivot.1) | copy-start | bytes 147460
  130.5 9.9 %collective-permute-start.4 = (bf16[2,768,128]{2,1,0:T(8,128)(2,1)S(1)}, bf16[2,768,128]{2,1,0:T(8,128)(2,1)S(1)}, u32[]{:S(2)}, u32[]{:S(2)}) collective-permute-start(bf16[2,768,128]{2,1,0:T(8,128)(2,1)S(1)} %bitcast.7), channel_id=1, source_target_pairs={{0,16},{16,0},{1,17},{17,1},{2,18},{18,2},{3,19},{19,3},{4,20},{20... | collective-permute-start | bytes 1179656 | tf_op jit(solution)/shard_map/ppermute | solution.py:54

commit v12 on v11

--- a/solution.py
+++ b/solution.py
@@ -181,14 +181,9 @@
 
 
 def all_sum_body(received, pivot, copies):
-    near, chunk = PAIR, received.shape[1]
-    for n in range(near):
-        total = pivot[n * chunk : (n + 1) * chunk, :]
-        for i in range(n, received.shape[0], near):
-            total = total + received[i].astype(F32)
-        total = total.astype(BF16)
-        for i in range(copies.shape[0]):
-            copies[i, n * chunk : (n + 1) * chunk, :] = total
+    total = (reduced(received) + pivot[...]).astype(BF16)
+    for i in range(copies.shape[0]):
+        copies[i] = total
 
 
 def side_by_side(total, b, w):
@@ -240,7 +235,7 @@
     parity = lax.axis_index("pair").astype(jnp.int32)
     plane = lax.axis_index("far") * NEAR + lax.axis_index("mid") * PAIR + parity
     order = lax.dynamic_index_in_dim(jnp.array(places, jnp.int32), plane, 0, keepdims=False)
-    place = jnp.stack([core, chip])
+    place = jnp.stack([core, chip * PAIR + parity])
     flat = (w // LANES, 3 * w, LANES)
     chunk = 3 * w * w // LANES // (chips * PAIR)
     pivot = pl.pallas_call(
@@ -248,7 +243,7 @@
         name="pivot",
         in_specs=[SMEM, VMEM, VMEM, SMEM],
         out_specs=VMEM,
-        out_shape=jax.ShapeDtypeStruct((PAIR * chunk, LANES), F32),
+        out_shape=jax.ShapeDtypeStruct((chunk, LANES), F32),
         scratch_shapes=[pltpu.VMEM((3 * w * w // LANES, LANES), F32)],
     )(place, diag_inverse_one, diag_inverse_two, widths)
     ancestors = (ancestors_one, ancestors_two)
@@ -297,14 +292,14 @@
         functools.partial(core_sum_body, w), "core_sum", [VMEM] * 2, [(flat, BF16)]
     )(mine, other)
     sums = exchange(sums.reshape(chips * PAIR, chunk, LANES), ("chip", "pair"))
-    (sums,) = kernel_call(chunk_sum_body, "chunk_sum", [VMEM], [((planes, chunk, LANES), BF16)])(
+    (sums,) = kernel_call(chunk_sum_body, "chunk_sum", [VMEM], [((planes // PAIR, chunk, LANES), BF16)])(
         sums
     )
-    sums = exchange(sums, ("far", "mid", "pair"))
+    sums = exchange(sums, ("far", "mid"))
     (total,) = kernel_call(
-        all_sum_body, "all_sum", [VMEM] * 2, [((chips, PAIR * chunk, LANES), BF16)]
+        all_sum_body, "all_sum", [VMEM] * 2, [((chips * PAIR, chunk, LANES), BF16)]
     )(sums, pivot)
-    mine = exchange(total, "chip").reshape(flat)
+    mine = exchange(total, ("chip", "pair")).reshape(flat)
     other = swap_cores(mine)
     block_one, parent_rows, block_two = kernel_call(
         functools.partial(final_body, w),

time: 143 us -> 142 us (level)
  starting transfers between devices: 31.7 us -> 29.8 us
    ppermute x3, starting transfers between devices: 21.1 us -> 19.2 us  [swap_cores(): return lax.ppermute(block, 'core', [(0, 1), (1, 0)])]
where the time goes in v12:
time: 142 us
  blocking collectives  89 us (63%)
  starting transfers between devices  29.8 us (21%)
  waiting for transfers between devices  11.4 us (8%)
  Pallas kernels  6.23 us (4%)
  local copies, waits for them, and re-layouts  2.6 us (2%)
  other arithmetic  1.78 us (1%)
    all_to_all x5, blocking collectives, exchange(): return lax.all_to_all(blocks, axis, split_axis=0, concat_axis=0, tiled=True)  89 us
    ppermute x3, starting transfers between devices, swap_cores(): return lax.ppermute(block, 'core', [(0, 1), (1, 0)])  19.2 us
    ppermute x1, starting transfers between devices, local(): moved = lax.ppermute(lower, GRID, pairs)  7.65 us
    ppermute x1, waiting for transfers between devices, local(): got = lax.ppermute(give, 'pair', [(0, 1), (1, 0)])  6.43 us
    ppermute x3, waiting for transfers between devices, swap_cores(): return lax.ppermute(block, 'core', [(0, 1), (1, 0)])  4.73 us
    ppermute x1, starting transfers between devices, local(): got = lax.ppermute(give, 'pair', [(0, 1), (1, 0)])  2.97 us
  transfers between devices with their start and end apart: 5, of which 5 were waited for; matrix products, arithmetic and copies ran while one was open for 1% of the time, Pallas kernels for 1%

profile of v12, /device:TPU:1, one launch (start us, length us, event | category | flops | bytes accessed | tf_op | source)
XLA Modules:
  0.0 141.6 jit_solution(18097040487563392419)
XLA Ops:
  0.6 0.7 pad_maximum_fusion
  1.4 7.7 %collective-permute-start = (bf16[16,1024]{1,0:T(8,128)(2,1)S(1)}, bf16[16,1024]{1,0:T(8,128)(2,1)S(1)}, u32[]{:S(2)}, u32[]{:S(2)}) collective-permute-start(bf16[16,1024]{1,0:T(8,128)(2,1)S(1)} %pad_maximum_fusion), channel_id=1, source_target_pairs={{0,480},{1,448},{2,352},{3,416},{4,320},{5,224},{6,384},{7,288},{8... | collective-permute-start | bytes 98312 | tf_op jit(solution)/shard_map/ppermute | solution.py:234
  9.1 0.0 copy-start.8
  9.1 0.7 copy-done.8
  9.7 0.0 copy-start.9
  9.7 0.1 compare_reduce_fusion.3
  9.9 0.5 copy-done.9
  10.4 0.1 compare_reduce_fusion.2
  10.6 0.6 pad_add_fusion.place
  11.2 0.7 dynamic-slice_bitcast_fusion.order
  11.9 0.7 copy-done.5
  12.5 0.1 add_select_fusion.1
  12.6 0.1 pad_add_fusion.1.limits
  12.7 1.7 %pivot.1 = f32[48,128]{1,0:T(8,128)} custom-call(s32[2]{0:T(128)} %pad_add_fusion.place, bf16[2,256,256]{2,1,0:T(8,128)(2,1)} %one.2, bf16[2,256,256]{2,1,0:T(8,128)(2,1)} %two.2, s32[4]{0:T(128)} %widths.5), custom_call_target="tpu_custom_call" | custom-call | tf_op jit(solution)/shard_map/pivot/pallas_call | solution.py:241
  14.4 0.2 collective-permute-done.source
  14.7 0.0 copy-start.1
  14.7 24.6 %all_to_all.25.mine = bf16[16,16,1024]{2,1,0:T(8,128)(2,1)S(1)} all-to-all(bf16[16,16,1024]{2,1,0:T(8,128)(2,1)S(1)} %copies.1), channel_id=1, replica_groups=mesh['chip'=16,'core'=2,'far'=4,'mid'=2,'pair'=2] {'chip'}, dimensions={0} | all-to-all | bytes 1048576 | tf_op jit(solution)/shard_map/all_to_all | solution.py:35
  39.2 4.0 %collective-permute-start.1 = (bf16[16,16,1024]{2,1,0:T(8,128)(2,1)S(1)}, bf16[16,16,1024]{2,1,0:T(8,128)(2,1)S(1)}, u32[]{:S(2)}, u32[]{:S(2)}) collective-permute-start(bf16[16,16,1024]{2,1,0:T(8,128)(2,1)S(1)} %all_to_all.25.mine), channel_id=1, source_target_pairs={{0,16},{16,0},{1,17},{17,1},{2,18},{18,2},{3,19},{19,3},{4,20},{20... | collective-permute-start | bytes 1572872 | tf_op jit(solution)/shard_map/ppermute | solution.py:54
  43.3 1.5 %collective-permute-done.1.other = bf16[16,16,1024]{2,1,0:T(8,128)(2,1)S(1)} collective-permute-done((bf16[16,16,1024]{2,1,0:T(8,128)(2,1)S(1)}, bf16[16,16,1024]{2,1,0:T(8,128)(2,1)S(1)}, u32[]{:S(2)}, u32[]{:S(2)}) %collective-permute-start.1) | collective-permute-done | bytes 524320 | tf_op jit(solution)/shard_map/ppermute | solution.py:54
  44.8 0.0 copy-done.1
  44.8 1.0 product.1
  45.8 3.0 %collective-permute-start.2 = (bf16[8,16,1024]{2,1,0:T(8,128)(2,1)S(1)}, bf16[8,16,1024]{2,1,0:T(8,128)(2,1)S(1)}, u32[]{:S(2)}, u32[]{:S(2)}) collective-permute-start(bf16[8,16,1024]{2,1,0:T(8,128)(2,1)S(1)} %get-tuple-element.26), channel_id=1, source_target_pairs={{0,1},{1,0},{2,3},{3,2},{4,5},{5,4},{6,7},{7,6},{8,9},{9,8},{10,11... | collective-permute-start | bytes 786440 | tf_op jit(solution)/shard_map/ppermute | solution.py:277
  48.8 6.4 %collective-permute-done.2.got = bf16[8,16,1024]{2,1,0:T(8,128)(2,1)S(1)} collective-permute-done((bf16[8,16,1024]{2,1,0:T(8,128)(2,1)S(1)}, bf16[8,16,1024]{2,1,0:T(8,128)(2,1)S(1)}, u32[]{:S(2)}, u32[]{:S(2)}) %collective-permute-start.2) | collective-permute-done | bytes 262176 | tf_op jit(solution)/shard_map/ppermute | solution.py:277
  55.2 0.1 pair_sum.1
  55.3 0.0 copy-start
  55.3 0.0 copy-start.3
  55.3 0.0 copy-start.4
  55.3 0.0 copy-start.6
  55.3 0.0 copy-start.7
  55.4 23.6 %all_to_all.26.received = bf16[8,16,1024]{2,1,0:T(8,128)(2,1)S(1)} all-to-all(bf16[8,16,1024]{2,1,0:T(8,128)(2,1)S(1)} %pair_sum.1), channel_id=1, replica_groups=mesh['chip'=16,'core'=2,'far'=4,'mid'=2,'pair'=2] {'far','mid'}, dimensions={0} | all-to-all | bytes 524288 | tf_op jit(solution)/shard_map/all_to_all | solution.py:35
  79.0 0.0 copy-done
  79.0 0.0 copy-done.3
  79.0 0.0 copy-done.4
  79.0 0.0 copy-done.6
  79.0 0.0 copy-done.7
  79.0 1.4 columns.1
  80.4 8.5 %collective-permute-start.3 = (f32[3,256,256]{2,1,0:T(8,128)S(1)}, f32[3,256,256]{2,1,0:T(8,128)S(1)}, u32[]{:S(2)}, u32[]{:S(2)}) collective-permute-start(f32[3,256,256]{2,1,0:T(8,128)S(1)} %get-tuple-element.29), channel_id=1, source_target_pairs={{0,16},{16,0},{1,17},{17,1},{2,18},{18,2},{3,19},{19,3},{4,20},{20... | collective-permute-start | bytes 2359304 | tf_op jit(solution)/shard_map/ppermute | solution.py:54
  88.9 1.9 %collective-permute-done.3.other = f32[3,256,256]{2,1,0:T(8,128)S(1)} collective-permute-done((f32[3,256,256]{2,1,0:T(8,128)S(1)}, f32[3,256,256]{2,1,0:T(8,128)S(1)}, u32[]{:S(2)}, u32[]{:S(2)}) %collective-permute-start.3) | collective-permute-done | bytes 786464 | tf_op jit(solution)/shard_map/ppermute | solution.py:54
  90.8 0.1 core_sum.1
  90.9 13.0 %all_to_all.27.received = bf16[32,48,128]{2,1,0:T(8,128)(2,1)S(1)} all-to-all(bf16[32,48,128]{2,1,0:T(8,128)(2,1)S(1)} %bitcast.9), channel_id=1, replica_groups=mesh['chip'=16,'core'=2,'far'=4,'mid'=2,'pair'=2] {'chip','pair'}, dimensions={0} | all-to-all | bytes 786432 | tf_op jit(solution)/shard_map/all_to_all | solution.py:35
  103.9 0.1 chunk_sum.1
  104.0 0.0 copy-start.2
  104.0 15.2 %all_to_all.28.received = bf16[8,48,128]{2,1,0:T(8,128)(2,1)S(1)} all-to-all(bf16[8,48,128]{2,1,0:T(8,128)(2,1)S(1)} %chunk_sum.1), channel_id=1, replica_groups=mesh['chip'=16,'core'=2,'far'=4,'mid'=2,'pair'=2] {'far','mid'}, dimensions={0} | all-to-all | bytes 196608 | tf_op jit(solution)/shard_map/all_to_all | solution.py:35
  119.2 0.0 copy-done.2
  119.2 12.6 %all_to_all.29 = bf16[32,48,128]{2,1,0:T(8,128)(2,1)S(1)} all-to-all(bf16[32,48,128]{2,1,0:T(8,128)(2,1)S(1)} %all_sum.1), channel_id=1, replica_groups=mesh['chip'=16,'core'=2,'far'=4,'mid'=2,'pair'=2] {'chip','pair'}, dimensions={0} | all-to-all | bytes 786432 | tf_op jit(solution)/shard_map/all_to_all | solution.py:35
  131.8 6.7 %collective-permute-start.4 = (bf16[2,768,128]{2,1,0:T(8,128)(2,1)S(1)}, bf16[2,768,128]{2,1,0:T(8,128)(2,1)S(1)}, u32[]{:S(2)}, u32[]{:S(2)}) collective-permute-start(bf16[2,768,128]{2,1,0:T(8,128)(2,1)S(1)} %bitcast.7), channel_id=1, source_target_pairs={{0,16},{16,0},{1,17},{17,1},{2,18},{18,2},{3,19},{19,3},{4,20},{20... | collective-permute-start | bytes 1179656 | tf_op jit(solution)/shard_map/ppermute | solution.py:54
  138.5 1.3 collective-permute-done.4.other
  139.8 1.7 %final.1 = (bf16[2,256,256]{2,1,0:T(8,128)(2,1)}, bf16[2,256,256]{2,1,0:T(8,128)(2,1)}, bf16[2,256,256]{2,1,0:T(8,128)(2,1)}) custom-call(s32[1]{0:T(128)} %bitcast.1.core, bf16[2,768,128]{2,1,0:T(8,128)(2,1)S(1)} %bitcast.8, bf16[2,768,128]{2,1,0:T(8,128)(2,1)S(1)} %collective-permute-done.4.other, bf16[2,256,256]{2,1,0:T(8,128)(2,1)S(1)} %copy-done, ...), custom_call_target="tpu_custom_call" | custom-call | tf_op jit(solution)/shard_map/final/pallas_call | solution.py:304
  (3 shorter events, 0.1 us)
Async XLA Ops:
  1.4 13.2 %collective-permute-start = (bf16[16,1024]{1,0:T(8,128)(2,1)S(1)}, bf16[16,1024]{1,0:T(8,128)(2,1)S(1)}, u32[]{:S(2)}, u32[]{:S(2)}) collective-permute-start(bf16[16,1024]{1,0:T(8,128)(2,1)S(1)} %pad_maximum_fusion), channel_id=1, source_target_pairs={{0,480},{1,448},{2,352},{3,416},{4,320},{5,224},{6,384},{7,288},{8... | collective-permute-start | bytes 98312 | tf_op jit(solution)/shard_map/ppermute | solution.py:234
  9.1 0.7 copy-start.8
  9.7 0.7 copy-start.9
  11.9 0.7 copy-start.5
  14.7 30.1 %copy-start.1 = (bf16[256,512]{1,0:T(8,128)(2,1)S(1)}, bf16[256,512]{1,0:T(8,128)(2,1)}, u32[]{:S(2)}) copy-start(bf16[256,512]{1,0:T(8,128)(2,1)} %inverse.1) | copy-start | bytes 786436
  39.2 5.5 %collective-permute-start.1 = (bf16[16,16,1024]{2,1,0:T(8,128)(2,1)S(1)}, bf16[16,16,1024]{2,1,0:T(8,128)(2,1)S(1)}, u32[]{:S(2)}, u32[]{:S(2)}) collective-permute-start(bf16[16,16,1024]{2,1,0:T(8,128)(2,1)S(1)} %all_to_all.25.mine), channel_id=1, source_target_pairs={{0,16},{16,0},{1,17},{17,1},{2,18},{18,2},{3,19},{19,3},{4,20},{20... | collective-permute-start | bytes 1572872 | tf_op jit(solution)/shard_map/ppermute | solution.py:54
  45.8 9.4 %collective-permute-start.2 = (bf16[8,16,1024]{2,1,0:T(8,128)(2,1)S(1)}, bf16[8,16,1024]{2,1,0:T(8,128)(2,1)S(1)}, u32[]{:S(2)}, u32[]{:S(2)}) collective-permute-start(bf16[8,16,1024]{2,1,0:T(8,128)(2,1)S(1)} %get-tuple-element.26), channel_id=1, source_target_pairs={{0,1},{1,0},{2,3},{3,2},{4,5},{5,4},{6,7},{7,6},{8,9},{9,8},{10,11... | collective-permute-start | bytes 786440 | tf_op jit(solution)/shard_map/ppermute | solution.py:277
  55.3 23.7 %copy-start = (bf16[2,256,256]{2,1,0:T(8,128)(2,1)S(1)}, bf16[2,256,256]{2,1,0:T(8,128)(2,1)}, u32[]{:S(2)}) copy-start(bf16[2,256,256]{2,1,0:T(8,128)(2,1)} %link.3) | copy-start | bytes 786436
  55.3 23.7 %copy-start.3 = (bf16[16,512]{1,0:T(8,128)(2,1)S(1)}, bf16[16,512]{1,0:T(8,128)(2,1)}, u32[]{:S(2)}) copy-start(bf16[16,512]{1,0:T(8,128)(2,1)} %two.3) | copy-start | bytes 49156
  55.3 23.7 %copy-start.4 = (bf16[16,512]{1,0:T(8,128)(2,1)S(1)}, bf16[16,512]{1,0:T(8,128)(2,1)}, u32[]{:S(2)}) copy-start(bf16[16,512]{1,0:T(8,128)(2,1)} %one.3) | copy-start | bytes 49156
  55.3 23.7 %copy-start.6 = (s32[4]{0:T(128)S(1)}, s32[4]{0:T(128)}, u32[]{:S(2)}) copy-start(s32[4]{0:T(128)} %widths.5) | copy-start | bytes 52
  55.3 23.6 %copy-start.7 = (s32[2]{0:T(128)S(1)}, s32[2]{0:T(128)}, u32[]{:S(2)}) copy-start(s32[2]{0:T(128)} %pad_add_fusion.place) | copy-start | bytes 28
  80.4 10.4 %collective-permute-start.3 = (f32[3,256,256]{2,1,0:T(8,128)S(1)}, f32[3,256,256]{2,1,0:T(8,128)S(1)}, u32[]{:S(2)}, u32[]{:S(2)}) collective-permute-start(f32[3,256,256]{2,1,0:T(8,128)S(1)} %get-tuple-element.29), channel_id=1, source_target_pairs={{0,16},{16,0},{1,17},{17,1},{2,18},{18,2},{3,19},{19,3},{4,20},{20... | collective-permute-start | bytes 2359304 | tf_op jit(solution)/shard_map/ppermute | solution.py:54
  104.0 15.2 %copy-start.2 = (f32[48,128]{1,0:T(8,128)S(1)}, f32[48,128]{1,0:T(8,128)}, u32[]{:S(2)}) copy-start(f32[48,128]{1,0:T(8,128)} %pivot.1) | copy-start | bytes 73732
  131.8 8.0 %collective-permute-start.4 = (bf16[2,768,128]{2,1,0:T(8,128)(2,1)S(1)}, bf16[2,768,128]{2,1,0:T(8,128)(2,1)S(1)}, u32[]{:S(2)}, u32[]{:S(2)}) collective-permute-start(bf16[2,768,128]{2,1,0:T(8,128)(2,1)S(1)} %bitcast.7), channel_id=1, source_target_pairs={{0,16},{16,0},{1,17},{17,1},{2,18},{18,2},{3,19},{19,3},{4,20},{20... | collective-permute-start | bytes 1179656 | tf_op jit(solution)/shard_map/ppermute | solution.py:54

commit v13 on v12

--- a/solution.py
+++ b/solution.py
@@ -96,22 +96,32 @@
         copies[i] = value
 
 
+def masked_tile(source, order, limits, first, held):
+    blocks, share, wide = source.shape
+    inside = inside_limits(limits, first, (share, wide), wide // 4)
+    for i in range(blocks):
+        value = source[order[i]]
+        held[i * share : (i + 1) * share, :] = jnp.where(inside, value, jnp.zeros_like(value))
+
+
+def own_product_body(w, core, order, limits, inverse, mine, part, held):
+    masked_tile(mine, order, limits, 0, held)
+    half = held.shape[0]
+    left = inverse[:, pl.ds(pl.multiple_of(core[0] * half, half), half)]
+    for k in range(4):
+        span = slice(k * w, (k + 1) * w)
+        part[:, span] = dot(left, held[:, span])
+
+
 def product_body(
-    w, core, parity, order, limits, inverse, mine, other, keep, give, held, part
+    w, core, parity, order, limits, inverse, other, own, keep, give, held, part
 ):
-    blocks, share, _ = mine.shape
-    half = blocks * share
-    for source, first, start in ((mine, 0, 0), (other, 4, half)):
-        inside = inside_limits(limits, first, (share, 4 * w), w)
-        for i in range(blocks):
-            value = source[order[i]]
-            value = jnp.where(inside, value, jnp.zeros_like(value))
-            held[start + i * share : start + (i + 1) * share, :] = value
-    left = inverse[:, pl.ds(pl.multiple_of(core[0] * half, half), half)]
+    masked_tile(other, order, limits, 4, held)
+    half, share = held.shape[0], part.shape[1]
     right = inverse[:, pl.ds(pl.multiple_of((1 - core[0]) * half, half), half)]
     for k in range(4):
         span = slice(k * w, (k + 1) * w)
-        value = (dot(left, held[:half, span]) + dot(right, held[half:, span])).astype(BF16)
+        value = (own[:, span] + dot(right, held[:, span])).astype(BF16)
         for i in range(part.shape[0]):
             part[i, :, span] = value[i * share : (i + 1) * share]
     for i in range(keep.shape[0]):
@@ -125,7 +135,7 @@
 
 
 def column_body(
-    w, place, limits, received, one, two, link, widths, column_one, column_two, mine, other, lower
+    w, place, limits, received, one, two, link, widths, column_one, column_two, other, lower
 ):
     total = reduced(received)
     inside = inside_limits(limits, 0, lower.shape, w)
@@ -139,12 +149,19 @@
         column_one[:, span] = column
         second = total[:, (2 + s) * w : (3 + s) * w] + dot(column, masked_link(w, link, widths, s))
         column_two[:, span] = (-(second * here_two)).astype(BF16)
-    for out, sibling in ((mine, place[0]), (other, 1 - place[0])):
-        first = pl.ds(pl.multiple_of(sibling * w, w), w)
-        second = pl.ds(pl.multiple_of((2 + sibling) * w, w), w)
-        out[0] = -dot_t(lower[:, first], column_one[:, first])
-        out[1] = dot_t(column_one[:, first], lower[:, second])
-        out[2] = -dot_t(lower[:, second], column_two[:, first])
+    sibling_sums(w, 1 - place[0], lower, column_one, column_two, other)
+
+
+def sibling_sums(w, sibling, lower, column_one, column_two, out):
+    first = pl.ds(pl.multiple_of(sibling * w, w), w)
+    second = pl.ds(pl.multiple_of((2 + sibling) * w, w), w)
+    out[0] = -dot_t(lower[:, first], column_one[:, first])
+    out[1] = dot_t(column_one[:, first], lower[:, second])
+    out[2] = -dot_t(lower[:, second], column_two[:, first])
+
+
+def own_sums_body(w, place, lower, column_one, column_two, mine):
+    sibling_sums(w, place[0], lower, column_one, column_two, mine)
 
 
 def core_sum_body(w, mine, other, sums):
@@ -191,16 +208,25 @@
     return jnp.concatenate([total[h, span, :] for h in range(total.shape[0])], axis=1)
 
 
-def final_body(w, core, mine, other, link, widths, block_one, parent_rows, block_two):
-    for total, sibling in ((mine, core[0]), (other, 1 - core[0])):
-        tie = masked_link(w, link, widths, sibling)
-        block = side_by_side(total, 0, w)
-        cross = side_by_side(total, 1, w).astype(F32)
-        block_one[sibling] = block
-        parent = (-(dot(block, tie) + cross)).astype(BF16)
-        parent_rows[sibling] = parent
-        rest = side_by_side(total, 2, w).astype(F32) - dot_t(tie, parent)
-        block_two[sibling] = rest.astype(BF16)
+def sibling_blocks(w, total, link, widths, sibling):
+    tie = masked_link(w, link, widths, sibling)
+    block = side_by_side(total, 0, w)
+    cross = side_by_side(total, 1, w).astype(F32)
+    parent = (-(dot(block, tie) + cross)).astype(BF16)
+    rest = side_by_side(total, 2, w).astype(F32) - dot_t(tie, parent)
+    return block, parent, rest.astype(BF16)
+
+
+def own_final_body(w, core, mine, link, widths, *outs):
+    for out, value in zip(outs, sibling_blocks(w, mine, link, widths, core[0])):
+        out[...] = value
+
+
+def final_body(w, core, other, own_one, own_parent, own_two, link, widths, *outs):
+    values = sibling_blocks(w, other, link, widths, 1 - core[0])
+    for out, own, value in zip(outs, (own_one, own_parent, own_two), values):
+        out[core[0]] = own[...]
+        out[1 - core[0]] = value
 
 
 def local(
@@ -262,31 +288,47 @@
     other = swap_cores(mine)
 
     half = (planes // PAIR,) + whole
+    grant = pltpu.CompilerParams(vmem_limit_bytes=40 * 1024 * 1024)
+    tile_rows = (chips * share, 4 * w)
+    own = pl.pallas_call(
+        functools.partial(own_product_body, w),
+        name="own_product",
+        in_specs=[SMEM] * 3 + [VMEM] * 2,
+        out_specs=VMEM,
+        out_shape=jax.ShapeDtypeStruct((local_rows, 4 * w), F32),
+        scratch_shapes=[pltpu.VMEM(tile_rows, BF16)],
+        compiler_params=grant,
+    )(core_ref, order, away_limits, ancestor_inverse, mine)
+    other, own = lax.optimization_barrier((other, own))
     keep, give = pl.pallas_call(
         functools.partial(product_body, w),
         name="product",
         in_specs=[SMEM] * 4 + [VMEM] * 3,
         out_specs=[VMEM] * 2,
         out_shape=[jax.ShapeDtypeStruct(half, BF16)] * 2,
-        scratch_shapes=[
-            pltpu.VMEM((CORES * chips * share, 4 * w), BF16),
-            pltpu.VMEM((planes,) + whole, BF16),
-        ],
-        compiler_params=pltpu.CompilerParams(vmem_limit_bytes=40 * 1024 * 1024),
-    )(core_ref, parity.reshape(1), order, away_limits, ancestor_inverse, mine, other)
+        scratch_shapes=[pltpu.VMEM(tile_rows, BF16), pltpu.VMEM((planes,) + whole, BF16)],
+        compiler_params=grant,
+    )(core_ref, parity.reshape(1), order, away_limits, ancestor_inverse, other, own)
     got = lax.ppermute(give, "pair", [(0, 1), (1, 0)])
     (part,) = kernel_call(pair_sum_body, "pair_sum", [VMEM] * 2, [(half, BF16)])(keep, got)
     part = exchange(part, ("far", "mid"))
-    column_one, column_two, mine, other = pl.pallas_call(
+    column_one, column_two, other, lower = pl.pallas_call(
         functools.partial(column_body, w),
         name="columns",
         in_specs=[SMEM] * 2 + [VMEM] * 4 + [SMEM],
         out_specs=[VMEM] * 4,
         out_shape=[jax.ShapeDtypeStruct((share, 2 * w), BF16)] * 2
-        + [jax.ShapeDtypeStruct((3, w, w), F32)] * 2,
-        scratch_shapes=[pltpu.VMEM(whole, BF16)],
-        compiler_params=pltpu.CompilerParams(vmem_limit_bytes=40 * 1024 * 1024),
+        + [jax.ShapeDtypeStruct((3, w, w), F32), jax.ShapeDtypeStruct(whole, BF16)],
+        compiler_params=grant,
     )(place, limits, part, panel_one, panel_two, link_two, widths)
+    mine = pl.pallas_call(
+        functools.partial(own_sums_body, w),
+        name="own_sums",
+        in_specs=[SMEM] + [VMEM] * 3,
+        out_specs=VMEM,
+        out_shape=jax.ShapeDtypeStruct((3, w, w), F32),
+        compiler_params=grant,
+    )(place, lower, column_one, column_two)
     other = swap_cores(other)
     (sums,) = kernel_call(
         functools.partial(core_sum_body, w), "core_sum", [VMEM] * 2, [(flat, BF16)]
@@ -301,12 +343,16 @@
     )(sums, pivot)
     mine = exchange(total, ("chip", "pair")).reshape(flat)
     other = swap_cores(mine)
+    own_blocks = kernel_call(
+        functools.partial(own_final_body, w), "own_final", [SMEM, VMEM, VMEM, SMEM], [((w, w), BF16)] * 3
+    )(core_ref, mine, link_two, widths)
+    other, *own_blocks = lax.optimization_barrier((other, *own_blocks))
     block_one, parent_rows, block_two = kernel_call(
         functools.partial(final_body, w),
         "final",
-        [SMEM, VMEM, VMEM, VMEM, SMEM],
+        [SMEM] + [VMEM] * 5 + [SMEM],
         [((2, w, w), BF16)] * 3,
-    )(core_ref, mine, other, link_two, widths)
+    )(core_ref, other, *own_blocks, link_two, widths)
     return column_one, block_one, column_two, parent_rows, block_two
 
 

time: 142 us -> 143 us (level)
  waiting for transfers between devices: 11.4 us -> 7.66 us
  Pallas kernels: 6.23 us -> 8.65 us
  local copies, waits for them, and re-layouts: 2.6 us -> 4.03 us
    ppermute x3, waiting for transfers between devices: 4.73 us -> 1 us  [swap_cores(): return lax.ppermute(block, 'core', [(0, 1), (1, 0)])]
    pallas_call x1 -> x4, Pallas kernels: 1.75 us -> 4.34 us  [the longest x1 1.68 us: local(): kernel_call(functools.partial(final_body, w), 'final', [SMEM] + [VMEM] *...]
    unnamed x20 -> x24, local copies, waits for them, and re-layouts: 1.91 us -> 3.33 us
  transfers between devices with their start and end apart: 5 -> 5, of which waited for: 5 -> 4; matrix products, arithmetic and copies ran while one was open for 1% -> 1% of each run, Pallas kernels for 1% -> 3%
where the time goes in v13:
time: 143 us; the launch traced here: 142 us
  blocking collectives  89.3 us (62%)
  starting transfers between devices  29.8 us (21%)
  Pallas kernels  8.65 us (6%)
  waiting for transfers between devices  7.66 us (5%)
  local copies, waits for them, and re-layouts  4.03 us (3%)
  other arithmetic  1.77 us (1%)
    all_to_all x5, blocking collectives, exchange(): return lax.all_to_all(blocks, axis, split_axis=0, concat_axis=0, tiled=True)  89.3 us
    ppermute x3, starting transfers between devices, swap_cores(): return lax.ppermute(block, 'core', [(0, 1), (1, 0)])  19.2 us
    ppermute x1, starting transfers between devices, local(): moved = lax.ppermute(lower, GRID, pairs)  7.65 us
    ppermute x1, waiting for transfers between devices, local(): got = lax.ppermute(give, 'pair', [(0, 1), (1, 0)])  6.44 us
    unnamed x24, local copies, waits for them, and re-layouts  3.33 us
    ppermute x1, starting transfers between devices, local(): got = lax.ppermute(give, 'pair', [(0, 1), (1, 0)])  2.98 us
  transfers between devices with their start and end apart: 5, of which 4 were waited for; matrix products, arithmetic and copies ran while one was open for 1% of the time, Pallas kernels for 3%

profile of v13, /device:TPU:1, one launch (start us, length us, event | category | flops | bytes accessed | tf_op | source)
XLA Modules:
  0.0 142.1 jit_solution(10979219108729002069)
XLA Ops:
  0.6 0.7 pad_maximum_fusion
  1.4 7.7 %collective-permute-start = (bf16[16,1024]{1,0:T(8,128)(2,1)S(1)}, bf16[16,1024]{1,0:T(8,128)(2,1)S(1)}, u32[]{:S(2)}, u32[]{:S(2)}) collective-permute-start(bf16[16,1024]{1,0:T(8,128)(2,1)S(1)} %pad_maximum_fusion), channel_id=1, source_target_pairs={{0,480},{1,448},{2,352},{3,416},{4,320},{5,224},{6,384},{7,288},{8... | collective-permute-start | bytes 98312 | tf_op jit(solution)/shard_map/ppermute | solution.py:260
  9.1 0.0 copy-start.10
  9.1 0.7 copy-done.10
  9.7 0.1 compare_reduce_fusion.3
  9.9 0.5 copy-done.11
  10.4 0.1 compare_reduce_fusion.2
  10.6 0.0 copy-start.7
  10.6 0.7 copy-done.7
  11.2 0.1 add_select_fusion.1
  11.3 0.1 pad_add_fusion.1.limits
  11.4 0.7 dynamic-slice_bitcast_fusion.order
  12.1 0.6 pad_add_fusion.place
  12.7 1.7 %pivot.1 = f32[48,128]{1,0:T(8,128)} custom-call(s32[2]{0:T(128)} %pad_add_fusion.place, bf16[2,256,256]{2,1,0:T(8,128)(2,1)} %one.2, bf16[2,256,256]{2,1,0:T(8,128)(2,1)} %two.2, s32[4]{0:T(128)} %widths.7), custom_call_target="tpu_custom_call" | custom-call | tf_op jit(solution)/shard_map/pivot/pallas_call | solution.py:267
  14.4 0.2 collective-permute-done.source
  14.7 0.0 copy-start.1
  14.7 24.6 %all_to_all.25.mine = bf16[16,16,1024]{2,1,0:T(8,128)(2,1)S(1)} all-to-all(bf16[16,16,1024]{2,1,0:T(8,128)(2,1)S(1)} %copies.1), channel_id=1, replica_groups=mesh['chip'=16,'core'=2,'far'=4,'mid'=2,'pair'=2] {'chip'}, dimensions={0} | all-to-all | bytes 1048576 | tf_op jit(solution)/shard_map/all_to_all | solution.py:35
  39.2 4.0 %collective-permute-start.1 = (bf16[16,16,1024]{2,1,0:T(8,128)(2,1)S(1)}, bf16[16,16,1024]{2,1,0:T(8,128)(2,1)S(1)}, u32[]{:S(2)}, u32[]{:S(2)}) collective-permute-start(bf16[16,16,1024]{2,1,0:T(8,128)(2,1)S(1)} %all_to_all.25.mine), channel_id=1, source_target_pairs={{0,16},{16,0},{1,17},{17,1},{2,18},{18,2},{3,19},{19,3},{4,20},{20... | collective-permute-start | bytes 1572872 | tf_op jit(solution)/shard_map/ppermute | solution.py:54
  43.3 0.9 own_product.1.own
  44.1 0.6 collective-permute-done.1.other
  44.8 0.9 product.1
  45.7 3.0 %collective-permute-start.2 = (bf16[8,16,1024]{2,1,0:T(8,128)(2,1)S(1)}, bf16[8,16,1024]{2,1,0:T(8,128)(2,1)S(1)}, u32[]{:S(2)}, u32[]{:S(2)}) collective-permute-start(bf16[8,16,1024]{2,1,0:T(8,128)(2,1)S(1)} %get-tuple-element.37), channel_id=1, source_target_pairs={{0,1},{1,0},{2,3},{3,2},{4,5},{5,4},{6,7},{7,6},{8,9},{9,8},{10,11... | collective-permute-start | bytes 786440 | tf_op jit(solution)/shard_map/ppermute | solution.py:312
  48.6 6.4 %collective-permute-done.2.got = bf16[8,16,1024]{2,1,0:T(8,128)(2,1)S(1)} collective-permute-done((bf16[8,16,1024]{2,1,0:T(8,128)(2,1)S(1)}, bf16[8,16,1024]{2,1,0:T(8,128)(2,1)S(1)}, u32[]{:S(2)}, u32[]{:S(2)}) %collective-permute-start.2) | collective-permute-done | bytes 262176 | tf_op jit(solution)/shard_map/ppermute | solution.py:312
  55.1 0.1 pair_sum.1
  55.1 0.0 copy-start
  55.2 0.0 copy-start.3
  55.2 0.0 copy-start.4
  55.2 0.0 copy-start.8
  55.2 0.0 copy-start.9
  55.2 23.5 %all_to_all.26.received = bf16[8,16,1024]{2,1,0:T(8,128)(2,1)S(1)} all-to-all(bf16[8,16,1024]{2,1,0:T(8,128)(2,1)S(1)} %pair_sum.1), channel_id=1, replica_groups=mesh['chip'=16,'core'=2,'far'=4,'mid'=2,'pair'=2] {'far','mid'}, dimensions={0} | all-to-all | bytes 524288 | tf_op jit(solution)/shard_map/all_to_all | solution.py:35
  78.8 0.0 copy-done.3
  78.8 1.4 columns.1
  80.2 8.6 %collective-permute-start.3 = (f32[3,256,256]{2,1,0:T(8,128)S(1)}, f32[3,256,256]{2,1,0:T(8,128)S(1)}, u32[]{:S(2)}, u32[]{:S(2)}) collective-permute-start(f32[3,256,256]{2,1,0:T(8,128)S(1)} %get-tuple-element.41), channel_id=1, source_target_pairs={{0,16},{16,0},{1,17},{17,1},{2,18},{18,2},{3,19},{19,3},{4,20},{20... | collective-permute-start | bytes 2359304 | tf_op jit(solution)/shard_map/ppermute | solution.py:54
  88.7 0.0 copy-start.5
  88.8 0.7 copy-done.5
  89.5 0.7 copy-done.6
  90.2 0.8 own_sums.1.mine
  91.0 0.0 collective-permute-done.3.other
  91.0 0.1 core_sum.1
  91.1 13.4 %all_to_all.27.received = bf16[32,48,128]{2,1,0:T(8,128)(2,1)S(1)} all-to-all(bf16[32,48,128]{2,1,0:T(8,128)(2,1)S(1)} %bitcast.9), channel_id=1, replica_groups=mesh['chip'=16,'core'=2,'far'=4,'mid'=2,'pair'=2] {'chip','pair'}, dimensions={0} | all-to-all | bytes 786432 | tf_op jit(solution)/shard_map/all_to_all | solution.py:35
  104.6 0.1 chunk_sum.1
  104.6 0.0 copy-start.2
  104.7 15.0 %all_to_all.28.received = bf16[8,48,128]{2,1,0:T(8,128)(2,1)S(1)} all-to-all(bf16[8,48,128]{2,1,0:T(8,128)(2,1)S(1)} %chunk_sum.1), channel_id=1, replica_groups=mesh['chip'=16,'core'=2,'far'=4,'mid'=2,'pair'=2] {'far','mid'}, dimensions={0} | all-to-all | bytes 196608 | tf_op jit(solution)/shard_map/all_to_all | solution.py:35
  119.7 12.8 %all_to_all.29 = bf16[32,48,128]{2,1,0:T(8,128)(2,1)S(1)} all-to-all(bf16[32,48,128]{2,1,0:T(8,128)(2,1)S(1)} %all_sum.1), channel_id=1, replica_groups=mesh['chip'=16,'core'=2,'far'=4,'mid'=2,'pair'=2] {'chip','pair'}, dimensions={0} | all-to-all | bytes 786432 | tf_op jit(solution)/shard_map/all_to_all | solution.py:35
  132.5 6.6 %collective-permute-start.4 = (bf16[2,768,128]{2,1,0:T(8,128)(2,1)S(1)}, bf16[2,768,128]{2,1,0:T(8,128)(2,1)S(1)}, u32[]{:S(2)}, u32[]{:S(2)}) collective-permute-start(bf16[2,768,128]{2,1,0:T(8,128)(2,1)S(1)} %bitcast.7), channel_id=1, source_target_pairs={{0,16},{16,0},{1,17},{17,1},{2,18},{18,2},{3,19},{19,3},{4,20},{20... | collective-permute-start | bytes 1179656 | tf_op jit(solution)/shard_map/ppermute | solution.py:54
  139.1 1.0 own_final.1
  140.1 0.4 collective-permute-done.4.other
  140.4 1.7 %final.1 = (bf16[2,256,256]{2,1,0:T(8,128)(2,1)}, bf16[2,256,256]{2,1,0:T(8,128)(2,1)}, bf16[2,256,256]{2,1,0:T(8,128)(2,1)}) custom-call(s32[1]{0:T(128)} %bitcast.1.core, bf16[2,768,128]{2,1,0:T(8,128)(2,1)S(1)} %collective-permute-done.4.other, bf16[256,256]{1,0:T(8,128)(2,1)S(1)} %get-tuple-element.47.own_one, ...), custom_call_target="tpu_custom_call" | custom-call | tf_op jit(solution)/shard_map/final/pallas_call | solution.py:350
  (10 shorter events, 0.1 us)
Async XLA Ops:
  1.4 13.2 %collective-permute-start = (bf16[16,1024]{1,0:T(8,128)(2,1)S(1)}, bf16[16,1024]{1,0:T(8,128)(2,1)S(1)}, u32[]{:S(2)}, u32[]{:S(2)}) collective-permute-start(bf16[16,1024]{1,0:T(8,128)(2,1)S(1)} %pad_maximum_fusion), channel_id=1, source_target_pairs={{0,480},{1,448},{2,352},{3,416},{4,320},{5,224},{6,384},{7,288},{8... | collective-permute-start | bytes 98312 | tf_op jit(solution)/shard_map/ppermute | solution.py:260
  9.1 0.7 copy-start.10
  9.7 0.7 copy-start.11
  10.6 0.7 copy-start.7
  14.7 28.6 %copy-start.1 = (bf16[256,512]{1,0:T(8,128)(2,1)S(1)}, bf16[256,512]{1,0:T(8,128)(2,1)}, u32[]{:S(2)}) copy-start(bf16[256,512]{1,0:T(8,128)(2,1)} %inverse.3) | copy-start | bytes 786436
  39.2 5.5 %collective-permute-start.1 = (bf16[16,16,1024]{2,1,0:T(8,128)(2,1)S(1)}, bf16[16,16,1024]{2,1,0:T(8,128)(2,1)S(1)}, u32[]{:S(2)}, u32[]{:S(2)}) collective-permute-start(bf16[16,16,1024]{2,1,0:T(8,128)(2,1)S(1)} %all_to_all.25.mine), channel_id=1, source_target_pairs={{0,16},{16,0},{1,17},{17,1},{2,18},{18,2},{3,19},{19,3},{4,20},{20... | collective-permute-start | bytes 1572872 | tf_op jit(solution)/shard_map/ppermute | solution.py:54
  45.7 9.4 %collective-permute-start.2 = (bf16[8,16,1024]{2,1,0:T(8,128)(2,1)S(1)}, bf16[8,16,1024]{2,1,0:T(8,128)(2,1)S(1)}, u32[]{:S(2)}, u32[]{:S(2)}) collective-permute-start(bf16[8,16,1024]{2,1,0:T(8,128)(2,1)S(1)} %get-tuple-element.37), channel_id=1, source_target_pairs={{0,1},{1,0},{2,3},{3,2},{4,5},{5,4},{6,7},{7,6},{8,9},{9,8},{10,11... | collective-permute-start | bytes 786440 | tf_op jit(solution)/shard_map/ppermute | solution.py:312
  55.1 23.6 %copy-start = (bf16[2,256,256]{2,1,0:T(8,128)(2,1)S(1)}, bf16[2,256,256]{2,1,0:T(8,128)(2,1)}, u32[]{:S(2)}) copy-start(bf16[2,256,256]{2,1,0:T(8,128)(2,1)} %link.5) | copy-start | bytes 786436
  55.2 23.6 %copy-start.3 = (bf16[16,512]{1,0:T(8,128)(2,1)S(1)}, bf16[16,512]{1,0:T(8,128)(2,1)}, u32[]{:S(2)}) copy-start(bf16[16,512]{1,0:T(8,128)(2,1)} %two.3) | copy-start | bytes 49156
  55.2 23.6 %copy-start.4 = (bf16[16,512]{1,0:T(8,128)(2,1)S(1)}, bf16[16,512]{1,0:T(8,128)(2,1)}, u32[]{:S(2)}) copy-start(bf16[16,512]{1,0:T(8,128)(2,1)} %one.3) | copy-start | bytes 49156
  55.2 23.6 %copy-start.8 = (s32[4]{0:T(128)S(1)}, s32[4]{0:T(128)}, u32[]{:S(2)}) copy-start(s32[4]{0:T(128)} %widths.7) | copy-start | bytes 52
  55.2 23.6 %copy-start.9 = (s32[2]{0:T(128)S(1)}, s32[2]{0:T(128)}, u32[]{:S(2)}) copy-start(s32[2]{0:T(128)} %pad_add_fusion.place) | copy-start | bytes 28
  80.2 10.8 %collective-permute-start.3 = (f32[3,256,256]{2,1,0:T(8,128)S(1)}, f32[3,256,256]{2,1,0:T(8,128)S(1)}, u32[]{:S(2)}, u32[]{:S(2)}) collective-permute-start(f32[3,256,256]{2,1,0:T(8,128)S(1)} %get-tuple-element.41), channel_id=1, source_target_pairs={{0,16},{16,0},{1,17},{17,1},{2,18},{18,2},{3,19},{19,3},{4,20},{20... | collective-permute-start | bytes 2359304 | tf_op jit(solution)/shard_map/ppermute | solution.py:54
  88.7 0.7 copy-start.5
  89.5 0.7 copy-start.6
  104.6 15.0 %copy-start.2 = (f32[48,128]{1,0:T(8,128)S(1)}, f32[48,128]{1,0:T(8,128)}, u32[]{:S(2)}) copy-start(f32[48,128]{1,0:T(8,128)} %pivot.1) | copy-start | bytes 73732
  132.5 8.0 %collective-permute-start.4 = (bf16[2,768,128]{2,1,0:T(8,128)(2,1)S(1)}, bf16[2,768,128]{2,1,0:T(8,128)(2,1)S(1)}, u32[]{:S(2)}, u32[]{:S(2)}) collective-permute-start(bf16[2,768,128]{2,1,0:T(8,128)(2,1)S(1)} %bitcast.7), channel_id=1, source_target_pairs={{0,16},{16,0},{1,17},{17,1},{2,18},{18,2},{3,19},{19,3},{4,20},{20... | collective-permute-start | bytes 1179656 | tf_op jit(solution)/shard_map/ppermute | solution.py:54

commit v14 on v12

--- a/solution.py
+++ b/solution.py
@@ -124,13 +124,8 @@
         sums[i] = (keep[i].astype(F32) + got[i].astype(F32)).astype(BF16)
 
 
-def column_body(
-    w, place, limits, received, one, two, link, widths, column_one, column_two, mine, other, lower
-):
+def column_body(w, place, limits, received, link, widths, column_one, column_two, own, give):
     total = reduced(received)
-    inside = inside_limits(limits, 0, lower.shape, w)
-    value = jnp.concatenate([one[...], two[...]], axis=1)
-    lower[...] = jnp.where(inside, value, jnp.zeros_like(value))
     for s in range(2):
         span = slice(s * w, (s + 1) * w)
         here_one = jnp.where(limits[s] > 0, 1.0, 0.0)
@@ -139,18 +134,30 @@
         column_one[:, span] = column
         second = total[:, (2 + s) * w : (3 + s) * w] + dot(column, masked_link(w, link, widths, s))
         column_two[:, span] = (-(second * here_two)).astype(BF16)
-    for out, sibling in ((mine, place[0]), (other, 1 - place[0])):
-        first = pl.ds(pl.multiple_of(sibling * w, w), w)
-        second = pl.ds(pl.multiple_of((2 + sibling) * w, w), w)
-        out[0] = -dot_t(lower[:, first], column_one[:, first])
-        out[1] = dot_t(column_one[:, first], lower[:, second])
-        out[2] = -dot_t(lower[:, second], column_two[:, first])
-
-
-def core_sum_body(w, mine, other, sums):
-    lanes = sums.shape[2]
+    for out, sibling in ((own, place[0]), (give, 1 - place[0])):
+        span = pl.ds(pl.multiple_of(sibling * w, w), w)
+        out[:, :w] = column_one[:, span]
+        out[:, w:] = column_two[:, span]
+
+
+def sums_body(w, place, limits, own, got, lower, partner, sums, columns, panels):
+    share, lanes, sibling = own.shape[0], sums.shape[2], place[0]
+    column = lax.broadcasted_iota(jnp.int32, (share, w), 1)
+    for n, (new, panel) in enumerate(((own, lower), (got, partner))):
+        rows = slice(n * share, (n + 1) * share)
+        columns[rows, :] = new[...]
+        for b in range(2):
+            value = panel[:, pl.ds(pl.multiple_of((2 * b + sibling) * w, w), w)]
+            inside = column < limits[4 * n + 2 * b + sibling]
+            panels[rows, b * w : (b + 1) * w] = jnp.where(inside, value, jnp.zeros_like(value))
+    first, second = slice(0, w), slice(w, 2 * w)
+    totals = (
+        -dot_t(panels[:, first], columns[:, first]),
+        dot_t(columns[:, first], panels[:, second]),
+        -dot_t(panels[:, second], columns[:, second]),
+    )
     for b in range(3):
-        value = (mine[b] + other[b]).astype(BF16)
+        value = totals[b].astype(BF16)
         for h in range(w // lanes):
             sums[h, b * w : (b + 1) * w, :] = value[:, h * lanes : (h + 1) * lanes]
 
@@ -247,7 +254,12 @@
         scratch_shapes=[pltpu.VMEM((3 * w * w // LANES, LANES), F32)],
     )(place, diag_inverse_one, diag_inverse_two, widths)
     ancestors = (ancestors_one, ancestors_two)
-    limits = column_limits(ancestors, widths, chip * CORES + core)
+    limits = jnp.concatenate(
+        [
+            column_limits(ancestors, widths, chip * CORES + core),
+            column_limits(ancestors, widths, chip * CORES + 1 - core),
+        ]
+    )
     away_limits = jnp.concatenate(
         [
             column_limits(ancestors, widths, plane * CORES + core),
@@ -275,22 +287,24 @@
         compiler_params=pltpu.CompilerParams(vmem_limit_bytes=40 * 1024 * 1024),
     )(core_ref, parity.reshape(1), order, away_limits, ancestor_inverse, mine, other)
     got = lax.ppermute(give, "pair", [(0, 1), (1, 0)])
+    got, partner = lax.optimization_barrier((got, swap_cores(lower)))
     (part,) = kernel_call(pair_sum_body, "pair_sum", [VMEM] * 2, [(half, BF16)])(keep, got)
     part = exchange(part, ("far", "mid"))
-    column_one, column_two, mine, other = pl.pallas_call(
+    column_one, column_two, own, give = kernel_call(
         functools.partial(column_body, w),
-        name="columns",
-        in_specs=[SMEM] * 2 + [VMEM] * 4 + [SMEM],
-        out_specs=[VMEM] * 4,
-        out_shape=[jax.ShapeDtypeStruct((share, 2 * w), BF16)] * 2
-        + [jax.ShapeDtypeStruct((3, w, w), F32)] * 2,
-        scratch_shapes=[pltpu.VMEM(whole, BF16)],
+        "columns",
+        [SMEM] * 2 + [VMEM] * 2 + [SMEM],
+        [((share, 2 * w), BF16)] * 4,
+    )(place, limits, part, link_two, widths)
+    sums = pl.pallas_call(
+        functools.partial(sums_body, w),
+        name="sums",
+        in_specs=[SMEM] * 2 + [VMEM] * 4,
+        out_specs=VMEM,
+        out_shape=jax.ShapeDtypeStruct(flat, BF16),
+        scratch_shapes=[pltpu.VMEM((CORES * share, 2 * w), BF16)] * 2,
         compiler_params=pltpu.CompilerParams(vmem_limit_bytes=40 * 1024 * 1024),
-    )(place, limits, part, panel_one, panel_two, link_two, widths)
-    other = swap_cores(other)
-    (sums,) = kernel_call(
-        functools.partial(core_sum_body, w), "core_sum", [VMEM] * 2, [(flat, BF16)]
-    )(mine, other)
+    )(place, limits, own, swap_cores(give), lower, partner)
     sums = exchange(sums.reshape(chips * PAIR, chunk, LANES), ("chip", "pair"))
     (sums,) = kernel_call(chunk_sum_body, "chunk_sum", [VMEM], [((planes // PAIR, chunk, LANES), BF16)])(
         sums

time: 142 us -> 142 us (level)
  waiting for transfers between devices: 11.4 us -> 7.74 us
  starting transfers between devices: 29.8 us -> 32.4 us
    ppermute x1, waiting for transfers between devices: 6.43 us -> 3.02 us  [local(): got = lax.ppermute(give, 'pair', [(0, 1), (1, 0)])]
    ppermute x3 -> x4, starting transfers between devices: 19.2 us -> 21.8 us  [swap_cores(): return lax.ppermute(block, 'core', [(0, 1), (1, 0)])]
    ppermute x3 -> x4, waiting for transfers between devices: 4.73 us -> 4.5 us  [swap_cores(): return lax.ppermute(block, 'core', [(0, 1), (1, 0)])]
  transfers between devices with their start and end apart: 5 -> 6, of which waited for: 5 -> 6; matrix products, arithmetic and copies ran while one was open for 1% -> 1% of each run, Pallas kernels for 1% -> 1%
where the time goes in v14:
time: 142 us; the launch traced here: 141 us
  blocking collectives  89 us (63%)
  starting transfers between devices  32.4 us (23%)
  waiting for transfers between devices  7.74 us (5%)
  Pallas kernels  6.95 us (5%)
  local copies, waits for them, and re-layouts  3.32 us (2%)
    all_to_all x5, blocking collectives, exchange(): return lax.all_to_all(blocks, axis, split_axis=0, concat_axis=0, tiled=True)  89 us
    ppermute x4, starting transfers between devices, swap_cores(): return lax.ppermute(block, 'core', [(0, 1), (1, 0)])  21.8 us
    ppermute x1, starting transfers between devices, local(): moved = lax.ppermute(lower, GRID, pairs)  7.66 us
    ppermute x4, waiting for transfers between devices, swap_cores(): return lax.ppermute(block, 'core', [(0, 1), (1, 0)])  4.5 us
    ppermute x1, waiting for transfers between devices, local(): got = lax.ppermute(give, 'pair', [(0, 1), (1, 0)])  3.02 us
    ppermute x1, starting transfers between devices, local(): got = lax.ppermute(give, 'pair', [(0, 1), (1, 0)])  2.98 us
  transfers between devices with their start and end apart: 6, of which 6 were waited for; matrix products, arithmetic and copies ran while one was open for 1% of the time, Pallas kernels for 1%

profile of v14, /device:TPU:1, one launch (start us, length us, event | category | flops | bytes accessed | tf_op | source)
XLA Modules:
  0.0 141.3 jit_solution(2435552036479971494)
XLA Ops:
  0.6 0.0 copy-start.6
  0.6 0.7 constant_dynamic-update-slice_fusion.1
  1.4 0.0 copy-done.6
  1.4 7.7 %collective-permute-start = (bf16[16,1024]{1,0:T(8,128)(2,1)S(1)}, bf16[16,1024]{1,0:T(8,128)(2,1)S(1)}, u32[]{:S(2)}, u32[]{:S(2)}) collective-permute-start(bf16[16,1024]{1,0:T(8,128)(2,1)S(1)} %constant_dynamic-update-slice_fusion.lower), channel_id=1, source_target_pairs={{0,480},{1,448},{2,352},{3,416},{4,320},{5,224},{6,384},{7,288},{8... | collective-permute-start | bytes 98312 | tf_op jit(solution)/shard_map/ppermute | solution.py:241
  9.1 0.0 copy-start.7
  9.1 0.7 copy-done.7
  9.7 0.0 copy-start.8
  9.7 0.1 compare_reduce_fusion.3
  9.9 0.5 copy-done.8
  10.4 0.1 compare_reduce_fusion.2
  10.6 0.7 dynamic-slice_bitcast_fusion.order
  11.3 0.7 copy-done.3
  11.9 0.1 add_select_fusion.2
  12.0 0.1 pad_add_fusion.1
  12.1 0.6 pad_add_fusion.place
  12.7 1.7 %pivot.1 = f32[48,128]{1,0:T(8,128)} custom-call(s32[2]{0:T(128)} %pad_add_fusion.place, bf16[2,256,256]{2,1,0:T(8,128)(2,1)} %one.1, bf16[2,256,256]{2,1,0:T(8,128)(2,1)} %two.1, s32[4]{0:T(128)} %widths.5), custom_call_target="tpu_custom_call" | custom-call | tf_op jit(solution)/shard_map/pivot/pallas_call | solution.py:248
  14.4 0.2 collective-permute-done.source
  14.7 0.0 copy-start.1
  14.7 24.6 %all_to_all.25.mine = bf16[16,16,1024]{2,1,0:T(8,128)(2,1)S(1)} all-to-all(bf16[16,16,1024]{2,1,0:T(8,128)(2,1)S(1)} %copies.1), channel_id=1, replica_groups=mesh['chip'=16,'core'=2,'far'=4,'mid'=2,'pair'=2] {'chip'}, dimensions={0} | all-to-all | bytes 1048576 | tf_op jit(solution)/shard_map/all_to_all | solution.py:35
  39.2 4.0 %collective-permute-start.1 = (bf16[16,16,1024]{2,1,0:T(8,128)(2,1)S(1)}, bf16[16,16,1024]{2,1,0:T(8,128)(2,1)S(1)}, u32[]{:S(2)}, u32[]{:S(2)}) collective-permute-start(bf16[16,16,1024]{2,1,0:T(8,128)(2,1)S(1)} %all_to_all.25.mine), channel_id=1, source_target_pairs={{0,16},{16,0},{1,17},{17,1},{2,18},{18,2},{3,19},{19,3},{4,20},{20... | collective-permute-start | bytes 1572872 | tf_op jit(solution)/shard_map/ppermute | solution.py:54
  43.3 1.5 %collective-permute-done.1.other = bf16[16,16,1024]{2,1,0:T(8,128)(2,1)S(1)} collective-permute-done((bf16[16,16,1024]{2,1,0:T(8,128)(2,1)S(1)}, bf16[16,16,1024]{2,1,0:T(8,128)(2,1)S(1)}, u32[]{:S(2)}, u32[]{:S(2)}) %collective-permute-start.1) | collective-permute-done | bytes 524320 | tf_op jit(solution)/shard_map/ppermute | solution.py:54
  44.8 0.0 copy-done.1
  44.8 1.0 product.1
  45.8 3.0 %collective-permute-start.2 = (bf16[8,16,1024]{2,1,0:T(8,128)(2,1)S(1)}, bf16[8,16,1024]{2,1,0:T(8,128)(2,1)S(1)}, u32[]{:S(2)}, u32[]{:S(2)}) collective-permute-start(bf16[8,16,1024]{2,1,0:T(8,128)(2,1)S(1)} %get-tuple-element.28), channel_id=1, source_target_pairs={{0,1},{1,0},{2,3},{3,2},{4,5},{5,4},{6,7},{7,6},{8,9},{9,8},{10,11... | collective-permute-start | bytes 786440 | tf_op jit(solution)/shard_map/ppermute | solution.py:289
  48.8 2.6 %collective-permute-start.3 = (bf16[16,1024]{1,0:T(8,128)(2,1)S(1)}, bf16[16,1024]{1,0:T(8,128)(2,1)S(1)}, u32[]{:S(2)}, u32[]{:S(2)}) collective-permute-start(bf16[16,1024]{1,0:T(8,128)(2,1)S(1)} %constant_dynamic-update-slice_fusion.lower), channel_id=1, source_target_pairs={{0,16},{16,0},{1,17},{17,1},{2,18},{18,2},{3,19},{19,3},{4,20},{20... | collective-permute-start | bytes 98312 | tf_op jit(solution)/shard_map/ppermute | solution.py:54
  51.4 0.8 collective-permute-done.3.partner
  52.2 3.0 %collective-permute-done.2.got = bf16[8,16,1024]{2,1,0:T(8,128)(2,1)S(1)} collective-permute-done((bf16[8,16,1024]{2,1,0:T(8,128)(2,1)S(1)}, bf16[8,16,1024]{2,1,0:T(8,128)(2,1)S(1)}, u32[]{:S(2)}, u32[]{:S(2)}) %collective-permute-start.2) | collective-permute-done | bytes 262176 | tf_op jit(solution)/shard_map/ppermute | solution.py:289
  55.2 0.1 pair_sum.1
  55.3 0.0 copy-start
  55.3 0.0 copy-start.4
  55.3 0.0 copy-start.5
  55.3 23.6 %all_to_all.26.received = bf16[8,16,1024]{2,1,0:T(8,128)(2,1)S(1)} all-to-all(bf16[8,16,1024]{2,1,0:T(8,128)(2,1)S(1)} %pair_sum.1), channel_id=1, replica_groups=mesh['chip'=16,'core'=2,'far'=4,'mid'=2,'pair'=2] {'far','mid'}, dimensions={0} | all-to-all | bytes 524288 | tf_op jit(solution)/shard_map/all_to_all | solution.py:35
  79.0 0.0 copy-done
  79.0 0.0 copy-done.4
  79.0 0.0 copy-done.5
  79.0 1.4 columns.1
  80.4 8.5 %collective-permute-start.4 = (bf16[16,512]{1,0:T(8,128)(2,1)S(1)}, bf16[16,512]{1,0:T(8,128)(2,1)S(1)}, u32[]{:S(2)}, u32[]{:S(2)}) collective-permute-start(bf16[16,512]{1,0:T(8,128)(2,1)S(1)} %get-tuple-element.32), channel_id=1, source_target_pairs={{0,16},{16,0},{1,17},{17,1},{2,18},{18,2},{3,19},{19,3},{4,20},{20... | collective-permute-start | bytes 49160 | tf_op jit(solution)/shard_map/ppermute | solution.py:54
  88.9 0.8 collective-permute-done.4.got
  89.7 0.8 sums.1
  90.5 13.1 %all_to_all.27.received = bf16[32,48,128]{2,1,0:T(8,128)(2,1)S(1)} all-to-all(bf16[32,48,128]{2,1,0:T(8,128)(2,1)S(1)} %bitcast.9), channel_id=1, replica_groups=mesh['chip'=16,'core'=2,'far'=4,'mid'=2,'pair'=2] {'chip','pair'}, dimensions={0} | all-to-all | bytes 786432 | tf_op jit(solution)/shard_map/all_to_all | solution.py:35
  103.6 0.1 chunk_sum.1
  103.7 0.0 copy-start.2
  103.7 15.1 %all_to_all.28.received = bf16[8,48,128]{2,1,0:T(8,128)(2,1)S(1)} all-to-all(bf16[8,48,128]{2,1,0:T(8,128)(2,1)S(1)} %chunk_sum.1), channel_id=1, replica_groups=mesh['chip'=16,'core'=2,'far'=4,'mid'=2,'pair'=2] {'far','mid'}, dimensions={0} | all-to-all | bytes 196608 | tf_op jit(solution)/shard_map/all_to_all | solution.py:35
  118.8 0.0 copy-done.2
  118.9 12.6 %all_to_all.29 = bf16[32,48,128]{2,1,0:T(8,128)(2,1)S(1)} all-to-all(bf16[32,48,128]{2,1,0:T(8,128)(2,1)S(1)} %all_sum.1), channel_id=1, replica_groups=mesh['chip'=16,'core'=2,'far'=4,'mid'=2,'pair'=2] {'chip','pair'}, dimensions={0} | all-to-all | bytes 786432 | tf_op jit(solution)/shard_map/all_to_all | solution.py:35
  131.4 6.7 %collective-permute-start.5 = (bf16[2,768,128]{2,1,0:T(8,128)(2,1)S(1)}, bf16[2,768,128]{2,1,0:T(8,128)(2,1)S(1)}, u32[]{:S(2)}, u32[]{:S(2)}) collective-permute-start(bf16[2,768,128]{2,1,0:T(8,128)(2,1)S(1)} %bitcast.7), channel_id=1, source_target_pairs={{0,16},{16,0},{1,17},{17,1},{2,18},{18,2},{3,19},{19,3},{4,20},{20... | collective-permute-start | bytes 1179656 | tf_op jit(solution)/shard_map/ppermute | solution.py:54
  138.2 1.3 collective-permute-done.5.other
  139.5 1.7 %final.1 = (bf16[2,256,256]{2,1,0:T(8,128)(2,1)}, bf16[2,256,256]{2,1,0:T(8,128)(2,1)}, bf16[2,256,256]{2,1,0:T(8,128)(2,1)}) custom-call(s32[1]{0:T(128)} %bitcast.1.core, bf16[2,768,128]{2,1,0:T(8,128)(2,1)S(1)} %bitcast.8, bf16[2,768,128]{2,1,0:T(8,128)(2,1)S(1)} %collective-permute-done.5.other, bf16[2,256,256]{2,1,0:T(8,128)(2,1)S(1)} %copy-done, ...), custom_call_target="tpu_custom_call" | custom-call | tf_op jit(solution)/shard_map/final/pallas_call | solution.py:318
  (4 shorter events, 0.1 us)
Async XLA Ops:
  0.6 0.7 copy-start.6
  1.4 13.2 %collective-permute-start = (bf16[16,1024]{1,0:T(8,128)(2,1)S(1)}, bf16[16,1024]{1,0:T(8,128)(2,1)S(1)}, u32[]{:S(2)}, u32[]{:S(2)}) collective-permute-start(bf16[16,1024]{1,0:T(8,128)(2,1)S(1)} %constant_dynamic-update-slice_fusion.lower), channel_id=1, source_target_pairs={{0,480},{1,448},{2,352},{3,416},{4,320},{5,224},{6,384},{7,288},{8... | collective-permute-start | bytes 98312 | tf_op jit(solution)/shard_map/ppermute | solution.py:241
  9.1 0.7 copy-start.7
  9.7 0.7 copy-start.8
  11.3 0.7 copy-start.3
  14.7 30.1 %copy-start.1 = (bf16[256,512]{1,0:T(8,128)(2,1)S(1)}, bf16[256,512]{1,0:T(8,128)(2,1)}, u32[]{:S(2)}) copy-start(bf16[256,512]{1,0:T(8,128)(2,1)} %inverse.1) | copy-start | bytes 786436
  39.2 5.5 %collective-permute-start.1 = (bf16[16,16,1024]{2,1,0:T(8,128)(2,1)S(1)}, bf16[16,16,1024]{2,1,0:T(8,128)(2,1)S(1)}, u32[]{:S(2)}, u32[]{:S(2)}) collective-permute-start(bf16[16,16,1024]{2,1,0:T(8,128)(2,1)S(1)} %all_to_all.25.mine), channel_id=1, source_target_pairs={{0,16},{16,0},{1,17},{17,1},{2,18},{18,2},{3,19},{19,3},{4,20},{20... | collective-permute-start | bytes 1572872 | tf_op jit(solution)/shard_map/ppermute | solution.py:54
  45.8 9.4 %collective-permute-start.2 = (bf16[8,16,1024]{2,1,0:T(8,128)(2,1)S(1)}, bf16[8,16,1024]{2,1,0:T(8,128)(2,1)S(1)}, u32[]{:S(2)}, u32[]{:S(2)}) collective-permute-start(bf16[8,16,1024]{2,1,0:T(8,128)(2,1)S(1)} %get-tuple-element.28), channel_id=1, source_target_pairs={{0,1},{1,0},{2,3},{3,2},{4,5},{5,4},{6,7},{7,6},{8,9},{9,8},{10,11... | collective-permute-start | bytes 786440 | tf_op jit(solution)/shard_map/ppermute | solution.py:289
  48.8 3.4 %collective-permute-start.3 = (bf16[16,1024]{1,0:T(8,128)(2,1)S(1)}, bf16[16,1024]{1,0:T(8,128)(2,1)S(1)}, u32[]{:S(2)}, u32[]{:S(2)}) collective-permute-start(bf16[16,1024]{1,0:T(8,128)(2,1)S(1)} %constant_dynamic-update-slice_fusion.lower), channel_id=1, source_target_pairs={{0,16},{16,0},{1,17},{17,1},{2,18},{18,2},{3,19},{19,3},{4,20},{20... | collective-permute-start | bytes 98312 | tf_op jit(solution)/shard_map/ppermute | solution.py:54
  55.3 23.7 %copy-start = (bf16[2,256,256]{2,1,0:T(8,128)(2,1)S(1)}, bf16[2,256,256]{2,1,0:T(8,128)(2,1)}, u32[]{:S(2)}) copy-start(bf16[2,256,256]{2,1,0:T(8,128)(2,1)} %link.3) | copy-start | bytes 786436
  55.3 23.7 %copy-start.4 = (s32[4]{0:T(128)S(1)}, s32[4]{0:T(128)}, u32[]{:S(2)}) copy-start(s32[4]{0:T(128)} %widths.5) | copy-start | bytes 52
  55.3 23.7 %copy-start.5 = (s32[2]{0:T(128)S(1)}, s32[2]{0:T(128)}, u32[]{:S(2)}) copy-start(s32[2]{0:T(128)} %pad_add_fusion.place) | copy-start | bytes 28
  80.4 9.3 %collective-permute-start.4 = (bf16[16,512]{1,0:T(8,128)(2,1)S(1)}, bf16[16,512]{1,0:T(8,128)(2,1)S(1)}, u32[]{:S(2)}, u32[]{:S(2)}) collective-permute-start(bf16[16,512]{1,0:T(8,128)(2,1)S(1)} %get-tuple-element.32), channel_id=1, source_target_pairs={{0,16},{16,0},{1,17},{17,1},{2,18},{18,2},{3,19},{19,3},{4,20},{20... | collective-permute-start | bytes 49160 | tf_op jit(solution)/shard_map/ppermute | solution.py:54
  103.7 15.1 %copy-start.2 = (f32[48,128]{1,0:T(8,128)S(1)}, f32[48,128]{1,0:T(8,128)}, u32[]{:S(2)}) copy-start(f32[48,128]{1,0:T(8,128)} %pivot.1) | copy-start | bytes 73732
  131.4 8.1 %collective-permute-start.5 = (bf16[2,768,128]{2,1,0:T(8,128)(2,1)S(1)}, bf16[2,768,128]{2,1,0:T(8,128)(2,1)S(1)}, u32[]{:S(2)}, u32[]{:S(2)}) collective-permute-start(bf16[2,768,128]{2,1,0:T(8,128)(2,1)S(1)} %bitcast.7), channel_id=1, source_target_pairs={{0,16},{16,0},{1,17},{17,1},{2,18},{18,2},{3,19},{19,3},{4,20},{20... | collective-permute-start | bytes 1179656 | tf_op jit(solution)/shard_map/ppermute | solution.py:54

commit v15 on v14

--- a/solution.py
+++ b/solution.py
@@ -124,42 +124,37 @@
         sums[i] = (keep[i].astype(F32) + got[i].astype(F32)).astype(BF16)
 
 
-def column_body(w, place, limits, received, link, widths, column_one, column_two, own, give):
+def column_body(w, place, limits, received, link, widths, column_one, column_two, packed):
     total = reduced(received)
     for s in range(2):
         span = slice(s * w, (s + 1) * w)
-        here_one = jnp.where(limits[s] > 0, 1.0, 0.0)
-        here_two = jnp.where(limits[2 + s] > 0, 1.0, 0.0)
+        here_one = jnp.where(limits[4 * place[0] + s] > 0, 1.0, 0.0)
+        here_two = jnp.where(limits[4 * place[0] + 2 + s] > 0, 1.0, 0.0)
         column = (-(total[:, span] * here_one)).astype(BF16)
         column_one[:, span] = column
         second = total[:, (2 + s) * w : (3 + s) * w] + dot(column, masked_link(w, link, widths, s))
         column_two[:, span] = (-(second * here_two)).astype(BF16)
-    for out, sibling in ((own, place[0]), (give, 1 - place[0])):
-        span = pl.ds(pl.multiple_of(sibling * w, w), w)
-        out[:, :w] = column_one[:, span]
-        out[:, w:] = column_two[:, span]
-
-
-def sums_body(w, place, limits, own, got, lower, partner, sums, columns, panels):
-    share, lanes, sibling = own.shape[0], sums.shape[2], place[0]
+    for n in range(packed.shape[0]):
+        span = slice((n // PAIR) * w, (n // PAIR + 1) * w)
+        packed[n, :, :w] = column_one[:, span]
+        packed[n, :, w:] = column_two[:, span]
+
+
+def sums_body(w, place, limits, received, lowers, sums, columns, panels):
+    share, sibling = received.shape[1], place[0]
     column = lax.broadcasted_iota(jnp.int32, (share, w), 1)
-    for n, (new, panel) in enumerate(((own, lower), (got, partner))):
+    for n in range(received.shape[0]):
         rows = slice(n * share, (n + 1) * share)
-        columns[rows, :] = new[...]
+        columns[rows, :] = received[n]
         for b in range(2):
-            value = panel[:, pl.ds(pl.multiple_of((2 * b + sibling) * w, w), w)]
-            inside = column < limits[4 * n + 2 * b + sibling]
+            value = lowers[n, :, pl.ds(pl.multiple_of((2 * b + sibling) * w, w), w)]
+            inside = column < limits[4 * (n // PAIR) + 2 * b + sibling]
             panels[rows, b * w : (b + 1) * w] = jnp.where(inside, value, jnp.zeros_like(value))
-    first, second = slice(0, w), slice(w, 2 * w)
-    totals = (
-        -dot_t(panels[:, first], columns[:, first]),
-        dot_t(columns[:, first], panels[:, second]),
-        -dot_t(panels[:, second], columns[:, second]),
-    )
-    for b in range(3):
-        value = totals[b].astype(BF16)
-        for h in range(w // lanes):
-            sums[h, b * w : (b + 1) * w, :] = value[:, h * lanes : (h + 1) * lanes]
+    start = pl.multiple_of(place[2] * LANES, LANES)
+    low, high = pl.ds(start, LANES), pl.ds(pl.multiple_of(w + start, LANES), LANES)
+    sums[0:w, :] = (-dot_t(panels[:, :w], columns[:, low])).astype(BF16)
+    sums[w : 2 * w, :] = dot_t(columns[:, :w], panels[:, high]).astype(BF16)
+    sums[2 * w :, :] = (-dot_t(panels[:, w:], columns[:, high])).astype(BF16)
 
 
 def chunk_sum_body(received, copies):
@@ -242,7 +237,7 @@
     parity = lax.axis_index("pair").astype(jnp.int32)
     plane = lax.axis_index("far") * NEAR + lax.axis_index("mid") * PAIR + parity
     order = lax.dynamic_index_in_dim(jnp.array(places, jnp.int32), plane, 0, keepdims=False)
-    place = jnp.stack([core, chip * PAIR + parity])
+    place = jnp.stack([core, parity * chips + chip, parity])
     flat = (w // LANES, 3 * w, LANES)
     chunk = 3 * w * w // LANES // (chips * PAIR)
     pivot = pl.pallas_call(
@@ -256,8 +251,8 @@
     ancestors = (ancestors_one, ancestors_two)
     limits = jnp.concatenate(
         [
-            column_limits(ancestors, widths, chip * CORES + core),
-            column_limits(ancestors, widths, chip * CORES + 1 - core),
+            column_limits(ancestors, widths, chip * CORES),
+            column_limits(ancestors, widths, chip * CORES + 1),
         ]
     )
     away_limits = jnp.concatenate(
@@ -286,26 +281,28 @@
         ],
         compiler_params=pltpu.CompilerParams(vmem_limit_bytes=40 * 1024 * 1024),
     )(core_ref, parity.reshape(1), order, away_limits, ancestor_inverse, mine, other)
+    give, late = lax.optimization_barrier((give, lower))
     got = lax.ppermute(give, "pair", [(0, 1), (1, 0)])
-    got, partner = lax.optimization_barrier((got, swap_cores(lower)))
+    lowers = exchange(jnp.broadcast_to(late[None], (CORES * PAIR,) + whole), ("core", "pair"))
+    got, lowers = lax.optimization_barrier((got, lowers))
     (part,) = kernel_call(pair_sum_body, "pair_sum", [VMEM] * 2, [(half, BF16)])(keep, got)
     part = exchange(part, ("far", "mid"))
-    column_one, column_two, own, give = kernel_call(
+    column_one, column_two, packed = kernel_call(
         functools.partial(column_body, w),
         "columns",
         [SMEM] * 2 + [VMEM] * 2 + [SMEM],
-        [((share, 2 * w), BF16)] * 4,
+        [((share, 2 * w), BF16)] * 2 + [((CORES * PAIR, share, 2 * w), BF16)],
     )(place, limits, part, link_two, widths)
     sums = pl.pallas_call(
         functools.partial(sums_body, w),
         name="sums",
-        in_specs=[SMEM] * 2 + [VMEM] * 4,
+        in_specs=[SMEM] * 2 + [VMEM] * 2,
         out_specs=VMEM,
-        out_shape=jax.ShapeDtypeStruct(flat, BF16),
-        scratch_shapes=[pltpu.VMEM((CORES * share, 2 * w), BF16)] * 2,
+        out_shape=jax.ShapeDtypeStruct(flat[1:], BF16),
+        scratch_shapes=[pltpu.VMEM((CORES * PAIR * share, 2 * w), BF16)] * 2,
         compiler_params=pltpu.CompilerParams(vmem_limit_bytes=40 * 1024 * 1024),
-    )(place, limits, own, swap_cores(give), lower, partner)
-    sums = exchange(sums.reshape(chips * PAIR, chunk, LANES), ("chip", "pair"))
+    )(place, limits, exchange(packed, ("core", "pair")), lowers)
+    sums = exchange(sums.reshape(chips, chunk, LANES), "chip")
     (sums,) = kernel_call(chunk_sum_body, "chunk_sum", [VMEM], [((planes // PAIR, chunk, LANES), BF16)])(
         sums
     )
@@ -313,7 +310,7 @@
     (total,) = kernel_call(
         all_sum_body, "all_sum", [VMEM] * 2, [((chips * PAIR, chunk, LANES), BF16)]
     )(sums, pivot)
-    mine = exchange(total, ("chip", "pair")).reshape(flat)
+    mine = exchange(total, ("pair", "chip")).reshape(flat)
     other = swap_cores(mine)
     block_one, parent_rows, block_two = kernel_call(
         functools.partial(final_body, w),

time: 142 us -> 146 us (1.028)
  blocking collectives: 89 us -> 97.3 us
  starting transfers between devices: 32.4 us -> 25.3 us
  waiting for transfers between devices: 7.74 us -> 9.55 us
    ppermute x4 -> x2, starting transfers between devices: 21.8 us -> 10.7 us  [swap_cores(): return lax.ppermute(block, 'core', [(0, 1), (1, 0)])]
    all_to_all x5 -> x6, blocking collectives: 89 us -> 97.3 us  [exchange(): return lax.all_to_all(blocks, axis, split_axis=0, concat_axis=0, tiled=True)]
    all_to_all x0 -> x1, starting transfers between devices: none -> 3.67 us  [exchange(): return lax.all_to_all(blocks, axis, split_axis=0, concat_axis=0, tiled=True)]
    ppermute x1, waiting for transfers between devices: 3.02 us -> 6.48 us  [local(): got = lax.ppermute(give, 'pair', [(0, 1), (1, 0)])]
    ppermute x4 -> x2, waiting for transfers between devices: 4.5 us -> 2.84 us  [swap_cores(): return lax.ppermute(block, 'core', [(0, 1), (1, 0)])]
  transfers between devices with their start and end apart: 6 -> 5, of which waited for: 6 -> 4; matrix products, arithmetic and copies ran while one was open for 1% -> 1% of each run, Pallas kernels for 1% -> 1%
where the time goes in v15:
time: 146 us; the launch traced here: 145 us
  blocking collectives  97.3 us (67%)
  starting transfers between devices  25.3 us (17%)
  waiting for transfers between devices  9.55 us (7%)
  Pallas kernels  6.86 us (5%)
  local copies, waits for them, and re-layouts  3.99 us (3%)
    all_to_all x6, blocking collectives, exchange(): return lax.all_to_all(blocks, axis, split_axis=0, concat_axis=0, tiled=True)  97.3 us
    ppermute x2, starting transfers between devices, swap_cores(): return lax.ppermute(block, 'core', [(0, 1), (1, 0)])  10.7 us
    ppermute x1, starting transfers between devices, local(): moved = lax.ppermute(lower, GRID, pairs)  7.66 us
    ppermute x1, waiting for transfers between devices, local(): got = lax.ppermute(give, 'pair', [(0, 1), (1, 0)])  6.48 us
    all_to_all x1, starting transfers between devices, exchange(): return lax.all_to_all(blocks, axis, split_axis=0, concat_axis=0, tiled=True)  3.67 us
    ppermute x1, starting transfers between devices, local(): got = lax.ppermute(give, 'pair', [(0, 1), (1, 0)])  3.28 us
  transfers between devices with their start and end apart: 5, of which 4 were waited for; matrix products, arithmetic and copies ran while one was open for 1% of the time, Pallas kernels for 1%

profile of v15, /device:TPU:1, one launch (start us, length us, event | category | flops | bytes accessed | tf_op | source)
XLA Modules:
  0.0 144.9 jit_solution(3627926459348787144)
XLA Ops:
  0.6 0.0 copy-start.6
  0.6 0.7 constant_dynamic-update-slice_fusion.1
  1.4 0.0 copy-done.6
  1.4 7.7 %collective-permute-start = (bf16[16,1024]{1,0:T(8,128)(2,1)S(1)}, bf16[16,1024]{1,0:T(8,128)(2,1)S(1)}, u32[]{:S(2)}, u32[]{:S(2)}) collective-permute-start(bf16[16,1024]{1,0:T(8,128)(2,1)S(1)} %constant_dynamic-update-slice_fusion), channel_id=1, source_target_pairs={{0,480},{1,448},{2,352},{3,416},{4,320},{5,224},{6,384},{7,288},{8... | collective-permute-start | bytes 98312 | tf_op jit(solution)/shard_map/ppermute | solution.py:236
  9.1 0.0 copy-start.7
  9.1 0.7 copy-done.7
  9.7 0.0 copy-start.8
  9.7 0.1 compare_reduce_fusion.3
  9.9 0.5 copy-done.8
  10.4 0.1 compare_reduce_fusion.2
  10.6 0.7 dynamic-slice_bitcast_fusion.order
  11.3 0.0 copy-start.3
  11.3 0.7 copy-done.3
  11.9 0.1 add_select_fusion.2
  12.0 0.1 pad_add_fusion.1
  12.1 0.6 pad_add_fusion.place
  12.7 1.7 %pivot.1 = f32[48,128]{1,0:T(8,128)} custom-call(s32[3]{0:T(128)} %pad_add_fusion.place, bf16[2,256,256]{2,1,0:T(8,128)(2,1)} %one.1, bf16[2,256,256]{2,1,0:T(8,128)(2,1)} %two.1, s32[4]{0:T(128)} %widths.5), custom_call_target="tpu_custom_call" | custom-call | tf_op jit(solution)/shard_map/pivot/pallas_call | solution.py:243
  14.4 0.2 collective-permute-done.source
  14.7 0.0 copy-start.1
  14.7 24.6 %all_to_all.35.mine = bf16[16,16,1024]{2,1,0:T(8,128)(2,1)S(1)} all-to-all(bf16[16,16,1024]{2,1,0:T(8,128)(2,1)S(1)} %copies.1), channel_id=1, replica_groups=mesh['chip'=16,'core'=2,'far'=4,'mid'=2,'pair'=2] {'chip'}, dimensions={0} | all-to-all | bytes 1048576 | tf_op jit(solution)/shard_map/all_to_all | solution.py:35
  39.2 4.0 %collective-permute-start.1 = (bf16[16,16,1024]{2,1,0:T(8,128)(2,1)S(1)}, bf16[16,16,1024]{2,1,0:T(8,128)(2,1)S(1)}, u32[]{:S(2)}, u32[]{:S(2)}) collective-permute-start(bf16[16,16,1024]{2,1,0:T(8,128)(2,1)S(1)} %all_to_all.35.mine), channel_id=1, source_target_pairs={{0,16},{16,0},{1,17},{17,1},{2,18},{18,2},{3,19},{19,3},{4,20},{20... | collective-permute-start | bytes 1572872 | tf_op jit(solution)/shard_map/ppermute | solution.py:54
  43.3 1.5 %collective-permute-done.1.other = bf16[16,16,1024]{2,1,0:T(8,128)(2,1)S(1)} collective-permute-done((bf16[16,16,1024]{2,1,0:T(8,128)(2,1)S(1)}, bf16[16,16,1024]{2,1,0:T(8,128)(2,1)S(1)}, u32[]{:S(2)}, u32[]{:S(2)}) %collective-permute-start.1) | collective-permute-done | bytes 524320 | tf_op jit(solution)/shard_map/ppermute | solution.py:54
  44.8 0.0 copy-done.1
  44.8 1.0 product.1
  45.8 0.7 broadcast_in_dim.14
  46.5 3.7 %all-to-all-start.1 = ((bf16[4,16,1024]{2,1,0:T(8,128)(2,1)}), bf16[4,16,1024]{2,1,0:T(8,128)(2,1)S(1)}, u32[]{:S(2)}, u32[]{:S(2)}) async-start(bf16[4,16,1024]{2,1,0:T(8,128)(2,1)} %broadcast_in_dim.14), calls=%async_computation.1 | async-start | bytes 262144 | tf_op jit(solution)/shard_map/all_to_all | solution.py:35
  50.1 3.3 %collective-permute-start.2 = (bf16[8,16,1024]{2,1,0:T(8,128)(2,1)S(1)}, bf16[8,16,1024]{2,1,0:T(8,128)(2,1)S(1)}, u32[]{:S(2)}, u32[]{:S(2)}) collective-permute-start(bf16[8,16,1024]{2,1,0:T(8,128)(2,1)S(1)} %get-tuple-element.30), channel_id=1, source_target_pairs={{0,1},{1,0},{2,3},{3,2},{4,5},{5,4},{6,7},{7,6},{8,9},{9,8},{10,11... | collective-permute-start | bytes 786440 | tf_op jit(solution)/shard_map/ppermute | solution.py:285
  53.4 6.5 %collective-permute-done.2.got = bf16[8,16,1024]{2,1,0:T(8,128)(2,1)S(1)} collective-permute-done((bf16[8,16,1024]{2,1,0:T(8,128)(2,1)S(1)}, bf16[8,16,1024]{2,1,0:T(8,128)(2,1)S(1)}, u32[]{:S(2)}, u32[]{:S(2)}) %collective-permute-start.2) | collective-permute-done | bytes 262176 | tf_op jit(solution)/shard_map/ppermute | solution.py:285
  59.9 0.0 all-to-all-done.1.lowers
  59.9 0.1 pair_sum.1
  60.0 0.0 copy-start
  60.0 0.0 copy-start.4
  60.0 0.0 copy-start.5
  60.0 24.5 %all_to_all.36.received = bf16[8,16,1024]{2,1,0:T(8,128)(2,1)S(1)} all-to-all(bf16[8,16,1024]{2,1,0:T(8,128)(2,1)S(1)} %pair_sum.1), channel_id=1, replica_groups=mesh['chip'=16,'core'=2,'far'=4,'mid'=2,'pair'=2] {'far','mid'}, dimensions={0} | all-to-all | bytes 524288 | tf_op jit(solution)/shard_map/all_to_all | solution.py:35
  84.6 0.0 copy-done
  84.6 0.0 copy-done.4
  84.6 0.0 copy-done.5
  84.6 1.4 columns.1
  86.0 11.4 %all_to_all.37.received = bf16[4,16,512]{2,1,0:T(8,128)(2,1)S(1)} all-to-all(bf16[4,16,512]{2,1,0:T(8,128)(2,1)S(1)} %get-tuple-element.34), channel_id=1, replica_groups=mesh['chip'=16,'core'=2,'far'=4,'mid'=2,'pair'=2] {'core','pair'}, dimensions={0} | all-to-all | bytes 131072 | tf_op jit(solution)/shard_map/all_to_all | solution.py:35
  97.4 0.8 sums.1
  98.2 10.0 %all_to_all.38.received = bf16[16,48,128]{2,1,0:T(8,128)(2,1)S(1)} all-to-all(bf16[16,48,128]{2,1,0:T(8,128)(2,1)S(1)} %bitcast.9), channel_id=1, replica_groups=mesh['chip'=16,'core'=2,'far'=4,'mid'=2,'pair'=2] {'chip'}, dimensions={0} | all-to-all | bytes 393216 | tf_op jit(solution)/shard_map/all_to_all | solution.py:35
  108.2 0.0 copy-start.2
  108.3 14.9 %all_to_all.39.received = bf16[8,48,128]{2,1,0:T(8,128)(2,1)S(1)} all-to-all(bf16[8,48,128]{2,1,0:T(8,128)(2,1)S(1)} %chunk_sum.1), channel_id=1, replica_groups=mesh['chip'=16,'core'=2,'far'=4,'mid'=2,'pair'=2] {'far','mid'}, dimensions={0} | all-to-all | bytes 196608 | tf_op jit(solution)/shard_map/all_to_all | solution.py:35
  123.1 0.0 copy-done.2
  123.2 11.9 %all_to_all.40 = bf16[32,48,128]{2,1,0:T(8,128)(2,1)S(1)} all-to-all(bf16[32,48,128]{2,1,0:T(8,128)(2,1)S(1)} %all_sum.1), channel_id=1, replica_groups=mesh['chip'=16,'core'=2,'far'=4,'mid'=2,'pair'=2] {'pair','chip'}, dimensions={0} | all-to-all | bytes 786432 | tf_op jit(solution)/shard_map/all_to_all | solution.py:35
  135.1 6.7 %collective-permute-start.3 = (bf16[2,768,128]{2,1,0:T(8,128)(2,1)S(1)}, bf16[2,768,128]{2,1,0:T(8,128)(2,1)S(1)}, u32[]{:S(2)}, u32[]{:S(2)}) collective-permute-start(bf16[2,768,128]{2,1,0:T(8,128)(2,1)S(1)} %bitcast.7), channel_id=1, source_target_pairs={{0,16},{16,0},{1,17},{17,1},{2,18},{18,2},{3,19},{19,3},{4,20},{20... | collective-permute-start | bytes 1179656 | tf_op jit(solution)/shard_map/ppermute | solution.py:54
  141.8 1.3 collective-permute-done.3.other
  143.1 1.7 %final.1 = (bf16[2,256,256]{2,1,0:T(8,128)(2,1)}, bf16[2,256,256]{2,1,0:T(8,128)(2,1)}, bf16[2,256,256]{2,1,0:T(8,128)(2,1)}) custom-call(s32[1]{0:T(128)} %bitcast.1.core, bf16[2,768,128]{2,1,0:T(8,128)(2,1)S(1)} %bitcast.8, bf16[2,768,128]{2,1,0:T(8,128)(2,1)S(1)} %collective-permute-done.3.other, bf16[2,256,256]{2,1,0:T(8,128)(2,1)S(1)} %copy-done, ...), custom_call_target="tpu_custom_call" | custom-call | tf_op jit(solution)/shard_map/final/pallas_call | solution.py:315
  (4 shorter events, 0.1 us)
Async XLA Ops:
  0.6 0.7 copy-start.6
  1.4 13.2 %collective-permute-start = (bf16[16,1024]{1,0:T(8,128)(2,1)S(1)}, bf16[16,1024]{1,0:T(8,128)(2,1)S(1)}, u32[]{:S(2)}, u32[]{:S(2)}) collective-permute-start(bf16[16,1024]{1,0:T(8,128)(2,1)S(1)} %constant_dynamic-update-slice_fusion), channel_id=1, source_target_pairs={{0,480},{1,448},{2,352},{3,416},{4,320},{5,224},{6,384},{7,288},{8... | collective-permute-start | bytes 98312 | tf_op jit(solution)/shard_map/ppermute | solution.py:236
  9.1 0.7 copy-start.7
  9.7 0.7 copy-start.8
  11.3 0.7 copy-start.3
  14.7 30.1 %copy-start.1 = (bf16[256,512]{1,0:T(8,128)(2,1)S(1)}, bf16[256,512]{1,0:T(8,128)(2,1)}, u32[]{:S(2)}) copy-start(bf16[256,512]{1,0:T(8,128)(2,1)} %inverse.1) | copy-start | bytes 786436
  39.2 5.5 %collective-permute-start.1 = (bf16[16,16,1024]{2,1,0:T(8,128)(2,1)S(1)}, bf16[16,16,1024]{2,1,0:T(8,128)(2,1)S(1)}, u32[]{:S(2)}, u32[]{:S(2)}) collective-permute-start(bf16[16,16,1024]{2,1,0:T(8,128)(2,1)S(1)} %all_to_all.35.mine), channel_id=1, source_target_pairs={{0,16},{16,0},{1,17},{17,1},{2,18},{18,2},{3,19},{19,3},{4,20},{20... | collective-permute-start | bytes 1572872 | tf_op jit(solution)/shard_map/ppermute | solution.py:54
  46.5 13.4 %all-to-all-start.1 = ((bf16[4,16,1024]{2,1,0:T(8,128)(2,1)}), bf16[4,16,1024]{2,1,0:T(8,128)(2,1)S(1)}, u32[]{:S(2)}, u32[]{:S(2)}) async-start(bf16[4,16,1024]{2,1,0:T(8,128)(2,1)} %broadcast_in_dim.14), calls=%async_computation.1 | async-start | bytes 262144 | tf_op jit(solution)/shard_map/all_to_all | solution.py:35
  50.1 9.8 %collective-permute-start.2 = (bf16[8,16,1024]{2,1,0:T(8,128)(2,1)S(1)}, bf16[8,16,1024]{2,1,0:T(8,128)(2,1)S(1)}, u32[]{:S(2)}, u32[]{:S(2)}) collective-permute-start(bf16[8,16,1024]{2,1,0:T(8,128)(2,1)S(1)} %get-tuple-element.30), channel_id=1, source_target_pairs={{0,1},{1,0},{2,3},{3,2},{4,5},{5,4},{6,7},{7,6},{8,9},{9,8},{10,11... | collective-permute-start | bytes 786440 | tf_op jit(solution)/shard_map/ppermute | solution.py:285
  60.0 24.6 %copy-start = (bf16[2,256,256]{2,1,0:T(8,128)(2,1)S(1)}, bf16[2,256,256]{2,1,0:T(8,128)(2,1)}, u32[]{:S(2)}) copy-start(bf16[2,256,256]{2,1,0:T(8,128)(2,1)} %link.3) | copy-start | bytes 786436
  60.0 24.6 %copy-start.4 = (s32[4]{0:T(128)S(1)}, s32[4]{0:T(128)}, u32[]{:S(2)}) copy-start(s32[4]{0:T(128)} %widths.5) | copy-start | bytes 52
  60.0 24.6 %copy-start.5 = (s32[3]{0:T(128)S(1)}, s32[3]{0:T(128)}, u32[]{:S(2)}) copy-start(s32[3]{0:T(128)} %pad_add_fusion.place) | copy-start | bytes 40
  108.2 14.9 %copy-start.2 = (f32[48,128]{1,0:T(8,128)S(1)}, f32[48,128]{1,0:T(8,128)}, u32[]{:S(2)}) copy-start(f32[48,128]{1,0:T(8,128)} %pivot.1) | copy-start | bytes 73732
  135.1 8.1 %collective-permute-start.3 = (bf16[2,768,128]{2,1,0:T(8,128)(2,1)S(1)}, bf16[2,768,128]{2,1,0:T(8,128)(2,1)S(1)}, u32[]{:S(2)}, u32[]{:S(2)}) collective-permute-start(bf16[2,768,128]{2,1,0:T(8,128)(2,1)S(1)} %bitcast.7), channel_id=1, source_target_pairs={{0,16},{16,0},{1,17},{17,1},{2,18},{18,2},{3,19},{19,3},{4,20},{20... | collective-permute-start | bytes 1179656 | tf_op jit(solution)/shard_map/ppermute | solution.py:54

commit v16 on v15

--- a/solution.py
+++ b/solution.py
@@ -124,37 +124,40 @@
         sums[i] = (keep[i].astype(F32) + got[i].astype(F32)).astype(BF16)
 
 
-def column_body(w, place, limits, received, link, widths, column_one, column_two, packed):
+def column_body(
+    w, place, limits, received, panels, link, widths, column_one, column_two, packed
+):
     total = reduced(received)
     for s in range(2):
         span = slice(s * w, (s + 1) * w)
-        here_one = jnp.where(limits[4 * place[0] + s] > 0, 1.0, 0.0)
-        here_two = jnp.where(limits[4 * place[0] + 2 + s] > 0, 1.0, 0.0)
+        here_one = jnp.where(limits[s] > 0, 1.0, 0.0)
+        here_two = jnp.where(limits[2 + s] > 0, 1.0, 0.0)
         column = (-(total[:, span] * here_one)).astype(BF16)
         column_one[:, span] = column
         second = total[:, (2 + s) * w : (3 + s) * w] + dot(column, masked_link(w, link, widths, s))
         column_two[:, span] = (-(second * here_two)).astype(BF16)
+    inside = inside_limits(limits, 0, panels.shape, w)
+    lower = jnp.where(inside, panels[...], jnp.zeros_like(panels[...]))
     for n in range(packed.shape[0]):
         span = slice((n // PAIR) * w, (n // PAIR + 1) * w)
         packed[n, :, :w] = column_one[:, span]
-        packed[n, :, w:] = column_two[:, span]
-
-
-def sums_body(w, place, limits, received, lowers, sums, columns, panels):
-    share, sibling = received.shape[1], place[0]
-    column = lax.broadcasted_iota(jnp.int32, (share, w), 1)
+        packed[n, :, w : 2 * w] = column_two[:, span]
+        packed[n, :, 2 * w : 3 * w] = lower[:, span]
+        other = slice((2 + n // PAIR) * w, (3 + n // PAIR) * w)
+        packed[n, :, 3 * w :] = lower[:, other]
+
+
+def sums_body(w, place, received, sums, held):
+    share = received.shape[1]
     for n in range(received.shape[0]):
-        rows = slice(n * share, (n + 1) * share)
-        columns[rows, :] = received[n]
-        for b in range(2):
-            value = lowers[n, :, pl.ds(pl.multiple_of((2 * b + sibling) * w, w), w)]
-            inside = column < limits[4 * (n // PAIR) + 2 * b + sibling]
-            panels[rows, b * w : (b + 1) * w] = jnp.where(inside, value, jnp.zeros_like(value))
+        held[n * share : (n + 1) * share, :] = received[n]
     start = pl.multiple_of(place[2] * LANES, LANES)
     low, high = pl.ds(start, LANES), pl.ds(pl.multiple_of(w + start, LANES), LANES)
-    sums[0:w, :] = (-dot_t(panels[:, :w], columns[:, low])).astype(BF16)
-    sums[w : 2 * w, :] = dot_t(columns[:, :w], panels[:, high]).astype(BF16)
-    sums[2 * w :, :] = (-dot_t(panels[:, w:], columns[:, high])).astype(BF16)
+    late = pl.ds(pl.multiple_of(3 * w + start, LANES), LANES)
+    first, second = held[:, 2 * w : 3 * w], held[:, 3 * w :]
+    sums[0:w, :] = (-dot_t(first, held[:, low])).astype(BF16)
+    sums[w : 2 * w, :] = dot_t(held[:, :w], held[:, late]).astype(BF16)
+    sums[2 * w :, :] = (-dot_t(second, held[:, high])).astype(BF16)
 
 
 def chunk_sum_body(received, copies):
@@ -249,12 +252,7 @@
         scratch_shapes=[pltpu.VMEM((3 * w * w // LANES, LANES), F32)],
     )(place, diag_inverse_one, diag_inverse_two, widths)
     ancestors = (ancestors_one, ancestors_two)
-    limits = jnp.concatenate(
-        [
-            column_limits(ancestors, widths, chip * CORES),
-            column_limits(ancestors, widths, chip * CORES + 1),
-        ]
-    )
+    limits = column_limits(ancestors, widths, chip * CORES + core)
     away_limits = jnp.concatenate(
         [
             column_limits(ancestors, widths, plane * CORES + core),
@@ -281,27 +279,24 @@
         ],
         compiler_params=pltpu.CompilerParams(vmem_limit_bytes=40 * 1024 * 1024),
     )(core_ref, parity.reshape(1), order, away_limits, ancestor_inverse, mine, other)
-    give, late = lax.optimization_barrier((give, lower))
     got = lax.ppermute(give, "pair", [(0, 1), (1, 0)])
-    lowers = exchange(jnp.broadcast_to(late[None], (CORES * PAIR,) + whole), ("core", "pair"))
-    got, lowers = lax.optimization_barrier((got, lowers))
     (part,) = kernel_call(pair_sum_body, "pair_sum", [VMEM] * 2, [(half, BF16)])(keep, got)
     part = exchange(part, ("far", "mid"))
     column_one, column_two, packed = kernel_call(
         functools.partial(column_body, w),
         "columns",
-        [SMEM] * 2 + [VMEM] * 2 + [SMEM],
-        [((share, 2 * w), BF16)] * 2 + [((CORES * PAIR, share, 2 * w), BF16)],
-    )(place, limits, part, link_two, widths)
+        [SMEM] * 2 + [VMEM] * 3 + [SMEM],
+        [((share, 2 * w), BF16)] * 2 + [((CORES * PAIR,) + whole, BF16)],
+    )(place, limits, part, lower, link_two, widths)
     sums = pl.pallas_call(
         functools.partial(sums_body, w),
         name="sums",
-        in_specs=[SMEM] * 2 + [VMEM] * 2,
+        in_specs=[SMEM, VMEM],
         out_specs=VMEM,
         out_shape=jax.ShapeDtypeStruct(flat[1:], BF16),
-        scratch_shapes=[pltpu.VMEM((CORES * PAIR * share, 2 * w), BF16)] * 2,
+        scratch_shapes=[pltpu.VMEM((CORES * PAIR * share, 4 * w), BF16)],
         compiler_params=pltpu.CompilerParams(vmem_limit_bytes=40 * 1024 * 1024),
-    )(place, limits, exchange(packed, ("core", "pair")), lowers)
+    )(place, exchange(packed, ("core", "pair")))
     sums = exchange(sums.reshape(chips, chunk, LANES), "chip")
     (sums,) = kernel_call(chunk_sum_body, "chunk_sum", [VMEM], [((planes // PAIR, chunk, LANES), BF16)])(
         sums

time: 146 us -> 141 us (0.966)
  starting transfers between devices: 25.3 us -> 20.9 us
    all_to_all x1 -> x0, starting transfers between devices: 3.67 us -> none  [exchange(): return lax.all_to_all(blocks, axis, split_axis=0, concat_axis=0, tiled=True)]
  transfers between devices with their start and end apart: 5 -> 4, of which waited for: 4 -> 4; matrix products, arithmetic and copies ran while one was open for 1% -> 1% of each run, Pallas kernels for 1% -> 1%
where the time goes in v16:
time: 141 us; the launch traced here: 140 us
  blocking collectives  97.5 us (69%)
  starting transfers between devices  20.9 us (15%)
  waiting for transfers between devices  9.49 us (7%)
  Pallas kernels  6.86 us (5%)
  local copies, waits for them, and re-layouts  3.33 us (2%)
    all_to_all x6, blocking collectives, exchange(): return lax.all_to_all(blocks, axis, split_axis=0, concat_axis=0, tiled=True)  97.5 us
    ppermute x2, starting transfers between devices, swap_cores(): return lax.ppermute(block, 'core', [(0, 1), (1, 0)])  10.3 us
    ppermute x1, starting transfers between devices, local(): moved = lax.ppermute(lower, GRID, pairs)  7.66 us
    ppermute x1, waiting for transfers between devices, local(): got = lax.ppermute(give, 'pair', [(0, 1), (1, 0)])  6.43 us
    ppermute x1, starting transfers between devices, local(): got = lax.ppermute(give, 'pair', [(0, 1), (1, 0)])  2.98 us
    ppermute x2, waiting for transfers between devices, swap_cores(): return lax.ppermute(block, 'core', [(0, 1), (1, 0)])  2.84 us
  transfers between devices with their start and end apart: 4, of which 4 were waited for; matrix products, arithmetic and copies ran while one was open for 1% of the time, Pallas kernels for 1%

profile of v16, /device:TPU:1, one launch (start us, length us, event | category | flops | bytes accessed | tf_op | source)
XLA Modules:
  0.0 139.9 jit_solution(13972788192531605729)
XLA Ops:
  0.6 0.0 copy-start.6
  0.6 0.7 constant_dynamic-update-slice_fusion.1
  1.4 0.0 copy-done.6
  1.4 7.7 %collective-permute-start = (bf16[16,1024]{1,0:T(8,128)(2,1)S(1)}, bf16[16,1024]{1,0:T(8,128)(2,1)S(1)}, u32[]{:S(2)}, u32[]{:S(2)}) collective-permute-start(bf16[16,1024]{1,0:T(8,128)(2,1)S(1)} %constant_dynamic-update-slice_fusion.panels), channel_id=1, source_target_pairs={{0,480},{1,448},{2,352},{3,416},{4,320},{5,224},{6,384},{7,288},{8... | collective-permute-start | bytes 98312 | tf_op jit(solution)/shard_map/ppermute | solution.py:239
  9.1 0.0 copy-start.7
  9.1 0.7 copy-done.7
  9.7 0.0 copy-start.8
  9.7 0.1 compare_reduce_fusion.3
  9.9 0.5 copy-done.8
  10.4 0.1 compare_reduce_fusion.2
  10.6 0.7 dynamic-slice_bitcast_fusion.order
  11.3 0.0 copy-start.3
  11.3 0.7 copy-done.3
  11.9 0.1 add_select_fusion.1
  12.0 0.1 pad_add_fusion.1.limits
  12.1 0.6 pad_add_fusion.place
  12.7 1.7 %pivot.1 = f32[48,128]{1,0:T(8,128)} custom-call(s32[3]{0:T(128)} %pad_add_fusion.place, bf16[2,256,256]{2,1,0:T(8,128)(2,1)} %one.1, bf16[2,256,256]{2,1,0:T(8,128)(2,1)} %two.1, s32[4]{0:T(128)} %widths.5), custom_call_target="tpu_custom_call" | custom-call | tf_op jit(solution)/shard_map/pivot/pallas_call | solution.py:246
  14.4 0.2 collective-permute-done.source
  14.7 0.0 copy-start.1
  14.7 24.6 %all_to_all.30.mine = bf16[16,16,1024]{2,1,0:T(8,128)(2,1)S(1)} all-to-all(bf16[16,16,1024]{2,1,0:T(8,128)(2,1)S(1)} %copies.1), channel_id=1, replica_groups=mesh['chip'=16,'core'=2,'far'=4,'mid'=2,'pair'=2] {'chip'}, dimensions={0} | all-to-all | bytes 1048576 | tf_op jit(solution)/shard_map/all_to_all | solution.py:35
  39.2 4.0 %collective-permute-start.1 = (bf16[16,16,1024]{2,1,0:T(8,128)(2,1)S(1)}, bf16[16,16,1024]{2,1,0:T(8,128)(2,1)S(1)}, u32[]{:S(2)}, u32[]{:S(2)}) collective-permute-start(bf16[16,16,1024]{2,1,0:T(8,128)(2,1)S(1)} %all_to_all.30.mine), channel_id=1, source_target_pairs={{0,16},{16,0},{1,17},{17,1},{2,18},{18,2},{3,19},{19,3},{4,20},{20... | collective-permute-start | bytes 1572872 | tf_op jit(solution)/shard_map/ppermute | solution.py:54
  43.3 1.5 %collective-permute-done.1.other = bf16[16,16,1024]{2,1,0:T(8,128)(2,1)S(1)} collective-permute-done((bf16[16,16,1024]{2,1,0:T(8,128)(2,1)S(1)}, bf16[16,16,1024]{2,1,0:T(8,128)(2,1)S(1)}, u32[]{:S(2)}, u32[]{:S(2)}) %collective-permute-start.1) | collective-permute-done | bytes 524320 | tf_op jit(solution)/shard_map/ppermute | solution.py:54
  44.8 0.0 copy-done.1
  44.8 1.0 product.1
  45.8 3.0 %collective-permute-start.2 = (bf16[8,16,1024]{2,1,0:T(8,128)(2,1)S(1)}, bf16[8,16,1024]{2,1,0:T(8,128)(2,1)S(1)}, u32[]{:S(2)}, u32[]{:S(2)}) collective-permute-start(bf16[8,16,1024]{2,1,0:T(8,128)(2,1)S(1)} %get-tuple-element.25), channel_id=1, source_target_pairs={{0,1},{1,0},{2,3},{3,2},{4,5},{5,4},{6,7},{7,6},{8,9},{9,8},{10,11... | collective-permute-start | bytes 786440 | tf_op jit(solution)/shard_map/ppermute | solution.py:282
  48.8 6.4 %collective-permute-done.2.got = bf16[8,16,1024]{2,1,0:T(8,128)(2,1)S(1)} collective-permute-done((bf16[8,16,1024]{2,1,0:T(8,128)(2,1)S(1)}, bf16[8,16,1024]{2,1,0:T(8,128)(2,1)S(1)}, u32[]{:S(2)}, u32[]{:S(2)}) %collective-permute-start.2) | collective-permute-done | bytes 262176 | tf_op jit(solution)/shard_map/ppermute | solution.py:282
  55.2 0.1 pair_sum.1
  55.3 0.0 copy-start
  55.3 0.0 copy-start.4
  55.3 0.0 copy-start.5
  55.3 23.6 %all_to_all.31.received = bf16[8,16,1024]{2,1,0:T(8,128)(2,1)S(1)} all-to-all(bf16[8,16,1024]{2,1,0:T(8,128)(2,1)S(1)} %pair_sum.1), channel_id=1, replica_groups=mesh['chip'=16,'core'=2,'far'=4,'mid'=2,'pair'=2] {'far','mid'}, dimensions={0} | all-to-all | bytes 524288 | tf_op jit(solution)/shard_map/all_to_all | solution.py:35
  79.0 0.0 copy-done
  79.0 0.0 copy-done.4
  79.0 0.0 copy-done.5
  79.0 1.4 %columns.1 = (bf16[16,512]{1,0:T(8,128)(2,1)}, bf16[16,512]{1,0:T(8,128)(2,1)}, bf16[4,16,1024]{2,1,0:T(8,128)(2,1)S(1)}) custom-call(s32[3]{0:T(128)S(1)} %copy-done.5, s32[4]{0:T(128)S(1)} %get-tuple-element.20.limits, bf16[8,16,1024]{2,1,0:T(8,128)(2,1)S(1)} %all_to_all.31.received, bf16[16,1024]{1,0:T(8,128)(2,1)S(1)} %constant_dynamic-update-slice_fusion.panels, ...), custom_call_target="tpu_custom_call" | custom-call | tf_op jit(solution)/shard_map/columns/pallas_call | solution.py:285
  80.4 12.5 %all_to_all.32.received = bf16[4,16,1024]{2,1,0:T(8,128)(2,1)S(1)} all-to-all(bf16[4,16,1024]{2,1,0:T(8,128)(2,1)S(1)} %get-tuple-element.27), channel_id=1, replica_groups=mesh['chip'=16,'core'=2,'far'=4,'mid'=2,'pair'=2] {'core','pair'}, dimensions={0} | all-to-all | bytes 262144 | tf_op jit(solution)/shard_map/all_to_all | solution.py:35
  92.9 0.8 sums.1
  93.7 9.8 %all_to_all.33.received = bf16[16,48,128]{2,1,0:T(8,128)(2,1)S(1)} all-to-all(bf16[16,48,128]{2,1,0:T(8,128)(2,1)S(1)} %bitcast.9), channel_id=1, replica_groups=mesh['chip'=16,'core'=2,'far'=4,'mid'=2,'pair'=2] {'chip'}, dimensions={0} | all-to-all | bytes 393216 | tf_op jit(solution)/shard_map/all_to_all | solution.py:35
  103.5 0.0 copy-start.2
  103.5 15.1 %all_to_all.34.received = bf16[8,48,128]{2,1,0:T(8,128)(2,1)S(1)} all-to-all(bf16[8,48,128]{2,1,0:T(8,128)(2,1)S(1)} %chunk_sum.1), channel_id=1, replica_groups=mesh['chip'=16,'core'=2,'far'=4,'mid'=2,'pair'=2] {'far','mid'}, dimensions={0} | all-to-all | bytes 196608 | tf_op jit(solution)/shard_map/all_to_all | solution.py:35
  118.6 0.0 copy-done.2
  118.6 11.9 %all_to_all.35 = bf16[32,48,128]{2,1,0:T(8,128)(2,1)S(1)} all-to-all(bf16[32,48,128]{2,1,0:T(8,128)(2,1)S(1)} %all_sum.1), channel_id=1, replica_groups=mesh['chip'=16,'core'=2,'far'=4,'mid'=2,'pair'=2] {'pair','chip'}, dimensions={0} | all-to-all | bytes 786432 | tf_op jit(solution)/shard_map/all_to_all | solution.py:35
  130.5 6.3 %collective-permute-start.3 = (bf16[2,768,128]{2,1,0:T(8,128)(2,1)S(1)}, bf16[2,768,128]{2,1,0:T(8,128)(2,1)S(1)}, u32[]{:S(2)}, u32[]{:S(2)}) collective-permute-start(bf16[2,768,128]{2,1,0:T(8,128)(2,1)S(1)} %bitcast.7), channel_id=1, source_target_pairs={{0,16},{16,0},{1,17},{17,1},{2,18},{18,2},{3,19},{19,3},{4,20},{20... | collective-permute-start | bytes 1179656 | tf_op jit(solution)/shard_map/ppermute | solution.py:54
  136.8 1.3 collective-permute-done.3.other
  138.1 1.7 %final.1 = (bf16[2,256,256]{2,1,0:T(8,128)(2,1)}, bf16[2,256,256]{2,1,0:T(8,128)(2,1)}, bf16[2,256,256]{2,1,0:T(8,128)(2,1)}) custom-call(s32[1]{0:T(128)} %bitcast.1.core, bf16[2,768,128]{2,1,0:T(8,128)(2,1)S(1)} %bitcast.8, bf16[2,768,128]{2,1,0:T(8,128)(2,1)S(1)} %collective-permute-done.3.other, bf16[2,256,256]{2,1,0:T(8,128)(2,1)S(1)} %copy-done, ...), custom_call_target="tpu_custom_call" | custom-call | tf_op jit(solution)/shard_map/final/pallas_call | solution.py:310
  (4 shorter events, 0.1 us)
Async XLA Ops:
  0.6 0.7 copy-start.6
  1.4 13.2 %collective-permute-start = (bf16[16,1024]{1,0:T(8,128)(2,1)S(1)}, bf16[16,1024]{1,0:T(8,128)(2,1)S(1)}, u32[]{:S(2)}, u32[]{:S(2)}) collective-permute-start(bf16[16,1024]{1,0:T(8,128)(2,1)S(1)} %constant_dynamic-update-slice_fusion.panels), channel_id=1, source_target_pairs={{0,480},{1,448},{2,352},{3,416},{4,320},{5,224},{6,384},{7,288},{8... | collective-permute-start | bytes 98312 | tf_op jit(solution)/shard_map/ppermute | solution.py:239
  9.1 0.7 copy-start.7
  9.7 0.7 copy-start.8
  11.3 0.7 copy-start.3
  14.7 30.1 %copy-start.1 = (bf16[256,512]{1,0:T(8,128)(2,1)S(1)}, bf16[256,512]{1,0:T(8,128)(2,1)}, u32[]{:S(2)}) copy-start(bf16[256,512]{1,0:T(8,128)(2,1)} %inverse.1) | copy-start | bytes 786436
  39.2 5.5 %collective-permute-start.1 = (bf16[16,16,1024]{2,1,0:T(8,128)(2,1)S(1)}, bf16[16,16,1024]{2,1,0:T(8,128)(2,1)S(1)}, u32[]{:S(2)}, u32[]{:S(2)}) collective-permute-start(bf16[16,16,1024]{2,1,0:T(8,128)(2,1)S(1)} %all_to_all.30.mine), channel_id=1, source_target_pairs={{0,16},{16,0},{1,17},{17,1},{2,18},{18,2},{3,19},{19,3},{4,20},{20... | collective-permute-start | bytes 1572872 | tf_op jit(solution)/shard_map/ppermute | solution.py:54
  45.8 9.4 %collective-permute-start.2 = (bf16[8,16,1024]{2,1,0:T(8,128)(2,1)S(1)}, bf16[8,16,1024]{2,1,0:T(8,128)(2,1)S(1)}, u32[]{:S(2)}, u32[]{:S(2)}) collective-permute-start(bf16[8,16,1024]{2,1,0:T(8,128)(2,1)S(1)} %get-tuple-element.25), channel_id=1, source_target_pairs={{0,1},{1,0},{2,3},{3,2},{4,5},{5,4},{6,7},{7,6},{8,9},{9,8},{10,11... | collective-permute-start | bytes 786440 | tf_op jit(solution)/shard_map/ppermute | solution.py:282
  55.3 23.7 %copy-start = (bf16[2,256,256]{2,1,0:T(8,128)(2,1)S(1)}, bf16[2,256,256]{2,1,0:T(8,128)(2,1)}, u32[]{:S(2)}) copy-start(bf16[2,256,256]{2,1,0:T(8,128)(2,1)} %link.3) | copy-start | bytes 786436
  55.3 23.7 %copy-start.4 = (s32[4]{0:T(128)S(1)}, s32[4]{0:T(128)}, u32[]{:S(2)}) copy-start(s32[4]{0:T(128)} %widths.5) | copy-start | bytes 52
  55.3 23.7 %copy-start.5 = (s32[3]{0:T(128)S(1)}, s32[3]{0:T(128)}, u32[]{:S(2)}) copy-start(s32[3]{0:T(128)} %pad_add_fusion.place) | copy-start | bytes 40
  103.5 15.1 %copy-start.2 = (f32[48,128]{1,0:T(8,128)S(1)}, f32[48,128]{1,0:T(8,128)}, u32[]{:S(2)}) copy-start(f32[48,128]{1,0:T(8,128)} %pivot.1) | copy-start | bytes 73732
  130.5 7.6 %collective-permute-start.3 = (bf16[2,768,128]{2,1,0:T(8,128)(2,1)S(1)}, bf16[2,768,128]{2,1,0:T(8,128)(2,1)S(1)}, u32[]{:S(2)}, u32[]{:S(2)}) collective-permute-start(bf16[2,768,128]{2,1,0:T(8,128)(2,1)S(1)} %bitcast.7), channel_id=1, source_target_pairs={{0,16},{16,0},{1,17},{17,1},{2,18},{18,2},{3,19},{19,3},{4,20},{20... | collective-permute-start | bytes 1179656 | tf_op jit(solution)/shard_map/ppermute | solution.py:54

commit v17 on v16

--- a/solution.py
+++ b/solution.py
@@ -125,26 +125,24 @@
 
 
 def column_body(
-    w, place, limits, received, panels, link, widths, column_one, column_two, packed
+    w, place, limits, received, panels, link, widths, packed
 ):
     total = reduced(received)
+    inside = inside_limits(limits, 0, panels.shape, w)
+    lower = jnp.where(inside, panels[...], jnp.zeros_like(panels[...]))
     for s in range(2):
-        span = slice(s * w, (s + 1) * w)
+        first = slice(s * w, (s + 1) * w)
+        second = slice((2 + s) * w, (3 + s) * w)
         here_one = jnp.where(limits[s] > 0, 1.0, 0.0)
         here_two = jnp.where(limits[2 + s] > 0, 1.0, 0.0)
-        column = (-(total[:, span] * here_one)).astype(BF16)
-        column_one[:, span] = column
-        second = total[:, (2 + s) * w : (3 + s) * w] + dot(column, masked_link(w, link, widths, s))
-        column_two[:, span] = (-(second * here_two)).astype(BF16)
-    inside = inside_limits(limits, 0, panels.shape, w)
-    lower = jnp.where(inside, panels[...], jnp.zeros_like(panels[...]))
-    for n in range(packed.shape[0]):
-        span = slice((n // PAIR) * w, (n // PAIR + 1) * w)
-        packed[n, :, :w] = column_one[:, span]
-        packed[n, :, w : 2 * w] = column_two[:, span]
-        packed[n, :, 2 * w : 3 * w] = lower[:, span]
-        other = slice((2 + n // PAIR) * w, (3 + n // PAIR) * w)
-        packed[n, :, 3 * w :] = lower[:, other]
+        one = (-(total[:, first] * here_one)).astype(BF16)
+        two = total[:, second] + dot(one, masked_link(w, link, widths, s))
+        two = (-(two * here_two)).astype(BF16)
+        for n in range(s * PAIR, (s + 1) * PAIR):
+            packed[n, :, :w] = one
+            packed[n, :, w : 2 * w] = two
+            packed[n, :, 2 * w : 3 * w] = lower[:, first]
+            packed[n, :, 3 * w :] = lower[:, second]
 
 
 def sums_body(w, place, received, sums, held):
@@ -282,11 +280,11 @@
     got = lax.ppermute(give, "pair", [(0, 1), (1, 0)])
     (part,) = kernel_call(pair_sum_body, "pair_sum", [VMEM] * 2, [(half, BF16)])(keep, got)
     part = exchange(part, ("far", "mid"))
-    column_one, column_two, packed = kernel_call(
+    (packed,) = kernel_call(
         functools.partial(column_body, w),
         "columns",
         [SMEM] * 2 + [VMEM] * 3 + [SMEM],
-        [((share, 2 * w), BF16)] * 2 + [((CORES * PAIR,) + whole, BF16)],
+        [((CORES * PAIR,) + whole, BF16)],
     )(place, limits, part, lower, link_two, widths)
     sums = pl.pallas_call(
         functools.partial(sums_body, w),
@@ -307,6 +305,8 @@
     )(sums, pivot)
     mine = exchange(total, ("pair", "chip")).reshape(flat)
     other = swap_cores(mine)
+    column_one = jnp.concatenate([packed[0, :, :w], packed[PAIR, :, :w]], axis=1)
+    column_two = jnp.concatenate([packed[0, :, w : 2 * w], packed[PAIR, :, w : 2 * w]], axis=1)
     block_one, parent_rows, block_two = kernel_call(
         functools.partial(final_body, w),
         "final",

time: 141 us -> 140 us (level)
  transfers between devices with their start and end apart: 4 -> 4, of which waited for: 4 -> 4; matrix products, arithmetic and copies ran while one was open for 1% -> 2% of each run, Pallas kernels for 1% -> 1%
where the time goes in v17:
time: 140 us; the launch traced here: 139 us
  blocking collectives  97.5 us (70%)
  starting transfers between devices  20.9 us (15%)
  waiting for transfers between devices  8.86 us (6%)
  Pallas kernels  6.25 us (4%)
  local copies, waits for them, and re-layouts  3.33 us (2%)
  other arithmetic  1.65 us (1%)
    all_to_all x6, blocking collectives, exchange(): return lax.all_to_all(blocks, axis, split_axis=0, concat_axis=0, tiled=True)  97.5 us
    ppermute x2, starting transfers between devices, swap_cores(): return lax.ppermute(block, 'core', [(0, 1), (1, 0)])  10.3 us
    ppermute x1, starting transfers between devices, local(): moved = lax.ppermute(lower, GRID, pairs)  7.66 us
    ppermute x1, waiting for transfers between devices, local(): got = lax.ppermute(give, 'pair', [(0, 1), (1, 0)])  6.43 us
    ppermute x1, starting transfers between devices, local(): got = lax.ppermute(give, 'pair', [(0, 1), (1, 0)])  2.98 us
  transfers between devices with their start and end apart: 4, of which 4 were waited for; matrix products, arithmetic and copies ran while one was open for 2% of the time, Pallas kernels for 1%

profile of v17, /device:TPU:1, one launch (start us, length us, event | category | flops | bytes accessed | tf_op | source)
XLA Modules:
  0.0 139.3 jit_solution(16196065561801519594)
XLA Ops:
  0.6 0.0 copy-start.6
  0.6 0.7 constant_dynamic-update-slice_fusion.1
  1.4 0.0 copy-done.6
  1.4 7.7 %collective-permute-start = (bf16[16,1024]{1,0:T(8,128)(2,1)S(1)}, bf16[16,1024]{1,0:T(8,128)(2,1)S(1)}, u32[]{:S(2)}, u32[]{:S(2)}) collective-permute-start(bf16[16,1024]{1,0:T(8,128)(2,1)S(1)} %constant_dynamic-update-slice_fusion.panels), channel_id=1, source_target_pairs={{0,480},{1,448},{2,352},{3,416},{4,320},{5,224},{6,384},{7,288},{8... | collective-permute-start | bytes 98312 | tf_op jit(solution)/shard_map/ppermute | solution.py:237
  9.1 0.0 copy-start.7
  9.1 0.7 copy-done.7
  9.7 0.0 copy-start.8
  9.7 0.1 compare_reduce_fusion.3
  9.9 0.5 copy-done.8
  10.4 0.1 compare_reduce_fusion.2
  10.6 0.7 dynamic-slice_bitcast_fusion.order
  11.3 0.0 copy-start.3
  11.3 0.7 copy-done.3
  11.9 0.1 add_select_fusion.1
  12.0 0.1 pad_add_fusion.1.limits
  12.1 0.6 pad_add_fusion.place
  12.7 1.7 %pivot.1 = f32[48,128]{1,0:T(8,128)} custom-call(s32[3]{0:T(128)} %pad_add_fusion.place, bf16[2,256,256]{2,1,0:T(8,128)(2,1)} %one.1, bf16[2,256,256]{2,1,0:T(8,128)(2,1)} %two.1, s32[4]{0:T(128)} %widths.5), custom_call_target="tpu_custom_call" | custom-call | tf_op jit(solution)/shard_map/pivot/pallas_call | solution.py:244
  14.4 0.2 collective-permute-done.source
  14.7 0.0 copy-start.1
  14.7 24.6 %all_to_all.30.mine = bf16[16,16,1024]{2,1,0:T(8,128)(2,1)S(1)} all-to-all(bf16[16,16,1024]{2,1,0:T(8,128)(2,1)S(1)} %copies.1), channel_id=1, replica_groups=mesh['chip'=16,'core'=2,'far'=4,'mid'=2,'pair'=2] {'chip'}, dimensions={0} | all-to-all | bytes 1048576 | tf_op jit(solution)/shard_map/all_to_all | solution.py:35
  39.2 4.0 %collective-permute-start.1 = (bf16[16,16,1024]{2,1,0:T(8,128)(2,1)S(1)}, bf16[16,16,1024]{2,1,0:T(8,128)(2,1)S(1)}, u32[]{:S(2)}, u32[]{:S(2)}) collective-permute-start(bf16[16,16,1024]{2,1,0:T(8,128)(2,1)S(1)} %all_to_all.30.mine), channel_id=1, source_target_pairs={{0,16},{16,0},{1,17},{17,1},{2,18},{18,2},{3,19},{19,3},{4,20},{20... | collective-permute-start | bytes 1572872 | tf_op jit(solution)/shard_map/ppermute | solution.py:54
  43.3 1.5 %collective-permute-done.1.other = bf16[16,16,1024]{2,1,0:T(8,128)(2,1)S(1)} collective-permute-done((bf16[16,16,1024]{2,1,0:T(8,128)(2,1)S(1)}, bf16[16,16,1024]{2,1,0:T(8,128)(2,1)S(1)}, u32[]{:S(2)}, u32[]{:S(2)}) %collective-permute-start.1) | collective-permute-done | bytes 524320 | tf_op jit(solution)/shard_map/ppermute | solution.py:54
  44.8 0.0 copy-done.1
  44.8 1.0 product.1
  45.8 3.0 %collective-permute-start.2 = (bf16[8,16,1024]{2,1,0:T(8,128)(2,1)S(1)}, bf16[8,16,1024]{2,1,0:T(8,128)(2,1)S(1)}, u32[]{:S(2)}, u32[]{:S(2)}) collective-permute-start(bf16[8,16,1024]{2,1,0:T(8,128)(2,1)S(1)} %get-tuple-element.22), channel_id=1, source_target_pairs={{0,1},{1,0},{2,3},{3,2},{4,5},{5,4},{6,7},{7,6},{8,9},{9,8},{10,11... | collective-permute-start | bytes 786440 | tf_op jit(solution)/shard_map/ppermute | solution.py:280
  48.8 6.4 %collective-permute-done.2.got = bf16[8,16,1024]{2,1,0:T(8,128)(2,1)S(1)} collective-permute-done((bf16[8,16,1024]{2,1,0:T(8,128)(2,1)S(1)}, bf16[8,16,1024]{2,1,0:T(8,128)(2,1)S(1)}, u32[]{:S(2)}, u32[]{:S(2)}) %collective-permute-start.2) | collective-permute-done | bytes 262176 | tf_op jit(solution)/shard_map/ppermute | solution.py:280
  55.2 0.1 pair_sum.1
  55.3 0.0 copy-start
  55.3 0.0 copy-start.4
  55.3 0.0 copy-start.5
  55.3 23.6 %all_to_all.31.received = bf16[8,16,1024]{2,1,0:T(8,128)(2,1)S(1)} all-to-all(bf16[8,16,1024]{2,1,0:T(8,128)(2,1)S(1)} %pair_sum.1), channel_id=1, replica_groups=mesh['chip'=16,'core'=2,'far'=4,'mid'=2,'pair'=2] {'far','mid'}, dimensions={0} | all-to-all | bytes 524288 | tf_op jit(solution)/shard_map/all_to_all | solution.py:35
  79.0 0.0 copy-done
  79.0 0.0 copy-done.4
  79.0 0.0 copy-done.5
  79.0 0.8 columns.1
  79.8 12.6 %all_to_all.32.received = bf16[4,16,1024]{2,1,0:T(8,128)(2,1)S(1)} all-to-all(bf16[4,16,1024]{2,1,0:T(8,128)(2,1)S(1)} %columns.1), channel_id=1, replica_groups=mesh['chip'=16,'core'=2,'far'=4,'mid'=2,'pair'=2] {'core','pair'}, dimensions={0} | all-to-all | bytes 262144 | tf_op jit(solution)/shard_map/all_to_all | solution.py:35
  92.3 0.8 sums.1
  93.1 9.8 %all_to_all.33.received = bf16[16,48,128]{2,1,0:T(8,128)(2,1)S(1)} all-to-all(bf16[16,48,128]{2,1,0:T(8,128)(2,1)S(1)} %bitcast.17), channel_id=1, replica_groups=mesh['chip'=16,'core'=2,'far'=4,'mid'=2,'pair'=2] {'chip'}, dimensions={0} | all-to-all | bytes 393216 | tf_op jit(solution)/shard_map/all_to_all | solution.py:35
  102.9 0.0 copy-start.2
  102.9 15.1 %all_to_all.34.received = bf16[8,48,128]{2,1,0:T(8,128)(2,1)S(1)} all-to-all(bf16[8,48,128]{2,1,0:T(8,128)(2,1)S(1)} %chunk_sum.1), channel_id=1, replica_groups=mesh['chip'=16,'core'=2,'far'=4,'mid'=2,'pair'=2] {'far','mid'}, dimensions={0} | all-to-all | bytes 196608 | tf_op jit(solution)/shard_map/all_to_all | solution.py:35
  118.0 0.0 copy-done.2
  118.0 11.9 %all_to_all.35 = bf16[32,48,128]{2,1,0:T(8,128)(2,1)S(1)} all-to-all(bf16[32,48,128]{2,1,0:T(8,128)(2,1)S(1)} %all_sum.1), channel_id=1, replica_groups=mesh['chip'=16,'core'=2,'far'=4,'mid'=2,'pair'=2] {'pair','chip'}, dimensions={0} | all-to-all | bytes 786432 | tf_op jit(solution)/shard_map/all_to_all | solution.py:35
  129.9 6.3 %collective-permute-start.3 = (bf16[2,768,128]{2,1,0:T(8,128)(2,1)S(1)}, bf16[2,768,128]{2,1,0:T(8,128)(2,1)S(1)}, u32[]{:S(2)}, u32[]{:S(2)}) collective-permute-start(bf16[2,768,128]{2,1,0:T(8,128)(2,1)S(1)} %bitcast.15), channel_id=1, source_target_pairs={{0,16},{16,0},{1,17},{17,1},{2,18},{18,2},{3,19},{19,3},{4,20},{20... | collective-permute-start | bytes 1179656 | tf_op jit(solution)/shard_map/ppermute | solution.py:54
  136.2 0.6 pad_maximum_fusion
  136.8 0.7 collective-permute-done.3.other
  137.5 1.7 %final.1 = (bf16[2,256,256]{2,1,0:T(8,128)(2,1)}, bf16[2,256,256]{2,1,0:T(8,128)(2,1)}, bf16[2,256,256]{2,1,0:T(8,128)(2,1)}) custom-call(s32[1]{0:T(128)} %bitcast.1.core, bf16[2,768,128]{2,1,0:T(8,128)(2,1)S(1)} %bitcast.16, bf16[2,768,128]{2,1,0:T(8,128)(2,1)S(1)} %collective-permute-done.3.other, bf16[2,256,256]{2,1,0:T(8,128)(2,1)S(1)} %copy-done, ...), custom_call_target="tpu_custom_call" | custom-call | tf_op jit(solution)/shard_map/final/pallas_call | solution.py:310
  (5 shorter events, 0.1 us)
Async XLA Ops:
  0.6 0.7 copy-start.6
  1.4 13.2 %collective-permute-start = (bf16[16,1024]{1,0:T(8,128)(2,1)S(1)}, bf16[16,1024]{1,0:T(8,128)(2,1)S(1)}, u32[]{:S(2)}, u32[]{:S(2)}) collective-permute-start(bf16[16,1024]{1,0:T(8,128)(2,1)S(1)} %constant_dynamic-update-slice_fusion.panels), channel_id=1, source_target_pairs={{0,480},{1,448},{2,352},{3,416},{4,320},{5,224},{6,384},{7,288},{8... | collective-permute-start | bytes 98312 | tf_op jit(solution)/shard_map/ppermute | solution.py:237
  9.1 0.7 copy-start.7
  9.7 0.7 copy-start.8
  11.3 0.7 copy-start.3
  14.7 30.1 %copy-start.1 = (bf16[256,512]{1,0:T(8,128)(2,1)S(1)}, bf16[256,512]{1,0:T(8,128)(2,1)}, u32[]{:S(2)}) copy-start(bf16[256,512]{1,0:T(8,128)(2,1)} %inverse.1) | copy-start | bytes 786436
  39.2 5.5 %collective-permute-start.1 = (bf16[16,16,1024]{2,1,0:T(8,128)(2,1)S(1)}, bf16[16,16,1024]{2,1,0:T(8,128)(2,1)S(1)}, u32[]{:S(2)}, u32[]{:S(2)}) collective-permute-start(bf16[16,16,1024]{2,1,0:T(8,128)(2,1)S(1)} %all_to_all.30.mine), channel_id=1, source_target_pairs={{0,16},{16,0},{1,17},{17,1},{2,18},{18,2},{3,19},{19,3},{4,20},{20... | collective-permute-start | bytes 1572872 | tf_op jit(solution)/shard_map/ppermute | solution.py:54
  45.8 9.4 %collective-permute-start.2 = (bf16[8,16,1024]{2,1,0:T(8,128)(2,1)S(1)}, bf16[8,16,1024]{2,1,0:T(8,128)(2,1)S(1)}, u32[]{:S(2)}, u32[]{:S(2)}) collective-permute-start(bf16[8,16,1024]{2,1,0:T(8,128)(2,1)S(1)} %get-tuple-element.22), channel_id=1, source_target_pairs={{0,1},{1,0},{2,3},{3,2},{4,5},{5,4},{6,7},{7,6},{8,9},{9,8},{10,11... | collective-permute-start | bytes 786440 | tf_op jit(solution)/shard_map/ppermute | solution.py:280
  55.3 23.7 %copy-start = (bf16[2,256,256]{2,1,0:T(8,128)(2,1)S(1)}, bf16[2,256,256]{2,1,0:T(8,128)(2,1)}, u32[]{:S(2)}) copy-start(bf16[2,256,256]{2,1,0:T(8,128)(2,1)} %link.3) | copy-start | bytes 786436
  55.3 23.7 %copy-start.4 = (s32[4]{0:T(128)S(1)}, s32[4]{0:T(128)}, u32[]{:S(2)}) copy-start(s32[4]{0:T(128)} %widths.5) | copy-start | bytes 52
  55.3 23.7 %copy-start.5 = (s32[3]{0:T(128)S(1)}, s32[3]{0:T(128)}, u32[]{:S(2)}) copy-start(s32[3]{0:T(128)} %pad_add_fusion.place) | copy-start | bytes 40
  102.9 15.1 %copy-start.2 = (f32[48,128]{1,0:T(8,128)S(1)}, f32[48,128]{1,0:T(8,128)}, u32[]{:S(2)}) copy-start(f32[48,128]{1,0:T(8,128)} %pivot.1) | copy-start | bytes 73732
  129.9 7.6 %collective-permute-start.3 = (bf16[2,768,128]{2,1,0:T(8,128)(2,1)S(1)}, bf16[2,768,128]{2,1,0:T(8,128)(2,1)S(1)}, u32[]{:S(2)}, u32[]{:S(2)}) collective-permute-start(bf16[2,768,128]{2,1,0:T(8,128)(2,1)S(1)} %bitcast.15), channel_id=1, source_target_pairs={{0,16},{16,0},{1,17},{17,1},{2,18},{18,2},{3,19},{19,3},{4,20},{20... | collective-permute-start | bytes 1179656 | tf_op jit(solution)/shard_map/ppermute | solution.py:54

commit v18 on v17

--- a/solution.py
+++ b/solution.py
@@ -257,8 +257,8 @@
             column_limits(ancestors, widths, plane * CORES + 1 - core),
         ]
     )
-    moved, order, place, pivot, limits, away_limits = lax.optimization_barrier(
-        (moved, order, place, pivot, limits, away_limits)
+    moved, order, limits, away_limits = lax.optimization_barrier(
+        (moved, order, limits, away_limits)
     )
     (moved,) = kernel_call(copy_body, "copies", [VMEM], [((chips,) + whole, BF16)])(moved)
     mine = exchange(moved, "chip")
@@ -278,6 +278,7 @@
         compiler_params=pltpu.CompilerParams(vmem_limit_bytes=40 * 1024 * 1024),
     )(core_ref, parity.reshape(1), order, away_limits, ancestor_inverse, mine, other)
     got = lax.ppermute(give, "pair", [(0, 1), (1, 0)])
+    got, place, pivot = lax.optimization_barrier((got, place, pivot))
     (part,) = kernel_call(pair_sum_body, "pair_sum", [VMEM] * 2, [(half, BF16)])(keep, got)
     part = exchange(part, ("far", "mid"))
     (packed,) = kernel_call(

time: 140 us -> 140 us (level)
    ppermute x1, waiting for transfers between devices: 6.43 us -> 4.1 us  [local(): got = lax.ppermute(give, 'pair', [(0, 1), (1, 0)])]
    ppermute x1, waiting for transfers between devices: 0.22 us -> 2.54 us  [local(): moved = lax.ppermute(lower, GRID, pairs)]
where the time goes in v18:
time: 140 us; the launch traced here: 139 us
  blocking collectives  97.5 us (70%)
  starting transfers between devices  20.8 us (15%)
  waiting for transfers between devices  8.85 us (6%)
  Pallas kernels  6.25 us (4%)
  local copies, waits for them, and re-layouts  3.33 us (2%)
  other arithmetic  1.65 us (1%)
    all_to_all x6, blocking collectives, exchange(): return lax.all_to_all(blocks, axis, split_axis=0, concat_axis=0, tiled=True)  97.5 us
    ppermute x2, starting transfers between devices, swap_cores(): return lax.ppermute(block, 'core', [(0, 1), (1, 0)])  10.2 us
    ppermute x1, starting transfers between devices, local(): moved = lax.ppermute(lower, GRID, pairs)  7.66 us
    ppermute x1, waiting for transfers between devices, local(): got = lax.ppermute(give, 'pair', [(0, 1), (1, 0)])  4.1 us
    ppermute x1, starting transfers between devices, local(): got = lax.ppermute(give, 'pair', [(0, 1), (1, 0)])  2.97 us
  transfers between devices with their start and end apart: 4, of which 4 were waited for; matrix products, arithmetic and copies ran while one was open for 2% of the time, Pallas kernels for 1%

profile of v18, /device:TPU:1, one launch (start us, length us, event | category | flops | bytes accessed | tf_op | source)
XLA Modules:
  0.0 139.2 jit_solution(1329542758306605922)
XLA Ops:
  0.6 0.0 copy-start.6
  0.6 0.7 constant_dynamic-update-slice_fusion.1
  1.4 0.0 copy-done.6
  1.4 7.7 %collective-permute-start = (bf16[16,1024]{1,0:T(8,128)(2,1)S(1)}, bf16[16,1024]{1,0:T(8,128)(2,1)S(1)}, u32[]{:S(2)}, u32[]{:S(2)}) collective-permute-start(bf16[16,1024]{1,0:T(8,128)(2,1)S(1)} %constant_dynamic-update-slice_fusion.panels), channel_id=1, source_target_pairs={{0,480},{1,448},{2,352},{3,416},{4,320},{5,224},{6,384},{7,288},{8... | collective-permute-start | bytes 98312 | tf_op jit(solution)/shard_map/ppermute | solution.py:237
  9.1 0.0 copy-start.7
  9.1 0.7 copy-done.7
  9.7 0.0 copy-start.8
  9.7 0.1 compare_reduce_fusion.2
  9.9 0.5 copy-done.8
  10.4 0.1 compare_reduce_fusion.3
  10.6 0.7 dynamic-slice_bitcast_fusion.order
  11.3 0.0 copy-start.3
  11.3 0.7 copy-done.3
  11.9 0.1 add_select_fusion.1
  12.0 0.1 pad_add_fusion.limits
  12.1 2.5 %collective-permute-done.source = bf16[16,1024]{1,0:T(8,128)(2,1)S(1)} collective-permute-done((bf16[16,1024]{1,0:T(8,128)(2,1)S(1)}, bf16[16,1024]{1,0:T(8,128)(2,1)S(1)}, u32[]{:S(2)}, u32[]{:S(2)}) %collective-permute-start) | collective-permute-done | bytes 32800 | tf_op jit(solution)/shard_map/ppermute | solution.py:237
  14.7 0.0 copy-start.1
  14.7 22.2 %all_to_all.30.mine = bf16[16,16,1024]{2,1,0:T(8,128)(2,1)S(1)} all-to-all(bf16[16,16,1024]{2,1,0:T(8,128)(2,1)S(1)} %copies.1), channel_id=1, replica_groups=mesh['chip'=16,'core'=2,'far'=4,'mid'=2,'pair'=2] {'chip'}, dimensions={0} | all-to-all | bytes 1048576 | tf_op jit(solution)/shard_map/all_to_all | solution.py:35
  36.9 4.0 %collective-permute-start.1 = (bf16[16,16,1024]{2,1,0:T(8,128)(2,1)S(1)}, bf16[16,16,1024]{2,1,0:T(8,128)(2,1)S(1)}, u32[]{:S(2)}, u32[]{:S(2)}) collective-permute-start(bf16[16,16,1024]{2,1,0:T(8,128)(2,1)S(1)} %all_to_all.30.mine), channel_id=1, source_target_pairs={{0,16},{16,0},{1,17},{17,1},{2,18},{18,2},{3,19},{19,3},{4,20},{20... | collective-permute-start | bytes 1572872 | tf_op jit(solution)/shard_map/ppermute | solution.py:54
  40.9 1.5 %collective-permute-done.1.other = bf16[16,16,1024]{2,1,0:T(8,128)(2,1)S(1)} collective-permute-done((bf16[16,16,1024]{2,1,0:T(8,128)(2,1)S(1)}, bf16[16,16,1024]{2,1,0:T(8,128)(2,1)S(1)}, u32[]{:S(2)}, u32[]{:S(2)}) %collective-permute-start.1) | collective-permute-done | bytes 524320 | tf_op jit(solution)/shard_map/ppermute | solution.py:54
  42.5 0.0 copy-done.1
  42.5 1.0 product.1
  43.5 3.0 %collective-permute-start.2 = (bf16[8,16,1024]{2,1,0:T(8,128)(2,1)S(1)}, bf16[8,16,1024]{2,1,0:T(8,128)(2,1)S(1)}, u32[]{:S(2)}, u32[]{:S(2)}) collective-permute-start(bf16[8,16,1024]{2,1,0:T(8,128)(2,1)S(1)} %get-tuple-element.20), channel_id=1, source_target_pairs={{0,1},{1,0},{2,3},{3,2},{4,5},{5,4},{6,7},{7,6},{8,9},{9,8},{10,11... | collective-permute-start | bytes 786440 | tf_op jit(solution)/shard_map/ppermute | solution.py:280
  46.5 0.6 pad_add_fusion.1.place
  47.1 1.7 %pivot.1 = f32[48,128]{1,0:T(8,128)} custom-call(s32[3]{0:T(128)} %pad_add_fusion.1.place, bf16[2,256,256]{2,1,0:T(8,128)(2,1)} %one.1, bf16[2,256,256]{2,1,0:T(8,128)(2,1)} %two.1, s32[4]{0:T(128)} %widths.5), custom_call_target="tpu_custom_call" | custom-call | tf_op jit(solution)/shard_map/pivot/pallas_call | solution.py:244
  48.8 4.1 %collective-permute-done.2.got = bf16[8,16,1024]{2,1,0:T(8,128)(2,1)S(1)} collective-permute-done((bf16[8,16,1024]{2,1,0:T(8,128)(2,1)S(1)}, bf16[8,16,1024]{2,1,0:T(8,128)(2,1)S(1)}, u32[]{:S(2)}, u32[]{:S(2)}) %collective-permute-start.2) | collective-permute-done | bytes 262176 | tf_op jit(solution)/shard_map/ppermute | solution.py:280
  52.9 0.1 pair_sum.1
  53.0 0.0 copy-start
  53.0 0.0 copy-start.4
  53.0 0.0 copy-start.5
  53.0 26.0 %all_to_all.31.received = bf16[8,16,1024]{2,1,0:T(8,128)(2,1)S(1)} all-to-all(bf16[8,16,1024]{2,1,0:T(8,128)(2,1)S(1)} %pair_sum.1), channel_id=1, replica_groups=mesh['chip'=16,'core'=2,'far'=4,'mid'=2,'pair'=2] {'far','mid'}, dimensions={0} | all-to-all | bytes 524288 | tf_op jit(solution)/shard_map/all_to_all | solution.py:35
  79.0 0.0 copy-done
  79.0 0.0 copy-done.4
  79.0 0.0 copy-done.5
  79.0 0.8 columns.1
  79.8 12.5 %all_to_all.32.received = bf16[4,16,1024]{2,1,0:T(8,128)(2,1)S(1)} all-to-all(bf16[4,16,1024]{2,1,0:T(8,128)(2,1)S(1)} %columns.1), channel_id=1, replica_groups=mesh['chip'=16,'core'=2,'far'=4,'mid'=2,'pair'=2] {'core','pair'}, dimensions={0} | all-to-all | bytes 262144 | tf_op jit(solution)/shard_map/all_to_all | solution.py:35
  92.3 0.8 sums.1
  93.1 9.8 %all_to_all.33.received = bf16[16,48,128]{2,1,0:T(8,128)(2,1)S(1)} all-to-all(bf16[16,48,128]{2,1,0:T(8,128)(2,1)S(1)} %bitcast.17), channel_id=1, replica_groups=mesh['chip'=16,'core'=2,'far'=4,'mid'=2,'pair'=2] {'chip'}, dimensions={0} | all-to-all | bytes 393216 | tf_op jit(solution)/shard_map/all_to_all | solution.py:35
  102.9 0.0 copy-start.2
  102.9 15.1 %all_to_all.34.received = bf16[8,48,128]{2,1,0:T(8,128)(2,1)S(1)} all-to-all(bf16[8,48,128]{2,1,0:T(8,128)(2,1)S(1)} %chunk_sum.1), channel_id=1, replica_groups=mesh['chip'=16,'core'=2,'far'=4,'mid'=2,'pair'=2] {'far','mid'}, dimensions={0} | all-to-all | bytes 196608 | tf_op jit(solution)/shard_map/all_to_all | solution.py:35
  118.0 0.0 copy-done.2
  118.0 11.9 %all_to_all.35 = bf16[32,48,128]{2,1,0:T(8,128)(2,1)S(1)} all-to-all(bf16[32,48,128]{2,1,0:T(8,128)(2,1)S(1)} %all_sum.1), channel_id=1, replica_groups=mesh['chip'=16,'core'=2,'far'=4,'mid'=2,'pair'=2] {'pair','chip'}, dimensions={0} | all-to-all | bytes 786432 | tf_op jit(solution)/shard_map/all_to_all | solution.py:35
  129.9 6.2 %collective-permute-start.3 = (bf16[2,768,128]{2,1,0:T(8,128)(2,1)S(1)}, bf16[2,768,128]{2,1,0:T(8,128)(2,1)S(1)}, u32[]{:S(2)}, u32[]{:S(2)}) collective-permute-start(bf16[2,768,128]{2,1,0:T(8,128)(2,1)S(1)} %bitcast.15), channel_id=1, source_target_pairs={{0,16},{16,0},{1,17},{17,1},{2,18},{18,2},{3,19},{19,3},{4,20},{20... | collective-permute-start | bytes 1179656 | tf_op jit(solution)/shard_map/ppermute | solution.py:54
  136.2 0.6 pad_maximum_fusion
  136.8 0.7 collective-permute-done.3.other
  137.5 1.7 %final.1 = (bf16[2,256,256]{2,1,0:T(8,128)(2,1)}, bf16[2,256,256]{2,1,0:T(8,128)(2,1)}, bf16[2,256,256]{2,1,0:T(8,128)(2,1)}) custom-call(s32[1]{0:T(128)} %bitcast.core, bf16[2,768,128]{2,1,0:T(8,128)(2,1)S(1)} %bitcast.16, bf16[2,768,128]{2,1,0:T(8,128)(2,1)S(1)} %collective-permute-done.3.other, bf16[2,256,256]{2,1,0:T(8,128)(2,1)S(1)} %copy-done, ...), custom_call_target="tpu_custom_call" | custom-call | tf_op jit(solution)/shard_map/final/pallas_call | solution.py:311
  (5 shorter events, 0.1 us)
Async XLA Ops:
  0.6 0.7 copy-start.6
  1.4 13.2 %collective-permute-start = (bf16[16,1024]{1,0:T(8,128)(2,1)S(1)}, bf16[16,1024]{1,0:T(8,128)(2,1)S(1)}, u32[]{:S(2)}, u32[]{:S(2)}) collective-permute-start(bf16[16,1024]{1,0:T(8,128)(2,1)S(1)} %constant_dynamic-update-slice_fusion.panels), channel_id=1, source_target_pairs={{0,480},{1,448},{2,352},{3,416},{4,320},{5,224},{6,384},{7,288},{8... | collective-permute-start | bytes 98312 | tf_op jit(solution)/shard_map/ppermute | solution.py:237
  9.1 0.7 copy-start.7
  9.7 0.7 copy-start.8
  11.3 0.7 copy-start.3
  14.7 27.8 %copy-start.1 = (bf16[256,512]{1,0:T(8,128)(2,1)S(1)}, bf16[256,512]{1,0:T(8,128)(2,1)}, u32[]{:S(2)}) copy-start(bf16[256,512]{1,0:T(8,128)(2,1)} %inverse.1) | copy-start | bytes 786436
  36.9 5.5 %collective-permute-start.1 = (bf16[16,16,1024]{2,1,0:T(8,128)(2,1)S(1)}, bf16[16,16,1024]{2,1,0:T(8,128)(2,1)S(1)}, u32[]{:S(2)}, u32[]{:S(2)}) collective-permute-start(bf16[16,16,1024]{2,1,0:T(8,128)(2,1)S(1)} %all_to_all.30.mine), channel_id=1, source_target_pairs={{0,16},{16,0},{1,17},{17,1},{2,18},{18,2},{3,19},{19,3},{4,20},{20... | collective-permute-start | bytes 1572872 | tf_op jit(solution)/shard_map/ppermute | solution.py:54
  43.5 9.4 %collective-permute-start.2 = (bf16[8,16,1024]{2,1,0:T(8,128)(2,1)S(1)}, bf16[8,16,1024]{2,1,0:T(8,128)(2,1)S(1)}, u32[]{:S(2)}, u32[]{:S(2)}) collective-permute-start(bf16[8,16,1024]{2,1,0:T(8,128)(2,1)S(1)} %get-tuple-element.20), channel_id=1, source_target_pairs={{0,1},{1,0},{2,3},{3,2},{4,5},{5,4},{6,7},{7,6},{8,9},{9,8},{10,11... | collective-permute-start | bytes 786440 | tf_op jit(solution)/shard_map/ppermute | solution.py:280
  53.0 26.0 %copy-start = (bf16[2,256,256]{2,1,0:T(8,128)(2,1)S(1)}, bf16[2,256,256]{2,1,0:T(8,128)(2,1)}, u32[]{:S(2)}) copy-start(bf16[2,256,256]{2,1,0:T(8,128)(2,1)} %link.3) | copy-start | bytes 786436
  53.0 26.0 %copy-start.4 = (s32[4]{0:T(128)S(1)}, s32[4]{0:T(128)}, u32[]{:S(2)}) copy-start(s32[4]{0:T(128)} %widths.5) | copy-start | bytes 52
  53.0 26.0 %copy-start.5 = (s32[3]{0:T(128)S(1)}, s32[3]{0:T(128)}, u32[]{:S(2)}) copy-start(s32[3]{0:T(128)} %pad_add_fusion.1.place) | copy-start | bytes 40
  102.9 15.1 %copy-start.2 = (f32[48,128]{1,0:T(8,128)S(1)}, f32[48,128]{1,0:T(8,128)}, u32[]{:S(2)}) copy-start(f32[48,128]{1,0:T(8,128)} %pivot.1) | copy-start | bytes 73732
  129.9 7.5 %collective-permute-start.3 = (bf16[2,768,128]{2,1,0:T(8,128)(2,1)S(1)}, bf16[2,768,128]{2,1,0:T(8,128)(2,1)S(1)}, u32[]{:S(2)}, u32[]{:S(2)}) collective-permute-start(bf16[2,768,128]{2,1,0:T(8,128)(2,1)S(1)} %bitcast.15), channel_id=1, source_target_pairs={{0,16},{16,0},{1,17},{17,1},{2,18},{18,2},{3,19},{19,3},{4,20},{20... | collective-permute-start | bytes 1179656 | tf_op jit(solution)/shard_map/ppermute | solution.py:54
